TPU v7x, 32 devices: a whole 2x2x4 slice. The times are simulated.
32 devices in a mesh: dp: 4 (over y, x), seq: 8 (over z, core).
Axes of the slice: x: 2, y: 2, z: 4, core: 2. Of those that a mesh axis runs over, the one named last changes fastest.
Arguments:
- tokens: bfloat16 [4, 1024, 2048], P('dp', 'seq'), may hold values from -6 to 6
- teacher: bfloat16 [4, 1024, 2048], P('dp', 'seq'), may hold values from -6 to 6
- valid: int32 [4, 1024], P('dp', 'seq'), may hold values from 0 to 1, as said below
- positions: int32 [4, 1024], P('dp', 'seq'), may hold values from 0 to 1023, as said below
- norm_gain: bfloat16 [2048], replicated, may hold values from 0.5 to 1.5
- norm_bias: bfloat16 [2048], replicated, may hold values from -1 to 1
- qkv_weight: bfloat16 [2048, 6144], P('dp'), may hold values from -0.21875 to 0.21875
- qkv_bias: bfloat16 [6144], replicated, may hold values from -1 to 1
- out_weight: bfloat16 [2048, 2048], P(None, 'dp'), may hold values from -0.25 to 0.25
- out_bias: bfloat16 [2048], replicated, may hold values from -1 to 1
- up_weight: bfloat16 [2048, 8192], P('dp'), may hold values from -0.125 to 0.125
- up_bias: bfloat16 [8192], replicated, may hold values from -1 to 1
- down_weight: bfloat16 [8192, 2048], P(None, 'dp'), may hold values from -0.0625 to 0.0625
- down_bias: bfloat16 [2048], replicated, may hold values from -1 to 1
Outputs:
- loss: float32 [], replicated
- tokens_grad: float32 [4, 1024, 2048], P('dp', 'seq')
- norm_gain_grad: float32 [2048], replicated
- norm_bias_grad: float32 [2048], replicated
- qkv_weight_grad: float32 [2048, 6144], P('dp')
- qkv_bias_grad: float32 [6144], replicated
- out_weight_grad: float32 [2048, 2048], P(None, 'dp')
- out_bias_grad: float32 [2048], replicated
- up_weight_grad: float32 [2048, 8192], P('dp')
- up_bias_grad: float32 [8192], replicated
- down_weight_grad: float32 [8192, 2048], P(None, 'dp')
- down_bias_grad: float32 [2048], replicated
Inputs may be any that keep to these rules, and one draw needn't show every extreme that they name: `valid`: in each sequence the last 1 to 256 positions are 0 and all others 1. `positions`: in each sequence the ids count up by one from 0 at the first position and fall back to 0 where a packed document starts; the first sequence is one document, every other holds two or more.
All inputs are finite; a program needn't handle non-finite values.
Results may differ from a plain program's by a relative error of at most 0.008.
The roundings to bfloat16 on the way count: a program that leaves them out, or rounds other values in their place, can miss the bound.
Values may be sent and summed in bfloat16 or wider, within the bound.
No kernel may reach another device: no remote copies, remote signals or barrier semaphores. Data moves between devices by JAX's collectives and lax.ppermute only.
A program may use at most 512 MiB of HBM per device.

v0:
```python
import jax
import jax.numpy as jnp
from jax import lax
from jax.sharding import PartitionSpec as P

HEADS = 32
HEAD_DIM = 64
ROTARY = 32


norm_eps = 1e-05
rope_base = 10000.0
masked_fill = -1e30


def layer_norm(values, gain, shift):
    centre = values - jnp.mean(values, axis=-1, keepdims=True)
    spread = jnp.mean(centre * centre, axis=-1, keepdims=True)
    return centre * lax.rsqrt(spread + norm_eps) * gain + shift


def gelu_tanh(values):
    return jax.nn.gelu(values, approximate=True)


def rotate(block, where):
    half = ROTARY // 2
    freqs = rope_base ** (-(jnp.arange(half, dtype=jnp.float32) * 2.0) / ROTARY)
    angles = where.astype(jnp.float32)[:, None] * freqs[None, :]
    cosine = jnp.cos(angles)[:, None, :]
    sine = jnp.sin(angles)[:, None, :]
    first = block[..., :half]
    second = block[..., half:ROTARY]
    return jnp.concatenate(
        [first * cosine - second * sine, second * cosine + first * sine, block[..., ROTARY:]],
        axis=-1,
    )


def causal_scores(rows, keys, start, scale):
    block = rows.shape[0]
    length = keys.shape[0]
    raw = jnp.einsum("bhd,khd->hbk", rows, keys, preferred_element_type=jnp.float32) * scale
    row_index = start + jnp.arange(block, dtype=jnp.int32)
    col_index = jnp.arange(length, dtype=jnp.int32)
    allowed = col_index[None, None, :] <= row_index[None, :, None]
    return jnp.where(allowed, raw, masked_fill)


def attend(query, keys, values, block):
    length = query.shape[0]
    scale = HEAD_DIM ** (-0.5)

    def one_block(carry, index):
        start = index * block
        rows = lax.dynamic_slice_in_dim(query, start, block, 0)
        scores = causal_scores(rows, keys, start, scale)
        top = jnp.max(scores, axis=-1, keepdims=True)
        expd = jnp.exp(scores - top)
        total = jnp.sum(expd, axis=-1, keepdims=True)
        probs = (expd / total).astype(jnp.bfloat16)
        result = jnp.einsum("hbk,khd->bhd", probs, values, preferred_element_type=jnp.float32)
        return (carry, (result, top[..., 0] + jnp.log(total[..., 0])))

    _, (outs, logsum) = lax.scan(one_block, None, jnp.arange(length // block, dtype=jnp.int32))
    return (outs.reshape(length, query.shape[1] * query.shape[2]), logsum)


def attend_back(query, keys, values, logsum, upstream_all, block):
    length = query.shape[0]
    scale = HEAD_DIM ** (-0.5)

    def one_block(carry, item):
        key_total, value_total = carry
        index, block_logsum = item
        start = index * block
        rows = lax.dynamic_slice_in_dim(query, start, block, 0)
        upstream = lax.dynamic_slice_in_dim(upstream_all, start, block, 0)
        scores = causal_scores(rows, keys, start, scale)
        probs = jnp.exp(scores - block_logsum[..., None])
        probs_low = probs.astype(jnp.bfloat16)
        prob_grad = jnp.einsum("bhd,khd->hbk", upstream, values, preferred_element_type=jnp.float32)
        inner = jnp.sum(probs * prob_grad, axis=-1, keepdims=True)
        score_grad = (probs * (prob_grad - inner)).astype(jnp.bfloat16)
        row_grad = (
            jnp.einsum("hbk,khd->bhd", score_grad, keys, preferred_element_type=jnp.float32) * scale
        )
        key_total = (
            key_total
            + jnp.einsum("hbk,bhd->khd", score_grad, rows, preferred_element_type=jnp.float32)
            * scale
        )
        value_total = value_total + jnp.einsum(
            "hbk,bhd->khd", probs_low, upstream, preferred_element_type=jnp.float32
        )
        return ((key_total, value_total), row_grad)

    zeros = jnp.zeros(keys.shape, jnp.float32)
    indices = jnp.arange(length // block, dtype=jnp.int32)
    (key_grad, value_grad), row_grads = lax.scan(one_block, (zeros, zeros), (indices, logsum))
    return (
        row_grads.reshape(length, -1),
        key_grad.reshape(length, -1),
        value_grad.reshape(length, -1),
    )


def local(
    tokens,
    teacher,
    valid,
    positions,
    norm_gain,
    norm_bias,
    qkv_weight,
    qkv_bias,
    out_weight,
    out_bias,
    up_weight,
    up_bias,
    down_weight,
    down_bias,
):
    inputs = tokens[0].astype(jnp.float32)
    target = teacher[0].astype(jnp.float32)
    mask = valid[0].astype(jnp.float32)
    where = positions[0]
    rows_here, width = inputs.shape
    seq_count = lax.axis_size("seq")
    data_count = lax.axis_size("dp")
    length = rows_here * seq_count
    block = min(512, length)
    local_heads = HEADS // seq_count
    gain = norm_gain.astype(jnp.float32)
    shift = norm_bias.astype(jnp.float32)
    qkv_bias_full = qkv_bias.astype(jnp.float32)
    up_bias_full = up_bias.astype(jnp.float32)
    b_out = out_bias.astype(jnp.float32)
    b_down = down_bias.astype(jnp.float32)
    normed, norm_back = jax.vjp(layer_norm, inputs, gain, shift)
    normed_low = normed.astype(jnp.bfloat16)
    w_qkv, w_up, w_out, w_down = (
        lax.all_gather(qkv_weight, "dp", axis=0, tiled=True),
        lax.all_gather(up_weight, "dp", axis=0, tiled=True),
        lax.all_gather(out_weight, "dp", axis=1, tiled=True),
        lax.all_gather(down_weight, "dp", axis=1, tiled=True),
    )
    mixed = jnp.dot(normed_low, w_qkv, preferred_element_type=jnp.float32) + qkv_bias_full
    query_pre = mixed[:, :width].reshape(rows_here, HEADS, HEAD_DIM)
    keys_pre = mixed[:, width : 2 * width].reshape(rows_here, HEADS, HEAD_DIM)
    query, query_turn = jax.vjp(lambda part_block: rotate(part_block, where), query_pre)
    keys, keys_turn = jax.vjp(lambda part_block: rotate(part_block, where), keys_pre)
    sent = jnp.stack(
        [query.reshape(rows_here, width), keys.reshape(rows_here, width), mixed[:, 2 * width :]],
        axis=1,
    ).astype(jnp.bfloat16)
    heads = lax.all_to_all(sent, "seq", split_axis=2, concat_axis=0, tiled=True)
    head_query = heads[:, 0].reshape(length, local_heads, HEAD_DIM)
    head_keys = heads[:, 1].reshape(length, local_heads, HEAD_DIM)
    head_values = heads[:, 2].reshape(length, local_heads, HEAD_DIM)
    attended, logsum = attend(head_query, head_keys, head_values, block)
    merged = lax.all_to_all(
        attended.astype(jnp.bfloat16), "seq", split_axis=0, concat_axis=1, tiled=True
    )
    attn_branch = jnp.dot(merged, w_out, preferred_element_type=jnp.float32) + b_out
    hidden = jnp.dot(normed_low, w_up, preferred_element_type=jnp.float32) + up_bias_full
    activated, gelu_back = jax.vjp(gelu_tanh, hidden)
    act_low = activated.astype(jnp.bfloat16)
    mlp_branch = jnp.dot(act_low, w_down, preferred_element_type=jnp.float32) + b_down
    output = inputs + attn_branch + mlp_branch
    weighted = mask[:, None] * (output - target)
    count, squares = lax.psum((jnp.sum(mask), jnp.sum(weighted * (output - target))), ("dp", "seq"))
    loss = squares / (2.0 * width * count)
    grad_output = length * data_count / count * weighted
    grad_low = grad_output.astype(jnp.bfloat16)
    branch_bias_grad = jnp.sum(grad_low.astype(jnp.float32), axis=0)
    down_grad = jnp.einsum("tf,td->fd", act_low, grad_low, preferred_element_type=jnp.float32)
    act_grad = jnp.einsum("td,fd->tf", grad_low, w_down, preferred_element_type=jnp.float32)
    (hidden_grad,) = gelu_back(act_grad)
    hidden_low = hidden_grad.astype(jnp.bfloat16)
    up_grad = jnp.einsum("td,tf->df", normed_low, hidden_low, preferred_element_type=jnp.float32)
    up_bias_grad = jnp.sum(hidden_low.astype(jnp.float32), axis=0)
    normed_grad = jnp.einsum("tf,df->td", hidden_low, w_up, preferred_element_type=jnp.float32)
    mlp_part = (
        lax.psum_scatter(up_grad, ("dp", "seq"), scatter_dimension=0, tiled=True),
        lax.psum_scatter(down_grad, ("dp", "seq"), scatter_dimension=1, tiled=True),
    )
    out_grad = jnp.einsum("te,td->ed", merged, grad_low, preferred_element_type=jnp.float32)
    merged_grad = jnp.einsum(
        "td,ed->te", grad_low, w_out, preferred_element_type=jnp.float32
    ).astype(jnp.bfloat16)
    head_grad = lax.all_to_all(merged_grad, "seq", split_axis=1, concat_axis=0, tiled=True).reshape(
        length, local_heads, HEAD_DIM
    )
    query_grad, key_grad, value_grad = attend_back(
        head_query, head_keys, head_values, logsum, head_grad, block
    )
    stacked = jnp.stack([query_grad, key_grad, value_grad], axis=1).astype(jnp.bfloat16)
    token_grads = lax.all_to_all(stacked, "seq", split_axis=0, concat_axis=2, tiled=True)
    (query_back,) = query_turn(
        token_grads[:, 0].astype(jnp.float32).reshape(rows_here, HEADS, HEAD_DIM)
    )
    (keys_back,) = keys_turn(
        token_grads[:, 1].astype(jnp.float32).reshape(rows_here, HEADS, HEAD_DIM)
    )
    mixed_grad = jnp.concatenate(
        [
            query_back.reshape(rows_here, width),
            keys_back.reshape(rows_here, width),
            token_grads[:, 2].astype(jnp.float32),
        ],
        axis=1,
    ).astype(jnp.bfloat16)
    qkv_grad = jnp.einsum("td,te->de", normed_low, mixed_grad, preferred_element_type=jnp.float32)
    qkv_bias_grad = jnp.sum(mixed_grad.astype(jnp.float32), axis=0)
    normed_grad = normed_grad + jnp.einsum(
        "te,de->td", mixed_grad, w_qkv, preferred_element_type=jnp.float32
    )
    input_grad, gain_grad, shift_grad = norm_back(normed_grad)
    attn_part = (
        lax.psum_scatter(qkv_grad, ("dp", "seq"), scatter_dimension=0, tiled=True),
        lax.psum_scatter(out_grad, ("dp", "seq"), scatter_dimension=1, tiled=True),
    )
    owned = (
        lax.all_gather(mlp_part[0].astype(jnp.bfloat16), "seq", axis=0, tiled=True).astype(
            jnp.float32
        ),
        lax.all_gather(mlp_part[1].astype(jnp.bfloat16), "seq", axis=1, tiled=True).astype(
            jnp.float32
        ),
        lax.all_gather(attn_part[0].astype(jnp.bfloat16), "seq", axis=0, tiled=True).astype(
            jnp.float32
        ),
        lax.all_gather(attn_part[1].astype(jnp.bfloat16), "seq", axis=1, tiled=True).astype(
            jnp.float32
        ),
    )
    up_weight_grad, down_weight_grad, qkv_weight_grad, out_weight_grad = (
        owned[0],
        owned[1],
        owned[2],
        owned[3],
    )
    small = lax.psum(
        (gain_grad, shift_grad, qkv_bias_grad, up_bias_grad, branch_bias_grad), ("dp", "seq")
    )
    tokens_grad = (grad_output + input_grad)[None]
    return (
        loss,
        tokens_grad,
        small[0],
        small[1],
        qkv_weight_grad,
        small[2],
        out_weight_grad,
        small[4],
        up_weight_grad,
        small[3],
        down_weight_grad,
        small[4],
    )


def solution(mesh):
    placed = (
        P("dp", "seq", None),
        P("dp", "seq", None),
        P("dp", "seq"),
        P("dp", "seq"),
        P(),
        P(),
        P("dp", None),
        P(),
        P(None, "dp"),
        P(),
        P("dp", None),
        P(),
        P(None, "dp"),
        P(),
    )
    return jax.shard_map(
        local,
        mesh=mesh,
        in_specs=placed,
        out_specs=(
            P(),
            P("dp", "seq", None),
            P(),
            P(),
            P("dp", None),
            P(),
            P(None, "dp"),
            P(),
            P("dp", None),
            P(),
            P(None, "dp"),
            P(),
        ),
        check_vma=False,
    )
```

profile of v0, /device:TPU:0, one launch (start us, length us, event | category | flops | bytes accessed | tf_op | source)
XLA Modules:
  0.0 3344.0 jit_solution(9349291631186061919)
XLA Ops:
  11.6 228.7 %all-gather.9.cloned.1.call-done = bf16[2048,6144]{1,0:T(8,128)(2,1)} async-done(((bf16[512,6144]{1,0:T(8,128)(2,1)}), bf16[2048,6144]{1,0:T(8,128)(2,1)}) %all-gather.9.cloned.1.call-update) | async-done | bytes 25165840 | tf_op jit(solution)/shard_map/all_gather | solution.py:143
  240.3 10.1 convolution_add_fusion.1
  260.9 4.6 all-to-all-start
  265.5 49.1 %all-to-all-done = bf16[128,3,2048]{0,1,2:T(4,128)(2,1)S(1)} async-done(((bf16[128,3,2048]{0,1,2:T(4,128)(2,1)}), bf16[128,3,2048]{0,1,2:T(4,128)(2,1)S(1)}, u32[]{:S(2)}, u32[]{:S(2)}) %all-to-all-start) | async-done | bytes 1572896 | tf_op jit(solution)/shard_map/all_to_all | solution.py:157
  320.3 17.4 while.27
  325.9 3.0 fusion.123
  334.7 3.0 fusion.123
  339.6 3.5 all-to-all-start.1
  343.8 40.7 %psum.50 = f32[]{:T(128)} all-reduce(f32[]{:T(128)} %convert_reduce_fusion.4), channel_id=1, replica_groups=mesh['dp'=4,'seq'=8] {'dp','seq'}, use_global_device_ids=true, to_apply=%region_9.10 | all-reduce | flops 1 | bytes 8 | tf_op jit(solution)/shard_map/psum | solution.py:172
  385.3 5.6 fusion.45
  390.9 239.0 %all-gather.13.cloned.1.call-done = bf16[2048,8192]{1,0:T(8,128)(2,1)} async-done(((bf16[512,8192]{1,0:T(8,128)(2,1)}), bf16[2048,8192]{1,0:T(8,128)(2,1)}) %all-gather.13.cloned.1.call-update) | async-done | bytes 33554448 | tf_op jit(solution)/shard_map/all_gather | solution.py:144
  629.9 20.1 convolution_add_fusion
  650.0 278.7 %all-gather.15.cloned.1.call-done = bf16[8192,2048]{1,0:T(8,128)(2,1)} async-done(((bf16[8192,512]{1,0:T(8,128)(2,1)}), bf16[8192,2048]{1,0:T(8,128)(2,1)}) %all-gather.15.cloned.1.call-update) | async-done | bytes 33554448 | tf_op jit(solution)/shard_map/all_gather | solution.py:146
  928.7 19.1 convert_reduce_fusion.3
  947.8 18.8 fusion.77
  966.6 6.3 convolution_convert_fusion
  973.7 4.6 all-to-all-start.2
  978.4 24.1 all-to-all-done.2
  1006.5 42.3 %while.28 = (s32[]{:T(128)}, f32[1024,4,64]{0,2,1:T(8,128)S(1)}, f32[1024,4,64]{0,2,1:T(8,128)}, bf16[2,512,4,64]{1,3,2,0:T(8,128)(2,1)}, s32[2]{0:T(128)S(1)}, ...) while((s32[]{:T(128)}, f32[1024,4,64]{0,2,1:T(8,128)S(1)}, ...), condition=%wide.region_12.13_spmd.clone, body=%wide.region_10.12_spmd.clone.sunk | while | flops 1375599104 | bytes 166785504 | solution.py:100
  1009.5 3.2 multiply_reduce_fusion.2
  1012.7 3.7 multiply_convert_fusion.5
  1016.4 3.3 fusion.134
  1021.2 3.6 fusion.135
  1030.0 3.2 multiply_reduce_fusion.2
  1033.2 3.7 multiply_convert_fusion.5
  1036.9 3.4 fusion.134
  1041.8 4.8 fusion.135
  1053.4 3.0 copy.95
  1056.4 82.0 %all_to_all.68 = bf16[1024,3,256]{2,1,0:T(4,128)(2,1)} all-to-all(bf16[1024,3,256]{2,1,0:T(4,128)(2,1)S(1)} %copy.95), channel_id=1, replica_groups=mesh['dp'=4,'seq'=8] {'seq'}, dimensions={0} | all-to-all | bytes 3145728 | tf_op jit(solution)/shard_map/all_to_all | solution.py:199
  1138.4 3.0 copy.96
  1142.5 21.4 fusion.62
  1164.0 18.3 convert_reduce_fusion
  1182.3 23.9 fusion.65
  1206.2 36.9 %fusion.64 = f32[8192,2048]{0,1:T(8,128)} fusion(bf16[128,2048]{1,0:T(8,128)(2,1)} %copy-done.13, f32[128,8192]{1,0:T(8,128)} %convolution_add_fusion), kind=kOutput, calls=%fused_computation.121 | convolution fusion | flops 4304404480 | bytes 71827456 | tf_op jit(solution)/shard_map/tf,td->fd/dot_general | solution.py:177
  1245.2 398.9 %reduce-scatter.5.cloned.1.call-done = f32[64,6144]{1,0:T(8,128)} async-done(((f32[2048,6144]{1,0:T(8,128)}), f32[64,6144]{1,0:T(8,128)}) %reduce-scatter.5.cloned.1.call-update) | async-done | bytes 1572880 | tf_op jit(solution)/shard_map/reduce_scatter | solution.py:221
  1646.6 708.3 %reduce-scatter.9.cloned.1.call-done = f32[64,8192]{1,0:T(8,128)} async-done(((f32[2048,8192]{1,0:T(8,128)}), f32[64,8192]{1,0:T(8,128)}) %reduce-scatter.9.cloned.1.call-update) | async-done | bytes 2097168 | tf_op jit(solution)/shard_map/reduce_scatter | solution.py:185
  2354.9 2.7 convert_element_type.168
  2357.6 705.5 %reduce-scatter.11.cloned.1.call-done = f32[8192,64]{0,1:T(8,128)} async-done(((f32[8192,2048]{0,1:T(8,128)}), f32[8192,64]{0,1:T(8,128)}) %reduce-scatter.11.cloned.1.call-update) | async-done | bytes 2097168 | tf_op jit(solution)/shard_map/reduce_scatter | solution.py:186
  3066.5 17.4 fusion.76
  3084.4 13.8 fusion.70
  3101.0 42.4 %all-reduce.8 = (f32[]{:T(128)}, f32[2048]{0:T(1024)}, f32[2048]{0:T(1024)}, f32[6144]{0:T(1024)}, f32[2048]{0:T(1024)S(1)}, /*index=5*/f32[8192]{0:T(1024)}) all-reduce(f32[]{:T(128)} %get-tuple-element.298, f32[2048]{0:T(1024)S(1)} %get-tuple-element.229, ...), channel_id=1, replica_groups=mesh['dp'=4,'seq'=8] {'dp','seq'}, use_global_device_ids=true, to_apply=%region_7.8 | all-reduce | flops 20481 | bytes 163848 | tf_op jit(solution)/shard_map/psum | solution.py:172
  3144.1 4.2 copy.97
  3148.3 9.5 all-gather.17.cloned.1.call-done
  3157.8 9.4 convert_element_type.163
  3167.2 73.5 %all-gather.21.cloned.1.call-done = bf16[512,8192]{1,0:T(8,128)(2,1)} async-done(((bf16[64,8192]{1,0:T(8,128)(2,1)}), bf16[512,8192]{1,0:T(8,128)(2,1)}) %all-gather.21.cloned.1.call-update) | async-done | bytes 8388624 | tf_op jit(solution)/shard_map/all_gather | solution.py:225
  3240.7 12.5 convert_element_type.169
  3253.2 69.6 %all-gather.23.cloned.1.call-done = bf16[8192,512]{0,1:T(8,128)(2,1)} async-done(((bf16[8192,64]{0,1:T(8,128)(2,1)}), bf16[8192,512]{0,1:T(8,128)(2,1)}) %all-gather.23.cloned.1.call-update) | async-done | bytes 8388624 | tf_op jit(solution)/shard_map/all_gather | solution.py:228
  3322.8 12.4 copy.98
  (206 shorter events, 66.5 us)
Async XLA Ops:
  7.2 233.1 %all-gather.9.cloned.1.call-start = ((), (), s32[]{:S(2)}) async-start(), calls=%async_computation.8 | async-start | bytes 31457280 | tf_op jit(solution)/shard_map/all_gather | solution.py:143
  7.9 377.3 %all-gather.11.cloned.1.call-start = ((), (), s32[]{:S(2)}) async-start(), calls=%async_computation.9 | async-start | bytes 10485760 | tf_op jit(solution)/shard_map/all_gather | solution.py:145
  8.7 621.2 %all-gather.13.cloned.1.call-start = ((), (), s32[]{:S(2)}) async-start(), calls=%async_computation.10 | async-start | bytes 41943040 | tf_op jit(solution)/shard_map/all_gather | solution.py:144
  9.4 2.0 copy-start.33
  9.4 919.2 %all-gather.15.cloned.1.call-start = ((), (), s32[]{:S(2)}) async-start(), calls=%async_computation.11 | async-start | bytes 41943040 | tf_op jit(solution)/shard_map/all_gather | solution.py:146
  11.6 243.5 %copy-start.17 = (f32[128,16]{0,1:T(8,128)}, f32[128,16]{0,1:T(8,128)S(1)}, u32[]{:S(2)}) copy-start(f32[128,16]{0,1:T(8,128)S(1)} %get-tuple-element.303) | copy-start | bytes 24580
  11.6 243.5 %copy-start.19 = (f32[128,16]{0,1:T(8,128)}, f32[128,16]{0,1:T(8,128)S(1)}, u32[]{:S(2)}) copy-start(f32[128,16]{0,1:T(8,128)S(1)} %get-tuple-element.304) | copy-start | bytes 24580
  250.4 1.7 copy-start.6
  260.9 53.7 %all-to-all-start = ((bf16[128,3,2048]{0,1,2:T(4,128)(2,1)}), bf16[128,3,2048]{0,1,2:T(4,128)(2,1)S(1)}, u32[]{:S(2)}, u32[]{:S(2)}) async-start(bf16[128,3,2048]{0,1,2:T(4,128)(2,1)} %copy.84), calls=%async_computation | async-start | bytes 4194304 | tf_op jit(solution)/shard_map/all_to_all | solution.py:157
  337.7 53.2 %copy-start.4 = (bf16[1024,4,64]{0,2,1:T(8,128)(2,1)}, bf16[1024,4,64]{0,2,1:T(8,128)(2,1)S(1)}, u32[]{:S(2)}) copy-start(bf16[1024,4,64]{0,2,1:T(8,128)(2,1)S(1)} %get-tuple-element.541) | copy-start | bytes 1572868
  337.7 5.4 copy-start.34
  337.7 46.7 %copy-start.27 = (bf16[2048]{0:T(1024)(128)(2,1)S(1)}, bf16[2048]{0:T(1024)(128)(2,1)}, u32[]{:S(2)}) copy-start(bf16[2048]{0:T(1024)(128)(2,1)} %param.27) | copy-start | bytes 12292
  337.8 46.7 %copy-start.28 = (bf16[2048]{0:T(1024)(128)(2,1)S(1)}, bf16[2048]{0:T(1024)(128)(2,1)}, u32[]{:S(2)}) copy-start(bf16[2048]{0:T(1024)(128)(2,1)} %param.31) | copy-start | bytes 12292
  337.8 46.7 %copy-start.21 = (bf16[8192]{0:T(1024)(128)(2,1)S(1)}, bf16[8192]{0:T(1024)(128)(2,1)}, u32[]{:S(2)}) copy-start(bf16[8192]{0:T(1024)(128)(2,1)} %param.29) | copy-start | bytes 49156
  339.6 45.7 %all-to-all-start.1 = ((bf16[8,128,256]{1,2,0:T(8,128)(2,1)}), bf16[8,128,256]{1,2,0:T(8,128)(2,1)S(1)}, u32[]{:S(2)}, u32[]{:S(2)}) async-start(bf16[8,128,256]{1,2,0:T(8,128)(2,1)} %copy.91), calls=%async_computation.1 | async-start | bytes 1048576 | tf_op jit(solution)/shard_map/all_to_all | solution.py:162
  343.1 900.1 %reduce-scatter.7.cloned.1.call-start = ((), (), s32[]{:S(2)}) async-start(), calls=%async_computation.14 | async-start | bytes 17301504 | tf_op jit(solution)/shard_map/reduce_scatter | solution.py:222
  385.2 543.5 %copy-start.29 = (f32[128]{0:T(128)}, f32[128]{0:T(128)S(1)}, u32[]{:S(2)}) copy-start(f32[128]{0:T(128)S(1)} %convert_bitcast_fusion.2) | copy-start | bytes 1540
  947.8 18.8 copy-start.13
  973.7 28.8 all-to-all-start.2
  978.3 665.8 %reduce-scatter.5.cloned.1.call-start = ((), (), s32[]{:S(2)}) async-start(), calls=%async_computation.12 | async-start | bytes 51904512 | tf_op jit(solution)/shard_map/reduce_scatter | solution.py:221
  1007.7 1.7 copy-start.5
  1007.7 1.7 copy-start.7
  1009.1 3.6 copy-start
  1016.4 4.8 copy-start.1
  1016.4 4.9 copy-start.8
  1021.2 3.6 copy-start.2
  1021.2 3.6 copy-start.14
  1028.3 1.7 copy-start.5
  1028.3 1.7 copy-start.7
  1029.6 3.6 copy-start
  1036.9 4.8 copy-start.1
  1036.9 4.8 copy-start.8
  1041.8 4.8 copy-start.2
  1041.8 4.8 copy-start.14
  1142.5 21.4 copy-start.9
  1163.9 1190.9 %reduce-scatter.9.cloned.1.call-start = ((), (), s32[]{:S(2)}) async-start(), calls=%async_computation.16 | async-start | bytes 69206016 | tf_op jit(solution)/shard_map/reduce_scatter | solution.py:185
  1206.2 1857.0 %reduce-scatter.11.cloned.1.call-start = ((), (), s32[]{:S(2)}) async-start(), calls=%async_computation.18 | async-start | bytes 69206016 | tf_op jit(solution)/shard_map/reduce_scatter | solution.py:186
  1243.2 1901.0 %all-gather.19.cloned.1.call-start = ((), (), s32[]{:S(2)}) async-start(), calls=%async_computation.15 | async-start | bytes 2359296 | tf_op jit(solution)/shard_map/all_gather | solution.py:234
  1245.2 1912.6 %all-gather.17.cloned.1.call-start = ((), (), s32[]{:S(2)}) async-start(), calls=%async_computation.13 | async-start | bytes 7077888 | tf_op jit(solution)/shard_map/all_gather | solution.py:231
  1646.5 1594.2 %all-gather.21.cloned.1.call-start = ((), (), s32[]{:S(2)}) async-start(), calls=%async_computation.17 | async-start | bytes 9437184 | tf_op jit(solution)/shard_map/all_gather | solution.py:225
  2357.6 965.2 %all-gather.23.cloned.1.call-start = ((), (), s32[]{:S(2)}) async-start(), calls=%async_computation.19 | async-start | bytes 9437184 | tf_op jit(solution)/shard_map/all_gather | solution.py:228
  3066.5 17.4 copy-start.10
  3066.5 17.4 copy-start.12
  3084.4 13.9 copy-start.32
  3084.4 14.4 copy-start.16
  3084.4 14.4 copy-start.30
  3098.2 2.7 copy-start.23
  3143.4 191.7 %copy-start.24 = (f32[2048]{0:T(1024)}, f32[2048]{0:T(1024)S(1)}, u32[]{:S(2)}) copy-start(f32[2048]{0:T(1024)S(1)} %get-tuple-element.519) | copy-start | bytes 24580
  (10 other events, 7.7 us)
Sparse Core Ops, SparseCore 0:
  9.9 230.3 all-gather.8
  242.1 87.4 all-gather.10
  331.5 298.3 all-gather.12
  631.6 297.0 all-gather.14
  966.7 237.5 reduce-scatter.6
  1210.6 433.4 reduce-scatter.4
  1646.5 708.3 reduce-scatter.8
  2357.2 705.8 reduce-scatter.10
  3064.8 25.6 all-gather.18
  3092.5 65.2 all-gather.16
  3160.0 80.6 all-gather.20
  3242.1 80.5 all-gather.22
where the time goes:
time: 3350 us; the launch traced here: 3340 us
  waiting for transfers between devices  2790 us (83%)
  matrix products  248 us (7%)
  blocking collectives  165 us (5%)
  local copies, waits for them, and re-layouts  54.7 us (2%)
  other arithmetic  54.1 us (2%)
    reduce_scatter x1, waiting for transfers between devices, local(): lax.psum_scatter(up_grad, ('dp', 'seq'), scatter_dimension=0, tiled=True)  708 us
    reduce_scatter x1, waiting for transfers between devices, local(): lax.psum_scatter(down_grad, ('dp', 'seq'), scatter_dimension=1, tiled=True)  706 us
    reduce_scatter x1, waiting for transfers between devices, local(): lax.psum_scatter(qkv_grad, ('dp', 'seq'), scatter_dimension=0, tiled=True)  399 us
    all_gather x1, waiting for transfers between devices, local(): lax.all_gather(down_weight, 'dp', axis=1, tiled=True)  279 us
    all_gather x1, waiting for transfers between devices, local(): lax.all_gather(up_weight, 'dp', axis=0, tiled=True)  239 us
    all_gather x1, waiting for transfers between devices, local(): lax.all_gather(qkv_weight, 'dp', axis=0, tiled=True)  229 us
    psum x2, blocking collectives, local(): lax.psum((jnp.sum(mask), jnp.sum(weighted * (output - target))), ('dp', '...  83.1 us
    all_to_all x1, blocking collectives, local(): lax.all_to_all(stacked, 'seq', split_axis=0, concat_axis=2, tiled=True)  82 us
  transfers between devices with their start and end apart: 15, of which 11 were waited for; matrix products, arithmetic and copies ran while one was open for 9% of the time, Pallas kernels for 0%

commit v1 on v0

v1 whole, which is shorter than its diff:
```python
import jax
import jax.numpy as jnp
from jax import lax
from jax.sharding import PartitionSpec as P

HEADS = 32
HEAD_DIM = 64
ROTARY = 32


norm_eps = 1e-05
rope_base = 10000.0
masked_fill = -1e30


def gelu_tanh(values):
    return jax.nn.gelu(values, approximate=True)


def rotate(block, where):
    half = ROTARY // 2
    freqs = rope_base ** (-(jnp.arange(half, dtype=jnp.float32) * 2.0) / ROTARY)
    angles = where.astype(jnp.float32)[:, None] * freqs[None, :]
    cosine = jnp.cos(angles)[:, None, :]
    sine = jnp.sin(angles)[:, None, :]
    first = block[..., :half]
    second = block[..., half:ROTARY]
    return jnp.concatenate(
        [first * cosine - second * sine, second * cosine + first * sine, block[..., ROTARY:]],
        axis=-1,
    )


def causal_scores(rows, keys, start, scale):
    block = rows.shape[0]
    length = keys.shape[0]
    raw = jnp.einsum("bhd,khd->hbk", rows, keys, preferred_element_type=jnp.float32) * scale
    row_index = start + jnp.arange(block, dtype=jnp.int32)
    col_index = jnp.arange(length, dtype=jnp.int32)
    allowed = col_index[None, None, :] <= row_index[None, :, None]
    return jnp.where(allowed, raw, masked_fill)


def attend(query, keys, values, block):
    length = query.shape[0]
    scale = HEAD_DIM ** (-0.5)

    def one_block(carry, index):
        start = index * block
        rows = lax.dynamic_slice_in_dim(query, start, block, 0)
        scores = causal_scores(rows, keys, start, scale)
        top = jnp.max(scores, axis=-1, keepdims=True)
        expd = jnp.exp(scores - top)
        total = jnp.sum(expd, axis=-1, keepdims=True)
        probs = (expd / total).astype(jnp.bfloat16)
        result = jnp.einsum("hbk,khd->bhd", probs, values, preferred_element_type=jnp.float32)
        return (carry, (result, top[..., 0] + jnp.log(total[..., 0])))

    _, (outs, logsum) = lax.scan(one_block, None, jnp.arange(length // block, dtype=jnp.int32))
    return (outs.reshape(length, query.shape[1] * query.shape[2]), logsum)


def attend_back(query, keys, values, logsum, upstream_all, block):
    length = query.shape[0]
    scale = HEAD_DIM ** (-0.5)

    def one_block(carry, item):
        key_total, value_total = carry
        index, block_logsum = item
        start = index * block
        rows = lax.dynamic_slice_in_dim(query, start, block, 0)
        upstream = lax.dynamic_slice_in_dim(upstream_all, start, block, 0)
        scores = causal_scores(rows, keys, start, scale)
        probs = jnp.exp(scores - block_logsum[..., None])
        probs_low = probs.astype(jnp.bfloat16)
        prob_grad = jnp.einsum("bhd,khd->hbk", upstream, values, preferred_element_type=jnp.float32)
        inner = jnp.sum(probs * prob_grad, axis=-1, keepdims=True)
        score_grad = (probs * (prob_grad - inner)).astype(jnp.bfloat16)
        row_grad = (
            jnp.einsum("hbk,khd->bhd", score_grad, keys, preferred_element_type=jnp.float32) * scale
        )
        key_total = (
            key_total
            + jnp.einsum("hbk,bhd->khd", score_grad, rows, preferred_element_type=jnp.float32)
            * scale
        )
        value_total = value_total + jnp.einsum(
            "hbk,bhd->khd", probs_low, upstream, preferred_element_type=jnp.float32
        )
        return ((key_total, value_total), row_grad)

    zeros = jnp.zeros(keys.shape, jnp.float32)
    indices = jnp.arange(length // block, dtype=jnp.int32)
    (key_grad, value_grad), row_grads = lax.scan(one_block, (zeros, zeros), (indices, logsum))
    return (
        row_grads.reshape(length, -1),
        key_grad.reshape(length, -1),
        value_grad.reshape(length, -1),
    )


def dot(a, b, dims):
    return lax.dot_general(a, b, (dims, ((), ())), preferred_element_type=jnp.float32)


def local(
    tokens,
    teacher,
    valid,
    positions,
    norm_gain,
    norm_bias,
    qkv_weight,
    qkv_bias,
    out_weight,
    out_bias,
    up_weight,
    up_bias,
    down_weight,
    down_bias,
):
    low = jnp.bfloat16
    inputs = tokens[0].astype(jnp.float32)
    target = teacher[0].astype(jnp.float32)
    mask = valid[0].astype(jnp.float32)
    rows_here, width = inputs.shape
    seq_count = lax.axis_size("seq")
    data_count = lax.axis_size("dp")
    part = lax.axis_index("seq")
    length = rows_here * seq_count
    block = min(512, length)
    local_heads = HEADS // seq_count
    head_width = local_heads * HEAD_DIM
    units = up_weight.shape[1] // seq_count
    depth = qkv_weight.shape[0]
    gain = norm_gain.astype(jnp.float32)
    shift = norm_bias.astype(jnp.float32)

    centre = inputs - jnp.mean(inputs, axis=-1, keepdims=True)
    spread = jnp.mean(centre * centre, axis=-1, keepdims=True)
    rstd = lax.rsqrt(spread + norm_eps)
    xhat = centre * rstd
    normed_low = (xhat * gain + shift).astype(low)
    count = lax.psum(jnp.sum(mask), ("dp", "seq"))

    def my_heads(array):
        grouped = array.reshape(array.shape[:-1] + (3, seq_count, head_width))
        mine = lax.dynamic_index_in_dim(grouped, part, array.ndim, keepdims=False)
        return mine.reshape(array.shape[:-1] + (3 * head_width,))

    normed_all = lax.all_gather(normed_low, "seq", axis=0, tiled=True)
    where = lax.all_gather(positions[0], "seq", axis=0, tiled=True)
    w_in = jnp.concatenate(
        [my_heads(qkv_weight), lax.dynamic_slice_in_dim(up_weight, part * units, units, 1)], axis=1
    )
    w_back = jnp.concatenate(
        [
            lax.dynamic_slice_in_dim(out_weight, part * head_width, head_width, 0),
            lax.dynamic_slice_in_dim(down_weight, part * units, units, 0),
        ],
        axis=0,
    )
    w_in = lax.all_gather(w_in, "dp", axis=0, tiled=True)
    w_back = lax.all_gather(w_back, "dp", axis=1, tiled=True)
    b_in = jnp.concatenate(
        [my_heads(qkv_bias), lax.dynamic_slice_in_dim(up_bias, part * units, units, 0)]
    ).astype(jnp.float32)
    three = 3 * head_width

    mixed = dot(normed_all, w_in[:, :three], ((1,), (0,))) + b_in[:three]
    query_pre = mixed[:, :head_width].reshape(length, local_heads, HEAD_DIM)
    keys_pre = mixed[:, head_width : 2 * head_width].reshape(length, local_heads, HEAD_DIM)
    query, query_turn = jax.vjp(lambda part_block: rotate(part_block, where), query_pre)
    keys, keys_turn = jax.vjp(lambda part_block: rotate(part_block, where), keys_pre)
    query, keys = query.astype(low), keys.astype(low)
    values = mixed[:, 2 * head_width :].astype(low).reshape(length, local_heads, HEAD_DIM)
    attended, logsum = attend(query, keys, values, block)
    attended = attended.astype(low)

    hidden = dot(normed_all, w_in[:, three:], ((1,), (0,))) + b_in[three:]
    activated, gelu_back = jax.vjp(gelu_tanh, hidden)
    stacked = jnp.concatenate([attended, activated.astype(low)], axis=1)
    branches = dot(stacked, w_back, ((1,), (0,)))
    branches = lax.psum_scatter(branches, "seq", scatter_dimension=0, tiled=True)
    output = inputs + branches + (out_bias.astype(jnp.float32) + down_bias.astype(jnp.float32))

    weighted = mask[:, None] * (output - target)
    squares = jnp.sum(weighted * (output - target))
    grad_output = length * data_count / count * weighted
    grad_low = grad_output.astype(low)
    branch_bias_grad = jnp.sum(grad_low.astype(jnp.float32), axis=0)
    grad_all = lax.all_gather(grad_low, "seq", axis=0, tiled=True)

    back_grad = dot(stacked, grad_all, ((0,), (0,)))
    back_grad = lax.psum_scatter(back_grad, "dp", scatter_dimension=1, tiled=True).astype(low)
    back_grad = lax.all_gather(back_grad, "seq", axis=0, tiled=False)
    out_grad = back_grad[:, :head_width].reshape(-1, back_grad.shape[2])
    down_grad = back_grad[:, head_width:].reshape(-1, back_grad.shape[2])

    stacked_grad = dot(grad_all, w_back, ((1,), (1,)))
    (hidden_grad,) = gelu_back(stacked_grad[:, head_width:])
    hidden_low = hidden_grad.astype(low)
    head_grad = stacked_grad[:, :head_width].astype(low).reshape(length, local_heads, HEAD_DIM)
    query_grad, key_grad, value_grad = attend_back(query, keys, values, logsum, head_grad, block)

    def turned(turn, grad):
        grad = grad.astype(low).astype(jnp.float32).reshape(length, local_heads, HEAD_DIM)
        return turn(grad)[0].reshape(length, head_width).astype(low)

    mixed_low = jnp.concatenate(
        [turned(query_turn, query_grad), turned(keys_turn, key_grad), value_grad.astype(low)],
        axis=1,
    )
    in_low = jnp.concatenate([mixed_low, hidden_low], axis=1)
    in_grad = dot(normed_all, in_low, ((0,), (0,)))
    in_bias_grad = jnp.sum(in_low.astype(jnp.float32), axis=0)
    in_grad = lax.psum_scatter(in_grad, "dp", scatter_dimension=0, tiled=True).astype(low)
    in_grad = lax.all_gather(in_grad, "seq", axis=0, tiled=False)
    qkv_grad = (
        in_grad[:, :, :three]
        .reshape(seq_count, depth, 3, head_width)
        .transpose(1, 2, 0, 3)
        .reshape(depth, -1)
    )
    up_grad = in_grad[:, :, three:].transpose(1, 0, 2).reshape(depth, -1)

    normed_grad = dot(in_low, w_in, ((1,), (1,)))
    normed_grad = lax.psum_scatter(normed_grad, "seq", scatter_dimension=0, tiled=True)
    gain_grad = jnp.sum(normed_grad * xhat, axis=0)
    shift_grad = jnp.sum(normed_grad, axis=0)
    spread_grad = normed_grad * gain
    input_grad = rstd * (
        spread_grad
        - jnp.mean(spread_grad, axis=-1, keepdims=True)
        - xhat * jnp.mean(spread_grad * xhat, axis=-1, keepdims=True)
    )
    tokens_grad = (grad_output + input_grad)[None]

    slots = jnp.zeros((seq_count, in_bias_grad.shape[0]), jnp.float32)
    slots = lax.dynamic_update_slice_in_dim(slots, in_bias_grad[None], part, 0)
    gain_grad, shift_grad, slots, branch_bias_grad, squares = lax.psum(
        (gain_grad, shift_grad, slots, branch_bias_grad, squares), ("dp", "seq")
    )
    qkv_bias_grad = (
        slots[:, :three].reshape(seq_count, 3, head_width).transpose(1, 0, 2).reshape(-1)
    )
    up_bias_grad = slots[:, three:].reshape(-1)
    loss = squares / (2.0 * width * count)
    return (
        loss,
        tokens_grad,
        gain_grad,
        shift_grad,
        qkv_grad.astype(jnp.float32),
        qkv_bias_grad,
        out_grad.astype(jnp.float32),
        branch_bias_grad,
        up_grad.astype(jnp.float32),
        up_bias_grad,
        down_grad.astype(jnp.float32),
        branch_bias_grad,
    )


def solution(mesh):
    placed = (
        P("dp", "seq", None),
        P("dp", "seq", None),
        P("dp", "seq"),
        P("dp", "seq"),
        P(),
        P(),
        P("dp", None),
        P(),
        P(None, "dp"),
        P(),
        P("dp", None),
        P(),
        P(None, "dp"),
        P(),
    )
    return jax.shard_map(
        local,
        mesh=mesh,
        in_specs=placed,
        out_specs=(
            P(),
            P("dp", "seq", None),
            P(),
            P(),
            P("dp", None),
            P(),
            P(None, "dp"),
            P(),
            P("dp", None),
            P(),
            P(None, "dp"),
            P(),
        ),
        check_vma=False,
    )
```

time: 3350 us -> 1030 us (0.31)
  waiting for transfers between devices: 2790 us -> 616 us
  matrix products: 248 us -> 100 us
  blocking collectives: 165 us -> 99.8 us
  local copies, waits for them, and re-layouts: 54.7 us -> 96.7 us
    reduce_scatter x4, waiting for transfers between devices: 1810 us -> 286 us  [the longest x1 139 us: local(): lax.psum_scatter(in_grad, 'dp', scatter_dimension=0, tiled=True).astype(low)]
    all_gather x8 -> x6, waiting for transfers between devices: 899 us -> 330 us  [the longest x1 109 us: local(): in_grad = lax.all_gather(in_grad, 'seq', axis=0, tiled=False)]
    dot_general x12 -> x7, matrix products: 212 us -> 72.1 us  [dot(): lax.dot_general(a, b, (dims, ((), ())), preferred_element_type=jnp.float32)]
    all_to_all x1 -> x0, blocking collectives: 82 us -> none  [local(): lax.all_to_all(stacked, 'seq', split_axis=0, concat_axis=2, tiled=True)]
    all_to_all x3 -> x0, waiting for transfers between devices: 73.2 us -> none  [the longest x1 49.1 us: local(): heads = lax.all_to_all(sent, 'seq', split_axis=2, concat_axis=0, tiled=True)]
  transfers between devices with their start and end apart: 15 -> 10, of which waited for: 11 -> 10; matrix products, arithmetic and copies ran while one was open for 9% -> 16% of each run, Pallas kernels for 0% -> 0%
where the time goes in v1:
time: 1030 us; the launch traced here: 1020 us
  waiting for transfers between devices  616 us (60%)
  matrix products  100 us (10%)
  blocking collectives  99.8 us (10%)
  local copies, waits for them, and re-layouts  96.7 us (9%)
  other arithmetic  74.3 us (7%)
  between operations  18.5 us (2%)
  loops' own time  11.8 us (1%)
    reduce_scatter x1, waiting for transfers between devices, local(): lax.psum_scatter(in_grad, 'dp', scatter_dimension=0, tiled=True).astype(low)  139 us
    all_gather x1, waiting for transfers between devices, local(): in_grad = lax.all_gather(in_grad, 'seq', axis=0, tiled=False)  109 us
    reduce_scatter x1, waiting for transfers between devices, local(): lax.psum_scatter(normed_grad, 'seq', scatter_dimension=0, tiled=True)  86.1 us
    all_gather x1, waiting for transfers between devices, local(): w_in = lax.all_gather(w_in, 'dp', axis=0, tiled=True)  80 us
    dot_general x7, matrix products, dot(): lax.dot_general(a, b, (dims, ((), ())), preferred_element_type=jnp.float32)  72.1 us
    all_gather x1, waiting for transfers between devices, local(): back_grad = lax.all_gather(back_grad, 'seq', axis=0, tiled=False)  49.4 us
    reduce_scatter x1, waiting for transfers between devices, local(): lax.psum_scatter(branches, 'seq', scatter_dimension=0, tiled=True)  47.5 us
    all_gather x1, waiting for transfers between devices, local(): grad_all = lax.all_gather(grad_low, 'seq', axis=0, tiled=True)  45.6 us
  transfers between devices with their start and end apart: 10, of which 10 were waited for; matrix products, arithmetic and copies ran while one was open for 16% of the time, Pallas kernels for 0%

profile of v1, /device:TPU:0, one launch (start us, length us, event | category | flops | bytes accessed | tf_op | source)
XLA Modules:
  0.0 1017.7 jit_solution(11691290738752595213)
XLA Ops:
  13.7 8.6 copy.39
  31.4 13.3 %all-gather = s32[1,1024]{1,0:T(1,128)S(1)} all-gather(s32[1,128]{1,0:T(1,128)S(1)} %copy-done.39), channel_id=2, replica_groups=mesh['dp'=4,'seq'=8] {'seq'}, dimensions={1}, use_global_device_ids=true | all-gather | bytes 4608 | tf_op jit(solution)/shard_map/all_gather | solution.py:152
  45.1 18.6 %all-gather.10.cloned.1.call-done = bf16[1024,2048]{1,0:T(8,128)(2,1)} async-done(((bf16[128,2048]{1,0:T(8,128)(2,1)}), bf16[1024,2048]{1,0:T(8,128)(2,1)}) %all-gather.10.cloned.1.call-update) | async-done | bytes 4194320 | tf_op jit(solution)/shard_map/all_gather | solution.py:151
  63.6 80.0 %all-gather.12.cloned.1.call-done = bf16[2048,1792]{1,0:T(8,128)(2,1)} async-done(((bf16[512,1792]{1,0:T(8,128)(2,1)}), bf16[2048,1792]{1,0:T(8,128)(2,1)}) %all-gather.12.cloned.1.call-update) | async-done | bytes 7340048 | tf_op jit(solution)/shard_map/all_gather | solution.py:163
  143.7 6.2 fusion.47
  150.6 17.7 %while.27 = (s32[]{:T(128)}, bf16[2,512,4,64]{1,3,2,0:T(8,128)(2,1)S(1)}, f32[2,4,512]{2,1,0:T(4,128)S(1)}, s32[2]{0:T(128)S(1)}, bf16[1024,4,64]{0,2,1:T(8,128)...) while((s32[]{:T(128)}, ...), condition=%wide.region_5.6_spmd, body=%wide.region_2.5_spmd.sunk | while | flops 562559488 | bytes 29167808 | solution.py:59
  156.3 3.0 fusion.117
  165.0 3.0 fusion.117
  168.9 11.8 %multiply_convert_fusion.1 = (bf16[1024,1024]{0,1:T(8,128)(2,1)}, f32[1024,1024]{0,1:T(8,128)}) fusion(f32[1024]{0:T(1024)S(1)} %slice.100, bf16[1024,2048]{1,0:T(8,128)(2,1)} %all-gather.10.cloned.1.call-done, bf16[2048,1792]{1,0:T(8,128)(2,1)} %all-gather.12.cloned.1.call-done), kind=kOutput, calls=%fused_computation.60 | convolution fusion | flops 4305453056 | bytes 14684160 | tf_op jit(solution)/shard_map/dot_general | solution.py:103
  180.7 26.7 %all-gather.14.cloned.1.call-done = bf16[1280,2048]{1,0:T(8,128)(2,1)} async-done(((bf16[1280,512]{1,0:T(8,128)(2,1)}), bf16[1280,2048]{1,0:T(8,128)(2,1)}) %all-gather.14.cloned.1.call-update) | async-done | bytes 5242896 | tf_op jit(solution)/shard_map/all_gather | solution.py:164
  207.4 10.7 %fusion.51 = f32[1024,2048]{1,0:T(8,128)} fusion(bf16[1280,2048]{1,0:T(8,128)(2,1)} %all-gather.14.cloned.1.call-done, bf16[1024,1024]{0,1:T(8,128)(2,1)} %get-tuple-element.230, bf16[1024,256]{0,1:T(8,128)(2,1)S(1)} %bitcast.204), kind=kOutput, calls=%fused_computation.69 | convolution fusion | flops 5373952000 | bytes 16252928 | tf_op jit(solution)/shard_map/dot_general | solution.py:103
  219.4 41.4 %psum.43 = f32[]{:T(128)} all-reduce(f32[]{:T(128)} %convert_reduce_fusion.3), channel_id=1, replica_groups=mesh['dp'=4,'seq'=8] {'dp','seq'}, use_global_device_ids=true, to_apply=%region_10.11 | all-reduce | flops 1 | bytes 8 | tf_op jit(solution)/shard_map/psum | solution.py:144
  261.6 47.5 %reduce-scatter.5.cloned.1.call-done = f32[128,2048]{1,0:T(8,128)} async-done(((f32[1024,2048]{1,0:T(8,128)}), f32[128,2048]{1,0:T(8,128)}) %reduce-scatter.5.cloned.1.call-update) | async-done | bytes 1048592 | tf_op jit(solution)/shard_map/reduce_scatter | solution.py:184
  309.0 2.9 convert_reduce_fusion.2
  312.0 45.6 %all-gather.16.cloned.1.call-done = bf16[1024,2048]{1,0:T(8,128)(2,1)} async-done(((bf16[128,2048]{1,0:T(8,128)(2,1)}), bf16[1024,2048]{1,0:T(8,128)(2,1)}) %all-gather.16.cloned.1.call-update) | async-done | bytes 4194320 | tf_op jit(solution)/shard_map/all_gather | solution.py:192
  357.6 10.7 %fusion.50 = f32[1280,2048]{1,0:T(8,128)} fusion(bf16[1024,2048]{1,0:T(8,128)(2,1)} %all-gather.16.cloned.1.call-done, bf16[1024,1024]{0,1:T(8,128)(2,1)} %get-tuple-element.230, bf16[1024,256]{0,1:T(8,128)(2,1)S(1)} %bitcast.205), kind=kOutput, calls=%fused_computation.68 | convolution fusion | flops 5373952000 | bytes 17301504 | tf_op jit(solution)/shard_map/dot_general | solution.py:103
  368.4 9.0 fusion.79
  378.2 2.5 slice.102
  380.8 5.5 copy.49
  388.4 35.8 %while.28 = (s32[]{:T(128)}, f32[1024,4,64]{0,2,1:T(8,128)S(1)}, f32[1024,4,64]{0,2,1:T(8,128)}, bf16[2,512,4,64]{1,3,2,0:T(8,128)(2,1)}, s32[2]{0:T(128)S(1)}, ...) while((s32[]{:T(128)}, f32[1024,4,64]{0,2,1:T(8,128)S(1)}, ...), condition=%wide.region_13.14_spmd.clone, body=%wide.region_11.13_spmd.clone.sunk | while | flops 1375599104 | bytes 84996448 | solution.py:94
  400.0 2.6 fusion.129
  402.5 3.2 multiply_reduce_fusion.3
  405.7 2.4 multiply_convert_fusion.3
  413.6 2.6 fusion.129
  416.2 3.2 multiply_reduce_fusion.3
  419.4 2.4 multiply_convert_fusion.3
  429.5 3.4 fusion.42
  433.0 11.4 %fusion.75 = f32[2048,1792]{1,0:T(8,128)} fusion(bf16[1024,2048]{1,0:T(8,128)(2,1)S(1)} %copy-done.40, bf16[1024,1024]{0,1:T(8,128)(2,1)S(1)} %fusion.42, bf16[1024,256]{0,1:T(8,128)(2,1)S(1)} %bitcast.194, bf16[1024,256]{0,1:T(8,128)(2,1)S(1)} %bitcast.197, bf16[1024,256]{0,1:T(8,128)(2,1)S(1)} %bitcast.200), kind=kOutput, calls=%fused_computation.136 | convolution fusion | flops 7530872832 | bytes 22544384 | tf_op jit(solution)/shard_map/dot_general | solution.py:103
  444.4 12.4 %fusion.76 = f32[1024,2048]{1,0:T(8,128)} fusion(bf16[2048,1792]{1,0:T(8,128)(2,1)} %all-gather.12.cloned.1.call-done, bf16[1024,1024]{0,1:T(8,128)(2,1)S(1)} %fusion.42, bf16[1024,256]{0,1:T(8,128)(2,1)S(1)} %bitcast.195, bf16[1024,256]{0,1:T(8,128)(2,1)S(1)} %bitcast.198, bf16[1024,256]{0,1:T(8,128)(2,1)} %bitcast.201), kind=kOutput, calls=%fused_computation.137 | convolution fusion | flops 7530872832 | bytes 19398656 | tf_op jit(solution)/shard_map/dot_general | solution.py:103
  456.9 13.9 %reduce-scatter.11.cloned.1.call-done = f32[1280,512]{1,0:T(8,128)} async-done(((f32[1280,2048]{1,0:T(8,128)}), f32[1280,512]{1,0:T(8,128)}) %reduce-scatter.11.cloned.1.call-update) | async-done | bytes 2621456 | tf_op jit(solution)/shard_map/reduce_scatter | solution.py:195
  470.7 3.0 convert_element_type.190
  473.8 138.5 %reduce-scatter.9.cloned.1.call-done = f32[512,1792]{1,0:T(8,128)} async-done(((f32[2048,1792]{1,0:T(8,128)}), f32[512,1792]{1,0:T(8,128)}) %reduce-scatter.9.cloned.1.call-update) | async-done | bytes 3670032 | tf_op jit(solution)/shard_map/reduce_scatter | solution.py:217
  612.4 3.5 convert_element_type.184
  618.7 86.1 %reduce-scatter.7.cloned.1.call-done = f32[128,2048]{1,0:T(8,128)} async-done(((f32[1024,2048]{1,0:T(8,128)}), f32[128,2048]{1,0:T(8,128)}) %reduce-scatter.7.cloned.1.call-update) | async-done | bytes 1048592 | tf_op jit(solution)/shard_map/reduce_scatter | solution.py:228
  704.9 2.7 fusion.67
  707.7 45.1 %all-reduce.8 = (f32[]{:T(128)}, f32[2048]{0:T(1024)}, f32[2048]{0:T(1024)}, f32[8,1792]{1,0:T(8,128)S(1)}, f32[2048]{0:T(1024)S(1)}) all-reduce(f32[]{:T(128)} %get-tuple-element.168, f32[2048]{0:T(1024)S(1)} %get-tuple-element.164, f32[2048]{0:T(1024)S(1)} %get-tuple-element.167, ...), channel_id=1, replica_groups=mesh['dp'=4,'seq'=8] {'dp','seq'}, use_global_device_ids=true, to_apply=%region_8.9 | all-reduce | flops 20481 | bytes 163848 | tf_op jit(solution)/shard_map/psum | solution.py:241
  756.4 49.4 %all-gather.20.cloned.1.call-done = bf16[10240,512]{1,0:T(8,128)(2,1)} async-done(((bf16[1280,512]{1,0:T(8,128)(2,1)}), bf16[10240,512]{1,0:T(8,128)(2,1)}) %all-gather.20.cloned.1.call-update) | async-done | bytes 10485776 | tf_op jit(solution)/shard_map/all_gather | solution.py:196
  807.5 7.9 slice.108
  815.5 2.9 bitcast_convert_fusion.1
  818.4 12.0 %bitcast_convert_fusion = f32[8192,512]{1,0:T(8,128)} fusion(bf16[8,1024,512]{2,1,0:T(8,128)(2,1)} %slice.108), kind=kLoop, calls=%fused_computation.47 | loop fusion | flops 4194304 | bytes 25165824 | tf_op jit(solution)/shard_map/convert_element_type | solution.py:260
  830.3 109.4 %all-gather.18.cloned.1.call-done = bf16[4096,1792]{1,0:T(8,128)(2,1)} async-done(((bf16[512,1792]{1,0:T(8,128)(2,1)}), bf16[4096,1792]{1,0:T(8,128)(2,1)}) %all-gather.18.cloned.1.call-update) | async-done | bytes 14680080 | tf_op jit(solution)/shard_map/all_gather | solution.py:218
  939.7 5.9 slice.103
  945.6 11.3 %convert_bitcast_fusion = f32[8,64,8,1024]{3,2,1,0:T(8,128)} fusion(bf16[8,512,1792]{2,1,0:T(8,128)(2,1)} %bitcast.182), kind=kLoop, calls=%fused_computation.45 | loop fusion | flops 4194304 | bytes 25165824
  956.9 8.7 copy.50
  965.5 12.4 %copy.52 = f32[8,64,8,1024]{3,2,0,1:T(8,128)} copy(f32[8,64,8,1024]{3,2,1,0:T(8,128)} %convert_bitcast_fusion) | data formatting | bytes 33554432 | tf_op jit(solution)/shard_map/convert_element_type | solution.py:258
  978.1 6.5 convert_bitcast_fusion.1
  984.6 11.4 %copy.46 = f32[512,3,8,256]{0,3,2,1:T(8,128)} copy(f32[512,3,8,256]{0,3,1,2:T(8,128)} %convert_bitcast_fusion.1) | data formatting | bytes 25165824 | tf_op jit(solution)/shard_map/convert_element_type | solution.py:254
  996.0 12.8 %copy.48 = f32[512,6144]{1,0:T(8,128)} copy(f32[512,6144]{0,1:T(8,128)} %bitcast.177) | data formatting | bytes 25165824
  (205 shorter events, 53.9 us)
Async XLA Ops:
  7.2 21.5 %copy-start = (bf16[2048,512]{1,0:T(8,128)(2,1)S(1)}, bf16[2048,512]{1,0:T(8,128)(2,1)}, u32[]{:S(2)}) copy-start(bf16[2048,512]{1,0:T(8,128)(2,1)} %param.26) | copy-start | bytes 6291460
  7.2 56.4 %all-gather.10.cloned.1.call-start = ((), (), s32[]{:S(2)}) async-start(), calls=%async_computation.4 | async-start | bytes 4718592 | tf_op jit(solution)/shard_map/all_gather | solution.py:151
  8.6 2.7 copy-start.30
  13.6 130.1 %all-gather.12.cloned.1.call-start = ((), (), s32[]{:S(2)}) async-start(), calls=%async_computation.5 | async-start | bytes 9175040 | tf_op jit(solution)/shard_map/all_gather | solution.py:163
  28.6 2.7 copy-start.29
  28.6 2.7 dynamic-slice-start
  28.6 2.8 copy-start.39
  28.7 178.7 %all-gather.14.cloned.1.call-start = ((), (), s32[]{:S(2)}) async-start(), calls=%async_computation.6 | async-start | bytes 6553600 | tf_op jit(solution)/shard_map/all_gather | solution.py:164
  31.2 277.8 %reduce-scatter.5.cloned.1.call-start = ((), (), s32[]{:S(2)}) async-start(), calls=%async_computation.7 | async-start | bytes 9437184 | tf_op jit(solution)/shard_map/reduce_scatter | solution.py:184
  31.4 137.5 %copy-start.27 = (f32[1024]{0:T(1024)}, f32[1024]{0:T(1024)S(1)}, u32[]{:S(2)}) copy-start(f32[1024]{0:T(1024)S(1)} %slice.100) | copy-start | bytes 12292
  45.1 105.2 %copy-start.18 = (f32[1024,16]{0,1:T(8,128)}, f32[1024,16]{0,1:T(8,128)S(1)}, u32[]{:S(2)}) copy-start(f32[1024,16]{0,1:T(8,128)S(1)} %get-tuple-element.228) | copy-start | bytes 196612
  45.1 105.2 %copy-start.20 = (f32[1024,16]{0,1:T(8,128)}, f32[1024,16]{0,1:T(8,128)S(1)}, u32[]{:S(2)}) copy-start(f32[1024,16]{0,1:T(8,128)S(1)} %get-tuple-element.229) | copy-start | bytes 196612
  218.1 43.4 %copy-start.37 = (bf16[2048]{0:T(1024)(128)(2,1)S(1)}, bf16[2048]{0:T(1024)(128)(2,1)}, u32[]{:S(2)}) copy-start(bf16[2048]{0:T(1024)(128)(2,1)} %param.31) | copy-start | bytes 12292
  218.1 43.4 %copy-start.38 = (bf16[2048]{0:T(1024)(128)(2,1)S(1)}, bf16[2048]{0:T(1024)(128)(2,1)}, u32[]{:S(2)}) copy-start(bf16[2048]{0:T(1024)(128)(2,1)} %param.27) | copy-start | bytes 12292
  218.1 90.9 %copy-start.3 = (bf16[1,128,2048]{2,1,0:T(8,128)(2,1)S(1)}, bf16[1,128,2048]{2,1,0:T(8,128)(2,1)}, u32[]{:S(2)}) copy-start(bf16[1,128,2048]{2,1,0:T(8,128)(2,1)} %param.18) | copy-start | bytes 1572868
  218.1 90.9 %copy-start.8 = (bf16[1,128,2048]{2,1,0:T(8,128)(2,1)S(1)}, bf16[1,128,2048]{2,1,0:T(8,128)(2,1)}, u32[]{:S(2)}) copy-start(bf16[1,128,2048]{2,1,0:T(8,128)(2,1)} %param.19) | copy-start | bytes 1572868
  218.2 139.4 %all-gather.16.cloned.1.call-start = ((), (), s32[]{:S(2)}) async-start(), calls=%async_computation.8 | async-start | bytes 4718592 | tf_op jit(solution)/shard_map/all_gather | solution.py:192
  261.5 106.8 %copy-start.35 = (f32[128]{0:T(128)}, f32[128]{0:T(128)S(1)}, u32[]{:S(2)}) copy-start(f32[128]{0:T(128)S(1)} %convert_bitcast_fusion.4) | copy-start | bytes 1540
  261.5 106.7 %copy-start.24 = (f32[2048]{0:T(1024)}, f32[2048]{0:T(1024)S(1)}, u32[]{:S(2)}) copy-start(f32[2048]{0:T(1024)S(1)} %convert_add_fusion) | copy-start | bytes 24580
  312.0 158.8 %reduce-scatter.11.cloned.1.call-start = ((), (), s32[]{:S(2)}) async-start(), calls=%async_computation.11 | async-start | bytes 13107200 | tf_op jit(solution)/shard_map/reduce_scatter | solution.py:195
  368.3 244.1 %reduce-scatter.9.cloned.1.call-start = ((), (), s32[]{:S(2)}) async-start(), calls=%async_computation.10 | async-start | bytes 18350080 | tf_op jit(solution)/shard_map/reduce_scatter | solution.py:217
  402.5 3.2 copy-start.16
  405.7 2.4 copy-start.13
  416.2 3.2 copy-start.16
  419.4 2.4 copy-start.13
  424.2 1.4 copy-start.17
  425.7 2.5 copy-start.5
  425.7 3.8 copy-start.10
  425.8 3.8 copy-start.28
  426.7 6.3 copy-start.12
  429.5 3.4 copy-start.40
  432.9 11.5 %copy-start.7 = (bf16[1024,1024]{0,1:T(8,128)(2,1)}, bf16[1024,1024]{0,1:T(8,128)(2,1)S(1)}, u32[]{:S(2)}) copy-start(bf16[1024,1024]{0,1:T(8,128)(2,1)S(1)} %fusion.42) | copy-start | bytes 6291460
  444.4 260.5 %reduce-scatter.7.cloned.1.call-start = ((), (), s32[]{:S(2)}) async-start(), calls=%async_computation.9 | async-start | bytes 9437184 | tf_op jit(solution)/shard_map/reduce_scatter | solution.py:228
  456.8 349.0 %all-gather.20.cloned.1.call-start = ((), (), s32[]{:S(2)}) async-start(), calls=%async_computation.13 | async-start | bytes 11796480 | tf_op jit(solution)/shard_map/all_gather | solution.py:196
  473.7 231.1 %copy-start.4 = (bf16[1,128,2048]{2,1,0:T(8,128)(2,1)S(1)}, bf16[1,128,2048]{2,1,0:T(8,128)(2,1)}, u32[]{:S(2)}) copy-start(bf16[1,128,2048]{2,1,0:T(8,128)(2,1)} %param.18) | copy-start | bytes 1572868
  473.7 231.1 %copy-start.6 = (f32[128,2048]{1,0:T(8,128)S(1)}, f32[128,2048]{1,0:T(8,128)}, u32[]{:S(2)}) copy-start(f32[128,2048]{1,0:T(8,128)} %reduce-scatter.5.cloned.1.call-done) | copy-start | bytes 3145732
  473.7 231.1 %copy-start.9 = (bf16[1,128,2048]{2,1,0:T(8,128)(2,1)S(1)}, bf16[1,128,2048]{2,1,0:T(8,128)(2,1)}, u32[]{:S(2)}) copy-start(bf16[1,128,2048]{2,1,0:T(8,128)(2,1)} %param.19) | copy-start | bytes 1572868
  473.7 231.1 %copy-start.23 = (f32[2048]{0:T(1024)S(1)}, f32[2048]{0:T(1024)}, u32[]{:S(2)}) copy-start(f32[2048]{0:T(1024)} %copy-done.22) | copy-start | bytes 24580
  473.8 231.1 %copy-start.25 = (f32[2048]{0:T(1024)S(1)}, f32[2048]{0:T(1024)}, u32[]{:S(2)}) copy-start(f32[2048]{0:T(1024)} %copy-done.24) | copy-start | bytes 24580
  473.8 231.1 %copy-start.31 = (f32[128]{0:T(128)S(1)}, f32[128]{0:T(128)}, u32[]{:S(2)}) copy-start(f32[128]{0:T(128)} %copy-done.30) | copy-start | bytes 1540
  473.8 231.1 %copy-start.34 = (f32[128]{0:T(128)S(1)}, f32[128]{0:T(128)}, u32[]{:S(2)}) copy-start(f32[128]{0:T(128)} %copy-done.33) | copy-start | bytes 1540
  473.8 231.1 %copy-start.36 = (f32[128]{0:T(128)S(1)}, f32[128]{0:T(128)}, u32[]{:S(2)}) copy-start(f32[128]{0:T(128)} %copy-done.35) | copy-start | bytes 1540
  473.8 465.9 %all-gather.18.cloned.1.call-start = ((), (), s32[]{:S(2)}) async-start(), calls=%async_computation.12 | async-start | bytes 16515072 | tf_op jit(solution)/shard_map/all_gather | solution.py:218
  615.8 91.8 %copy-start.26 = (f32[2048]{0:T(1024)S(1)}, f32[2048]{0:T(1024)}, u32[]{:S(2)}) copy-start(f32[2048]{0:T(1024)} %get-tuple-element.208) | copy-start | bytes 24580
  704.9 49.8 %copy-start.11 = (f32[128,2048]{1,0:T(8,128)S(1)}, f32[128,2048]{1,0:T(8,128)}, u32[]{:S(2)}) copy-start(f32[128,2048]{1,0:T(8,128)} %reduce-scatter.7.cloned.1.call-done) | copy-start | bytes 3145732
  752.7 256.0 %copy-start.32 = (f32[2048]{0:T(1024)}, f32[2048]{0:T(1024)S(1)}, u32[]{:S(2)}) copy-start(f32[2048]{0:T(1024)S(1)} %get-tuple-element.444) | copy-start | bytes 24580
  965.5 12.5 %copy-start.2 = (bf16[8,512,768]{1,2,0:T(8,128)(2,1)S(1)}, bf16[8,512,768]{1,2,0:T(8,128)(2,1)}, u32[]{:S(2)}) copy-start(bf16[8,512,768]{1,2,0:T(8,128)(2,1)} %copy.50) | copy-start | bytes 18874372
  996.0 13.4 %copy-start.1 = (bf16[2048,512]{1,0:T(8,128)(2,1)S(1)}, bf16[2048,512]{1,0:T(8,128)(2,1)}, u32[]{:S(2)}) copy-start(bf16[2048,512]{1,0:T(8,128)(2,1)} %param.26) | copy-start | bytes 6291460
  (9 other events, 9.2 us)
Sparse Core Ops, SparseCore 0:
  13.7 49.8 all-gather.9
  66.1 77.5 all-gather.11
  146.1 61.2 all-gather.13
  218.3 90.6 reduce-scatter.4
  312.1 45.4 all-gather.15
  368.4 102.2 reduce-scatter.10
  474.4 137.9 reduce-scatter.8
  615.2 89.5 reduce-scatter.6
  707.1 98.7 all-gather.19
  807.3 132.3 all-gather.17

commit v2 on v0

v2 whole, which is shorter than its diff:
```python
import functools

import jax
import jax.numpy as jnp
from jax import lax
from jax.experimental import pallas as pl
from jax.experimental.pallas import tpu as pltpu
from jax.sharding import PartitionSpec as P

HEADS = 32
HEAD_DIM = 64
ROTARY = 32


norm_eps = 1e-05
rope_base = 10000.0
masked_fill = -1e30
LANES = 128
RADIX = 64

low = jnp.bfloat16
wide = jnp.float32


def dot(a, b, dims):
    return lax.dot_general(a, b, (dims, ((), ())), preferred_element_type=wide)


def after(array, *earlier):
    return lax.optimization_barrier((array, *earlier))[0]


def swap(array, axis, bit):
    return lax.ppermute(array, axis, [(s, s ^ bit) for s in range(lax.axis_size(axis))])


def gather_dp(shard, pair):
    first, second = pair
    half = shard.shape[0] // 2
    third = [swap(first[:half], "dp", 2), swap(second[half:], "dp", 1)]
    return [shard, first, second, jnp.concatenate(third, axis=0)]


def gather_seq(rows):
    count = lax.axis_size("seq")
    near = jnp.concatenate([rows] + [swap(rows, "seq", k) for k in range(2, count, 2)], axis=0)
    return jnp.concatenate([near, swap(near, "seq", 1)], axis=0)


def scatter_seq(partial):
    count = lax.axis_size("seq")
    half = partial.shape[0] // 2
    rows = half // (count // 2)
    chip = partial[:half] + swap(partial[half:].astype(low), "seq", 1).astype(wide)
    total = chip[:rows]
    for k in range(1, count // 2):
        sent = chip[k * rows : (k + 1) * rows].astype(low)
        total = total + swap(sent, "seq", 2 * k).astype(wide)
    return total


def scatter_dp(blocks, *earlier):
    sent = [block.astype(low) for block in blocks[1:]]
    if earlier:
        sent = lax.optimization_barrier((*sent, *earlier))[: len(sent)]
    total = blocks[0]
    for k in range(1, len(blocks)):
        total = total + swap(sent[k - 1], "dp", k).astype(wide)
    return total.astype(low)


def total_dp(array):
    bit = 1
    while bit < lax.axis_size("dp"):
        array = array + swap(array, "dp", bit)
        bit *= 2
    return array


def normalise(values):
    centre = values - jnp.mean(values, axis=-1, keepdims=True)
    spread = jnp.mean(centre * centre, axis=-1, keepdims=True)
    rstd = lax.rsqrt(spread + norm_eps)
    return centre * rstd, rstd


def enter_kernel(
    owners, owner, tokens, teacher, gain, shift, bias_a, bias_b, place, normed, base, held, kept
):
    inputs = tokens[...].astype(wide)
    xhat, _ = normalise(inputs)
    held[...] = xhat * gain[...].astype(wide) + shift[...].astype(wide)
    biases = bias_a[...].astype(wide) + bias_b[...].astype(wide)
    kept[...] = inputs + biases - teacher[...].astype(wide)
    width = inputs.shape[1]
    depth = width // owners
    for k in range(owners):
        theirs = pl.ds(pl.multiple_of((owner[0] ^ k) * depth, LANES), depth)
        normed[:, k * depth : (k + 1) * depth] = held[:, theirs].astype(low)
        base[:, k * depth : (k + 1) * depth] = kept[:, theirs]
    lane = lax.broadcasted_iota(jnp.int32, (inputs.shape[0], LANES), 1)
    facts = jnp.where(lane < 2, place[...] // RADIX, place[...] % RADIX)
    counts = jnp.where(lane < 2, owner[1] // RADIX, owner[1] % RADIX)
    normed[:, width:] = jnp.where(lane % 2 == 0, facts, counts).astype(wide).astype(low)


def enter(tokens, teacher, gain, shift, bias_a, bias_b, place, owner, counted, owners):
    rows, width = tokens.shape
    whole = pl.BlockSpec(memory_space=pltpu.VMEM)
    return pl.pallas_call(
        functools.partial(enter_kernel, owners),
        in_specs=[pl.BlockSpec(memory_space=pltpu.SMEM)] + [whole] * 7,
        out_specs=[whole] * 2,
        out_shape=[
            jax.ShapeDtypeStruct((rows, width + LANES), low),
            jax.ShapeDtypeStruct((rows, width), wide),
        ],
        scratch_shapes=[pltpu.VMEM((rows, width), wide)] * 2,
        name="enter",
    )(
        jnp.stack([owner, counted]),
        tokens,
        teacher,
        gain[None],
        shift[None],
        bias_a[None],
        bias_b[None],
        place[:, None],
    )


def leave_kernel(
    owners, owner, tokens, gain, summed, grad, bias, token_grad, gain_grad, shift_grad, bias_grad
):
    inputs = tokens[...].astype(wide)
    xhat, rstd = normalise(inputs)
    depth = inputs.shape[1] // owners
    for k in range(owners):
        theirs = pl.ds(pl.multiple_of((owner[0] ^ k) * depth, LANES), depth)
        token_grad[:, theirs] = summed[:, k * depth : (k + 1) * depth]
        bias_grad[:, theirs] = bias[:, k * depth : (k + 1) * depth]
    normed_grad = token_grad[...]
    gain_grad[...] = jnp.sum(normed_grad * xhat, axis=0, keepdims=True)
    shift_grad[...] = jnp.sum(normed_grad, axis=0, keepdims=True)
    scaled = normed_grad * gain[...].astype(wide)
    token_grad[...] = rstd * (
        scaled
        - jnp.mean(scaled, axis=-1, keepdims=True)
        - xhat * jnp.mean(scaled * xhat, axis=-1, keepdims=True)
    )
    for k in range(owners):
        theirs = pl.ds(pl.multiple_of((owner[0] ^ k) * depth, LANES), depth)
        token_grad[:, theirs] += grad[:, k * depth : (k + 1) * depth]


def leave(tokens, gain, summed, grad, bias, owner, owners):
    rows, width = tokens.shape
    whole = pl.BlockSpec(memory_space=pltpu.VMEM)
    line = jax.ShapeDtypeStruct((1, width), wide)
    return pl.pallas_call(
        functools.partial(leave_kernel, owners),
        in_specs=[pl.BlockSpec(memory_space=pltpu.SMEM)] + [whole] * 5,
        out_specs=[whole] * 4,
        out_shape=[jax.ShapeDtypeStruct((rows, width), wide), line, line, line],
        name="leave",
    )(owner[None], tokens, gain[None], summed, grad, bias[None])


def pick_kernel(first, part, a_ref, b_ref, out_ref):
    piece = pl.program_id(0)

    @pl.when(piece < first)
    def _():
        out_ref[...] = a_ref[...]

    @pl.when(piece >= first)
    def _():
        out_ref[...] = b_ref[...]


def pick(a, b, part, block, first, pieces, a_map, b_map, out_map, out_shape):
    return pl.pallas_call(
        functools.partial(pick_kernel, first),
        grid_spec=pltpu.PrefetchScalarGridSpec(
            num_scalar_prefetch=1,
            grid=(pieces,),
            in_specs=[
                pl.BlockSpec(block, lambda p, part: a_map(jnp.minimum(p, first - 1), part[0])),
                pl.BlockSpec(block, lambda p, part: b_map(jnp.maximum(p - first, 0), part[0])),
            ],
            out_specs=pl.BlockSpec(block, lambda p, part: out_map(p)),
        ),
        out_shape=jax.ShapeDtypeStruct(out_shape, a.dtype),
        name="pick",
    )(part[None], a, b)


def gelu_parts(values):
    root = (2.0 / jnp.pi) ** 0.5
    square = values * values
    bent = jnp.tanh(root * (values + 0.044715 * (values * square)))
    factor = 0.5 * (1.0 + bent)
    slope = 0.5 * values * (1.0 - bent * bent) * (root * (1.0 + 3.0 * 0.044715 * square))
    return factor, factor + slope


def turn(values, cosine, sine):
    lane = lax.broadcasted_iota(jnp.int32, values.shape, 1) % HEAD_DIM
    half, width = ROTARY // 2, values.shape[1]
    partner = jnp.where(
        lane < half, pltpu.roll(values, width - half, 1), pltpu.roll(values, half, 1)
    )
    return values * cosine + partner * sine


def project_kernel(count, normed, cosine, sine, bias, *refs):
    weights, (qkv, hidden, stacked) = refs[:count], refs[count:]
    tile = pl.program_id(0)
    depth = weights[0].shape[0]
    total = jnp.dot(normed[:, :depth], weights[0][...], preferred_element_type=wide)
    for k in range(1, count):
        block = normed[:, k * depth : (k + 1) * depth]
        total = total + jnp.dot(block, weights[k][...], preferred_element_type=wide)
    total = total + bias[...]
    repeats = total.shape[1] // LANES

    @pl.when(tile < 2)
    def _():
        turned = turn(
            total,
            jnp.concatenate([cosine[...]] * repeats, axis=1),
            jnp.concatenate([sine[...]] * repeats, axis=1),
        )
        qkv[...] = turned.astype(low)

    @pl.when(tile == 2)
    def _():
        qkv[...] = total.astype(low)

    @pl.when(tile > 2)
    def _():
        hidden[...] = total
        stacked[...] = (total * gelu_parts(total)[0]).astype(low)


def project(normed, cosine, sine, bias, weights, head_width):
    count = len(weights)
    length = normed.shape[0]
    depth, inside = weights[0].shape
    units = inside - 3 * head_width
    table = pl.BlockSpec((length, LANES), lambda t: (0, 0))
    return pl.pallas_call(
        functools.partial(project_kernel, count),
        grid=(inside // head_width,),
        in_specs=[
            pl.BlockSpec(normed.shape, lambda t: (0, 0)),
            table,
            table,
            pl.BlockSpec((1, head_width), lambda t: (0, t)),
        ]
        + [pl.BlockSpec((depth, head_width), lambda t: (0, t))] * count,
        out_specs=[
            pl.BlockSpec((length, head_width), lambda t: (0, jnp.minimum(t, 2))),
            pl.BlockSpec((length, head_width), lambda t: (0, jnp.maximum(t - 3, 0))),
            pl.BlockSpec((length, head_width), lambda t: (0, jnp.maximum(t - 2, 1))),
        ],
        out_shape=[
            jax.ShapeDtypeStruct((length, 3 * head_width), low),
            jax.ShapeDtypeStruct((length, units), wide),
            jax.ShapeDtypeStruct((length, head_width + units), low),
        ],
        cost_estimate=pl.CostEstimate(
            flops=2 * length * count * depth * inside,
            bytes_accessed=2 * (count * depth * inside + normed.size) + 8 * length * inside,
            transcendentals=length * units,
        ),
        name="project",
    )(normed, cosine, sine, bias, *weights)


def slot_of(block, part, chips):
    apart = block ^ part
    return (apart % 2) * chips + apart // 2


def scores_of(rows, keys, start):
    raw = lax.dot_general(rows, keys, (((1,), (1,)), ((), ())), preferred_element_type=wide)
    place = start + lax.broadcasted_iota(jnp.int32, raw.shape, 0)
    kept = lax.broadcasted_iota(jnp.int32, raw.shape, 1) <= place
    return jnp.where(kept, raw * HEAD_DIM ** (-0.5), masked_fill)


def attend_kernel(chips, step, part, qkv, stacked, out, logsum, held, result):
    del stacked
    length, head_width = out.shape
    rows = length // (2 * chips)
    for n in range(2 * chips):
        source = pl.ds(pl.multiple_of(slot_of(n, part[0], chips) * rows, rows), rows)
        held[n * rows : (n + 1) * rows, :] = qkv[source, :]
    lane = lax.broadcasted_iota(jnp.int32, (step, LANES), 1)
    for first in range(0, length, step):
        last = first + step
        sums = jnp.zeros((step, LANES), wide)
        outs = []
        for h in range(head_width // HEAD_DIM):
            a, b = h * HEAD_DIM, (h + 1) * HEAD_DIM
            keys = held[:last, head_width + a : head_width + b]
            values = held[:last, 2 * head_width + a : 2 * head_width + b]
            scores = scores_of(held[first:last, a:b], keys, first)
            top = jnp.max(scores, axis=-1, keepdims=True)
            expd = jnp.exp(scores - top)
            total = jnp.sum(expd, axis=-1, keepdims=True)
            probs = (expd * (1.0 / total)).astype(low)
            outs.append(jnp.dot(probs, values, preferred_element_type=wide))
            sums = jnp.where(lane == h, top + jnp.log(total), sums)
        result[first:last, :] = jnp.concatenate(outs, axis=1).astype(low)
        logsum[first:last, :] = sums
    for n in range(2 * chips):
        target = pl.ds(pl.multiple_of(slot_of(n, part[0], chips) * rows, rows), rows)
        out[target, :] = result[n * rows : (n + 1) * rows, :]


def attend(qkv, stacked, part, chips):
    length, three = qkv.shape
    head_width = three // 3
    heads = head_width // HEAD_DIM
    whole = pl.BlockSpec(memory_space=pltpu.VMEM)
    return pl.pallas_call(
        functools.partial(attend_kernel, chips, min(256, length)),
        grid=(1,),
        in_specs=[
            pl.BlockSpec(memory_space=pltpu.SMEM),
            whole,
            pl.BlockSpec(memory_space=pl.ANY),
        ],
        out_specs=[pl.BlockSpec((length, head_width), lambda n: (0, 0)), whole],
        out_shape=[
            jax.ShapeDtypeStruct(stacked.shape, low),
            jax.ShapeDtypeStruct((length, LANES), wide),
        ],
        scratch_shapes=[pltpu.VMEM((length, three), low), pltpu.VMEM((length, head_width), low)],
        input_output_aliases={2: 0},
        cost_estimate=pl.CostEstimate(
            flops=4 * heads * length * length * LANES,
            bytes_accessed=8 * length * three,
            transcendentals=heads * length * length,
        ),
        name="attend",
    )(part[None], qkv, stacked)


def attend_back_kernel(
    chips, step, part, qkv, grad, logsum, cosine, sine, entered, out, held, given, gone
):
    del entered
    length, head_width = grad.shape
    rows = length // (2 * chips)
    scale = HEAD_DIM ** (-0.5)
    for n in range(2 * chips):
        source = pl.ds(pl.multiple_of(slot_of(n, part[0], chips) * rows, rows), rows)
        held[n * rows : (n + 1) * rows, :] = qkv[source, :]
        given[n * rows : (n + 1) * rows, :] = grad[source, :]
    over_rows = (((0,), (0,)), ((), ()))
    for first in reversed(range(0, length, step)):
        last = first + step
        parts = [[], [], []]
        for h in range(head_width // HEAD_DIM):
            a, b = h * HEAD_DIM, (h + 1) * HEAD_DIM
            query = held[first:last, a:b]
            keys = held[:last, head_width + a : head_width + b]
            values = held[:last, 2 * head_width + a : 2 * head_width + b]
            upstream = given[first:last, a:b]
            probs = jnp.exp(scores_of(query, keys, first) - logsum[first:last, h : h + 1])
            prob_grad = lax.dot_general(
                upstream, values, (((1,), (1,)), ((), ())), preferred_element_type=wide
            )
            inner = jnp.sum(probs * prob_grad, axis=-1, keepdims=True)
            score_grad = (probs * (prob_grad - inner)).astype(low)
            parts[0].append(jnp.dot(score_grad, keys, preferred_element_type=wide) * scale)
            parts[1].append(
                lax.dot_general(score_grad, query, over_rows, preferred_element_type=wide) * scale
            )
            parts[2].append(
                lax.dot_general(
                    probs.astype(low), upstream, over_rows, preferred_element_type=wide
                )
            )
        parts = [jnp.concatenate(part_list, axis=1) for part_list in parts]
        gone[first:last, :head_width] = parts[0]
        for t in (1, 2):
            columns = slice(t * head_width, (t + 1) * head_width)
            if last == length:
                gone[:, columns] = parts[t]
            else:
                gone[:last, columns] += parts[t]
    repeats = head_width // LANES
    for n in range(2 * chips):
        target = pl.ds(pl.multiple_of(slot_of(n, part[0], chips) * rows, rows), rows)
        here = slice(n * rows, (n + 1) * rows)
        ahead = jnp.concatenate([cosine[target, :]] * repeats, axis=1)
        aside = -jnp.concatenate([sine[target, :]] * repeats, axis=1)
        for t in range(3):
            columns = slice(t * head_width, (t + 1) * head_width)
            value = gone[here, columns].astype(low)
            if t < 2:
                value = turn(value.astype(wide), ahead, aside).astype(low)
            out[target, columns] = value


def attend_back(qkv, grad, logsum, cosine, sine, entered, part, chips):
    length, three = qkv.shape
    head_width = three // 3
    heads = head_width // HEAD_DIM
    whole = pl.BlockSpec(memory_space=pltpu.VMEM)
    return pl.pallas_call(
        functools.partial(attend_back_kernel, chips, min(256, length)),
        grid=(1,),
        in_specs=[pl.BlockSpec(memory_space=pltpu.SMEM)]
        + [whole] * 5
        + [pl.BlockSpec(memory_space=pl.ANY)],
        out_specs=pl.BlockSpec((length, three), lambda n: (0, 0)),
        out_shape=jax.ShapeDtypeStruct(entered.shape, low),
        scratch_shapes=[
            pltpu.VMEM((length, three), low),
            pltpu.VMEM((length, head_width), low),
            pltpu.VMEM((length, three), wide),
        ],
        input_output_aliases={6: 0},
        cost_estimate=pl.CostEstimate(
            flops=10 * heads * length * length * LANES,
            bytes_accessed=8 * length * three,
            transcendentals=heads * length * length,
        ),
        name="attend_back",
    )(part[None], qkv, grad, logsum, cosine, sine, entered)


def reject_kernel(count, hidden, *refs):
    grads, weights = refs[:count], refs[count : 2 * count]
    head_grad, entered = refs[2 * count :]
    over = (((1,), (1,)), ((), ()))
    total = lax.dot_general(grads[0][...], weights[0][...], over, preferred_element_type=wide)
    for k in range(1, count):
        total = total + lax.dot_general(
            grads[k][...], weights[k][...], over, preferred_element_type=wide
        )

    @pl.when(pl.program_id(0) == 0)
    def _():
        head_grad[...] = total.astype(low)

    @pl.when(pl.program_id(0) > 0)
    def _():
        entered[...] = (total * gelu_parts(hidden[...])[1]).astype(low)


def reject(grads, weights, hidden, head_width):
    count = len(grads)
    length, depth = grads[0].shape
    behind = weights[0].shape[0]
    inside = behind + 2 * head_width
    return pl.pallas_call(
        functools.partial(reject_kernel, count),
        grid=(behind // head_width,),
        in_specs=[pl.BlockSpec((length, head_width), lambda t: (0, jnp.maximum(t - 1, 0)))]
        + [pl.BlockSpec((length, depth), lambda t: (0, 0))] * count
        + [pl.BlockSpec((head_width, depth), lambda t: (t, 0))] * count,
        out_specs=[
            pl.BlockSpec((length, head_width), lambda t: (0, 0)),
            pl.BlockSpec((length, head_width), lambda t: (0, jnp.maximum(t + 2, 3))),
        ],
        out_shape=[
            jax.ShapeDtypeStruct((length, head_width), low),
            jax.ShapeDtypeStruct((length, inside), low),
        ],
        cost_estimate=pl.CostEstimate(
            flops=2 * length * count * depth * behind,
            bytes_accessed=2 * count * depth * (behind + length) + 8 * length * behind,
            transcendentals=length * behind,
        ),
        name="reject",
    )(hidden, *grads, *weights)


def widen_kernel(*refs):
    refs[-1][...] = refs[0][0].astype(wide)


def widen(gathered, shape, block_shape, grid, source, target, into=None):
    in_specs = [pl.BlockSpec((1, *block_shape), lambda j, p: (j, *source(p)))]
    operands = [gathered]
    if into is not None:
        in_specs.append(pl.BlockSpec(memory_space=pl.ANY))
        operands.append(into)
    moved = 6 * grid[0] * grid[1] * block_shape[0] * block_shape[1]
    return pl.pallas_call(
        widen_kernel,
        grid=grid,
        in_specs=in_specs,
        out_specs=pl.BlockSpec(block_shape, target),
        out_shape=jax.ShapeDtypeStruct(shape, wide),
        input_output_aliases={} if into is None else {1: 0},
        cost_estimate=pl.CostEstimate(flops=0, bytes_accessed=moved, transcendentals=0),
        name="widen",
    )(*operands)


def local(
    tokens,
    teacher,
    valid,
    positions,
    norm_gain,
    norm_bias,
    qkv_weight,
    qkv_bias,
    out_weight,
    out_bias,
    up_weight,
    up_bias,
    down_weight,
    down_bias,
):
    rows_here, width = tokens.shape[1:]
    seq_count = lax.axis_size("seq")
    data_count = lax.axis_size("dp")
    part = lax.axis_index("seq")
    owner = lax.axis_index("dp")
    length = rows_here * seq_count
    chips = seq_count // 2
    head_width = HEADS // seq_count * HEAD_DIM
    three = 3 * head_width
    units = up_weight.shape[1] // seq_count
    inside = three + units
    depth = qkv_weight.shape[0]
    chunks = units // head_width
    mask = valid[0].astype(wide)

    counted = total_dp(jnp.sum(valid[0]).reshape(1, 1))
    normed_low, base = enter(
        tokens[0],
        teacher[0],
        norm_gain,
        norm_bias,
        out_bias,
        down_bias,
        positions[0],
        owner,
        counted[0, 0],
        data_count,
    )

    w_in = pick(
        qkv_weight,
        up_weight,
        part,
        (depth, head_width),
        3,
        3 + chunks,
        lambda p, part: (0, p * seq_count + part),
        lambda p, part: (0, part * chunks + p),
        lambda p: (0, p),
        (depth, inside),
    )
    w_back = pick(
        out_weight,
        down_weight,
        after(part, normed_low),
        (head_width, depth),
        1,
        1 + chunks,
        lambda p, part: (part, 0),
        lambda p, part: (part * chunks + p, 0),
        lambda p: (p, 0),
        (head_width + units, depth),
    )
    in_sent = after(w_in, counted)
    if data_count == 4:
        in_pair = (swap(in_sent, "dp", 1), swap(in_sent, "dp", 2))
        *in_pair, back_sent = lax.optimization_barrier((*in_pair, w_back))
        back_pair = (swap(back_sent, "dp", 1), swap(back_sent, "dp", 2))
        w_in = gather_dp(w_in, in_pair)
        w_back = gather_dp(w_back, back_pair)
    else:
        w_in = [w_in] + [swap(in_sent, "dp", k) for k in range(1, data_count)]
        w_back = [w_back] + [swap(w_back, "dp", k) for k in range(1, data_count)]
    normed_all = gather_seq(normed_low)
    facts = normed_all[:, width : width + 4].astype(jnp.int32)
    where = facts[:, 0] * RADIX + facts[:, 2]
    count = jnp.sum((facts[:, 1] * RADIX + facts[:, 3])[::rows_here]).astype(wide)

    half = ROTARY // 2
    lane = jnp.arange(LANES, dtype=jnp.int32) % HEAD_DIM
    freqs = rope_base ** (-((lane % half).astype(wide) * 2.0) / ROTARY)
    angles = where.astype(wide)[:, None] * jnp.where(lane < ROTARY, freqs, 0.0)[None, :]
    cosine = jnp.cos(angles)
    sine = jnp.sin(angles) * jnp.where(lane < half, -1.0, 1.0)[None, :]

    b_in = jnp.concatenate(
        [
            lax.dynamic_slice_in_dim(qkv_bias, t * width + part * head_width, head_width, 0)
            for t in range(3)
        ]
        + [lax.dynamic_slice_in_dim(up_bias, part * units, units, 0)]
    ).astype(wide)[None]

    def piece(k):
        return normed_all[:, k * depth : (k + 1) * depth]

    qkv, hidden, stacked = project(normed_all, cosine, sine, b_in, w_in, head_width)
    stacked, logsum = attend(qkv, stacked, part, chips)

    if data_count == 4:
        groups = [[0], [1, 2], [3]]
    else:
        groups = [[k] for k in range(data_count)]
    scale = length * data_count / count
    squares = jnp.zeros((), wide)
    grad_output, grad_all = [], []
    for group in groups:
        branches = jnp.concatenate([dot(stacked, w_back[k], ((1,), (0,))) for k in group], axis=1)
        error = base[:, group[0] * depth : (group[-1] + 1) * depth] + scatter_seq(branches)
        weighted = mask[:, None] * error
        squares = squares + jnp.sum(weighted * error)
        grad_output.append(scale * weighted)
        gathered = gather_seq((scale * weighted).astype(low))
        grad_all += [gathered[:, n * depth : (n + 1) * depth] for n in range(len(group))]
    grad_output = jnp.concatenate(grad_output, axis=1)
    branch_bias_grad = jnp.concatenate([jnp.sum(item.astype(wide), axis=0) for item in grad_all])

    def owned(left, right):
        return dot(left, right, ((0,), (0,)))

    cut = units // 4

    def of_stacked(first, last):
        return [owned(stacked[:, first:last], grad) for grad in grad_all]

    down_a = scatter_dp(of_stacked(head_width, head_width + cut))
    down_b = scatter_dp(of_stacked(head_width + cut, head_width + units), down_a)

    head_grad, in_low = reject(grad_all, w_back, hidden, head_width)
    hidden_low = in_low[:, three:]
    up_grad = scatter_dp([owned(piece(k), hidden_low) for k in range(data_count)], down_b)

    head_grad = after(head_grad, down_b)
    in_low = attend_back(qkv, head_grad, logsum, cosine, sine, in_low, part, chips)
    in_low = after(in_low, up_grad)
    mixed_low = in_low[:, :three]
    qkv_grad = scatter_dp([owned(piece(k), mixed_low) for k in range(data_count)], up_grad)
    out_grad = scatter_dp(of_stacked(0, head_width), qkv_grad)

    normed_grad = jnp.concatenate(
        [dot(in_low, w_in[k], ((1,), (1,))) for k in range(data_count)], axis=1
    )
    token_grad, gain_grad, shift_grad, branch_bias_grad = leave(
        tokens[0],
        norm_gain,
        scatter_seq(normed_grad),
        grad_output,
        branch_bias_grad,
        owner,
        data_count,
    )

    in_bias = jnp.sum(in_low.astype(wide), axis=0)
    small = jnp.concatenate(
        [in_bias, gain_grad[0], shift_grad[0], squares[None], branch_bias_grad[0]]
    )
    small = total_dp(small[None])[0]
    branch_bias_grad = small[-width:]
    small = small[:-width]
    lines = -(-small.size // depth)
    lines += -lines % 8
    high = jnp.pad(small, (0, lines * depth - small.size)).reshape(lines, depth)
    first = lax.reduce_precision(high, 8, 7)
    beside = jnp.concatenate([first.astype(low), (high - first).astype(low)])

    def gather(array):
        return lax.all_gather(array, "seq", axis=0, tiled=False)

    down_a, down_b = gather(down_a), gather(down_b)
    all_units = seq_count * units
    down_weight_grad = widen(
        down_a,
        (all_units, depth),
        (cut, depth),
        (seq_count, 1),
        lambda p: (p, 0),
        lambda j, p: (4 * j, 0),
    )
    down_weight_grad = widen(
        down_b,
        (all_units, depth),
        (cut, depth),
        (seq_count, 3),
        lambda p: (p, 0),
        lambda j, p: (4 * j + 1 + p, 0),
        down_weight_grad,
    )
    up_all = gather(after(up_grad, down_a))
    qkv_all = gather(after(qkv_grad, down_weight_grad))
    up_weight_grad = widen(
        up_all,
        (depth, all_units),
        (depth, units),
        (seq_count, 1),
        lambda p: (0, 0),
        lambda j, p: (0, j),
    )
    qkv_weight_grad = widen(
        qkv_all,
        (depth, 3 * width),
        (depth, head_width),
        (seq_count, 3),
        lambda p: (0, p),
        lambda j, p: (0, p * seq_count + j),
    )
    beside = after(jnp.concatenate([out_grad, beside], axis=0), up_weight_grad)
    out_all = gather(beside)
    out_weight_grad = widen(
        out_all,
        (width, depth),
        (head_width, depth),
        (seq_count, 1),
        lambda p: (0, 0),
        lambda j, p: (j, 0),
    )
    slots = out_all[:, head_width:].astype(wide)
    slots = (slots[:, :lines] + slots[:, lines:]).reshape(seq_count, -1)
    norm_grads = jnp.sum(slots[:, inside : inside + 2 * width + 1], axis=0)
    qkv_bias_grad = slots[:, :three].reshape(seq_count, 3, head_width).transpose(1, 0, 2)
    up_bias_grad = slots[:, three:inside].reshape(-1)
    loss = norm_grads[-1] / (2.0 * width * count)
    return (
        loss,
        token_grad[None],
        norm_grads[:width],
        norm_grads[width : 2 * width],
        qkv_weight_grad,
        qkv_bias_grad.reshape(-1),
        out_weight_grad,
        branch_bias_grad,
        up_weight_grad,
        up_bias_grad,
        down_weight_grad,
        branch_bias_grad,
    )


def solution(mesh):
    placed = (
        P("dp", "seq", None),
        P("dp", "seq", None),
        P("dp", "seq"),
        P("dp", "seq"),
        P(),
        P(),
        P("dp", None),
        P(),
        P(None, "dp"),
        P(),
        P("dp", None),
        P(),
        P(None, "dp"),
        P(),
    )
    return jax.shard_map(
        local,
        mesh=mesh,
        in_specs=placed,
        out_specs=(
            P(),
            P("dp", "seq", None),
            P(),
            P(),
            P("dp", None),
            P(),
            P(None, "dp"),
            P(),
            P("dp", None),
            P(),
            P(None, "dp"),
            P(),
        ),
        check_vma=False,
    )
```

time: 3350 us -> 704 us (0.21)
  waiting for transfers between devices: 2790 us -> 337 us
  matrix products: 248 us -> 70.2 us
  blocking collectives: 165 us -> 0 us
  Pallas kernels: 0 us -> 127 us
  starting transfers between devices: 13.3 us -> 88.3 us
    reduce_scatter x4 -> x0, waiting for transfers between devices: 1810 us -> none  [the longest x1 708 us: local(): lax.psum_scatter(up_grad, ('dp', 'seq'), scatter_dimension=0, tiled=True)]
    all_gather x8 -> x5, waiting for transfers between devices: 899 us -> 82.1 us  [gather(): return lax.all_gather(array, 'seq', axis=0, tiled=False)]
    ppermute x0 -> x59, waiting for transfers between devices: none -> 254 us  [swap(): lax.ppermute(array, axis, [(s, s ^ bit) for s in range(lax.axis_size(axis...]
    dot_general x26 -> x28, matrix products: 248 us -> 70.2 us  [dot(): return lax.dot_general(a, b, (dims, ((), ())), preferred_element_type=wide)]
    pallas_call x0 -> x13, Pallas kernels: none -> 127 us  [the longest x5 53.6 us: widen(): pl.pallas_call(widen_kernel, grid=grid, in_specs=in_specs, out_specs=pl.B...]
    ppermute x0 -> x59, starting transfers between devices: none -> 87.9 us  [swap(): lax.ppermute(array, axis, [(s, s ^ bit) for s in range(lax.axis_size(axis...]
    psum x2 -> x0, blocking collectives: 83.1 us -> none  [local(): lax.psum((jnp.sum(mask), jnp.sum(weighted * (output - target))), ('dp', '...]
    all_to_all x1 -> x0, blocking collectives: 82 us -> none  [local(): lax.all_to_all(stacked, 'seq', split_axis=0, concat_axis=2, tiled=True)]
  transfers between devices with their start and end apart: 15 -> 64, of which waited for: 11 -> 27; matrix products, arithmetic and copies ran while one was open for 9% -> 16% of each run, Pallas kernels for 0% -> 16%
where the time goes in v2:
time: 704 us; the launch traced here: 697 us
  waiting for transfers between devices  337 us (48%)
  Pallas kernels  127 us (18%)
  starting transfers between devices  88.3 us (13%)
  matrix products  70.2 us (10%)
  local copies, waits for them, and re-layouts  30 us (4%)
  other arithmetic  23 us (3%)
  between operations  21.3 us (3%)
    ppermute x59, waiting for transfers between devices, swap(): lax.ppermute(array, axis, [(s, s ^ bit) for s in range(lax.axis_size(axis...  254 us
    ppermute x59, starting transfers between devices, swap(): lax.ppermute(array, axis, [(s, s ^ bit) for s in range(lax.axis_size(axis...  87.9 us
    all_gather x5, waiting for transfers between devices, gather(): return lax.all_gather(array, 'seq', axis=0, tiled=False)  82.1 us
    dot_general x28, matrix products, dot(): return lax.dot_general(a, b, (dims, ((), ())), preferred_element_type=wide)  70.2 us
    pallas_call x5, Pallas kernels, widen(): pl.pallas_call(widen_kernel, grid=grid, in_specs=in_specs, out_specs=pl.B...  53.6 us
    pallas_call x1, Pallas kernels, project(): pl.pallas_call(functools.partial(project_kernel, count), grid=(inside //...  16.8 us
    pallas_call x1, Pallas kernels, attend_back(): pl.pallas_call(functools.partial(attend_back_kernel, chips, min(256, leng...  16.6 us
  transfers between devices with their start and end apart: 64, of which 27 were waited for; matrix products, arithmetic and copies ran while one was open for 16% of the time, Pallas kernels for 16%

profile of v2, /device:TPU:0, one launch (start us, length us, event | category | flops | bytes accessed | tf_op | source)
XLA Modules:
  0.0 696.5 jit_solution(4446199446794759439)
XLA Ops:
  11.6 5.3 pick.2.refs_0_
  37.3 16.6 %collective-permute-done.2 = bf16[128,2176]{1,0:T(8,128)(2,1)S(1)} collective-permute-done((bf16[128,2176]{1,0:T(8,128)(2,1)}, bf16[128,2176]{1,0:T(8,128)(2,1)S(1)}, u32[]{:S(2)}, u32[]{:S(2)}) %collective-permute-start.2) | collective-permute-done | bytes 557088 | tf_op jit(solution)/shard_map/ppermute | solution.py:34
  53.9 19.6 %collective-permute-done.3 = bf16[128,2176]{1,0:T(8,128)(2,1)S(1)} collective-permute-done((bf16[128,2176]{1,0:T(8,128)(2,1)}, bf16[128,2176]{1,0:T(8,128)(2,1)S(1)}, u32[]{:S(2)}, u32[]{:S(2)}) %collective-permute-start.3) | collective-permute-done | bytes 557088 | tf_op jit(solution)/shard_map/ppermute | solution.py:34
  76.7 4.1 pick.3.refs_4_
  87.9 17.4 %collective-permute-done.8 = bf16[256,1792]{1,0:T(8,128)(2,1)S(1)} collective-permute-done((bf16[256,1792]{1,0:T(8,128)(2,1)S(1)}, bf16[256,1792]{1,0:T(8,128)(2,1)S(1)}, u32[]{:S(2)}, u32[]{:S(2)}) %collective-permute-start.8) | collective-permute-done | bytes 917536 | tf_op jit(solution)/shard_map/ppermute | solution.py:34
  116.2 16.8 %project.1 = (bf16[1024,768]{1,0:T(8,128)(2,1)}, f32[1024,1024]{1,0:T(8,128)}, bf16[1024,1280]{1,0:T(8,128)(2,1)}) custom-call(bf16[1024,2176]{1,0:T(8,128)(2,1)} %copy-done.18, f32[1024,128]{1,0:T(8,128)} %get-tuple-element.129.cosine, f32[1024,128]{1,0:T(8,128)} %get-tuple-element.128.sine, f32[1,1792]{1,0:T(1,128)} %maximum_convert_fusion.bias, ...), custom_call_target="tpu_custom_call" | custom-call | flops 7516192768 | bytes 26476544 | tf_op jit(solution)/shard_map/project/pallas_call | solution.py:252
  133.1 10.1 %attend.1 = (bf16[1024,1280]{1,0:T(8,128)(2,1)}, f32[1024,128]{1,0:T(8,128)}) custom-call(s32[1]{0:T(128)} %bitcast.part, bf16[1024,768]{1,0:T(8,128)(2,1)} %get-tuple-element.52.qkv, bf16[1024,1280]{1,0:T(8,128)(2,1)} %get-tuple-element.53.stacked), custom_call_target="tpu_custom_call", output_to_operand_aliasing={{0}: (2, {})} | custom-call | flops 2147483648 | bytes 6291456 | tf_op jit(solution)/shard_map/attend/pallas_call | solution.py:328
  143.2 3.2 fusion.90
  155.3 3.6 fusion.92
  163.6 4.7 collective-permute-done.28
  175.0 7.9 %collective-permute-start.12 = (bf16[128,512]{1,0:T(8,128)(2,1)S(1)}, bf16[128,512]{1,0:T(8,128)(2,1)S(1)}, u32[]{:S(2)}, u32[]{:S(2)}) collective-permute-start(bf16[128,512]{1,0:T(8,128)(2,1)S(1)} %get-tuple-element.117), channel_id=1, source_target_pairs={{0,4},{1,5},{2,6},{3,7},{4,0},{5,1},{6,2},{7,3},{8,12},{9,13},{10,... | collective-permute-start | bytes 393224 | tf_op jit(solution)/shard_map/ppermute | solution.py:34
  190.6 7.8 %collective-permute-done.12 = bf16[128,512]{1,0:T(8,128)(2,1)S(1)} collective-permute-done((bf16[128,512]{1,0:T(8,128)(2,1)S(1)}, bf16[128,512]{1,0:T(8,128)(2,1)S(1)}, u32[]{:S(2)}, u32[]{:S(2)}) %collective-permute-start.12) | collective-permute-done | bytes 131104 | tf_op jit(solution)/shard_map/ppermute | solution.py:34
  202.8 12.5 %collective-permute-done.32 = bf16[128,512]{1,0:T(8,128)(2,1)S(1)} collective-permute-done((bf16[128,512]{1,0:T(8,128)(2,1)S(1)}, bf16[128,512]{1,0:T(8,128)(2,1)S(1)}, u32[]{:S(2)}, u32[]{:S(2)}) %collective-permute-start.32) | collective-permute-done | bytes 131104 | tf_op jit(solution)/shard_map/ppermute | solution.py:34
  220.8 11.4 %collective-permute-done.22 = bf16[128,1024]{1,0:T(8,128)(2,1)S(1)} collective-permute-done((bf16[128,1024]{1,0:T(8,128)(2,1)S(1)}, bf16[128,1024]{1,0:T(8,128)(2,1)S(1)}, u32[]{:S(2)}, u32[]{:S(2)}) %collective-permute-start.22) | collective-permute-done | bytes 262176 | tf_op jit(solution)/shard_map/ppermute | solution.py:34
  237.7 7.0 %collective-permute-start.25 = (bf16[128,1024]{1,0:T(8,128)(2,1)S(1)}, bf16[128,1024]{1,0:T(8,128)(2,1)S(1)}, u32[]{:S(2)}, u32[]{:S(2)}) collective-permute-start(bf16[128,1024]{1,0:T(8,128)(2,1)S(1)} %get-tuple-element.98), channel_id=1, source_target_pairs={{0,4},{1,5},{2,6},{3,7},{4,0},{5,1},{6,2},{7,3},{8,12},{9,13},{10,... | collective-permute-start | bytes 786440 | tf_op jit(solution)/shard_map/ppermute | solution.py:34
  247.0 3.2 collective-permute-done.24
  250.1 15.8 %collective-permute-done.25 = bf16[128,1024]{1,0:T(8,128)(2,1)S(1)} collective-permute-done((bf16[128,1024]{1,0:T(8,128)(2,1)S(1)}, bf16[128,1024]{1,0:T(8,128)(2,1)S(1)}, u32[]{:S(2)}, u32[]{:S(2)}) %collective-permute-start.25) | collective-permute-done | bytes 262176 | tf_op jit(solution)/shard_map/ppermute | solution.py:34
  278.6 4.9 collective-permute-done.39
  286.0 13.2 %reject.1 = (bf16[1024,256]{1,0:T(8,128)(2,1)}, bf16[1024,1792]{1,0:T(8,128)(2,1)}) custom-call(f32[1024,1024]{1,0:T(8,128)} %get-tuple-element.57.hidden, bf16[1024,512]{1,0:T(8,128)(2,1)} %copy-done.8, bf16[1024,512]{1,0:T(8,128)(2,1)} %get-tuple-element.111.refs_1_, bf16[1024,512]{1,0:T(8,128)(2,1)} %get-tuple-element.110.refs_2_, ...), custom_call_target="tpu_custom_call" | custom-call | flops 5368709120 | bytes 19922944 | tf_op jit(solution)/shard_map/reject/pallas_call | solution.py:462
  302.7 4.3 convolution_convert_fusion.2
  307.0 3.5 convolution_convert_fusion.1
  310.5 3.6 convolution_convert_fusion
  314.1 6.7 collective-permute-done.43
  320.8 14.3 %collective-permute-done.42 = bf16[768,512]{1,0:T(8,128)(2,1)S(1)} collective-permute-done((bf16[768,512]{1,0:T(8,128)(2,1)}, bf16[768,512]{1,0:T(8,128)(2,1)S(1)}, u32[]{:S(2)}, u32[]{:S(2)}) %collective-permute-start.42) | collective-permute-done | bytes 786464 | tf_op jit(solution)/shard_map/ppermute | solution.py:34
  340.6 23.8 %collective-permute-done.46 = bf16[512,1024]{1,0:T(8,128)(2,1)S(1)} collective-permute-done((bf16[512,1024]{1,0:T(8,128)(2,1)}, bf16[512,1024]{1,0:T(8,128)(2,1)S(1)}, u32[]{:S(2)}, u32[]{:S(2)}) %collective-permute-start.46) | collective-permute-done | bytes 1048608 | tf_op jit(solution)/shard_map/ppermute | solution.py:34
  364.4 20.7 %collective-permute-done.45 = bf16[512,1024]{1,0:T(8,128)(2,1)S(1)} collective-permute-done((bf16[512,1024]{1,0:T(8,128)(2,1)}, bf16[512,1024]{1,0:T(8,128)(2,1)S(1)}, u32[]{:S(2)}, u32[]{:S(2)}) %collective-permute-start.45) | collective-permute-done | bytes 1048608 | tf_op jit(solution)/shard_map/ppermute | solution.py:34
  385.6 4.4 add_convert_fusion
  391.0 16.6 %attend_back.1 = bf16[1024,1792]{1,0:T(8,128)(2,1)} custom-call(s32[1]{0:T(128)} %bitcast.part, bf16[1024,768]{1,0:T(8,128)(2,1)} %get-tuple-element.52.qkv, bf16[1024,256]{1,0:T(8,128)(2,1)} %get-tuple-element.62.grad, f32[1024,128]{1,0:T(8,128)} %get-tuple-element.63.logsum, ...), custom_call_target="tpu_custom_call", output_to_operand_aliasing={{}: (6, {})} | custom-call | flops 5368709120 | bytes 6291456 | tf_op jit(solution)/shard_map/attend_back/pallas_call | solution.py:415
  407.6 4.9 fusion.97
  412.5 3.6 fusion.96
  416.2 3.7 fusion.95
  422.8 3.4 copy-done
  442.7 3.1 fusion.78
  449.3 4.8 collective-permute-start.55
  459.3 14.5 %collective-permute-done.56 = bf16[128,2048]{1,0:T(8,128)(2,1)S(1)} collective-permute-done((bf16[128,2048]{1,0:T(8,128)(2,1)S(1)}, bf16[128,2048]{1,0:T(8,128)(2,1)S(1)}, u32[]{:S(2)}, u32[]{:S(2)}) %collective-permute-start.56) | collective-permute-done | bytes 524320 | tf_op jit(solution)/shard_map/ppermute | solution.py:34
  475.7 43.1 %collective-permute-done.55 = bf16[128,2048]{1,0:T(8,128)(2,1)S(1)} collective-permute-done((bf16[128,2048]{1,0:T(8,128)(2,1)S(1)}, bf16[128,2048]{1,0:T(8,128)(2,1)S(1)}, u32[]{:S(2)}, u32[]{:S(2)}) %collective-permute-start.55) | collective-permute-done | bytes 524320 | tf_op jit(solution)/shard_map/ppermute | solution.py:34
  520.1 3.7 leave.1
  526.2 4.3 add_convert_fusion.1
  535.5 5.3 collective-permute-done.52
  540.8 4.5 collective-permute-done.51
  547.8 10.3 %widen.5 = f32[512,8192]{1,0:T(8,128)} custom-call(bf16[8,512,1024]{2,1,0:T(8,128)(2,1)} %bitcast.60), custom_call_target="tpu_custom_call" | custom-call | bytes 25165824 | tf_op jit(solution)/shard_map/widen/pallas_call | solution.py:496
  558.2 6.0 widen.6.refs_1_
  564.2 9.9 %all-gather.17.cloned.1.call-done = bf16[6144,512]{1,0:T(8,128)(2,1)} async-done(((bf16[768,512]{1,0:T(8,128)(2,1)}), bf16[6144,512]{1,0:T(8,128)(2,1)}) %all-gather.17.cloned.1.call-update) | async-done | bytes 6291472 | tf_op jit(solution)/shard_map/all_gather | solution.py:680
  574.1 15.7 %widen.7 = f32[8192,512]{1,0:T(8,128)} custom-call(bf16[8,768,512]{2,1,0:T(8,128)(2,1)} %bitcast.61, f32[8192,512]{1,0:T(8,128)} %widen.6.refs_1_), custom_call_target="tpu_custom_call", output_to_operand_aliasing={{}: (1, {})} | custom-call | bytes 18874368 | tf_op jit(solution)/shard_map/widen/pallas_call | solution.py:496
  589.9 16.5 %all-gather.15.cloned.1.call-done = bf16[2304,512]{1,0:T(8,128)(2,1)} async-done(((bf16[288,512]{1,0:T(8,128)(2,1)}), bf16[2304,512]{1,0:T(8,128)(2,1)}) %all-gather.15.cloned.1.call-update) | async-done | bytes 2359312 | tf_op jit(solution)/shard_map/all_gather | solution.py:680
  606.5 6.0 widen.9
  616.7 55.7 %all-gather.19.cloned.1.call-done = bf16[4096,768]{1,0:T(8,128)(2,1)} async-done(((bf16[512,768]{1,0:T(8,128)(2,1)}), bf16[4096,768]{1,0:T(8,128)(2,1)}) %all-gather.19.cloned.1.call-update) | async-done | bytes 6291472 | tf_op jit(solution)/shard_map/all_gather | solution.py:680
  672.4 15.6 %widen.8 = f32[512,6144]{1,0:T(8,128)} custom-call(bf16[8,512,768]{2,1,0:T(8,128)(2,1)} %bitcast.62), custom_call_target="tpu_custom_call" | custom-call | bytes 18874368 | tf_op jit(solution)/shard_map/widen/pallas_call | solution.py:496
  (286 shorter events, 157.3 us)
Async XLA Ops:
  7.2 382.8 %all-gather.11.cloned.1.call-start = ((), (), s32[]{:S(2)}) async-start(), calls=%async_computation | async-start | bytes 2359296 | tf_op jit(solution)/shard_map/all_gather | solution.py:680
  22.5 58.4 %collective-permute-start.6 = (bf16[512,1792]{1,0:T(8,128)(2,1)}, bf16[512,1792]{1,0:T(8,128)(2,1)}, u32[]{:S(2)}, u32[]{:S(2)}) collective-permute-start(bf16[512,1792]{1,0:T(8,128)(2,1)} %pick.2.refs_0_), channel_id=1, source_target_pairs={{0,8},{8,0},{16,24},{24,16},{1,9},{9,1},{17,25},{25,17},{2,10},{10... | collective-permute-start | bytes 5505032 | tf_op jit(solution)/shard_map/ppermute | solution.py:34
  22.6 58.3 %collective-permute-start.7 = (bf16[512,1792]{1,0:T(8,128)(2,1)}, bf16[512,1792]{1,0:T(8,128)(2,1)}, u32[]{:S(2)}, u32[]{:S(2)}) collective-permute-start(bf16[512,1792]{1,0:T(8,128)(2,1)} %pick.2.refs_0_), channel_id=1, source_target_pairs={{0,16},{8,24},{16,0},{24,8},{1,17},{9,25},{17,1},{25,9},{2,18},{10... | collective-permute-start | bytes 5505032 | tf_op jit(solution)/shard_map/ppermute | solution.py:34
  31.4 22.5 %collective-permute-start.2 = (bf16[128,2176]{1,0:T(8,128)(2,1)}, bf16[128,2176]{1,0:T(8,128)(2,1)S(1)}, u32[]{:S(2)}, u32[]{:S(2)}) collective-permute-start(bf16[128,2176]{1,0:T(8,128)(2,1)} %get-tuple-element.47), channel_id=1, source_target_pairs={{0,2},{1,3},{2,0},{3,1},{4,6},{5,7},{6,4},{7,5},{8,10},{9,11},{10,... | collective-permute-start | bytes 1671176 | tf_op jit(solution)/shard_map/ppermute | solution.py:34
  33.0 40.5 %collective-permute-start.3 = (bf16[128,2176]{1,0:T(8,128)(2,1)}, bf16[128,2176]{1,0:T(8,128)(2,1)S(1)}, u32[]{:S(2)}, u32[]{:S(2)}) collective-permute-start(bf16[128,2176]{1,0:T(8,128)(2,1)} %get-tuple-element.47), channel_id=1, source_target_pairs={{0,4},{1,5},{2,6},{3,7},{4,0},{5,1},{6,2},{7,3},{8,12},{9,13},{10,... | collective-permute-start | bytes 1671176 | tf_op jit(solution)/shard_map/ppermute | solution.py:34
  35.5 38.0 %collective-permute-start.4 = (bf16[128,2176]{1,0:T(8,128)(2,1)}, bf16[128,2176]{1,0:T(8,128)(2,1)S(1)}, u32[]{:S(2)}, u32[]{:S(2)}) collective-permute-start(bf16[128,2176]{1,0:T(8,128)(2,1)} %get-tuple-element.47), channel_id=1, source_target_pairs={{0,6},{1,7},{2,4},{3,5},{4,2},{5,3},{6,0},{7,1},{8,14},{9,15},{10,... | collective-permute-start | bytes 1671176 | tf_op jit(solution)/shard_map/ppermute | solution.py:34
  76.1 32.6 %collective-permute-start.5 = (bf16[512,2176]{1,0:T(8,128)(2,1)}, bf16[512,2176]{1,0:T(8,128)(2,1)}, u32[]{:S(2)}, u32[]{:S(2)}) collective-permute-start(bf16[512,2176]{1,0:T(8,128)(2,1)} %pad_maximum_fusion.1), channel_id=1, source_target_pairs={{0,1},{1,0},{2,3},{3,2},{4,5},{5,4},{6,7},{7,6},{8,9},{9,8},{10,11... | collective-permute-start | bytes 6684680 | tf_op jit(solution)/shard_map/ppermute | solution.py:34
  82.1 23.2 %collective-permute-start.8 = (bf16[256,1792]{1,0:T(8,128)(2,1)S(1)}, bf16[256,1792]{1,0:T(8,128)(2,1)S(1)}, u32[]{:S(2)}, u32[]{:S(2)}) collective-permute-start(bf16[256,1792]{1,0:T(8,128)(2,1)S(1)} %slice.215), channel_id=1, source_target_pairs={{0,16},{8,24},{16,0},{24,8},{1,17},{9,25},{17,1},{25,9},{2,18},{10... | collective-permute-start | bytes 2752520 | tf_op jit(solution)/shard_map/ppermute | solution.py:34
  84.1 23.2 %collective-permute-start.9 = (bf16[256,1792]{1,0:T(8,128)(2,1)S(1)}, bf16[256,1792]{1,0:T(8,128)(2,1)S(1)}, u32[]{:S(2)}, u32[]{:S(2)}) collective-permute-start(bf16[256,1792]{1,0:T(8,128)(2,1)S(1)} %slice.216), channel_id=1, source_target_pairs={{0,8},{8,0},{16,24},{24,16},{1,9},{9,1},{17,25},{25,17},{2,10},{10... | collective-permute-start | bytes 2752520 | tf_op jit(solution)/shard_map/ppermute | solution.py:34
  85.8 64.1 %collective-permute-start.18 = (bf16[1280,512]{1,0:T(8,128)(2,1)S(1)}, bf16[1280,512]{1,0:T(8,128)(2,1)}, u32[]{:S(2)}, u32[]{:S(2)}) collective-permute-start(bf16[1280,512]{1,0:T(8,128)(2,1)S(1)} %copy-done.12), channel_id=1, source_target_pairs={{0,8},{8,0},{16,24},{24,16},{1,9},{9,1},{17,25},{25,17},{2,10},{10... | collective-permute-start | bytes 3932168 | tf_op jit(solution)/shard_map/ppermute | solution.py:34
  86.4 66.2 %collective-permute-start.19 = (bf16[1280,512]{1,0:T(8,128)(2,1)S(1)}, bf16[1280,512]{1,0:T(8,128)(2,1)}, u32[]{:S(2)}, u32[]{:S(2)}) collective-permute-start(bf16[1280,512]{1,0:T(8,128)(2,1)S(1)} %copy-done.12), channel_id=1, source_target_pairs={{0,16},{8,24},{16,0},{24,8},{1,17},{9,25},{17,1},{25,9},{2,18},{10... | collective-permute-start | bytes 3932168 | tf_op jit(solution)/shard_map/ppermute | solution.py:34
  147.9 14.1 %collective-permute-start.10 = (bf16[512,512]{1,0:T(8,128)(2,1)S(1)}, bf16[512,512]{1,0:T(8,128)(2,1)S(1)}, u32[]{:S(2)}, u32[]{:S(2)}) collective-permute-start(bf16[512,512]{1,0:T(8,128)(2,1)S(1)} %slice.463), channel_id=1, source_target_pairs={{0,1},{1,0},{2,3},{3,2},{4,5},{5,4},{6,7},{7,6},{8,9},{9,8},{10,11... | collective-permute-start | bytes 1572872 | tf_op jit(solution)/shard_map/ppermute | solution.py:34
  151.0 17.2 %collective-permute-start.28 = (bf16[640,512]{1,0:T(8,128)(2,1)S(1)}, bf16[640,512]{1,0:T(8,128)(2,1)S(1)}, u32[]{:S(2)}, u32[]{:S(2)}) collective-permute-start(bf16[640,512]{1,0:T(8,128)(2,1)S(1)} %slice.292), channel_id=1, source_target_pairs={{0,16},{8,24},{16,0},{24,8},{1,17},{9,25},{17,1},{25,9},{2,18},{10... | collective-permute-start | bytes 1966088 | tf_op jit(solution)/shard_map/ppermute | solution.py:34
  153.7 16.9 %collective-permute-start.29 = (bf16[640,512]{1,0:T(8,128)(2,1)S(1)}, bf16[640,512]{1,0:T(8,128)(2,1)S(1)}, u32[]{:S(2)}, u32[]{:S(2)}) collective-permute-start(bf16[640,512]{1,0:T(8,128)(2,1)S(1)} %slice.293), channel_id=1, source_target_pairs={{0,8},{8,0},{16,24},{24,16},{1,9},{9,1},{17,25},{25,17},{2,10},{10... | collective-permute-start | bytes 1966088 | tf_op jit(solution)/shard_map/ppermute | solution.py:34
  161.9 21.1 %collective-permute-start.20 = (bf16[512,1024]{1,0:T(8,128)(2,1)S(1)}, bf16[512,1024]{1,0:T(8,128)(2,1)S(1)}, u32[]{:S(2)}, u32[]{:S(2)}) collective-permute-start(bf16[512,1024]{1,0:T(8,128)(2,1)S(1)} %fusion.2), channel_id=1, source_target_pairs={{0,1},{1,0},{2,3},{3,2},{4,5},{5,4},{6,7},{7,6},{8,9},{9,8},{10,11... | collective-permute-start | bytes 3145736 | tf_op jit(solution)/shard_map/ppermute | solution.py:34
  172.4 15.2 %collective-permute-start.13 = (bf16[128,512]{1,0:T(8,128)(2,1)S(1)}, bf16[128,512]{1,0:T(8,128)(2,1)S(1)}, u32[]{:S(2)}, u32[]{:S(2)}) collective-permute-start(bf16[128,512]{1,0:T(8,128)(2,1)S(1)} %get-tuple-element.116), channel_id=1, source_target_pairs={{0,6},{1,7},{2,4},{3,5},{4,2},{5,3},{6,0},{7,1},{8,14},{9,15},{10,... | collective-permute-start | bytes 393224 | tf_op jit(solution)/shard_map/ppermute | solution.py:34
  175.0 23.5 %collective-permute-start.12 = (bf16[128,512]{1,0:T(8,128)(2,1)S(1)}, bf16[128,512]{1,0:T(8,128)(2,1)S(1)}, u32[]{:S(2)}, u32[]{:S(2)}) collective-permute-start(bf16[128,512]{1,0:T(8,128)(2,1)S(1)} %get-tuple-element.117), channel_id=1, source_target_pairs={{0,4},{1,5},{2,6},{3,7},{4,0},{5,1},{6,2},{7,3},{8,12},{9,13},{10,... | collective-permute-start | bytes 393224 | tf_op jit(solution)/shard_map/ppermute | solution.py:34
  182.9 18.0 %collective-permute-start.11 = (bf16[128,512]{1,0:T(8,128)(2,1)S(1)}, bf16[128,512]{1,0:T(8,128)(2,1)S(1)}, u32[]{:S(2)}, u32[]{:S(2)}) collective-permute-start(bf16[128,512]{1,0:T(8,128)(2,1)S(1)} %get-tuple-element.115), channel_id=1, source_target_pairs={{0,2},{1,3},{2,0},{3,1},{4,6},{5,7},{6,4},{7,5},{8,10},{9,11},{10,... | collective-permute-start | bytes 393224 | tf_op jit(solution)/shard_map/ppermute | solution.py:34
  183.7 17.2 %collective-permute-start.33 = (bf16[128,512]{1,0:T(8,128)(2,1)S(1)}, bf16[128,512]{1,0:T(8,128)(2,1)S(1)}, u32[]{:S(2)}, u32[]{:S(2)}) collective-permute-start(bf16[128,512]{1,0:T(8,128)(2,1)S(1)} %get-tuple-element.119), channel_id=1, source_target_pairs={{0,6},{1,7},{2,4},{3,5},{4,2},{5,3},{6,0},{7,1},{8,14},{9,15},{10,... | collective-permute-start | bytes 393224 | tf_op jit(solution)/shard_map/ppermute | solution.py:34
  186.5 28.8 %collective-permute-start.32 = (bf16[128,512]{1,0:T(8,128)(2,1)S(1)}, bf16[128,512]{1,0:T(8,128)(2,1)S(1)}, u32[]{:S(2)}, u32[]{:S(2)}) collective-permute-start(bf16[128,512]{1,0:T(8,128)(2,1)S(1)} %get-tuple-element.120), channel_id=1, source_target_pairs={{0,4},{1,5},{2,6},{3,7},{4,0},{5,1},{6,2},{7,3},{8,12},{9,13},{10,... | collective-permute-start | bytes 393224 | tf_op jit(solution)/shard_map/ppermute | solution.py:34
  187.6 27.7 %collective-permute-start.31 = (bf16[128,512]{1,0:T(8,128)(2,1)S(1)}, bf16[128,512]{1,0:T(8,128)(2,1)S(1)}, u32[]{:S(2)}, u32[]{:S(2)}) collective-permute-start(bf16[128,512]{1,0:T(8,128)(2,1)S(1)} %get-tuple-element.118), channel_id=1, source_target_pairs={{0,2},{1,3},{2,0},{3,1},{4,6},{5,7},{6,4},{7,5},{8,10},{9,11},{10,... | collective-permute-start | bytes 393224 | tf_op jit(solution)/shard_map/ppermute | solution.py:34
  198.4 20.9 %collective-permute-start.23 = (bf16[128,1024]{1,0:T(8,128)(2,1)S(1)}, bf16[128,1024]{1,0:T(8,128)(2,1)S(1)}, u32[]{:S(2)}, u32[]{:S(2)}) collective-permute-start(bf16[128,1024]{1,0:T(8,128)(2,1)S(1)} %get-tuple-element.113), channel_id=1, source_target_pairs={{0,6},{1,7},{2,4},{3,5},{4,2},{5,3},{6,0},{7,1},{8,14},{9,15},{10,... | collective-permute-start | bytes 786440 | tf_op jit(solution)/shard_map/ppermute | solution.py:34
  200.9 31.3 %collective-permute-start.22 = (bf16[128,1024]{1,0:T(8,128)(2,1)S(1)}, bf16[128,1024]{1,0:T(8,128)(2,1)S(1)}, u32[]{:S(2)}, u32[]{:S(2)}) collective-permute-start(bf16[128,1024]{1,0:T(8,128)(2,1)S(1)} %get-tuple-element.114), channel_id=1, source_target_pairs={{0,4},{1,5},{2,6},{3,7},{4,0},{5,1},{6,2},{7,3},{8,12},{9,13},{10,... | collective-permute-start | bytes 786440 | tf_op jit(solution)/shard_map/ppermute | solution.py:34
  200.9 31.3 %collective-permute-start.21 = (bf16[128,1024]{1,0:T(8,128)(2,1)S(1)}, bf16[128,1024]{1,0:T(8,128)(2,1)S(1)}, u32[]{:S(2)}, u32[]{:S(2)}) collective-permute-start(bf16[128,1024]{1,0:T(8,128)(2,1)S(1)} %get-tuple-element.112), channel_id=1, source_target_pairs={{0,2},{1,3},{2,0},{3,1},{4,6},{5,7},{6,4},{7,5},{8,10},{9,11},{10,... | collective-permute-start | bytes 786440 | tf_op jit(solution)/shard_map/ppermute | solution.py:34
  216.3 19.8 %collective-permute-start.14 = (bf16[128,512]{1,0:T(8,128)(2,1)S(1)}, bf16[128,512]{1,0:T(8,128)(2,1)S(1)}, u32[]{:S(2)}, u32[]{:S(2)}) collective-permute-start(bf16[128,512]{1,0:T(8,128)(2,1)S(1)} %get-tuple-element.131), channel_id=1, source_target_pairs={{0,2},{1,3},{2,0},{3,1},{4,6},{5,7},{6,4},{7,5},{8,10},{9,11},{10,... | collective-permute-start | bytes 393224 | tf_op jit(solution)/shard_map/ppermute | solution.py:34
  216.4 21.2 %collective-permute-start.15 = (bf16[128,512]{1,0:T(8,128)(2,1)S(1)}, bf16[128,512]{1,0:T(8,128)(2,1)S(1)}, u32[]{:S(2)}, u32[]{:S(2)}) collective-permute-start(bf16[128,512]{1,0:T(8,128)(2,1)S(1)} %get-tuple-element.131), channel_id=1, source_target_pairs={{0,4},{1,5},{2,6},{3,7},{4,0},{5,1},{6,2},{7,3},{8,12},{9,13},{10,... | collective-permute-start | bytes 393224 | tf_op jit(solution)/shard_map/ppermute | solution.py:34
  219.4 18.3 %collective-permute-start.16 = (bf16[128,512]{1,0:T(8,128)(2,1)S(1)}, bf16[128,512]{1,0:T(8,128)(2,1)S(1)}, u32[]{:S(2)}, u32[]{:S(2)}) collective-permute-start(bf16[128,512]{1,0:T(8,128)(2,1)S(1)} %get-tuple-element.131), channel_id=1, source_target_pairs={{0,6},{1,7},{2,4},{3,5},{4,2},{5,3},{6,0},{7,1},{8,14},{9,15},{10,... | collective-permute-start | bytes 393224 | tf_op jit(solution)/shard_map/ppermute | solution.py:34
  237.7 28.2 %collective-permute-start.25 = (bf16[128,1024]{1,0:T(8,128)(2,1)S(1)}, bf16[128,1024]{1,0:T(8,128)(2,1)S(1)}, u32[]{:S(2)}, u32[]{:S(2)}) collective-permute-start(bf16[128,1024]{1,0:T(8,128)(2,1)S(1)} %get-tuple-element.98), channel_id=1, source_target_pairs={{0,4},{1,5},{2,6},{3,7},{4,0},{5,1},{6,2},{7,3},{8,12},{9,13},{10,... | collective-permute-start | bytes 786440 | tf_op jit(solution)/shard_map/ppermute | solution.py:34
  244.8 21.1 %collective-permute-start.26 = (bf16[128,1024]{1,0:T(8,128)(2,1)S(1)}, bf16[128,1024]{1,0:T(8,128)(2,1)S(1)}, u32[]{:S(2)}, u32[]{:S(2)}) collective-permute-start(bf16[128,1024]{1,0:T(8,128)(2,1)S(1)} %get-tuple-element.98), channel_id=1, source_target_pairs={{0,6},{1,7},{2,4},{3,5},{4,2},{5,3},{6,0},{7,1},{8,14},{9,15},{10,... | collective-permute-start | bytes 786440 | tf_op jit(solution)/shard_map/ppermute | solution.py:34
  246.2 21.9 %collective-permute-start.17 = (bf16[512,512]{1,0:T(8,128)(2,1)S(1)}, bf16[512,512]{1,0:T(8,128)(2,1)S(1)}, u32[]{:S(2)}, u32[]{:S(2)}) collective-permute-start(bf16[512,512]{1,0:T(8,128)(2,1)S(1)} %pad_maximum_fusion.5), channel_id=1, source_target_pairs={{0,1},{1,0},{2,3},{3,2},{4,5},{5,4},{6,7},{7,6},{8,9},{9,8},{10,11... | collective-permute-start | bytes 1572872 | tf_op jit(solution)/shard_map/ppermute | solution.py:34
  246.3 19.9 %collective-permute-start.37 = (bf16[512,512]{1,0:T(8,128)(2,1)S(1)}, bf16[512,512]{1,0:T(8,128)(2,1)S(1)}, u32[]{:S(2)}, u32[]{:S(2)}) collective-permute-start(bf16[512,512]{1,0:T(8,128)(2,1)S(1)} %pad_maximum_fusion.6), channel_id=1, source_target_pairs={{0,1},{1,0},{2,3},{3,2},{4,5},{5,4},{6,7},{7,6},{8,9},{9,8},{10,11... | collective-permute-start | bytes 1572872 | tf_op jit(solution)/shard_map/ppermute | solution.py:34
  285.9 261.9 %all-gather.13.cloned.1.call-start = ((), (), s32[]{:S(2)}) async-start(), calls=%async_computation.1 | async-start | bytes 9437184 | tf_op jit(solution)/shard_map/all_gather | solution.py:680
  299.2 21.6 %collective-permute-start.43 = (bf16[768,512]{1,0:T(8,128)(2,1)}, bf16[768,512]{1,0:T(8,128)(2,1)S(1)}, u32[]{:S(2)}, u32[]{:S(2)}) collective-permute-start(bf16[768,512]{1,0:T(8,128)(2,1)} %convolution_convert_fusion.6), channel_id=1, source_target_pairs={{0,24},{8,16},{16,8},{24,0},{1,25},{9,17},{17,9},{25,1},{2,26},{10... | collective-permute-start | bytes 2359304 | tf_op jit(solution)/shard_map/ppermute | solution.py:34
  299.7 35.4 %collective-permute-start.42 = (bf16[768,512]{1,0:T(8,128)(2,1)}, bf16[768,512]{1,0:T(8,128)(2,1)S(1)}, u32[]{:S(2)}, u32[]{:S(2)}) collective-permute-start(bf16[768,512]{1,0:T(8,128)(2,1)} %convolution_convert_fusion.7), channel_id=1, source_target_pairs={{0,16},{8,24},{16,0},{24,8},{1,17},{9,25},{17,1},{25,9},{2,18},{10... | collective-permute-start | bytes 2359304 | tf_op jit(solution)/shard_map/ppermute | solution.py:34
  301.2 33.9 %collective-permute-start.41 = (bf16[768,512]{1,0:T(8,128)(2,1)}, bf16[768,512]{1,0:T(8,128)(2,1)S(1)}, u32[]{:S(2)}, u32[]{:S(2)}) collective-permute-start(bf16[768,512]{1,0:T(8,128)(2,1)} %convolution_convert_fusion.8), channel_id=1, source_target_pairs={{0,8},{8,0},{16,24},{24,16},{1,9},{9,1},{17,25},{25,17},{2,10},{10... | collective-permute-start | bytes 2359304 | tf_op jit(solution)/shard_map/ppermute | solution.py:34
  337.1 27.2 %collective-permute-start.46 = (bf16[512,1024]{1,0:T(8,128)(2,1)}, bf16[512,1024]{1,0:T(8,128)(2,1)S(1)}, u32[]{:S(2)}, u32[]{:S(2)}) collective-permute-start(bf16[512,1024]{1,0:T(8,128)(2,1)} %convolution_convert_fusion), channel_id=1, source_target_pairs={{0,24},{8,16},{16,8},{24,0},{1,25},{9,17},{17,9},{25,1},{2,26},{10... | collective-permute-start | bytes 3145736 | tf_op jit(solution)/shard_map/ppermute | solution.py:34
  338.3 46.8 %collective-permute-start.45 = (bf16[512,1024]{1,0:T(8,128)(2,1)}, bf16[512,1024]{1,0:T(8,128)(2,1)S(1)}, u32[]{:S(2)}, u32[]{:S(2)}) collective-permute-start(bf16[512,1024]{1,0:T(8,128)(2,1)} %convolution_convert_fusion.1), channel_id=1, source_target_pairs={{0,16},{8,24},{16,0},{24,8},{1,17},{9,25},{17,1},{25,9},{2,18},{10... | collective-permute-start | bytes 3145736 | tf_op jit(solution)/shard_map/ppermute | solution.py:34
  339.7 45.8 %collective-permute-start.44 = (bf16[512,1024]{1,0:T(8,128)(2,1)}, bf16[512,1024]{1,0:T(8,128)(2,1)S(1)}, u32[]{:S(2)}, u32[]{:S(2)}) collective-permute-start(bf16[512,1024]{1,0:T(8,128)(2,1)} %convolution_convert_fusion.2), channel_id=1, source_target_pairs={{0,8},{8,0},{16,24},{24,16},{1,9},{9,1},{17,25},{25,17},{2,10},{10... | collective-permute-start | bytes 3145736 | tf_op jit(solution)/shard_map/ppermute | solution.py:34
  390.0 184.1 %all-gather.17.cloned.1.call-start = ((), (), s32[]{:S(2)}) async-start(), calls=%async_computation.3 | async-start | bytes 7077888 | tf_op jit(solution)/shard_map/all_gather | solution.py:680
  390.7 215.7 %all-gather.15.cloned.1.call-start = ((), (), s32[]{:S(2)}) async-start(), calls=%async_computation.2 | async-start | bytes 2654208 | tf_op jit(solution)/shard_map/all_gather | solution.py:680
  427.9 14.7 %collective-permute-start.53 = (bf16[512,2048]{1,0:T(8,128)(2,1)}, bf16[512,2048]{1,0:T(8,128)(2,1)}, u32[]{:S(2)}, u32[]{:S(2)}) collective-permute-start(bf16[512,2048]{1,0:T(8,128)(2,1)} %slice.461), channel_id=1, source_target_pairs={{0,1},{1,0},{2,3},{3,2},{4,5},{5,4},{6,7},{7,6},{8,9},{9,8},{10,11... | collective-permute-start | bytes 6291464 | tf_op jit(solution)/shard_map/ppermute | solution.py:34
  445.9 27.9 %collective-permute-start.56 = (bf16[128,2048]{1,0:T(8,128)(2,1)S(1)}, bf16[128,2048]{1,0:T(8,128)(2,1)S(1)}, u32[]{:S(2)}, u32[]{:S(2)}) collective-permute-start(bf16[128,2048]{1,0:T(8,128)(2,1)S(1)} %get-tuple-element.108), channel_id=1, source_target_pairs={{0,6},{1,7},{2,4},{3,5},{4,2},{5,3},{6,0},{7,1},{8,14},{9,15},{10,... | collective-permute-start | bytes 1572872 | tf_op jit(solution)/shard_map/ppermute | solution.py:34
  449.3 69.5 %collective-permute-start.55 = (bf16[128,2048]{1,0:T(8,128)(2,1)S(1)}, bf16[128,2048]{1,0:T(8,128)(2,1)S(1)}, u32[]{:S(2)}, u32[]{:S(2)}) collective-permute-start(bf16[128,2048]{1,0:T(8,128)(2,1)S(1)} %get-tuple-element.109), channel_id=1, source_target_pairs={{0,4},{1,5},{2,6},{3,7},{4,0},{5,1},{6,2},{7,3},{8,12},{9,13},{10,... | collective-permute-start | bytes 1572872 | tf_op jit(solution)/shard_map/ppermute | solution.py:34
  454.1 64.8 %collective-permute-start.54 = (bf16[128,2048]{1,0:T(8,128)(2,1)S(1)}, bf16[128,2048]{1,0:T(8,128)(2,1)S(1)}, u32[]{:S(2)}, u32[]{:S(2)}) collective-permute-start(bf16[128,2048]{1,0:T(8,128)(2,1)S(1)} %get-tuple-element.107), channel_id=1, source_target_pairs={{0,2},{1,3},{2,0},{3,1},{4,6},{5,7},{6,4},{7,5},{8,10},{9,11},{10,... | collective-permute-start | bytes 1572872 | tf_op jit(solution)/shard_map/ppermute | solution.py:34
  456.5 69.7 %collective-permute-start.49 = (bf16[512,768]{1,0:T(8,128)(2,1)}, bf16[512,768]{1,0:T(8,128)(2,1)S(1)}, u32[]{:S(2)}, u32[]{:S(2)}) collective-permute-start(bf16[512,768]{1,0:T(8,128)(2,1)} %convolution_convert_fusion.3), channel_id=1, source_target_pairs={{0,24},{8,16},{16,8},{24,0},{1,25},{9,17},{17,9},{25,1},{2,26},{10... | collective-permute-start | bytes 2359304 | tf_op jit(solution)/shard_map/ppermute | solution.py:34
  457.8 68.4 %collective-permute-start.48 = (bf16[512,768]{1,0:T(8,128)(2,1)S(1)}, bf16[512,768]{1,0:T(8,128)(2,1)}, u32[]{:S(2)}, u32[]{:S(2)}) collective-permute-start(bf16[512,768]{1,0:T(8,128)(2,1)S(1)} %convolution_convert_fusion.4), channel_id=1, source_target_pairs={{0,16},{8,24},{16,0},{24,8},{1,17},{9,25},{17,1},{25,9},{2,18},{10... | collective-permute-start | bytes 2359304 | tf_op jit(solution)/shard_map/ppermute | solution.py:34
  473.8 52.4 %collective-permute-start.47 = (bf16[512,768]{1,0:T(8,128)(2,1)S(1)}, bf16[512,768]{1,0:T(8,128)(2,1)}, u32[]{:S(2)}, u32[]{:S(2)}) collective-permute-start(bf16[512,768]{1,0:T(8,128)(2,1)S(1)} %convolution_convert_fusion.5), channel_id=1, source_target_pairs={{0,8},{8,0},{16,24},{24,16},{1,9},{9,1},{17,25},{25,17},{2,10},{10... | collective-permute-start | bytes 2359304 | tf_op jit(solution)/shard_map/ppermute | solution.py:34
  558.2 114.3 %all-gather.19.cloned.1.call-start = ((), (), s32[]{:S(2)}) async-start(), calls=%async_computation.4 | async-start | bytes 7077888 | tf_op jit(solution)/shard_map/all_gather | solution.py:680
  (47 other events, 528.7 us)
Sparse Core Ops, SparseCore 0:
  286.1 31.6 all-gather.10
  390.1 118.9 all-gather.12
  510.8 63.2 all-gather.16
  576.2 30.2 all-gather.14
  608.5 63.8 all-gather.18

commit v3 on v2

v3 whole, which is shorter than its diff:
```python
import functools

import jax
import jax.numpy as jnp
from jax import lax
from jax.experimental import pallas as pl
from jax.experimental.pallas import tpu as pltpu
from jax.sharding import PartitionSpec as P

HEADS = 32
HEAD_DIM = 64
ROTARY = 32


norm_eps = 1e-05
rope_base = 10000.0
masked_fill = -1e30
LANES = 128
RADIX = 64
DIGIT = 16
SPARE = 16
ROWS = 64

low = jnp.bfloat16
wide = jnp.float32


def dot(a, b, dims):
    return lax.dot_general(a, b, (dims, ((), ())), preferred_element_type=wide)


def after(array, *earlier):
    return lax.optimization_barrier((array, *earlier))[0]


def swap(array, axis, bit):
    return lax.ppermute(array, axis, [(s, s ^ bit) for s in range(lax.axis_size(axis))])


def gather_seq(rows):
    return lax.all_gather(rows, "seq", axis=0, tiled=True)


def between(array, pairs):
    return lax.ppermute(
        array, "seq", [(2 * a + core, 2 * b + core) for a, b in pairs for core in range(2)]
    )


def scatter_chips(blocks):
    chips = len(blocks)
    if chips != 4:
        total = blocks[0]
        for k in range(1, chips):
            total = total + swap(blocks[k].astype(low), "seq", 2 * k).astype(wide)
        return total
    chip = lax.axis_index("seq") // 2
    far = between(blocks[3].astype(low), [(0, 1), (3, 2)])
    passed = (blocks[2] + far.astype(wide)).astype(low)
    upward = between(passed, [(0, 1), (1, 2)])
    downward = between(passed, [(3, 2), (2, 1)])
    upward = jnp.where(chip == 1, blocks[3], blocks[1]) + upward.astype(wide)
    downward = jnp.where(chip == 2, blocks[3], blocks[1]) + downward.astype(wide)
    upward = between(upward.astype(low), [(0, 1), (1, 2), (2, 3)])
    downward = between(downward.astype(low), [(3, 2), (2, 1), (1, 0)])
    return blocks[0] + upward.astype(wide) + downward.astype(wide)


def scatter_blocks(kept, sent):
    chips = lax.axis_size("seq") // 2
    rows = kept.shape[0] // chips
    chip = kept + swap(sent, "seq", 1).astype(wide)
    return scatter_chips([chip[k * rows : (k + 1) * rows] for k in range(chips)])


def scatter_seq(partial):
    return lax.psum_scatter(partial, "seq", scatter_dimension=0, tiled=True).astype(wide)


def total_dp(array):
    bit = 1
    while bit < lax.axis_size("dp"):
        array = array + swap(array, "dp", bit)
        bit *= 2
    return array


def normalise(values):
    centre = values - jnp.mean(values, axis=-1, keepdims=True)
    spread = jnp.mean(centre * centre, axis=-1, keepdims=True)
    rstd = lax.rsqrt(spread + norm_eps)
    return centre * rstd, rstd


def enter_kernel(
    owners, owner, tokens, teacher, gain, shift, bias_a, bias_b, place, normed, base, held, kept
):
    inputs = tokens[...].astype(wide)
    xhat, _ = normalise(inputs)
    held[...] = xhat * gain[...].astype(wide)[None] + shift[...].astype(wide)[None]
    biases = (bias_a[...].astype(wide) + bias_b[...].astype(wide))[None]
    kept[...] = inputs + biases - teacher[...].astype(wide)
    width = inputs.shape[1]
    depth = width // owners
    for k in range(owners):
        theirs = pl.ds(pl.multiple_of((owner[0] ^ k) * depth, LANES), depth)
        normed[:, k * depth : (k + 1) * depth] = held[:, theirs].astype(low)
        base[:, k * depth : (k + 1) * depth] = kept[:, theirs]
    lane = lax.broadcasted_iota(jnp.int32, (inputs.shape[0], LANES), 1)
    row = lax.broadcasted_iota(jnp.int32, (inputs.shape[0], inputs.shape[0]), 0)
    column = lax.broadcasted_iota(jnp.int32, row.shape, 1)
    ids = jnp.sum(
        jnp.where(row == column, place[...].astype(wide), 0.0), axis=1, keepdims=True
    ).astype(jnp.int32)
    facts = jnp.where(lane == 0, ids // RADIX, ids % RADIX)
    normed[:, width:] = facts.astype(wide).astype(low)


def enter(tokens, teacher, gain, shift, bias_a, bias_b, place, owner, owners):
    rows, width = tokens.shape
    whole = pl.BlockSpec(memory_space=pltpu.VMEM)
    return pl.pallas_call(
        functools.partial(enter_kernel, owners),
        in_specs=[pl.BlockSpec(memory_space=pltpu.SMEM)] + [whole] * 7,
        out_specs=[whole] * 2,
        out_shape=[
            jax.ShapeDtypeStruct((rows, width + LANES), low),
            jax.ShapeDtypeStruct((rows, width), wide),
        ],
        scratch_shapes=[pltpu.VMEM((rows, width), wide)] * 2,
        name="enter",
    )(
        owner[None],
        tokens,
        teacher,
        gain,
        shift,
        bias_a,
        bias_b,
        place,
    )


def leave_kernel(
    owners, owner, tokens, gain, summed, grad, bias, token_grad, gain_grad, shift_grad, bias_grad
):
    inputs = tokens[...].astype(wide)
    xhat, rstd = normalise(inputs)
    depth = inputs.shape[1] // owners
    for k in range(owners):
        theirs = pl.ds(pl.multiple_of((owner[0] ^ k) * depth, LANES), depth)
        token_grad[:, theirs] = summed[:, k * depth : (k + 1) * depth]
        bias_grad[:, theirs] = bias[:, k * depth : (k + 1) * depth]
    normed_grad = token_grad[...]
    gain_grad[...] = jnp.sum(normed_grad * xhat, axis=0, keepdims=True)
    shift_grad[...] = jnp.sum(normed_grad, axis=0, keepdims=True)
    scaled = normed_grad * gain[...].astype(wide)[None]
    token_grad[...] = rstd * (
        scaled
        - jnp.mean(scaled, axis=-1, keepdims=True)
        - xhat * jnp.mean(scaled * xhat, axis=-1, keepdims=True)
    )
    for k in range(owners):
        theirs = pl.ds(pl.multiple_of((owner[0] ^ k) * depth, LANES), depth)
        token_grad[:, theirs] += grad[:, k * depth : (k + 1) * depth]


def leave(tokens, gain, summed, grad, bias, owner, owners):
    rows, width = tokens.shape
    whole = pl.BlockSpec(memory_space=pltpu.VMEM)
    line = jax.ShapeDtypeStruct((1, width), wide)
    return pl.pallas_call(
        functools.partial(leave_kernel, owners),
        in_specs=[pl.BlockSpec(memory_space=pltpu.SMEM)] + [whole] * 5,
        out_specs=[whole] * 4,
        out_shape=[jax.ShapeDtypeStruct((rows, width), wide), line, line, line],
        name="leave",
    )(owner[None], tokens, gain, summed, grad, bias[None])


def pick_kernel(moves, part, counted, a, b, *refs):
    outs, arrived = refs[:2], refs[2]
    copies = []
    for which, source, half, target in moves:
        copies.append(
            pltpu.make_async_copy(
                (a, b)[which].at[source(part[0])],
                outs[half].at[target],
                arrived.at[len(copies)],
            )
        )
    for copy in copies:
        copy.start()
    tall = outs[0].shape[0]
    more = outs[1].shape[0] - tall
    if more:
        count = jnp.sum(counted[...].astype(wide), axis=1, keepdims=True)
        outs[1][tall:, :] = jnp.broadcast_to(count, (more, outs[1].shape[1])).astype(low)
    for copy in copies:
        copy.wait()


def pick(arrays, part, counted, moves, shapes):
    moved = 4 * sum(shape[0] * shape[1] for shape in shapes)
    return pl.pallas_call(
        functools.partial(pick_kernel, moves),
        in_specs=[
            pl.BlockSpec(memory_space=pltpu.SMEM),
            pl.BlockSpec(memory_space=pltpu.VMEM),
        ]
        + [pl.BlockSpec(memory_space=pl.ANY)] * 2,
        out_specs=[pl.BlockSpec(memory_space=pltpu.VMEM)] * 2,
        out_shape=[jax.ShapeDtypeStruct(shape, low) for shape in shapes],
        scratch_shapes=[pltpu.SemaphoreType.DMA((len(moves),))],
        cost_estimate=pl.CostEstimate(flops=0, bytes_accessed=moved, transcendentals=0),
        name="pick",
    )(part, counted, *arrays)


def gelu_parts(values):
    root = (2.0 / jnp.pi) ** 0.5
    square = values * values
    bent = jnp.tanh(root * (values + 0.044715 * (values * square)))
    factor = 0.5 * (1.0 + bent)
    slope = 0.5 * values * (1.0 - bent * bent) * (root * (1.0 + 3.0 * 0.044715 * square))
    return factor, factor + slope


def turn(values, cosine, sine):
    lane = lax.broadcasted_iota(jnp.int32, values.shape, 1) % HEAD_DIM
    half, width = ROTARY // 2, values.shape[1]
    partner = jnp.where(
        lane < half, pltpu.roll(values, width - half, 1), pltpu.roll(values, half, 1)
    )
    return values * cosine + partner * sine


def begin_kernel(count, normed, bias, *refs):
    weights, out = refs[:count], refs[count]
    tall = normed.shape[1] // count
    total = bias[...] + jnp.dot(normed[:, :tall], weights[0][...], preferred_element_type=wide)
    for k in range(1, count):
        block = normed[:, k * tall : (k + 1) * tall]
        total = total + jnp.dot(block, weights[k][...], preferred_element_type=wide)
    out[...] = total


def begin(normed, bias, weights, tall, head_width):
    count = len(weights)
    length = normed.shape[0]
    inside = weights[0].shape[1]
    return pl.pallas_call(
        functools.partial(begin_kernel, count),
        grid=(inside // head_width,),
        in_specs=[
            pl.BlockSpec((length, count * tall), lambda t: (0, 0)),
            pl.BlockSpec((1, head_width), lambda t: (0, t)),
        ]
        + [pl.BlockSpec((tall, head_width), lambda t: (0, t))] * count,
        out_specs=pl.BlockSpec((length, head_width), lambda t: (0, t)),
        out_shape=jax.ShapeDtypeStruct((length, inside), wide),
        cost_estimate=pl.CostEstimate(
            flops=2 * length * count * tall * inside,
            bytes_accessed=2 * (count * tall * inside + normed.size) + 4 * length * inside,
            transcendentals=0,
        ),
        name="begin",
    )(normed, bias, *weights)


def project_kernel(normed, other, cosine, sine, begun, weights, others, qkv, hidden, stacked):
    tile = pl.program_id(0)
    total = begun[...] + jnp.dot(normed[...], weights[...], preferred_element_type=wide)
    total = total + jnp.dot(other[...], others[...], preferred_element_type=wide)
    repeats = total.shape[1] // LANES

    @pl.when(tile < 2)
    def _():
        turned = turn(
            total,
            jnp.concatenate([cosine[...]] * repeats, axis=1),
            jnp.concatenate([sine[...]] * repeats, axis=1),
        )
        qkv[...] = turned.astype(low)

    @pl.when(tile == 2)
    def _():
        qkv[...] = total.astype(low)

    @pl.when(tile > 2)
    def _():
        hidden[...] = total
        stacked[...] = (total * gelu_parts(total)[0]).astype(low)


def project(normed, cosine, sine, begun, halves, tall, head_width):
    length = normed.shape[0]
    inside = begun.shape[1]
    units = inside - 3 * head_width
    first = 2 * (normed.shape[1] // (2 * tall)) - 2
    table = pl.BlockSpec((length, LANES), lambda t: (0, 0))
    weights, others = halves
    return pl.pallas_call(
        project_kernel,
        grid=(inside // head_width,),
        in_specs=[
            pl.BlockSpec((length, tall), lambda t: (0, first)),
            pl.BlockSpec((length, tall), lambda t: (0, first + 1)),
            table,
            table,
            pl.BlockSpec((length, head_width), lambda t: (0, t)),
            pl.BlockSpec((tall, head_width), lambda t: (0, t)),
            pl.BlockSpec((tall, head_width), lambda t: (0, t)),
        ],
        out_specs=[
            pl.BlockSpec((length, head_width), lambda t: (0, jnp.minimum(t, 2))),
            pl.BlockSpec((length, head_width), lambda t: (0, jnp.maximum(t - 3, 0))),
            pl.BlockSpec((length, head_width), lambda t: (0, jnp.maximum(t - 2, 1))),
        ],
        out_shape=[
            jax.ShapeDtypeStruct((length, 3 * head_width), low),
            jax.ShapeDtypeStruct((length, units), wide),
            jax.ShapeDtypeStruct((length, head_width + units), low),
        ],
        cost_estimate=pl.CostEstimate(
            flops=4 * length * tall * inside,
            bytes_accessed=4 * tall * (inside + length) + 12 * length * inside,
            transcendentals=length * units,
        ),
        name="project",
    )(normed, normed, cosine, sine, begun, weights, others)


def emit_kernel(owners, counts, stacked, *refs):
    counted, refs = refs[:counts], refs[counts:]
    weights, out = refs[: 2 * owners], refs[-1]
    middle = weights[0].shape[0]
    for k in range(owners):

        @pl.when(pl.program_id(0) // 2 == k)
        def _(k=k):
            total = jnp.dot(
                stacked[:, :middle], weights[2 * k][...], preferred_element_type=wide
            ) + jnp.dot(stacked[:, middle:], weights[2 * k + 1][...], preferred_element_type=wide)
            out[...] = total.astype(low)

    if not counted:
        return

    @pl.when(pl.program_id(0) == 2 * owners)
    def _():
        count = counted[0][...].astype(wide)
        for ref in counted[1:]:
            count = count + ref[...].astype(wide)
        count = count[:1].astype(jnp.int32)
        lane = lax.broadcasted_iota(jnp.int32, count.shape, 1)
        digits = jnp.where(lane == 0, count, count // DIGIT)
        digits = jnp.where(lane == 2, count // (DIGIT * DIGIT), digits) % DIGIT
        out[:, :LANES] = jnp.broadcast_to(digits.astype(wide), (out.shape[0], LANES)).astype(low)


def emit(stacked, weights, counted, first, all_owners, into=None):
    owners = len(weights)
    length, behind = stacked.shape
    middle, depth = weights[0][0].shape
    size = depth // 2
    steps = 2 * owners + (first + owners == all_owners)

    def at(k):
        return pl.BlockSpec((middle, size), lambda t: (0, jnp.clip(t - 2 * k, 0, 1)))

    row = size // SPARE
    operands = [stacked, *counted, *[item for pair in weights for item in pair]]
    in_specs = [pl.BlockSpec((length, behind), lambda t: (0, 0))]
    in_specs += [pl.BlockSpec((SPARE, LANES), lambda t: (row, 0))] * len(counted)
    in_specs += [at(k) for k in range(owners) for _ in range(2)]
    aliases = {}
    if into is not None:
        aliases = {len(operands): 0}
        operands.append(into)
        in_specs.append(pl.BlockSpec(memory_space=pl.ANY))
    return pl.pallas_call(
        functools.partial(emit_kernel, owners, len(counted)),
        grid=(steps,),
        in_specs=in_specs,
        out_specs=pl.BlockSpec((length, size), lambda t: (0, 2 * first + t)),
        out_shape=jax.ShapeDtypeStruct((length, all_owners * depth + LANES), low),
        input_output_aliases=aliases,
        cost_estimate=pl.CostEstimate(
            flops=2 * length * behind * owners * depth,
            bytes_accessed=2 * behind * (length + owners * depth) + 2 * length * steps * size,
            transcendentals=0,
        ),
        name="emit",
    )(*operands)


def scores_of(rows, keys, start):
    raw = lax.dot_general(rows, keys, (((1,), (1,)), ((), ())), preferred_element_type=wide)
    place = start + lax.broadcasted_iota(jnp.int32, raw.shape, 0)
    kept = lax.broadcasted_iota(jnp.int32, raw.shape, 1) <= place
    return jnp.where(kept, raw * HEAD_DIM ** (-0.5), masked_fill)


def attend_kernel(step, qkv, stacked, out, logsum):
    del stacked
    length, head_width = out.shape
    lane = lax.broadcasted_iota(jnp.int32, (step, LANES), 1)
    for first in range(0, length, step):
        last = first + step
        sums = jnp.zeros((step, LANES), wide)
        outs = []
        for h in range(head_width // HEAD_DIM):
            a, b = h * HEAD_DIM, (h + 1) * HEAD_DIM
            keys = qkv[:last, head_width + a : head_width + b]
            values = qkv[:last, 2 * head_width + a : 2 * head_width + b]
            scores = scores_of(qkv[first:last, a:b], keys, first)
            top = jnp.max(scores, axis=-1, keepdims=True)
            expd = jnp.exp(scores - top)
            total = jnp.sum(expd, axis=-1, keepdims=True)
            probs = (expd * (1.0 / total)).astype(low)
            outs.append(jnp.dot(probs, values, preferred_element_type=wide))
            sums = jnp.where(lane == h, top + jnp.log(total), sums)
        out[first:last, :] = jnp.concatenate(outs, axis=1).astype(low)
        logsum[first:last, :] = sums


def attend(qkv, stacked):
    length, three = qkv.shape
    head_width = three // 3
    heads = head_width // HEAD_DIM
    whole = pl.BlockSpec(memory_space=pltpu.VMEM)
    return pl.pallas_call(
        functools.partial(attend_kernel, min(256, length)),
        grid=(1,),
        in_specs=[whole, pl.BlockSpec(memory_space=pl.ANY)],
        out_specs=[pl.BlockSpec((length, head_width), lambda n: (0, 0)), whole],
        out_shape=[
            jax.ShapeDtypeStruct(stacked.shape, low),
            jax.ShapeDtypeStruct((length, LANES), wide),
        ],
        input_output_aliases={1: 0},
        cost_estimate=pl.CostEstimate(
            flops=4 * heads * length * length * LANES,
            bytes_accessed=8 * length * three,
            transcendentals=heads * length * length,
        ),
        name="attend",
    )(qkv, stacked)


def attend_back_kernel(step, qkv, grad, logsum, cosine, sine, entered, out, gone):
    del entered
    length, head_width = grad.shape
    scale = HEAD_DIM ** (-0.5)
    over_rows = (((0,), (0,)), ((), ()))
    for first in reversed(range(0, length, step)):
        last = first + step
        parts = [[], [], []]
        for h in range(head_width // HEAD_DIM):
            a, b = h * HEAD_DIM, (h + 1) * HEAD_DIM
            query = qkv[first:last, a:b]
            keys = qkv[:last, head_width + a : head_width + b]
            values = qkv[:last, 2 * head_width + a : 2 * head_width + b]
            upstream = grad[first:last, a:b]
            probs = jnp.exp(scores_of(query, keys, first) - logsum[first:last, h : h + 1])
            prob_grad = lax.dot_general(
                upstream, values, (((1,), (1,)), ((), ())), preferred_element_type=wide
            )
            inner = jnp.sum(probs * prob_grad, axis=-1, keepdims=True)
            score_grad = (probs * (prob_grad - inner)).astype(low)
            parts[0].append(jnp.dot(score_grad, keys, preferred_element_type=wide) * scale)
            parts[1].append(
                lax.dot_general(score_grad, query, over_rows, preferred_element_type=wide) * scale
            )
            parts[2].append(
                lax.dot_general(
                    probs.astype(low), upstream, over_rows, preferred_element_type=wide
                )
            )
        parts = [jnp.concatenate(part_list, axis=1) for part_list in parts]
        gone[first:last, :head_width] = parts[0]
        for t in (1, 2):
            columns = slice(t * head_width, (t + 1) * head_width)
            if last == length:
                gone[:, columns] = parts[t]
            else:
                gone[:last, columns] += parts[t]
    repeats = head_width // LANES
    for first in range(0, length, step):
        here = slice(first, first + step)
        ahead = jnp.concatenate([cosine[here, :]] * repeats, axis=1)
        aside = -jnp.concatenate([sine[here, :]] * repeats, axis=1)
        for t in range(3):
            columns = slice(t * head_width, (t + 1) * head_width)
            value = gone[here, columns].astype(low)
            if t < 2:
                value = turn(value.astype(wide), ahead, aside).astype(low)
            out[here, columns] = value


def attend_back(qkv, grad, logsum, cosine, sine, entered):
    length, three = qkv.shape
    head_width = three // 3
    heads = head_width // HEAD_DIM
    whole = pl.BlockSpec(memory_space=pltpu.VMEM)
    return pl.pallas_call(
        functools.partial(attend_back_kernel, min(256, length)),
        grid=(1,),
        in_specs=[whole] * 5 + [pl.BlockSpec(memory_space=pl.ANY)],
        out_specs=pl.BlockSpec((length, three), lambda n: (0, 0)),
        out_shape=jax.ShapeDtypeStruct(entered.shape, low),
        scratch_shapes=[
            pltpu.VMEM((length, three), wide),
        ],
        input_output_aliases={5: 0},
        cost_estimate=pl.CostEstimate(
            flops=10 * heads * length * length * LANES,
            bytes_accessed=8 * length * three,
            transcendentals=heads * length * length,
        ),
        name="attend_back",
    )(qkv, grad, logsum, cosine, sine, entered)


def reject_kernel(count, hidden, grads, *refs):
    weights, (head_grad, entered) = refs[:count], refs[count:]
    depth = weights[0].shape[1]
    over = (((1,), (1,)), ((), ()))
    total = lax.dot_general(grads[:, :depth], weights[0][...], over, preferred_element_type=wide)
    for k in range(1, count):
        total = total + lax.dot_general(
            grads[:, k * depth : (k + 1) * depth],
            weights[k][...],
            over,
            preferred_element_type=wide,
        )

    @pl.when(pl.program_id(0) == 0)
    def _():
        head_grad[...] = total.astype(low)

    @pl.when(pl.program_id(0) > 0)
    def _():
        entered[...] = (total * gelu_parts(hidden[...])[1]).astype(low)


def reject(grads, weights, hidden, head_width):
    count = len(weights)
    length = grads.shape[0]
    behind, depth = weights[0].shape
    inside = behind + 2 * head_width
    return pl.pallas_call(
        functools.partial(reject_kernel, count),
        grid=(behind // head_width,),
        in_specs=[pl.BlockSpec((length, head_width), lambda t: (0, jnp.maximum(t - 1, 0)))]
        + [pl.BlockSpec((length, count * depth), lambda t: (0, 0))]
        + [pl.BlockSpec((head_width, depth), lambda t: (t, 0))] * count,
        out_specs=[
            pl.BlockSpec((length, head_width), lambda t: (0, 0)),
            pl.BlockSpec((length, head_width), lambda t: (0, jnp.maximum(t + 2, 3))),
        ],
        out_shape=[
            jax.ShapeDtypeStruct((length, head_width), low),
            jax.ShapeDtypeStruct((length, inside), low),
        ],
        cost_estimate=pl.CostEstimate(
            flops=2 * length * count * depth * behind,
            bytes_accessed=2 * count * depth * (behind + length) + 8 * length * behind,
            transcendentals=length * behind,
        ),
        name="reject",
    )(hidden, grads, *weights)


def answer_kernel(count, chips, part, entered, *refs):
    weights, (kept, sent, held) = refs[:count], refs[count:]
    rows = kept.shape[0] // chips
    over = (((1,), (1,)), ((), ()))
    for n in range(count):

        @pl.when(pl.program_id(0) == n)
        def _(n=n):
            held[...] = lax.dot_general(
                entered[...], weights[n][...], over, preferred_element_type=wide
            )

    for k in range(chips):
        here = slice(k * rows, (k + 1) * rows)
        for core, out in enumerate((kept, sent)):
            block = part[0] ^ (2 * k + core)
            source = pl.ds(pl.multiple_of(block * rows, rows), rows)
            out[here, :] = held[source, :].astype(out.dtype)


def answer(entered, pieces, part, chips, tall):
    count = len(pieces)
    length, inside = entered.shape
    half = length // 2
    return pl.pallas_call(
        functools.partial(answer_kernel, count, chips),
        grid=(count,),
        in_specs=[
            pl.BlockSpec(memory_space=pltpu.SMEM),
            pl.BlockSpec((length, inside), lambda t: (0, 0)),
        ]
        + [pl.BlockSpec((tall, inside), lambda t: (0, 0))] * count,
        out_specs=[pl.BlockSpec((half, tall), lambda t: (0, t))] * 2,
        out_shape=[
            jax.ShapeDtypeStruct((half, count * tall), wide),
            jax.ShapeDtypeStruct((half, count * tall), low),
        ],
        scratch_shapes=[pltpu.VMEM((length, tall), wide)],
        cost_estimate=pl.CostEstimate(
            flops=2 * length * inside * count * tall,
            bytes_accessed=2 * inside * (length + count * tall) + 3 * length * count * tall,
            transcendentals=0,
        ),
        name="answer",
    )(part[None], entered, *pieces)


def widen_rows_kernel(head_width, a, b, down, out):
    cut = a.shape[1]
    out[...] = b[0, :head_width].astype(wide)
    down[:cut] = b[0, head_width:].astype(wide)
    down[cut:] = a[0].astype(wide)


def widen_rows(all_a, all_b, head_width, width):
    count, cut, depth = all_a.shape
    assert head_width + cut == all_b.shape[1]
    moved = 6 * count * depth * (head_width + 2 * cut)
    return pl.pallas_call(
        functools.partial(widen_rows_kernel, head_width),
        grid=(count,),
        in_specs=[
            pl.BlockSpec((1, cut, depth), lambda j: (j, 0, 0)),
            pl.BlockSpec((1, head_width + cut, depth), lambda j: (j, 0, 0)),
        ],
        out_specs=[
            pl.BlockSpec((2 * cut, depth), lambda j: (j, 0)),
            pl.BlockSpec((head_width, depth), lambda j: (j, 0)),
        ],
        out_shape=[
            jax.ShapeDtypeStruct((count * 2 * cut, depth), wide),
            jax.ShapeDtypeStruct((width, depth), wide),
        ],
        cost_estimate=pl.CostEstimate(flops=0, bytes_accessed=moved, transcendentals=0),
        name="widen_rows",
    )(all_a, all_b)


def widen_columns_kernel(groups, gathered, out):
    count, _, columns = gathered.shape
    size = columns // groups
    for j in range(count):
        for g in range(groups):
            at = (g * count + j) * size
            out[:, at : at + size] = gathered[j, :, g * size : (g + 1) * size].astype(wide)


def widen_columns(gathered, rows, groups):
    count, _, columns = gathered.shape
    tall = min(64, rows)
    moved = 6 * count * rows * columns
    return pl.pallas_call(
        functools.partial(widen_columns_kernel, groups),
        grid=(rows // tall,),
        in_specs=[pl.BlockSpec((count, tall, columns), lambda r: (0, r, 0))],
        out_specs=pl.BlockSpec((tall, count * columns), lambda r: (r, 0)),
        out_shape=jax.ShapeDtypeStruct((rows, count * columns), wide),
        cost_estimate=pl.CostEstimate(flops=0, bytes_accessed=moved, transcendentals=0),
        name="widen_columns",
    )(gathered)


def local(
    tokens,
    teacher,
    valid,
    positions,
    norm_gain,
    norm_bias,
    qkv_weight,
    qkv_bias,
    out_weight,
    out_bias,
    up_weight,
    up_bias,
    down_weight,
    down_bias,
):
    rows_here, width = tokens.shape[1:]
    seq_count = lax.axis_size("seq")
    data_count = lax.axis_size("dp")
    part = lax.axis_index("seq")
    owner = lax.axis_index("dp")
    length = rows_here * seq_count
    head_width = HEADS // seq_count * HEAD_DIM
    three = 3 * head_width
    units = up_weight.shape[1] // seq_count
    inside = three + units
    depth = qkv_weight.shape[0]
    mask = valid[0].astype(wide)

    tall = depth // 2
    behind = head_width + units

    def span(start, size, unit):
        return pl.ds(start if isinstance(start, int) else pl.multiple_of(start, unit), size)

    def block_at(row, rows, column, columns):
        return span(row, rows, ROWS), span(column, columns, LANES)

    moves = []
    for half in range(2):
        for t in range(3):
            moves.append(
                (
                    0,
                    lambda part, t=t, half=half: block_at(
                        half * tall, tall, t * width + part * head_width, head_width
                    ),
                    half,
                    block_at(0, tall, t * head_width, head_width),
                )
            )
        moves.append(
            (
                1,
                lambda part, half=half: block_at(half * tall, tall, part * units, units),
                half,
                block_at(0, tall, three, units),
            )
        )
    w_in = pick(
        (qkv_weight, up_weight),
        part[None],
        valid,
        moves,
        [(tall, inside), (tall + SPARE, inside)],
    )
    normed_low, base = enter(
        tokens[0],
        teacher[0],
        norm_gain,
        norm_bias,
        out_bias,
        down_bias,
        positions,
        after(owner, *w_in),
        data_count,
    )

    rest = behind // 2 - head_width
    moves = [
        (
            0,
            lambda part: block_at(part * head_width, head_width, 0, depth),
            0,
            block_at(0, head_width, 0, depth),
        ),
        (
            1,
            lambda part: block_at(part * units, rest, 0, depth),
            0,
            block_at(head_width, rest, 0, depth),
        ),
        (
            1,
            lambda part: block_at(part * units + rest, units - rest, 0, depth),
            1,
            block_at(0, units - rest, 0, depth),
        ),
    ]
    w_back = pick(
        (out_weight, down_weight),
        after(part[None], normed_low),
        valid,
        moves,
        [(behind // 2, depth)] * 2,
    )
    if data_count == 4:
        sides = [tuple(swap(item, "dp", k) for item in w_in) for k in (1, 2)]
        last_in = swap(sides[0][0], "dp", 2), swap(sides[1][1], "dp", 1)
        first_in = [w_in, *sides]
        w_back = lax.optimization_barrier((*w_back, *last_in))[:2]
        back_sides = [tuple(swap(item, "dp", k) for item in w_back) for k in (1, 2)]
    else:
        w_in = [w_in] + [tuple(swap(item, "dp", k) for item in w_in) for k in range(1, data_count)]
        w_back = [w_back] + [
            tuple(swap(item, "dp", k) for item in w_back) for k in range(1, data_count)
        ]
        first_in, last_in = w_in[:-1], w_in[-1]
    normed_all = gather_seq(normed_low)
    facts = normed_all[:, width : width + 2].astype(jnp.int32)
    where = facts[:, 0] * RADIX + facts[:, 1]

    half = ROTARY // 2
    lane = jnp.arange(LANES, dtype=jnp.int32) % HEAD_DIM
    freqs = rope_base ** (-((lane % half).astype(wide) * 2.0) / ROTARY)
    angles = where.astype(wide)[:, None] * jnp.where(lane < ROTARY, freqs, 0.0)[None, :]
    cosine = jnp.cos(angles)
    sine = jnp.sin(angles) * jnp.where(lane < half, -1.0, 1.0)[None, :]

    b_in = jnp.concatenate(
        [
            lax.dynamic_slice_in_dim(qkv_bias, t * width + part * head_width, head_width, 0)
            for t in range(3)
        ]
        + [lax.dynamic_slice_in_dim(up_bias, part * units, units, 0)]
    ).astype(wide)[None]

    def piece(array, k):
        return array[:, k * depth : (k + 1) * depth]

    flat_in = [item for pair in first_in for item in pair]
    begun = begin(normed_all, b_in, flat_in, tall, head_width)
    begun, cosine, sine = lax.optimization_barrier((begun, cosine, sine))
    qkv, hidden, stacked = project(normed_all, cosine, sine, begun, last_in, tall, head_width)
    stacked, logsum = attend(qkv, stacked)

    counted = [item[1] for item in (*first_in, last_in)]
    if data_count == 4:
        back_sides = [tuple(after(item, qkv) for item in pair) for pair in back_sides]
        w_back = [w_back, *back_sides]
        w_back.append((swap(back_sides[0][0], "dp", 2), swap(back_sides[1][1], "dp", 1)))
    branches = emit(stacked, w_back[:-1], [], 0, data_count)
    branches = emit(stacked, w_back[-1:], counted, data_count - 1, data_count, branches)
    branches = scatter_seq(branches)
    digits = branches[0, width : width + 3]
    count = digits[0] + DIGIT * digits[1] + DIGIT * DIGIT * digits[2]
    error = base + branches[:, :width]
    weighted = mask[:, None] * error
    squares = jnp.sum(weighted * error)
    grad_output = length * data_count / count * weighted
    grad_all = gather_seq(grad_output.astype(low))
    branch_bias_grad = jnp.sum(grad_all.astype(wide), axis=0)
    w_back = [jnp.concatenate(pair, axis=0) for pair in w_back]

    def owned(left, right):
        return dot(left, right, ((0,), (0,)))

    def gather(array):
        return lax.all_gather(array, "seq", axis=0, tiled=False)

    cut = units // 2

    def of_stacked(first, last):
        return [owned(stacked[:, first:last], piece(grad_all, k)) for k in range(data_count)]

    def of_normed(right):
        return [owned(piece(normed_all, k), right) for k in range(data_count)]

    def prepare(pieces):
        return pieces[0], [item.astype(low) for item in pieces[1:]]

    def send(sent, *meanwhile):
        got = [swap(item, "dp", k + 1) for k, item in enumerate(sent)]
        held = lax.optimization_barrier((*got, *jax.tree.leaves(meanwhile)))
        return held[: len(got)], jax.tree.unflatten(jax.tree.structure(meanwhile), held[len(got) :])

    def total(own, got):
        for item in got:
            own = own + item.astype(wide)
        return own.astype(low)

    own_a, sent_a = prepare(of_stacked(head_width + cut, head_width + units))
    own_b, sent_b = prepare(of_stacked(0, head_width + cut))
    head_grad, in_low = reject(grad_all, w_back, hidden, head_width)
    got, ((own_b, sent_b), head_grad, in_low) = send(
        sent_a, (own_b, sent_b), head_grad, in_low
    )
    down_a = total(own_a, got)
    all_a = gather(down_a)
    own_up, sent_up = prepare(of_normed(in_low[:, three:]))
    got, ((own_up, sent_up), head_grad) = send(sent_b, (own_up, sent_up), head_grad)
    down_b = total(own_b, got)
    all_b = gather(down_b)
    head_grad = after(head_grad, down_b)
    in_low = attend_back(qkv, head_grad, logsum, cosine, sine, in_low)
    own_qkv, sent_qkv = prepare(of_normed(in_low[:, :three]))
    kept, sent = answer(in_low, [*flat_in, *last_in], part, seq_count // 2, tall)
    got, ((own_qkv, sent_qkv), kept, sent, all_a) = send(
        sent_up, (own_qkv, sent_qkv), kept, sent, all_a
    )
    up_grad = total(own_up, got)
    all_up = gather(up_grad)
    summed = scatter_blocks(kept, sent)
    got, (summed, all_b) = send(sent_qkv, summed, all_b)
    qkv_grad = total(own_qkv, got)
    token_grad, gain_grad, shift_grad, branch_bias_grad = leave(
        tokens[0],
        norm_gain,
        summed,
        grad_output,
        branch_bias_grad,
        owner,
        data_count,
    )

    in_bias = jnp.sum(in_low.astype(wide), axis=0)
    small = jnp.concatenate(
        [in_bias, gain_grad[0], shift_grad[0], squares[None], branch_bias_grad[0]]
    )
    small = total_dp(small[None])[0]
    branch_bias_grad = small[-width:]
    small = small[:-width]
    lines = -(-small.size // three)
    lines += -lines % 8
    high = jnp.pad(small, (0, lines * three - small.size)).reshape(lines, three)
    first = lax.reduce_precision(high, 8, 7)
    beside = jnp.concatenate([qkv_grad, first.astype(low), (high - first).astype(low)])

    down_weight_grad, out_weight_grad = widen_rows(all_a, all_b, head_width, width)
    all_qkv = gather(after(beside, all_up))
    up_weight_grad = widen_columns(all_up, depth, 1)
    all_qkv = after(all_qkv, down_weight_grad, up_weight_grad)
    qkv_weight_grad = widen_columns(all_qkv, depth, 3)
    slots = all_qkv[:, depth:].astype(wide)
    slots = (slots[:, :lines] + slots[:, lines:]).reshape(seq_count, -1)
    norm_grads = jnp.sum(slots[:, inside : inside + 2 * width + 1], axis=0)
    qkv_bias_grad = slots[:, :three].reshape(seq_count, 3, head_width).transpose(1, 0, 2)
    up_bias_grad = slots[:, three:inside].reshape(-1)
    loss = norm_grads[-1] / (2.0 * width * count)
    return (
        loss,
        token_grad[None],
        norm_grads[:width],
        norm_grads[width : 2 * width],
        qkv_weight_grad,
        qkv_bias_grad.reshape(-1),
        out_weight_grad,
        branch_bias_grad,
        up_weight_grad,
        up_bias_grad,
        down_weight_grad,
        branch_bias_grad,
    )


def solution(mesh):
    placed = (
        P("dp", "seq", None),
        P("dp", "seq", None),
        P("dp", "seq"),
        P("dp", "seq"),
        P(),
        P(),
        P("dp", None),
        P(),
        P(None, "dp"),
        P(),
        P("dp", None),
        P(),
        P(None, "dp"),
        P(),
    )
    return jax.shard_map(
        local,
        mesh=mesh,
        in_specs=placed,
        out_specs=(
            P(),
            P("dp", "seq", None),
            P(),
            P(),
            P("dp", None),
            P(),
            P(None, "dp"),
            P(),
            P("dp", None),
            P(),
            P(None, "dp"),
            P(),
        ),
        check_vma=False,
    )
```

time: 704 us -> 597 us (0.85)
  waiting for transfers between devices: 337 us -> 283 us
  matrix products: 70.2 us -> 41.4 us
  starting transfers between devices: 88.3 us -> 60.4 us
  local copies, waits for them, and re-layouts: 30 us -> 10.9 us
  Pallas kernels: 127 us -> 139 us
  other arithmetic: 23 us -> 33.4 us
    ppermute x59 -> x27, waiting for transfers between devices: 254 us -> 76.4 us  [swap(): lax.ppermute(array, axis, [(s, s ^ bit) for s in range(lax.axis_size(axis...]
    ppermute x0 -> x5, waiting for transfers between devices: none -> 68.1 us  [between(): lax.ppermute(array, 'seq', [(2 * a + core, 2 * b + core) for a, b in pair...]
    ppermute x59 -> x27, starting transfers between devices: 87.9 us -> 32.9 us  [swap(): lax.ppermute(array, axis, [(s, s ^ bit) for s in range(lax.axis_size(axis...]
    reduce_scatter x0 -> x1, waiting for transfers between devices: none -> 52.2 us  [scatter_seq(): lax.psum_scatter(partial, 'seq', scatter_dimension=0, tiled=True)]
    all_gather x0 -> x2, waiting for transfers between devices: none -> 37.8 us  [gather_seq(): return lax.all_gather(rows, 'seq', axis=0, tiled=True)]
    all_gather x5 -> x4, waiting for transfers between devices: 82.1 us -> 48.2 us  [gather(): return lax.all_gather(array, 'seq', axis=0, tiled=False)]
    dot_general x28 -> x16, matrix products: 70.2 us -> 41.4 us  [dot(): return lax.dot_general(a, b, (dims, ((), ())), preferred_element_type=wide)]
    ppermute x0 -> x5, starting transfers between devices: none -> 26.8 us  [between(): lax.ppermute(array, 'seq', [(2 * a + core, 2 * b + core) for a, b in pair...]
  transfers between devices with their start and end apart: 64 -> 39, of which waited for: 27 -> 18; matrix products, arithmetic and copies ran while one was open for 16% -> 11% of each run, Pallas kernels for 16% -> 20%
where the time goes in v3:
time: 597 us; the launch traced here: 587 us
  waiting for transfers between devices  283 us (47%)
  Pallas kernels  139 us (23%)
  starting transfers between devices  60.4 us (10%)
  matrix products  41.4 us (7%)
  other arithmetic  33.4 us (6%)
  between operations  18.8 us (3%)
  local copies, waits for them, and re-layouts  10.9 us (2%)
    ppermute x27, waiting for transfers between devices, swap(): lax.ppermute(array, axis, [(s, s ^ bit) for s in range(lax.axis_size(axis...  76.4 us
    ppermute x5, waiting for transfers between devices, between(): lax.ppermute(array, 'seq', [(2 * a + core, 2 * b + core) for a, b in pair...  68.1 us
    reduce_scatter x1, waiting for transfers between devices, scatter_seq(): lax.psum_scatter(partial, 'seq', scatter_dimension=0, tiled=True)  52.2 us
    all_gather x4, waiting for transfers between devices, gather(): return lax.all_gather(array, 'seq', axis=0, tiled=False)  48.2 us
    dot_general x16, matrix products, dot(): return lax.dot_general(a, b, (dims, ((), ())), preferred_element_type=wide)  41.4 us
    all_gather x2, waiting for transfers between devices, gather_seq(): return lax.all_gather(rows, 'seq', axis=0, tiled=True)  37.8 us
    ppermute x27, starting transfers between devices, swap(): lax.ppermute(array, axis, [(s, s ^ bit) for s in range(lax.axis_size(axis...  32.9 us
    ppermute x5, starting transfers between devices, between(): lax.ppermute(array, 'seq', [(2 * a + core, 2 * b + core) for a, b in pair...  26.8 us
  transfers between devices with their start and end apart: 39, of which 18 were waited for; matrix products, arithmetic and copies ran while one was open for 11% of the time, Pallas kernels for 20%

profile of v3, /device:TPU:0, one launch (start us, length us, event | category | flops | bytes accessed | tf_op | source)
XLA Modules:
  0.0 586.8 jit_solution(1571364532032162470)
XLA Ops:
  7.2 3.5 pick.2
  10.7 3.0 enter.1
  13.8 3.0 collective-permute-start.3
  18.3 20.3 %collective-permute-done.3.refs_5_.refs_2_ = bf16[272,1792]{1,0:T(8,128)(2,1)S(1)} collective-permute-done((bf16[272,1792]{1,0:T(8,128)(2,1)}, bf16[272,1792]{1,0:T(8,128)(2,1)S(1)}, u32[]{:S(2)}, u32[]{:S(2)}) %collective-permute-start.3) | collective-permute-done | bytes 974880 | tf_op jit(solution)/shard_map/ppermute | solution.py:37
  44.2 3.1 pick.3
  47.9 16.0 %collective-permute-done.4.weights.refs_6_ = bf16[256,1792]{1,0:T(8,128)(2,1)} collective-permute-done((bf16[256,1792]{1,0:T(8,128)(2,1)}, bf16[256,1792]{1,0:T(8,128)(2,1)}, u32[]{:S(2)}, u32[]{:S(2)}) %collective-permute-start.4) | collective-permute-done | bytes 917536 | tf_op jit(solution)/shard_map/ppermute | solution.py:37
  68.9 3.1 fusion.43
  72.0 11.6 %collective-permute-done.2.refs_4_ = bf16[256,1792]{1,0:T(8,128)(2,1)} collective-permute-done((bf16[256,1792]{1,0:T(8,128)(2,1)}, bf16[256,1792]{1,0:T(8,128)(2,1)}, u32[]{:S(2)}, u32[]{:S(2)}) %collective-permute-start.2) | collective-permute-done | bytes 917536 | tf_op jit(solution)/shard_map/ppermute | solution.py:37
  86.1 12.1 %begin.1.begun = f32[1024,1792]{1,0:T(8,128)} custom-call(bf16[1024,2176]{1,0:T(8,128)(2,1)} %all-gather.11.cloned.1.call-done.normed.other, f32[1,1792]{1,0:T(1,128)} %maximum_convert_fusion.bias, bf16[256,1792]{1,0:T(8,128)(2,1)} %get-tuple-element.79.refs_0_, bf16[272,1792]{1,0:T(8,128)(2,1)} %get-tuple-element.80.refs_1_.refs_0_, ...), custom_call_target="tpu_custom_call" | custom-call | flops 5637144576 | bytes 17301504 | tf_op jit(solution)/shard_map/begin/pallas_call | solution.py:252
  98.2 12.0 %project.1 = (bf16[1024,768]{1,0:T(8,128)(2,1)}, f32[1024,1024]{1,0:T(8,128)}, bf16[1024,1280]{1,0:T(8,128)(2,1)}) custom-call(bf16[1024,2176]{1,0:T(8,128)(2,1)} %all-gather.11.cloned.1.call-done.normed.other, bf16[1024,2176]{1,0:T(8,128)(2,1)} %all-gather.11.cloned.1.call-done.normed.other, f32[1024,128]{1,0:T(8,128)} %get-tuple-element.83.cosine, ...), custom_call_target="tpu_custom_call" | custom-call | flops 1879048192 | bytes 24903680 | tf_op jit(solution)/shard_map/project/pallas_call | solution.py:303
  112.4 10.1 %attend.1 = (bf16[1024,1280]{1,0:T(8,128)(2,1)}, f32[1024,128]{1,0:T(8,128)}) custom-call(bf16[1024,768]{1,0:T(8,128)(2,1)} %get-tuple-element.86.qkv, bf16[1024,1280]{1,0:T(8,128)(2,1)} %get-tuple-element.87.stacked), custom_call_target="tpu_custom_call", output_to_operand_aliasing={{0}: (1, {})} | custom-call | flops 2147483648 | bytes 6291456 | tf_op jit(solution)/shard_map/attend/pallas_call | solution.py:433
  122.6 10.3 %emit.2.refs_6_ = bf16[1024,2176]{1,0:T(8,128)(2,1)} custom-call(bf16[1024,1280]{1,0:T(8,128)(2,1)} %get-tuple-element.88.stacked, bf16[640,512]{1,0:T(8,128)(2,1)} %get-tuple-element.92.refs_0_, bf16[640,512]{1,0:T(8,128)(2,1)} %get-tuple-element.94.refs_1_, bf16[640,512]{1,0:T(8,128)(2,1)} %collective-permute-done.6.refs_2_, ...), custom_call_target="tpu_custom_call" | custom-call | flops 4026531840 | bytes 9699328 | tf_op jit(solution)/shard_map/emit/pallas_call | solution.py:382
  134.6 4.9 emit.3
  140.1 52.2 %reduce-scatter.2.cloned.1.call-done = bf16[128,2176]{1,0:T(8,128)(2,1)} async-done(((bf16[1024,2176]{1,0:T(8,128)(2,1)}), bf16[128,2176]{1,0:T(8,128)(2,1)}) %reduce-scatter.2.cloned.1.call-update) | async-done | bytes 557072 | tf_op jit(solution)/shard_map/reduce_scatter | solution.py:77
  200.3 2.5 pad_maximum_fusion.1.refs_1_
  202.8 2.8 pad_maximum_fusion.2.refs_2_
  206.7 37.8 %all-gather.13.cloned.1.call-done.grads = bf16[1024,2048]{1,0:T(8,128)(2,1)} async-done(((bf16[128,2048]{1,0:T(8,128)(2,1)}), bf16[1024,2048]{1,0:T(8,128)(2,1)}) %all-gather.13.cloned.1.call-update) | async-done | bytes 4194320 | tf_op jit(solution)/shard_map/all_gather | solution.py:41
  244.5 2.9 convolution_convert_fusion.11
  258.9 2.2 fusion.16
  261.0 13.2 %reject.1 = (bf16[1024,256]{1,0:T(8,128)(2,1)}, bf16[1024,1792]{1,0:T(8,128)(2,1)}) custom-call(f32[1024,1024]{1,0:T(8,128)} %get-tuple-element.99.hidden, bf16[1024,2048]{1,0:T(8,128)(2,1)} %all-gather.13.cloned.1.call-done.grads, bf16[1280,512]{1,0:T(8,128)(2,1)} %pad_maximum_fusion.refs_0_, bf16[1280,512]{1,0:T(8,128)(2,1)} %pad_maximum_fusion.1.refs_1_, ...), custom_call_target="tpu_custom_call" | custom-call | flops 5368709120 | bytes 19922944 | tf_op jit(solution)/shard_map/reject/pallas_call | solution.py:553
  275.8 3.3 add_convert_fusion.5
  282.7 4.3 convolution_convert_fusion.2
  287.1 2.5 fusion.3
  289.6 3.5 convolution_convert_fusion.1
  293.1 3.6 convolution_convert_fusion
  296.6 3.3 collective-permute-done.15
  299.9 14.3 %collective-permute-done.16 = bf16[768,512]{1,0:T(8,128)(2,1)S(1)} collective-permute-done((bf16[768,512]{1,0:T(8,128)(2,1)}, bf16[768,512]{1,0:T(8,128)(2,1)S(1)}, u32[]{:S(2)}, u32[]{:S(2)}) %collective-permute-start.16) | collective-permute-done | bytes 786464 | tf_op jit(solution)/shard_map/ppermute | solution.py:37
  320.9 16.6 %attend_back.1.entered = bf16[1024,1792]{1,0:T(8,128)(2,1)} custom-call(bf16[1024,768]{1,0:T(8,128)(2,1)} %get-tuple-element.86.qkv, bf16[1024,256]{1,0:T(8,128)(2,1)} %get-tuple-element.115.grad, f32[1024,128]{1,0:T(8,128)} %get-tuple-element.116.logsum, f32[1024,128]{1,0:T(8,128)} %get-tuple-element.83.cosine, ...), custom_call_target="tpu_custom_call", output_to_operand_aliasing={{}: (5, {})} | custom-call | flops 5368709120 | bytes 6291456 | tf_op jit(solution)/shard_map/attend_back/pallas_call | solution.py:507
  337.5 3.8 convolution_convert_fusion.5
  341.3 3.2 convolution_convert_fusion.4
  344.5 2.2 fusion.11
  348.6 15.3 %answer.1 = (f32[512,2048]{1,0:T(8,128)}, bf16[512,2048]{1,0:T(8,128)(2,1)}) custom-call(s32[1]{0:T(128)} %bitcast.part, bf16[1024,1792]{1,0:T(8,128)(2,1)} %attend_back.1.entered, bf16[256,1792]{1,0:T(8,128)(2,1)} %get-tuple-element.79.refs_0_, bf16[272,1792]{1,0:T(8,128)(2,1)} %get-tuple-element.80.refs_1_.refs_0_, ...), custom_call_target="tpu_custom_call" | custom-call | flops 7516192768 | bytes 17301504 | tf_op jit(solution)/shard_map/answer/pallas_call | solution.py:600
  364.0 3.3 add_convert_fusion
  367.7 4.4 collective-permute-done.24
  372.1 2.9 convert_add_fusion
  376.9 18.4 %collective-permute-done.25 = bf16[128,2048]{1,0:T(8,128)(2,1)S(1)} collective-permute-done((bf16[128,2048]{1,0:T(8,128)(2,1)S(1)}, bf16[128,2048]{1,0:T(8,128)(2,1)S(1)}, u32[]{:S(2)}, u32[]{:S(2)}) %collective-permute-start.25) | collective-permute-done | bytes 524320 | tf_op jit(solution)/shard_map/ppermute | solution.py:45
  396.1 5.0 collective-permute-start.26
  401.1 18.0 %collective-permute-done.26 = bf16[128,2048]{1,0:T(8,128)(2,1)S(1)} collective-permute-done((bf16[128,2048]{1,0:T(8,128)(2,1)S(1)}, bf16[128,2048]{1,0:T(8,128)(2,1)S(1)}, u32[]{:S(2)}, u32[]{:S(2)}) %collective-permute-start.26) | collective-permute-done | bytes 524320 | tf_op jit(solution)/shard_map/ppermute | solution.py:45
  421.1 17.9 %collective-permute-start.27 = (bf16[128,2048]{1,0:T(8,128)(2,1)S(1)}, bf16[128,2048]{1,0:T(8,128)(2,1)S(1)}, u32[]{:S(2)}, u32[]{:S(2)}) collective-permute-start(bf16[128,2048]{1,0:T(8,128)(2,1)S(1)} %get-tuple-element.148), channel_id=1, source_target_pairs={{0,2},{1,3},{2,4},{3,5},{4,6},{5,7},{8,10},{9,11},{10,12},{11,13},... | collective-permute-start | bytes 1572872 | tf_op jit(solution)/shard_map/ppermute | solution.py:45
  445.6 14.3 %collective-permute-done.27 = bf16[128,2048]{1,0:T(8,128)(2,1)S(1)} collective-permute-done((bf16[128,2048]{1,0:T(8,128)(2,1)S(1)}, bf16[128,2048]{1,0:T(8,128)(2,1)S(1)}, u32[]{:S(2)}, u32[]{:S(2)}) %collective-permute-start.27) | collective-permute-done | bytes 524320 | tf_op jit(solution)/shard_map/ppermute | solution.py:45
  460.0 17.4 %collective-permute-done.29 = bf16[128,2048]{1,0:T(8,128)(2,1)S(1)} collective-permute-done((bf16[128,2048]{1,0:T(8,128)(2,1)S(1)}, bf16[128,2048]{1,0:T(8,128)(2,1)S(1)}, u32[]{:S(2)}, u32[]{:S(2)}) %collective-permute-start.29) | collective-permute-done | bytes 524320 | tf_op jit(solution)/shard_map/ppermute | solution.py:45
  477.4 2.4 fusion.7.summed
  479.8 3.7 leave.1
  486.4 2.5 collective-permute-done.30
  494.2 12.1 %widen_rows.1 = (f32[8192,512]{1,0:T(8,128)}, f32[2048,512]{1,0:T(8,128)}) custom-call(bf16[8,512,512]{2,1,0:T(8,128)(2,1)} %bitcast.40, bf16[8,768,512]{2,1,0:T(8,128)(2,1)} %bitcast.39), custom_call_target="tpu_custom_call" | custom-call | bytes 31457280 | tf_op jit(solution)/shard_map/widen_rows/pallas_call | solution.py:634
  506.4 10.4 %widen_columns.2 = f32[512,8192]{1,0:T(8,128)} custom-call(bf16[8,512,1024]{2,1,0:T(8,128)(2,1)} %bitcast.36), custom_call_target="tpu_custom_call" | custom-call | bytes 25165824 | tf_op jit(solution)/shard_map/widen_columns/pallas_call | solution.py:667
  516.8 48.1 %all-gather.21.cloned.1.call-done = bf16[4224,768]{1,0:T(8,128)(2,1)} async-done(((bf16[528,768]{1,0:T(8,128)(2,1)}), bf16[4224,768]{1,0:T(8,128)(2,1)}) %all-gather.21.cloned.1.call-update) | async-done | bytes 6488080 | tf_op jit(solution)/shard_map/all_gather | solution.py:846
  567.1 8.8 %widen_columns.3 = f32[512,6144]{1,0:T(8,128)} custom-call(bf16[8,528,768]{2,1,0:T(8,128)(2,1)} %bitcast.38), custom_call_target="tpu_custom_call" | custom-call | bytes 18874368 | tf_op jit(solution)/shard_map/widen_columns/pallas_call | solution.py:667
  (167 shorter events, 75.9 us)
Async XLA Ops:
  7.2 60.4 %all-gather.11.cloned.1.call-start = ((), (), s32[]{:S(2)}) async-start(), calls=%async_computation.1 | async-start | bytes 5013504 | tf_op jit(solution)/shard_map/all_gather | solution.py:41
  13.7 178.6 %reduce-scatter.2.cloned.1.call-start = ((), (), s32[]{:S(2)}) async-start(), calls=%async_computation.2 | async-start | bytes 5013504 | tf_op jit(solution)/shard_map/reduce_scatter | solution.py:77
  13.8 24.8 %collective-permute-start.3 = (bf16[272,1792]{1,0:T(8,128)(2,1)}, bf16[272,1792]{1,0:T(8,128)(2,1)S(1)}, u32[]{:S(2)}, u32[]{:S(2)}) collective-permute-start(bf16[272,1792]{1,0:T(8,128)(2,1)} %get-tuple-element.80.refs_1_.refs_0_), channel_id=1, source_target_pairs={{0,16},{8,24},{16,0},{24,8},{1,17},{9,25},{17,1},{25,9},{2,18},{10... | collective-permute-start | bytes 2924552 | tf_op jit(solution)/shard_map/ppermute | solution.py:37
  16.8 23.5 %collective-permute-start = (bf16[256,1792]{1,0:T(8,128)(2,1)}, bf16[256,1792]{1,0:T(8,128)(2,1)}, u32[]{:S(2)}, u32[]{:S(2)}) collective-permute-start(bf16[256,1792]{1,0:T(8,128)(2,1)} %get-tuple-element.79.refs_0_), channel_id=1, source_target_pairs={{0,8},{8,0},{16,24},{24,16},{1,9},{9,1},{17,25},{25,17},{2,10},{10... | collective-permute-start | bytes 2752520 | tf_op jit(solution)/shard_map/ppermute | solution.py:37
  38.6 25.3 %collective-permute-start.5 = (bf16[272,1792]{1,0:T(8,128)(2,1)S(1)}, bf16[272,1792]{1,0:T(8,128)(2,1)S(1)}, u32[]{:S(2)}, u32[]{:S(2)}) collective-permute-start(bf16[272,1792]{1,0:T(8,128)(2,1)S(1)} %collective-permute-done.3.refs_5_.refs_2_), channel_id=1, source_target_pairs={{0,8},{8,0},{16,24},{24,16},{1,9},{9,1},{17,25},{25,17},{2,10},{10... | collective-permute-start | bytes 2924552 | tf_op jit(solution)/shard_map/ppermute | solution.py:37
  40.3 23.6 %collective-permute-start.4 = (bf16[256,1792]{1,0:T(8,128)(2,1)}, bf16[256,1792]{1,0:T(8,128)(2,1)}, u32[]{:S(2)}, u32[]{:S(2)}) collective-permute-start(bf16[256,1792]{1,0:T(8,128)(2,1)} %collective-permute-done.refs_2_), channel_id=1, source_target_pairs={{0,16},{8,24},{16,0},{24,8},{1,17},{9,25},{17,1},{25,9},{2,18},{10... | collective-permute-start | bytes 2752520 | tf_op jit(solution)/shard_map/ppermute | solution.py:37
  41.8 41.7 %collective-permute-start.2 = (bf16[256,1792]{1,0:T(8,128)(2,1)}, bf16[256,1792]{1,0:T(8,128)(2,1)}, u32[]{:S(2)}, u32[]{:S(2)}) collective-permute-start(bf16[256,1792]{1,0:T(8,128)(2,1)} %get-tuple-element.79.refs_0_), channel_id=1, source_target_pairs={{0,16},{8,24},{16,0},{24,8},{1,17},{9,25},{17,1},{25,9},{2,18},{10... | collective-permute-start | bytes 2752520 | tf_op jit(solution)/shard_map/ppermute | solution.py:37
  42.4 42.8 %collective-permute-start.1 = (bf16[272,1792]{1,0:T(8,128)(2,1)}, bf16[272,1792]{1,0:T(8,128)(2,1)S(1)}, u32[]{:S(2)}, u32[]{:S(2)}) collective-permute-start(bf16[272,1792]{1,0:T(8,128)(2,1)} %get-tuple-element.80.refs_1_.refs_0_), channel_id=1, source_target_pairs={{0,8},{8,0},{16,24},{24,16},{1,9},{9,1},{17,25},{25,17},{2,10},{10... | collective-permute-start | bytes 2924552 | tf_op jit(solution)/shard_map/ppermute | solution.py:37
  63.9 34.3 %copy-start.3 = (bf16[272,1792]{1,0:T(8,128)(2,1)}, bf16[272,1792]{1,0:T(8,128)(2,1)S(1)}, u32[]{:S(2)}) copy-start(bf16[272,1792]{1,0:T(8,128)(2,1)S(1)} %collective-permute-done.5.others.refs_3_.refs_7_) | copy-start | bytes 2924548
  63.9 48.5 %collective-permute-start.11 = (bf16[640,512]{1,0:T(8,128)(2,1)}, bf16[640,512]{1,0:T(8,128)(2,1)}, u32[]{:S(2)}, u32[]{:S(2)}) collective-permute-start(bf16[640,512]{1,0:T(8,128)(2,1)} %get-tuple-element.92.refs_0_), channel_id=1, source_target_pairs={{0,16},{8,24},{16,0},{24,8},{1,17},{9,25},{17,1},{25,9},{2,18},{10... | collective-permute-start | bytes 1966088 | tf_op jit(solution)/shard_map/ppermute | solution.py:37
  65.5 44.7 %collective-permute-start.6 = (bf16[640,512]{1,0:T(8,128)(2,1)}, bf16[640,512]{1,0:T(8,128)(2,1)}, u32[]{:S(2)}, u32[]{:S(2)}) collective-permute-start(bf16[640,512]{1,0:T(8,128)(2,1)} %get-tuple-element.92.refs_0_), channel_id=1, source_target_pairs={{0,8},{8,0},{16,24},{24,16},{1,9},{9,1},{17,25},{25,17},{2,10},{10... | collective-permute-start | bytes 1966088 | tf_op jit(solution)/shard_map/ppermute | solution.py:37
  66.4 46.1 %collective-permute-start.10 = (bf16[640,512]{1,0:T(8,128)(2,1)}, bf16[640,512]{1,0:T(8,128)(2,1)}, u32[]{:S(2)}, u32[]{:S(2)}) collective-permute-start(bf16[640,512]{1,0:T(8,128)(2,1)} %get-tuple-element.94.refs_1_), channel_id=1, source_target_pairs={{0,8},{8,0},{16,24},{24,16},{1,9},{9,1},{17,25},{25,17},{2,10},{10... | collective-permute-start | bytes 1966088 | tf_op jit(solution)/shard_map/ppermute | solution.py:37
  83.6 26.6 %collective-permute-start.8 = (bf16[640,512]{1,0:T(8,128)(2,1)S(1)}, bf16[640,512]{1,0:T(8,128)(2,1)}, u32[]{:S(2)}, u32[]{:S(2)}) collective-permute-start(bf16[640,512]{1,0:T(8,128)(2,1)S(1)} %copy-done.18), channel_id=1, source_target_pairs={{0,16},{8,24},{16,0},{24,8},{1,17},{9,25},{17,1},{25,9},{2,18},{10... | collective-permute-start | bytes 1966088 | tf_op jit(solution)/shard_map/ppermute | solution.py:37
  110.2 22.6 %collective-permute-start.7 = (bf16[640,512]{1,0:T(8,128)(2,1)}, bf16[640,512]{1,0:T(8,128)(2,1)S(1)}, u32[]{:S(2)}, u32[]{:S(2)}) collective-permute-start(bf16[640,512]{1,0:T(8,128)(2,1)} %collective-permute-done.6.refs_2_), channel_id=1, source_target_pairs={{0,16},{8,24},{16,0},{24,8},{1,17},{9,25},{17,1},{25,9},{2,18},{10... | collective-permute-start | bytes 1966088 | tf_op jit(solution)/shard_map/ppermute | solution.py:37
  111.0 21.9 %collective-permute-start.9 = (bf16[640,512]{1,0:T(8,128)(2,1)}, bf16[640,512]{1,0:T(8,128)(2,1)S(1)}, u32[]{:S(2)}, u32[]{:S(2)}) collective-permute-start(bf16[640,512]{1,0:T(8,128)(2,1)} %collective-permute-done.8.refs_5_), channel_id=1, source_target_pairs={{0,8},{8,0},{16,24},{24,16},{1,9},{9,1},{17,25},{25,17},{2,10},{10... | collective-permute-start | bytes 1966088 | tf_op jit(solution)/shard_map/ppermute | solution.py:37
  139.5 57.5 %copy-start.14 = (f32[128,2048]{1,0:T(8,128)S(1)}, f32[128,2048]{1,0:T(8,128)}, u32[]{:S(2)}) copy-start(f32[128,2048]{1,0:T(8,128)} %get-tuple-element.98) | copy-start | bytes 3145732
  139.5 105.0 %all-gather.13.cloned.1.call-start = ((), (), s32[]{:S(2)}) async-start(), calls=%async_computation.3 | async-start | bytes 4718592 | tf_op jit(solution)/shard_map/all_gather | solution.py:41
  199.0 165.0 %all-gather.15.cloned.1.call-start = ((), (), s32[]{:S(2)}) async-start(), calls=%async_computation.4 | async-start | bytes 4718592 | tf_op jit(solution)/shard_map/all_gather | solution.py:846
  202.8 41.7 %copy-start.11 = (bf16[1024,1280]{1,0:T(8,128)(2,1)S(1)}, bf16[1024,1280]{1,0:T(8,128)(2,1)}, u32[]{:S(2)}) copy-start(bf16[1024,1280]{1,0:T(8,128)(2,1)} %get-tuple-element.88.stacked) | copy-start | bytes 7864324
  247.5 26.7 %collective-permute-start.12 = (bf16[512,512]{1,0:T(8,128)(2,1)}, bf16[512,512]{1,0:T(8,128)(2,1)}, u32[]{:S(2)}, u32[]{:S(2)}) collective-permute-start(bf16[512,512]{1,0:T(8,128)(2,1)} %convolution_convert_fusion.11), channel_id=1, source_target_pairs={{0,8},{8,0},{16,24},{24,16},{1,9},{9,1},{17,25},{25,17},{2,10},{10... | collective-permute-start | bytes 1572872 | tf_op jit(solution)/shard_map/ppermute | solution.py:37
  250.5 25.3 %collective-permute-start.13 = (bf16[512,512]{1,0:T(8,128)(2,1)}, bf16[512,512]{1,0:T(8,128)(2,1)}, u32[]{:S(2)}, u32[]{:S(2)}) collective-permute-start(bf16[512,512]{1,0:T(8,128)(2,1)} %convolution_convert_fusion.10), channel_id=1, source_target_pairs={{0,16},{8,24},{16,0},{24,8},{1,17},{9,25},{17,1},{25,9},{2,18},{10... | collective-permute-start | bytes 1572872 | tf_op jit(solution)/shard_map/ppermute | solution.py:37
  253.5 22.3 %collective-permute-start.14 = (bf16[512,512]{1,0:T(8,128)(2,1)}, bf16[512,512]{1,0:T(8,128)(2,1)}, u32[]{:S(2)}, u32[]{:S(2)}) collective-permute-start(bf16[512,512]{1,0:T(8,128)(2,1)} %convolution_convert_fusion.9), channel_id=1, source_target_pairs={{0,24},{8,16},{16,8},{24,0},{1,25},{9,17},{17,9},{25,1},{2,26},{10... | collective-permute-start | bytes 1572872 | tf_op jit(solution)/shard_map/ppermute | solution.py:37
  279.1 200.7 %all-gather.17.cloned.1.call-start = ((), (), s32[]{:S(2)}) async-start(), calls=%async_computation.5 | async-start | bytes 7077888 | tf_op jit(solution)/shard_map/all_gather | solution.py:846
  279.2 20.8 %collective-permute-start.15 = (bf16[768,512]{1,0:T(8,128)(2,1)}, bf16[768,512]{1,0:T(8,128)(2,1)S(1)}, u32[]{:S(2)}, u32[]{:S(2)}) collective-permute-start(bf16[768,512]{1,0:T(8,128)(2,1)} %convolution_convert_fusion.8), channel_id=1, source_target_pairs={{0,8},{8,0},{16,24},{24,16},{1,9},{9,1},{17,25},{25,17},{2,10},{10... | collective-permute-start | bytes 2359304 | tf_op jit(solution)/shard_map/ppermute | solution.py:37
  279.8 34.5 %collective-permute-start.16 = (bf16[768,512]{1,0:T(8,128)(2,1)}, bf16[768,512]{1,0:T(8,128)(2,1)S(1)}, u32[]{:S(2)}, u32[]{:S(2)}) collective-permute-start(bf16[768,512]{1,0:T(8,128)(2,1)} %convolution_convert_fusion.7), channel_id=1, source_target_pairs={{0,16},{8,24},{16,0},{24,8},{1,17},{9,25},{17,1},{25,9},{2,18},{10... | collective-permute-start | bytes 2359304 | tf_op jit(solution)/shard_map/ppermute | solution.py:37
  281.3 34.5 %collective-permute-start.17 = (bf16[768,512]{1,0:T(8,128)(2,1)S(1)}, bf16[768,512]{1,0:T(8,128)(2,1)S(1)}, u32[]{:S(2)}, u32[]{:S(2)}) collective-permute-start(bf16[768,512]{1,0:T(8,128)(2,1)S(1)} %convolution_convert_fusion.6), channel_id=1, source_target_pairs={{0,24},{8,16},{16,8},{24,0},{1,25},{9,17},{17,9},{25,1},{2,26},{10... | collective-permute-start | bytes 2359304 | tf_op jit(solution)/shard_map/ppermute | solution.py:37
  293.1 22.7 %copy-start.13 = (f32[768,512]{1,0:T(8,128)S(1)}, f32[768,512]{1,0:T(8,128)}, u32[]{:S(2)}) copy-start(f32[768,512]{1,0:T(8,128)} %fusion.16) | copy-start | bytes 4718596
  317.1 177.1 %all-gather.19.cloned.1.call-start = ((), (), s32[]{:S(2)}) async-start(), calls=%async_computation.6 | async-start | bytes 9437184 | tf_op jit(solution)/shard_map/all_gather | solution.py:846
  317.3 46.7 %collective-permute-start.18 = (bf16[512,1024]{1,0:T(8,128)(2,1)}, bf16[512,1024]{1,0:T(8,128)(2,1)S(1)}, u32[]{:S(2)}, u32[]{:S(2)}) collective-permute-start(bf16[512,1024]{1,0:T(8,128)(2,1)} %convolution_convert_fusion.2), channel_id=1, source_target_pairs={{0,8},{8,0},{16,24},{24,16},{1,9},{9,1},{17,25},{25,17},{2,10},{10... | collective-permute-start | bytes 3145736 | tf_op jit(solution)/shard_map/ppermute | solution.py:37
  318.2 45.8 %collective-permute-start.19 = (bf16[512,1024]{1,0:T(8,128)(2,1)}, bf16[512,1024]{1,0:T(8,128)(2,1)}, u32[]{:S(2)}, u32[]{:S(2)}) collective-permute-start(bf16[512,1024]{1,0:T(8,128)(2,1)} %convolution_convert_fusion.1), channel_id=1, source_target_pairs={{0,16},{8,24},{16,0},{24,8},{1,17},{9,25},{17,1},{25,9},{2,18},{10... | collective-permute-start | bytes 3145736 | tf_op jit(solution)/shard_map/ppermute | solution.py:37
  319.7 44.3 %collective-permute-start.20 = (bf16[512,1024]{1,0:T(8,128)(2,1)}, bf16[512,1024]{1,0:T(8,128)(2,1)}, u32[]{:S(2)}, u32[]{:S(2)}) collective-permute-start(bf16[512,1024]{1,0:T(8,128)(2,1)} %convolution_convert_fusion), channel_id=1, source_target_pairs={{0,24},{8,16},{16,8},{24,0},{1,25},{9,17},{17,9},{25,1},{2,26},{10... | collective-permute-start | bytes 3145736 | tf_op jit(solution)/shard_map/ppermute | solution.py:37
  367.3 197.5 %all-gather.21.cloned.1.call-start = ((), (), s32[]{:S(2)}) async-start(), calls=%async_computation.7 | async-start | bytes 7299072 | tf_op jit(solution)/shard_map/all_gather | solution.py:846
  367.6 4.4 collective-permute-start.24
  375.0 20.3 %copy-start = (f32[512,2048]{1,0:T(8,128)}, f32[512,2048]{1,0:T(8,128)S(1)}, u32[]{:S(2)}) copy-start(f32[512,2048]{1,0:T(8,128)S(1)} %convert_add_fusion) | copy-start | bytes 12582916
  375.0 20.2 %collective-permute-start.25 = (bf16[128,2048]{1,0:T(8,128)(2,1)S(1)}, bf16[128,2048]{1,0:T(8,128)(2,1)S(1)}, u32[]{:S(2)}, u32[]{:S(2)}) collective-permute-start(bf16[128,2048]{1,0:T(8,128)(2,1)S(1)} %slice.296), channel_id=1, source_target_pairs={{0,2},{1,3},{6,4},{7,5},{8,10},{9,11},{14,12},{15,13},{16,18},{17,... | collective-permute-start | bytes 1572872 | tf_op jit(solution)/shard_map/ppermute | solution.py:45
  395.4 5.8 collective-permute-start.28
  396.1 23.0 %collective-permute-start.26 = (bf16[128,2048]{1,0:T(8,128)(2,1)S(1)}, bf16[128,2048]{1,0:T(8,128)(2,1)S(1)}, u32[]{:S(2)}, u32[]{:S(2)}) collective-permute-start(bf16[128,2048]{1,0:T(8,128)(2,1)S(1)} %fusion.6), channel_id=1, source_target_pairs={{0,2},{1,3},{2,4},{3,5},{8,10},{9,11},{10,12},{11,13},{16,18},{17,... | collective-permute-start | bytes 1572872 | tf_op jit(solution)/shard_map/ppermute | solution.py:45
  401.1 39.2 %copy-start.2 = (bf16[1024,2048]{1,0:T(8,128)(2,1)S(1)}, bf16[1024,2048]{1,0:T(8,128)(2,1)}, u32[]{:S(2)}) copy-start(bf16[1024,2048]{1,0:T(8,128)(2,1)} %all-gather.13.cloned.1.call-done.grads) | copy-start | bytes 12582916
  421.1 24.0 %copy-start.6 = (bf16[1024,1792]{1,0:T(8,128)(2,1)S(1)}, bf16[1024,1792]{1,0:T(8,128)(2,1)}, u32[]{:S(2)}) copy-start(bf16[1024,1792]{1,0:T(8,128)(2,1)} %attend_back.1.entered) | copy-start | bytes 11010052
  421.1 38.9 %collective-permute-start.27 = (bf16[128,2048]{1,0:T(8,128)(2,1)S(1)}, bf16[128,2048]{1,0:T(8,128)(2,1)S(1)}, u32[]{:S(2)}, u32[]{:S(2)}) collective-permute-start(bf16[128,2048]{1,0:T(8,128)(2,1)S(1)} %get-tuple-element.148), channel_id=1, source_target_pairs={{0,2},{1,3},{2,4},{3,5},{4,6},{5,7},{8,10},{9,11},{10,12},{11,13},... | collective-permute-start | bytes 1572872 | tf_op jit(solution)/shard_map/ppermute | solution.py:45
  439.0 38.4 %collective-permute-start.29 = (bf16[128,2048]{1,0:T(8,128)(2,1)S(1)}, bf16[128,2048]{1,0:T(8,128)(2,1)S(1)}, u32[]{:S(2)}, u32[]{:S(2)}) collective-permute-start(bf16[128,2048]{1,0:T(8,128)(2,1)S(1)} %get-tuple-element.149), channel_id=1, source_target_pairs={{6,4},{7,5},{4,2},{5,3},{2,0},{3,1},{14,12},{15,13},{12,10},{13,11... | collective-permute-start | bytes 1572872 | tf_op jit(solution)/shard_map/ppermute | solution.py:45
  441.6 38.2 %collective-permute-start.21 = (bf16[512,768]{1,0:T(8,128)(2,1)}, bf16[512,768]{1,0:T(8,128)(2,1)S(1)}, u32[]{:S(2)}, u32[]{:S(2)}) collective-permute-start(bf16[512,768]{1,0:T(8,128)(2,1)} %convolution_convert_fusion.5), channel_id=1, source_target_pairs={{0,8},{8,0},{16,24},{24,16},{1,9},{9,1},{17,25},{25,17},{2,10},{10... | collective-permute-start | bytes 2359304 | tf_op jit(solution)/shard_map/ppermute | solution.py:37
  441.6 38.2 %collective-permute-start.22 = (bf16[512,768]{1,0:T(8,128)(2,1)}, bf16[512,768]{1,0:T(8,128)(2,1)}, u32[]{:S(2)}, u32[]{:S(2)}) collective-permute-start(bf16[512,768]{1,0:T(8,128)(2,1)} %convolution_convert_fusion.4), channel_id=1, source_target_pairs={{0,16},{8,24},{16,0},{24,8},{1,17},{9,25},{17,1},{25,9},{2,18},{10... | collective-permute-start | bytes 2359304 | tf_op jit(solution)/shard_map/ppermute | solution.py:37
  442.9 36.9 %collective-permute-start.23 = (bf16[512,768]{1,0:T(8,128)(2,1)}, bf16[512,768]{1,0:T(8,128)(2,1)}, u32[]{:S(2)}, u32[]{:S(2)}) collective-permute-start(bf16[512,768]{1,0:T(8,128)(2,1)} %convolution_convert_fusion.3), channel_id=1, source_target_pairs={{0,24},{8,16},{16,8},{24,0},{1,25},{9,17},{17,9},{25,1},{2,26},{10... | collective-permute-start | bytes 2359304 | tf_op jit(solution)/shard_map/ppermute | solution.py:37
  445.6 44.8 %copy-start.12 = (f32[512,768]{1,0:T(8,128)S(1)}, f32[512,768]{1,0:T(8,128)}, u32[]{:S(2)}) copy-start(f32[512,768]{1,0:T(8,128)} %fusion.11) | copy-start | bytes 4718596
  485.0 4.0 collective-permute-start.30
  489.0 4.0 collective-permute-start.31
  506.4 71.4 %copy-start.20 = (f32[1,2048]{1,0:T(1,128)}, f32[1,2048]{1,0:T(1,128)S(1)}, u32[]{:S(2)}) copy-start(f32[1,2048]{1,0:T(1,128)S(1)} %slice.193) | copy-start | bytes 24580
  (15 other events, 75.5 us)
Sparse Core Ops, SparseCore 0:
  13.9 52.2 all-gather.10
  139.6 52.6 reduce-scatter.1
  199.2 45.3 all-gather.12
  279.2 44.9 all-gather.14
  325.7 65.1 all-gather.16
  392.3 101.8 all-gather.18
  496.4 68.4 all-gather.20

commit v4 on v3

--- a/solution.py
+++ b/solution.py
@@ -74,15 +74,14 @@
 
 
 def scatter_seq(partial):
-    return lax.psum_scatter(partial, "seq", scatter_dimension=0, tiled=True).astype(wide)
+    return lax.psum_scatter(partial, "seq", scatter_dimension=0, tiled=True)
 
 
 def total_dp(array):
-    bit = 1
-    while bit < lax.axis_size("dp"):
-        array = array + swap(array, "dp", bit)
-        bit *= 2
-    return array
+    items = [array] + [swap(array, "dp", k) for k in range(1, lax.axis_size("dp"))]
+    while len(items) > 1:
+        items = [a + b for a, b in zip(items[::2], items[1::2])]
+    return items[0]
 
 
 def normalise(values):
@@ -107,11 +106,7 @@
         normed[:, k * depth : (k + 1) * depth] = held[:, theirs].astype(low)
         base[:, k * depth : (k + 1) * depth] = kept[:, theirs]
     lane = lax.broadcasted_iota(jnp.int32, (inputs.shape[0], LANES), 1)
-    row = lax.broadcasted_iota(jnp.int32, (inputs.shape[0], inputs.shape[0]), 0)
-    column = lax.broadcasted_iota(jnp.int32, row.shape, 1)
-    ids = jnp.sum(
-        jnp.where(row == column, place[...].astype(wide), 0.0), axis=1, keepdims=True
-    ).astype(jnp.int32)
+    ids = column_of(place[...]).astype(jnp.int32)
     facts = jnp.where(lane == 0, ids // RADIX, ids % RADIX)
     normed[:, width:] = facts.astype(wide).astype(low)
 
@@ -139,6 +134,47 @@
         bias_b,
         place,
     )
+
+
+def column_of(row):
+    size = row.shape[1]
+    here = lax.broadcasted_iota(jnp.int32, (size, size), 0)
+    there = lax.broadcasted_iota(jnp.int32, (size, size), 1)
+    return jnp.sum(jnp.where(here == there, row.astype(wide), 0.0), axis=1, keepdims=True)
+
+
+def grade_kernel(scale, branches, base, valid, grad, grad_low, sums):
+    width = base.shape[1]
+    lane = lax.broadcasted_iota(jnp.int32, (1, LANES), 1)
+    weight = jnp.where(lane == 1, float(DIGIT), jnp.where(lane == 2, float(DIGIT * DIGIT), 1.0))
+    digits = jnp.where(lane < 3, branches[:1, width:].astype(wide) * weight, 0.0)
+    count = jnp.sum(digits, axis=1, keepdims=True)
+    error = base[...] + branches[:, :width].astype(wide)
+    weighted = column_of(valid[...]) * error
+    squares = jnp.sum(jnp.sum(weighted * error, axis=0, keepdims=True), axis=1, keepdims=True)
+    result = scale / count * weighted
+    grad[...] = result
+    grad_low[...] = result.astype(low)
+    line = lax.broadcasted_iota(jnp.int32, sums.shape, 0)
+    sums[...] = jnp.where(line == 0, squares, count)
+
+
+def grade(branches, base, valid, scale):
+    whole = pl.BlockSpec(memory_space=pltpu.VMEM)
+    return pl.pallas_call(
+        functools.partial(grade_kernel, scale),
+        in_specs=[whole] * 3,
+        out_specs=[whole] * 3,
+        out_shape=[
+            jax.ShapeDtypeStruct(base.shape, wide),
+            jax.ShapeDtypeStruct(base.shape, low),
+            jax.ShapeDtypeStruct((8, LANES), wide),
+        ],
+        cost_estimate=pl.CostEstimate(
+            flops=4 * base.size, bytes_accessed=12 * base.size, transcendentals=0
+        ),
+        name="grade",
+    )(branches, base, valid)
 
 
 def leave_kernel(
@@ -235,43 +271,14 @@
     return values * cosine + partner * sine
 
 
-def begin_kernel(count, normed, bias, *refs):
-    weights, out = refs[:count], refs[count]
+def project_kernel(count, normed, cosine, sine, bias, *refs):
+    weights, (qkv, hidden, stacked) = refs[:count], refs[count:]
+    tile = pl.program_id(0)
     tall = normed.shape[1] // count
-    total = bias[...] + jnp.dot(normed[:, :tall], weights[0][...], preferred_element_type=wide)
-    for k in range(1, count):
+    total = bias[...]
+    for k in range(count):
         block = normed[:, k * tall : (k + 1) * tall]
         total = total + jnp.dot(block, weights[k][...], preferred_element_type=wide)
-    out[...] = total
-
-
-def begin(normed, bias, weights, tall, head_width):
-    count = len(weights)
-    length = normed.shape[0]
-    inside = weights[0].shape[1]
-    return pl.pallas_call(
-        functools.partial(begin_kernel, count),
-        grid=(inside // head_width,),
-        in_specs=[
-            pl.BlockSpec((length, count * tall), lambda t: (0, 0)),
-            pl.BlockSpec((1, head_width), lambda t: (0, t)),
-        ]
-        + [pl.BlockSpec((tall, head_width), lambda t: (0, t))] * count,
-        out_specs=pl.BlockSpec((length, head_width), lambda t: (0, t)),
-        out_shape=jax.ShapeDtypeStruct((length, inside), wide),
-        cost_estimate=pl.CostEstimate(
-            flops=2 * length * count * tall * inside,
-            bytes_accessed=2 * (count * tall * inside + normed.size) + 4 * length * inside,
-            transcendentals=0,
-        ),
-        name="begin",
-    )(normed, bias, *weights)
-
-
-def project_kernel(normed, other, cosine, sine, begun, weights, others, qkv, hidden, stacked):
-    tile = pl.program_id(0)
-    total = begun[...] + jnp.dot(normed[...], weights[...], preferred_element_type=wide)
-    total = total + jnp.dot(other[...], others[...], preferred_element_type=wide)
     repeats = total.shape[1] // LANES
 
     @pl.when(tile < 2)
@@ -293,25 +300,22 @@
         stacked[...] = (total * gelu_parts(total)[0]).astype(low)
 
 
-def project(normed, cosine, sine, begun, halves, tall, head_width):
+def project(normed, cosine, sine, bias, weights, tall, head_width):
+    count = len(weights)
     length = normed.shape[0]
-    inside = begun.shape[1]
+    inside = weights[0].shape[1]
     units = inside - 3 * head_width
-    first = 2 * (normed.shape[1] // (2 * tall)) - 2
     table = pl.BlockSpec((length, LANES), lambda t: (0, 0))
-    weights, others = halves
-    return pl.pallas_call(
-        project_kernel,
+    return pl.pallas_call(
+        functools.partial(project_kernel, count),
         grid=(inside // head_width,),
         in_specs=[
-            pl.BlockSpec((length, tall), lambda t: (0, first)),
-            pl.BlockSpec((length, tall), lambda t: (0, first + 1)),
+            pl.BlockSpec((length, count * tall), lambda t: (0, 0)),
             table,
             table,
-            pl.BlockSpec((length, head_width), lambda t: (0, t)),
-            pl.BlockSpec((tall, head_width), lambda t: (0, t)),
-            pl.BlockSpec((tall, head_width), lambda t: (0, t)),
-        ],
+            pl.BlockSpec((1, head_width), lambda t: (0, t)),
+        ]
+        + [pl.BlockSpec((tall, head_width), lambda t: (0, t))] * count,
         out_specs=[
             pl.BlockSpec((length, head_width), lambda t: (0, jnp.minimum(t, 2))),
             pl.BlockSpec((length, head_width), lambda t: (0, jnp.maximum(t - 3, 0))),
@@ -323,12 +327,12 @@
             jax.ShapeDtypeStruct((length, head_width + units), low),
         ],
         cost_estimate=pl.CostEstimate(
-            flops=4 * length * tall * inside,
-            bytes_accessed=4 * tall * (inside + length) + 12 * length * inside,
+            flops=2 * length * count * tall * inside,
+            bytes_accessed=2 * count * tall * (inside + length) + 8 * length * inside,
             transcendentals=length * units,
         ),
         name="project",
-    )(normed, normed, cosine, sine, begun, weights, others)
+    )(normed, cosine, sine, bias, *weights)
 
 
 def emit_kernel(owners, counts, stacked, *refs):
@@ -621,32 +625,34 @@
 
 
 def widen_rows_kernel(head_width, a, b, down, out):
-    cut = a.shape[1]
+    cut = b.shape[1] - head_width
     out[...] = b[0, :head_width].astype(wide)
     down[:cut] = b[0, head_width:].astype(wide)
     down[cut:] = a[0].astype(wide)
 
 
 def widen_rows(all_a, all_b, head_width, width):
-    count, cut, depth = all_a.shape
-    assert head_width + cut == all_b.shape[1]
-    moved = 6 * count * depth * (head_width + 2 * cut)
+    count, rest, depth = all_a.shape
+    tall = all_b.shape[1]
+    units = rest + tall - head_width
     return pl.pallas_call(
         functools.partial(widen_rows_kernel, head_width),
         grid=(count,),
         in_specs=[
-            pl.BlockSpec((1, cut, depth), lambda j: (j, 0, 0)),
-            pl.BlockSpec((1, head_width + cut, depth), lambda j: (j, 0, 0)),
+            pl.BlockSpec((1, rest, depth), lambda j: (j, 0, 0)),
+            pl.BlockSpec((1, tall, depth), lambda j: (j, 0, 0)),
         ],
         out_specs=[
-            pl.BlockSpec((2 * cut, depth), lambda j: (j, 0)),
+            pl.BlockSpec((units, depth), lambda j: (j, 0)),
             pl.BlockSpec((head_width, depth), lambda j: (j, 0)),
         ],
         out_shape=[
-            jax.ShapeDtypeStruct((count * 2 * cut, depth), wide),
+            jax.ShapeDtypeStruct((count * units, depth), wide),
             jax.ShapeDtypeStruct((width, depth), wide),
         ],
-        cost_estimate=pl.CostEstimate(flops=0, bytes_accessed=moved, transcendentals=0),
+        cost_estimate=pl.CostEstimate(
+            flops=0, bytes_accessed=6 * count * depth * (rest + tall), transcendentals=0
+        ),
         name="widen_rows",
     )(all_a, all_b)
 
@@ -702,7 +708,6 @@
     units = up_weight.shape[1] // seq_count
     inside = three + units
     depth = qkv_weight.shape[0]
-    mask = valid[0].astype(wide)
 
     tall = depth // 2
     behind = head_width + units
@@ -815,29 +820,23 @@
     def piece(array, k):
         return array[:, k * depth : (k + 1) * depth]
 
-    flat_in = [item for pair in first_in for item in pair]
-    begun = begin(normed_all, b_in, flat_in, tall, head_width)
-    begun, cosine, sine = lax.optimization_barrier((begun, cosine, sine))
-    qkv, hidden, stacked = project(normed_all, cosine, sine, begun, last_in, tall, head_width)
+    flat_in = [item for pair in (*first_in, last_in) for item in pair]
+    qkv, hidden, stacked = project(normed_all, cosine, sine, b_in, flat_in, tall, head_width)
     stacked, logsum = attend(qkv, stacked)
 
     counted = [item[1] for item in (*first_in, last_in)]
     if data_count == 4:
-        back_sides = [tuple(after(item, qkv) for item in pair) for pair in back_sides]
+        back_sides = [tuple(after(item, stacked) for item in pair) for pair in back_sides]
         w_back = [w_back, *back_sides]
         w_back.append((swap(back_sides[0][0], "dp", 2), swap(back_sides[1][1], "dp", 1)))
     branches = emit(stacked, w_back[:-1], [], 0, data_count)
     branches = emit(stacked, w_back[-1:], counted, data_count - 1, data_count, branches)
-    branches = scatter_seq(branches)
-    digits = branches[0, width : width + 3]
-    count = digits[0] + DIGIT * digits[1] + DIGIT * DIGIT * digits[2]
-    error = base + branches[:, :width]
-    weighted = mask[:, None] * error
-    squares = jnp.sum(weighted * error)
-    grad_output = length * data_count / count * weighted
-    grad_all = gather_seq(grad_output.astype(low))
+    w_back = [jnp.concatenate(pair, axis=0) for pair in w_back]
+    branches, *w_back = lax.optimization_barrier((scatter_seq(branches), *w_back))
+    grad_output, grad_low, sums = grade(branches, base, valid, float(length * data_count))
+    squares, count = sums[0, 0], sums[1, 0]
+    grad_all = gather_seq(grad_low)
     branch_bias_grad = jnp.sum(grad_all.astype(wide), axis=0)
-    w_back = [jnp.concatenate(pair, axis=0) for pair in w_back]
 
     def owned(left, right):
         return dot(left, right, ((0,), (0,)))
@@ -845,7 +844,7 @@
     def gather(array):
         return lax.all_gather(array, "seq", axis=0, tiled=False)
 
-    cut = units // 2
+    cut = units * 5 // 8
 
     def of_stacked(first, last):
         return [owned(stacked[:, first:last], piece(grad_all, k)) for k in range(data_count)]
@@ -868,23 +867,19 @@
 
     own_a, sent_a = prepare(of_stacked(head_width + cut, head_width + units))
     own_b, sent_b = prepare(of_stacked(0, head_width + cut))
-    head_grad, in_low = reject(grad_all, w_back, hidden, head_width)
-    got, ((own_b, sent_b), head_grad, in_low) = send(
-        sent_a, (own_b, sent_b), head_grad, in_low
-    )
+    got, ((own_b, sent_b),) = send(sent_a, (own_b, sent_b))
     down_a = total(own_a, got)
     all_a = gather(down_a)
-    own_up, sent_up = prepare(of_normed(in_low[:, three:]))
-    got, ((own_up, sent_up), head_grad) = send(sent_b, (own_up, sent_up), head_grad)
+    head_grad, in_low = reject(after(grad_all, down_a), w_back, hidden, head_width)
+    in_low = attend_back(qkv, head_grad, logsum, cosine, sine, in_low)
+    got, (in_low,) = send(sent_b, in_low)
     down_b = total(own_b, got)
     all_b = gather(down_b)
-    head_grad = after(head_grad, down_b)
-    in_low = attend_back(qkv, head_grad, logsum, cosine, sine, in_low)
-    own_qkv, sent_qkv = prepare(of_normed(in_low[:, :three]))
-    kept, sent = answer(in_low, [*flat_in, *last_in], part, seq_count // 2, tall)
-    got, ((own_qkv, sent_qkv), kept, sent, all_a) = send(
-        sent_up, (own_qkv, sent_qkv), kept, sent, all_a
-    )
+    in_low = after(in_low, down_b)
+    own_up, sent_up = prepare(of_normed(in_low[:, three:]))
+    own_qkv, sent_qkv = prepare(of_normed(after(in_low[:, :three], *sent_up)))
+    kept, sent = answer(in_low, flat_in, part, seq_count // 2, tall)
+    got, ((own_qkv, sent_qkv), kept, all_a) = send(sent_up, (own_qkv, sent_qkv), kept, all_a)
     up_grad = total(own_up, got)
     all_up = gather(up_grad)
     summed = scatter_blocks(kept, sent)

time: 597 us -> 592 us (level)
  waiting for transfers between devices: 283 us -> 290 us
  matrix products: 41.4 us -> 35.4 us
    ppermute x27 -> x28, waiting for transfers between devices: 76.4 us -> 93.7 us  [swap(): lax.ppermute(array, axis, [(s, s ^ bit) for s in range(lax.axis_size(axis...]
    ppermute x5, waiting for transfers between devices: 68.1 us -> 60.3 us  [between(): lax.ppermute(array, 'seq', [(2 * a + core, 2 * b + core) for a, b in pair...]
    all_gather x2, waiting for transfers between devices: 37.8 us -> 45.4 us  [gather_seq(): return lax.all_gather(rows, 'seq', axis=0, tiled=True)]
    reduce_scatter x1, waiting for transfers between devices: 52.2 us -> 44.8 us  [scatter_seq(): return lax.psum_scatter(partial, 'seq', scatter_dimension=0, tiled=True)]
    dot_general x16, matrix products: 41.4 us -> 35.4 us  [dot(): return lax.dot_general(a, b, (dims, ((), ())), preferred_element_type=wide)]
    ppermute x27 -> x28, starting transfers between devices: 32.9 us -> 33.5 us  [swap(): lax.ppermute(array, axis, [(s, s ^ bit) for s in range(lax.axis_size(axis...]
  transfers between devices with their start and end apart: 39 -> 40, of which waited for: 18 -> 21; matrix products, arithmetic and copies ran while one was open for 11% -> 12% of each run, Pallas kernels for 20% -> 19%
where the time goes in v4:
time: 592 us; the launch traced here: 581 us
  waiting for transfers between devices  290 us (49%)
  Pallas kernels  136 us (23%)
  starting transfers between devices  58.8 us (10%)
  matrix products  35.4 us (6%)
  other arithmetic  31.4 us (5%)
  between operations  17.2 us (3%)
  local copies, waits for them, and re-layouts  12.2 us (2%)
    ppermute x28, waiting for transfers between devices, swap(): lax.ppermute(array, axis, [(s, s ^ bit) for s in range(lax.axis_size(axis...  93.7 us
    ppermute x5, waiting for transfers between devices, between(): lax.ppermute(array, 'seq', [(2 * a + core, 2 * b + core) for a, b in pair...  60.3 us
    all_gather x4, waiting for transfers between devices, gather(): return lax.all_gather(array, 'seq', axis=0, tiled=False)  46.1 us
    all_gather x2, waiting for transfers between devices, gather_seq(): return lax.all_gather(rows, 'seq', axis=0, tiled=True)  45.4 us
    reduce_scatter x1, waiting for transfers between devices, scatter_seq(): return lax.psum_scatter(partial, 'seq', scatter_dimension=0, tiled=True)  44.8 us
    dot_general x16, matrix products, dot(): return lax.dot_general(a, b, (dims, ((), ())), preferred_element_type=wide)  35.4 us
    ppermute x28, starting transfers between devices, swap(): lax.ppermute(array, axis, [(s, s ^ bit) for s in range(lax.axis_size(axis...  33.5 us
    ppermute x5, starting transfers between devices, between(): lax.ppermute(array, 'seq', [(2 * a + core, 2 * b + core) for a, b in pair...  25 us
  transfers between devices with their start and end apart: 40, of which 21 were waited for; matrix products, arithmetic and copies ran while one was open for 12% of the time, Pallas kernels for 19%

profile of v4, /device:TPU:0, one launch (start us, length us, event | category | flops | bytes accessed | tf_op | source)
XLA Modules:
  0.0 581.4 jit_solution(12338349661472680372)
XLA Ops:
  7.2 3.6 pick.2
  10.8 3.0 enter.1
  13.9 3.0 collective-permute-start.3
  18.4 20.3 %collective-permute-done.3.refs_5_.refs_2_ = bf16[272,1792]{1,0:T(8,128)(2,1)S(1)} collective-permute-done((bf16[272,1792]{1,0:T(8,128)(2,1)}, bf16[272,1792]{1,0:T(8,128)(2,1)S(1)}, u32[]{:S(2)}, u32[]{:S(2)}) %collective-permute-start.3) | collective-permute-done | bytes 974880 | tf_op jit(solution)/shard_map/ppermute | solution.py:37
  44.3 3.1 pick.3
  48.0 16.1 %collective-permute-done.4.refs_6_ = bf16[256,1792]{1,0:T(8,128)(2,1)} collective-permute-done((bf16[256,1792]{1,0:T(8,128)(2,1)}, bf16[256,1792]{1,0:T(8,128)(2,1)}, u32[]{:S(2)}, u32[]{:S(2)}) %collective-permute-start.4) | collective-permute-done | bytes 917536 | tf_op jit(solution)/shard_map/ppermute | solution.py:37
  69.0 3.1 fusion.30
  72.1 11.5 %collective-permute-done.2.refs_4_ = bf16[256,1792]{1,0:T(8,128)(2,1)} collective-permute-done((bf16[256,1792]{1,0:T(8,128)(2,1)}, bf16[256,1792]{1,0:T(8,128)(2,1)}, u32[]{:S(2)}, u32[]{:S(2)}) %collective-permute-start.2) | collective-permute-done | bytes 917536 | tf_op jit(solution)/shard_map/ppermute | solution.py:37
  86.2 16.9 %project.1 = (bf16[1024,768]{1,0:T(8,128)(2,1)}, f32[1024,1024]{1,0:T(8,128)}, bf16[1024,1280]{1,0:T(8,128)(2,1)}) custom-call(bf16[1024,2176]{1,0:T(8,128)(2,1)} %all-gather.11.cloned.1.call-done.normed, f32[1024,128]{1,0:T(8,128)} %get-tuple-element.156.cosine, f32[1024,128]{1,0:T(8,128)} %get-tuple-element.155.sine, f32[1,1792]{1,0:T(1,128)} %maximum_convert_fusion.bias, ...), custom_call_target="tpu_custom_call" | custom-call | flops 7516192768 | bytes 26214400 | tf_op jit(solution)/shard_map/project/pallas_call | solution.py:309
  103.0 10.1 %attend.1 = (bf16[1024,1280]{1,0:T(8,128)(2,1)}, f32[1024,128]{1,0:T(8,128)}) custom-call(bf16[1024,768]{1,0:T(8,128)(2,1)} %get-tuple-element.83.qkv, bf16[1024,1280]{1,0:T(8,128)(2,1)} %get-tuple-element.84.stacked), custom_call_target="tpu_custom_call", output_to_operand_aliasing={{0}: (1, {})} | custom-call | flops 2147483648 | bytes 6291456 | tf_op jit(solution)/shard_map/attend/pallas_call | solution.py:437
  115.4 10.1 %emit.2.refs_6_ = bf16[1024,2176]{1,0:T(8,128)(2,1)} custom-call(bf16[1024,1280]{1,0:T(8,128)(2,1)} %get-tuple-element.85.stacked, bf16[640,512]{1,0:T(8,128)(2,1)} %get-tuple-element.89.refs_0_, bf16[640,512]{1,0:T(8,128)(2,1)} %get-tuple-element.91.refs_1_, bf16[640,512]{1,0:T(8,128)(2,1)} %collective-permute-done.6.refs_2_, ...), custom_call_target="tpu_custom_call" | custom-call | flops 4026531840 | bytes 9699328 | tf_op jit(solution)/shard_map/emit/pallas_call | solution.py:386
  127.6 4.9 emit.3
  134.9 2.6 pad_maximum_fusion.1.refs_1_
  137.6 2.4 pad_maximum_fusion.2.refs_2_
  141.2 44.8 %reduce-scatter.2.cloned.1.call-done.branches = bf16[128,2176]{1,0:T(8,128)(2,1)} async-done(((bf16[1024,2176]{1,0:T(8,128)(2,1)}), bf16[128,2176]{1,0:T(8,128)(2,1)}) %reduce-scatter.2.cloned.1.call-update) | async-done | bytes 557072 | tf_op jit(solution)/shard_map/reduce_scatter | solution.py:77
  186.0 3.0 grade.1
  189.0 45.4 %all-gather.13.cloned.1.call-done.grads = bf16[1024,2048]{1,0:T(8,128)(2,1)} async-done(((bf16[128,2048]{1,0:T(8,128)(2,1)}), bf16[1024,2048]{1,0:T(8,128)(2,1)}) %all-gather.13.cloned.1.call-update) | async-done | bytes 4194320 | tf_op jit(solution)/shard_map/all_gather | solution.py:41
  244.7 2.1 convolution_convert_fusion.4
  246.7 2.4 fusion.8
  251.2 8.1 %collective-permute-done.13 = bf16[384,512]{1,0:T(8,128)(2,1)S(1)} collective-permute-done((bf16[384,512]{1,0:T(8,128)(2,1)S(1)}, bf16[384,512]{1,0:T(8,128)(2,1)S(1)}, u32[]{:S(2)}, u32[]{:S(2)}) %collective-permute-start.13) | collective-permute-done | bytes 393248 | tf_op jit(solution)/shard_map/ppermute | solution.py:37
  264.3 13.9 %reject.1 = (bf16[1024,256]{1,0:T(8,128)(2,1)}, bf16[1024,1792]{1,0:T(8,128)(2,1)}) custom-call(f32[1024,1024]{1,0:T(8,128)} %get-tuple-element.101.hidden, bf16[1024,2048]{1,0:T(8,128)(2,1)} %all-gather.13.cloned.1.call-done.grads, bf16[1280,512]{1,0:T(8,128)(2,1)} %pad_maximum_fusion.refs_0_, bf16[1280,512]{1,0:T(8,128)(2,1)} %pad_maximum_fusion.1.refs_1_, ...), custom_call_target="tpu_custom_call" | custom-call | flops 5368709120 | bytes 19922944 | tf_op jit(solution)/shard_map/reject/pallas_call | solution.py:557
  278.2 16.9 %attend_back.1.entered = bf16[1024,1792]{1,0:T(8,128)(2,1)} custom-call(bf16[1024,768]{1,0:T(8,128)(2,1)} %get-tuple-element.83.qkv, bf16[1024,256]{1,0:T(8,128)(2,1)} %get-tuple-element.110.grad, f32[1024,128]{1,0:T(8,128)} %get-tuple-element.111.logsum, f32[1024,128]{1,0:T(8,128)} %get-tuple-element.156.cosine, ...), custom_call_target="tpu_custom_call", output_to_operand_aliasing={{}: (5, {})} | custom-call | flops 5368709120 | bytes 6291456 | tf_op jit(solution)/shard_map/attend_back/pallas_call | solution.py:511
  295.1 6.4 %collective-permute-done.16 = bf16[896,512]{1,0:T(8,128)(2,1)} collective-permute-done((bf16[896,512]{1,0:T(8,128)(2,1)}, bf16[896,512]{1,0:T(8,128)(2,1)}, u32[]{:S(2)}, u32[]{:S(2)}) %collective-permute-start.16) | collective-permute-done | bytes 917536 | tf_op jit(solution)/shard_map/ppermute | solution.py:37
  303.1 2.9 add_convert_fusion.1
  307.7 4.4 convolution_convert_fusion.2
  312.9 3.8 convolution_convert_fusion
  317.9 3.5 convolution_convert_fusion.1
  329.7 2.2 fusion.13
  331.9 15.6 %answer.1 = (f32[512,2048]{1,0:T(8,128)}, bf16[512,2048]{1,0:T(8,128)(2,1)}) custom-call(s32[1]{0:T(128)} %bitcast.part, bf16[1024,1792]{1,0:T(8,128)(2,1)} %attend_back.1.entered, bf16[256,1792]{1,0:T(8,128)(2,1)} %get-tuple-element.79.refs_0_, bf16[272,1792]{1,0:T(8,128)(2,1)} %get-tuple-element.80.refs_1_.refs_0_, ...), custom_call_target="tpu_custom_call" | custom-call | flops 7516192768 | bytes 17301504 | tf_op jit(solution)/shard_map/answer/pallas_call | solution.py:604
  347.5 10.7 %collective-permute-done.20 = bf16[512,1024]{1,0:T(8,128)(2,1)} collective-permute-done((bf16[512,1024]{1,0:T(8,128)(2,1)}, bf16[512,1024]{1,0:T(8,128)(2,1)}, u32[]{:S(2)}, u32[]{:S(2)}) %collective-permute-start.20) | collective-permute-done | bytes 1048608 | tf_op jit(solution)/shard_map/ppermute | solution.py:37
  358.2 8.3 %collective-permute-done.19 = bf16[512,1024]{1,0:T(8,128)(2,1)} collective-permute-done((bf16[512,1024]{1,0:T(8,128)(2,1)}, bf16[512,1024]{1,0:T(8,128)(2,1)}, u32[]{:S(2)}, u32[]{:S(2)}) %collective-permute-start.19) | collective-permute-done | bytes 1048608 | tf_op jit(solution)/shard_map/ppermute | solution.py:37
  366.5 3.3 add_convert_fusion
  369.9 4.4 collective-permute-done.24
  374.3 2.8 convert_add_fusion
  377.2 2.1 collective-permute-start.25
  379.3 16.4 %collective-permute-done.25 = bf16[128,2048]{1,0:T(8,128)(2,1)S(1)} collective-permute-done((bf16[128,2048]{1,0:T(8,128)(2,1)S(1)}, bf16[128,2048]{1,0:T(8,128)(2,1)S(1)}, u32[]{:S(2)}, u32[]{:S(2)}) %collective-permute-start.25) | collective-permute-done | bytes 524320 | tf_op jit(solution)/shard_map/ppermute | solution.py:45
  396.6 5.0 collective-permute-start.26
  403.1 21.2 %collective-permute-done.26 = bf16[128,2048]{1,0:T(8,128)(2,1)S(1)} collective-permute-done((bf16[128,2048]{1,0:T(8,128)(2,1)S(1)}, bf16[128,2048]{1,0:T(8,128)(2,1)S(1)}, u32[]{:S(2)}, u32[]{:S(2)}) %collective-permute-start.26) | collective-permute-done | bytes 524320 | tf_op jit(solution)/shard_map/ppermute | solution.py:45
  426.1 15.7 %collective-permute-start.27 = (bf16[128,2048]{1,0:T(8,128)(2,1)S(1)}, bf16[128,2048]{1,0:T(8,128)(2,1)S(1)}, u32[]{:S(2)}, u32[]{:S(2)}) collective-permute-start(bf16[128,2048]{1,0:T(8,128)(2,1)S(1)} %get-tuple-element.146), channel_id=1, source_target_pairs={{0,2},{1,3},{2,4},{3,5},{4,6},{5,7},{8,10},{9,11},{10,12},{11,13},... | collective-permute-start | bytes 1572872 | tf_op jit(solution)/shard_map/ppermute | solution.py:45
  448.6 15.0 %collective-permute-done.27 = bf16[128,2048]{1,0:T(8,128)(2,1)S(1)} collective-permute-done((bf16[128,2048]{1,0:T(8,128)(2,1)S(1)}, bf16[128,2048]{1,0:T(8,128)(2,1)S(1)}, u32[]{:S(2)}, u32[]{:S(2)}) %collective-permute-start.27) | collective-permute-done | bytes 524320 | tf_op jit(solution)/shard_map/ppermute | solution.py:45
  463.6 7.6 %collective-permute-done.29 = bf16[128,2048]{1,0:T(8,128)(2,1)S(1)} collective-permute-done((bf16[128,2048]{1,0:T(8,128)(2,1)S(1)}, bf16[128,2048]{1,0:T(8,128)(2,1)S(1)}, u32[]{:S(2)}, u32[]{:S(2)}) %collective-permute-start.29) | collective-permute-done | bytes 524320 | tf_op jit(solution)/shard_map/ppermute | solution.py:45
  471.2 2.4 fusion.11.summed
  473.6 4.1 collective-permute-done.23
  477.7 3.7 leave.1
  491.1 12.2 %widen_rows.1 = (f32[8192,512]{1,0:T(8,128)}, f32[2048,512]{1,0:T(8,128)}) custom-call(bf16[8,384,512]{2,1,0:T(8,128)(2,1)} %bitcast.39, bf16[8,896,512]{2,1,0:T(8,128)(2,1)} %bitcast.36), custom_call_target="tpu_custom_call" | custom-call | bytes 31457280 | tf_op jit(solution)/shard_map/widen_rows/pallas_call | solution.py:638
  503.3 10.3 %widen_columns.2 = f32[512,8192]{1,0:T(8,128)} custom-call(bf16[8,512,1024]{2,1,0:T(8,128)(2,1)} %bitcast.35), custom_call_target="tpu_custom_call" | custom-call | bytes 25165824 | tf_op jit(solution)/shard_map/widen_columns/pallas_call | solution.py:673
  513.6 46.1 %all-gather.21.cloned.1.call-done = bf16[4224,768]{1,0:T(8,128)(2,1)} async-done(((bf16[528,768]{1,0:T(8,128)(2,1)}), bf16[4224,768]{1,0:T(8,128)(2,1)}) %all-gather.21.cloned.1.call-update) | async-done | bytes 6488080 | tf_op jit(solution)/shard_map/all_gather | solution.py:845
  561.9 8.8 %widen_columns.3 = f32[512,6144]{1,0:T(8,128)} custom-call(bf16[8,528,768]{2,1,0:T(8,128)(2,1)} %bitcast.38), custom_call_target="tpu_custom_call" | custom-call | bytes 18874368 | tf_op jit(solution)/shard_map/widen_columns/pallas_call | solution.py:673
  (160 shorter events, 78.3 us)
Async XLA Ops:
  7.2 60.5 %all-gather.11.cloned.1.call-start = ((), (), s32[]{:S(2)}) async-start(), calls=%async_computation.1 | async-start | bytes 5013504 | tf_op jit(solution)/shard_map/all_gather | solution.py:41
  13.8 172.2 %reduce-scatter.2.cloned.1.call-start = ((), (), s32[]{:S(2)}) async-start(), calls=%async_computation.2 | async-start | bytes 5013504 | tf_op jit(solution)/shard_map/reduce_scatter | solution.py:77
  13.9 24.8 %collective-permute-start.3 = (bf16[272,1792]{1,0:T(8,128)(2,1)}, bf16[272,1792]{1,0:T(8,128)(2,1)S(1)}, u32[]{:S(2)}, u32[]{:S(2)}) collective-permute-start(bf16[272,1792]{1,0:T(8,128)(2,1)} %get-tuple-element.80.refs_1_.refs_0_), channel_id=1, source_target_pairs={{0,16},{8,24},{16,0},{24,8},{1,17},{9,25},{17,1},{25,9},{2,18},{10... | collective-permute-start | bytes 2924552 | tf_op jit(solution)/shard_map/ppermute | solution.py:37
  16.9 23.5 %collective-permute-start = (bf16[256,1792]{1,0:T(8,128)(2,1)}, bf16[256,1792]{1,0:T(8,128)(2,1)}, u32[]{:S(2)}, u32[]{:S(2)}) collective-permute-start(bf16[256,1792]{1,0:T(8,128)(2,1)} %get-tuple-element.79.refs_0_), channel_id=1, source_target_pairs={{0,8},{8,0},{16,24},{24,16},{1,9},{9,1},{17,25},{25,17},{2,10},{10... | collective-permute-start | bytes 2752520 | tf_op jit(solution)/shard_map/ppermute | solution.py:37
  38.7 25.3 %collective-permute-start.5 = (bf16[272,1792]{1,0:T(8,128)(2,1)S(1)}, bf16[272,1792]{1,0:T(8,128)(2,1)S(1)}, u32[]{:S(2)}, u32[]{:S(2)}) collective-permute-start(bf16[272,1792]{1,0:T(8,128)(2,1)S(1)} %collective-permute-done.3.refs_5_.refs_2_), channel_id=1, source_target_pairs={{0,8},{8,0},{16,24},{24,16},{1,9},{9,1},{17,25},{25,17},{2,10},{10... | collective-permute-start | bytes 2924552 | tf_op jit(solution)/shard_map/ppermute | solution.py:37
  40.4 23.6 %collective-permute-start.4 = (bf16[256,1792]{1,0:T(8,128)(2,1)}, bf16[256,1792]{1,0:T(8,128)(2,1)}, u32[]{:S(2)}, u32[]{:S(2)}) collective-permute-start(bf16[256,1792]{1,0:T(8,128)(2,1)} %collective-permute-done.refs_2_), channel_id=1, source_target_pairs={{0,16},{8,24},{16,0},{24,8},{1,17},{9,25},{17,1},{25,9},{2,18},{10... | collective-permute-start | bytes 2752520 | tf_op jit(solution)/shard_map/ppermute | solution.py:37
  41.9 41.7 %collective-permute-start.2 = (bf16[256,1792]{1,0:T(8,128)(2,1)}, bf16[256,1792]{1,0:T(8,128)(2,1)}, u32[]{:S(2)}, u32[]{:S(2)}) collective-permute-start(bf16[256,1792]{1,0:T(8,128)(2,1)} %get-tuple-element.79.refs_0_), channel_id=1, source_target_pairs={{0,16},{8,24},{16,0},{24,8},{1,17},{9,25},{17,1},{25,9},{2,18},{10... | collective-permute-start | bytes 2752520 | tf_op jit(solution)/shard_map/ppermute | solution.py:37
  42.4 42.8 %collective-permute-start.1 = (bf16[272,1792]{1,0:T(8,128)(2,1)}, bf16[272,1792]{1,0:T(8,128)(2,1)S(1)}, u32[]{:S(2)}, u32[]{:S(2)}) collective-permute-start(bf16[272,1792]{1,0:T(8,128)(2,1)} %get-tuple-element.80.refs_1_.refs_0_), channel_id=1, source_target_pairs={{0,8},{8,0},{16,24},{24,16},{1,9},{9,1},{17,25},{25,17},{2,10},{10... | collective-permute-start | bytes 2924552 | tf_op jit(solution)/shard_map/ppermute | solution.py:37
  64.0 21.2 %copy-start.13 = (bf16[272,1792]{1,0:T(8,128)(2,1)}, bf16[272,1792]{1,0:T(8,128)(2,1)S(1)}, u32[]{:S(2)}) copy-start(bf16[272,1792]{1,0:T(8,128)(2,1)S(1)} %collective-permute-done.5.refs_7_.refs_3_) | copy-start | bytes 2924548
  64.0 19.7 %copy-start.16 = (bf16[640,512]{1,0:T(8,128)(2,1)S(1)}, bf16[640,512]{1,0:T(8,128)(2,1)}, u32[]{:S(2)}) copy-start(bf16[640,512]{1,0:T(8,128)(2,1)} %get-tuple-element.91.refs_1_) | copy-start | bytes 1966084
  64.0 51.4 %collective-permute-start.11 = (bf16[640,512]{1,0:T(8,128)(2,1)}, bf16[640,512]{1,0:T(8,128)(2,1)}, u32[]{:S(2)}, u32[]{:S(2)}) collective-permute-start(bf16[640,512]{1,0:T(8,128)(2,1)} %get-tuple-element.89.refs_0_), channel_id=1, source_target_pairs={{0,16},{8,24},{16,0},{24,8},{1,17},{9,25},{17,1},{25,9},{2,18},{10... | collective-permute-start | bytes 1966088 | tf_op jit(solution)/shard_map/ppermute | solution.py:37
  65.6 47.6 %collective-permute-start.6 = (bf16[640,512]{1,0:T(8,128)(2,1)}, bf16[640,512]{1,0:T(8,128)(2,1)}, u32[]{:S(2)}, u32[]{:S(2)}) collective-permute-start(bf16[640,512]{1,0:T(8,128)(2,1)} %get-tuple-element.89.refs_0_), channel_id=1, source_target_pairs={{0,8},{8,0},{16,24},{24,16},{1,9},{9,1},{17,25},{25,17},{2,10},{10... | collective-permute-start | bytes 1966088 | tf_op jit(solution)/shard_map/ppermute | solution.py:37
  66.4 48.9 %collective-permute-start.10 = (bf16[640,512]{1,0:T(8,128)(2,1)}, bf16[640,512]{1,0:T(8,128)(2,1)}, u32[]{:S(2)}, u32[]{:S(2)}) collective-permute-start(bf16[640,512]{1,0:T(8,128)(2,1)} %get-tuple-element.91.refs_1_), channel_id=1, source_target_pairs={{0,8},{8,0},{16,24},{24,16},{1,9},{9,1},{17,25},{25,17},{2,10},{10... | collective-permute-start | bytes 1966088 | tf_op jit(solution)/shard_map/ppermute | solution.py:37
  83.7 29.5 %collective-permute-start.8 = (bf16[640,512]{1,0:T(8,128)(2,1)S(1)}, bf16[640,512]{1,0:T(8,128)(2,1)}, u32[]{:S(2)}, u32[]{:S(2)}) collective-permute-start(bf16[640,512]{1,0:T(8,128)(2,1)S(1)} %copy-done.16), channel_id=1, source_target_pairs={{0,16},{8,24},{16,0},{24,8},{1,17},{9,25},{17,1},{25,9},{2,18},{10... | collective-permute-start | bytes 1966088 | tf_op jit(solution)/shard_map/ppermute | solution.py:37
  113.2 12.7 %collective-permute-start.7 = (bf16[640,512]{1,0:T(8,128)(2,1)}, bf16[640,512]{1,0:T(8,128)(2,1)S(1)}, u32[]{:S(2)}, u32[]{:S(2)}) collective-permute-start(bf16[640,512]{1,0:T(8,128)(2,1)} %collective-permute-done.6.refs_2_), channel_id=1, source_target_pairs={{0,16},{8,24},{16,0},{24,8},{1,17},{9,25},{17,1},{25,9},{2,18},{10... | collective-permute-start | bytes 1966088 | tf_op jit(solution)/shard_map/ppermute | solution.py:37
  113.9 12.9 %collective-permute-start.9 = (bf16[640,512]{1,0:T(8,128)(2,1)}, bf16[640,512]{1,0:T(8,128)(2,1)S(1)}, u32[]{:S(2)}, u32[]{:S(2)}) collective-permute-start(bf16[640,512]{1,0:T(8,128)(2,1)} %collective-permute-done.8.refs_5_), channel_id=1, source_target_pairs={{0,8},{8,0},{16,24},{24,16},{1,9},{9,1},{17,25},{25,17},{2,10},{10... | collective-permute-start | bytes 1966088 | tf_op jit(solution)/shard_map/ppermute | solution.py:37
  132.5 101.9 %all-gather.13.cloned.1.call-start = ((), (), s32[]{:S(2)}) async-start(), calls=%async_computation.3 | async-start | bytes 4718592 | tf_op jit(solution)/shard_map/all_gather | solution.py:41
  140.0 94.5 %copy-start.9 = (bf16[1024,1280]{1,0:T(8,128)(2,1)S(1)}, bf16[1024,1280]{1,0:T(8,128)(2,1)}, u32[]{:S(2)}) copy-start(bf16[1024,1280]{1,0:T(8,128)(2,1)} %get-tuple-element.85.stacked) | copy-start | bytes 7864324
  189.0 177.5 %all-gather.15.cloned.1.call-start = ((), (), s32[]{:S(2)}) async-start(), calls=%async_computation.4 | async-start | bytes 3538944 | tf_op jit(solution)/shard_map/all_gather | solution.py:845
  236.5 14.7 %collective-permute-start.12 = (bf16[384,512]{1,0:T(8,128)(2,1)S(1)}, bf16[384,512]{1,0:T(8,128)(2,1)S(1)}, u32[]{:S(2)}, u32[]{:S(2)}) collective-permute-start(bf16[384,512]{1,0:T(8,128)(2,1)S(1)} %convolution_convert_fusion.11), channel_id=1, source_target_pairs={{0,8},{8,0},{16,24},{24,16},{1,9},{9,1},{17,25},{25,17},{2,10},{10... | collective-permute-start | bytes 1179656 | tf_op jit(solution)/shard_map/ppermute | solution.py:37
  239.8 19.5 %collective-permute-start.13 = (bf16[384,512]{1,0:T(8,128)(2,1)S(1)}, bf16[384,512]{1,0:T(8,128)(2,1)S(1)}, u32[]{:S(2)}, u32[]{:S(2)}) collective-permute-start(bf16[384,512]{1,0:T(8,128)(2,1)S(1)} %convolution_convert_fusion.10), channel_id=1, source_target_pairs={{0,16},{8,24},{16,0},{24,8},{1,17},{9,25},{17,1},{25,9},{2,18},{10... | collective-permute-start | bytes 1179656 | tf_op jit(solution)/shard_map/ppermute | solution.py:37
  242.0 17.3 %collective-permute-start.14 = (bf16[384,512]{1,0:T(8,128)(2,1)S(1)}, bf16[384,512]{1,0:T(8,128)(2,1)S(1)}, u32[]{:S(2)}, u32[]{:S(2)}) collective-permute-start(bf16[384,512]{1,0:T(8,128)(2,1)S(1)} %convolution_convert_fusion.9), channel_id=1, source_target_pairs={{0,24},{8,16},{16,8},{24,0},{1,25},{9,17},{17,9},{25,1},{2,26},{10... | collective-permute-start | bytes 1179656 | tf_op jit(solution)/shard_map/ppermute | solution.py:37
  260.7 216.9 %all-gather.17.cloned.1.call-start = ((), (), s32[]{:S(2)}) async-start(), calls=%async_computation.5 | async-start | bytes 8257536 | tf_op jit(solution)/shard_map/all_gather | solution.py:845
  260.8 34.4 %collective-permute-start.15 = (bf16[896,512]{1,0:T(8,128)(2,1)}, bf16[896,512]{1,0:T(8,128)(2,1)S(1)}, u32[]{:S(2)}, u32[]{:S(2)}) collective-permute-start(bf16[896,512]{1,0:T(8,128)(2,1)} %convolution_convert_fusion.5), channel_id=1, source_target_pairs={{0,8},{8,0},{16,24},{24,16},{1,9},{9,1},{17,25},{25,17},{2,10},{10... | collective-permute-start | bytes 2752520 | tf_op jit(solution)/shard_map/ppermute | solution.py:37
  261.4 40.1 %collective-permute-start.16 = (bf16[896,512]{1,0:T(8,128)(2,1)}, bf16[896,512]{1,0:T(8,128)(2,1)}, u32[]{:S(2)}, u32[]{:S(2)}) collective-permute-start(bf16[896,512]{1,0:T(8,128)(2,1)} %convolution_convert_fusion.4), channel_id=1, source_target_pairs={{0,16},{8,24},{16,0},{24,8},{1,17},{9,25},{17,1},{25,9},{2,18},{10... | collective-permute-start | bytes 2752520 | tf_op jit(solution)/shard_map/ppermute | solution.py:37
  262.9 40.2 %collective-permute-start.17 = (bf16[896,512]{1,0:T(8,128)(2,1)}, bf16[896,512]{1,0:T(8,128)(2,1)}, u32[]{:S(2)}, u32[]{:S(2)}) collective-permute-start(bf16[896,512]{1,0:T(8,128)(2,1)} %convolution_convert_fusion.3), channel_id=1, source_target_pairs={{0,24},{8,16},{16,8},{24,0},{1,25},{9,17},{17,9},{25,1},{2,26},{10... | collective-permute-start | bytes 2752520 | tf_op jit(solution)/shard_map/ppermute | solution.py:37
  278.2 24.9 %copy-start.10 = (f32[896,512]{1,0:T(8,128)S(1)}, f32[896,512]{1,0:T(8,128)}, u32[]{:S(2)}) copy-start(f32[896,512]{1,0:T(8,128)} %fusion.8) | copy-start | bytes 5505028
  306.1 184.3 %all-gather.19.cloned.1.call-start = ((), (), s32[]{:S(2)}) async-start(), calls=%async_computation.6 | async-start | bytes 9437184 | tf_op jit(solution)/shard_map/all_gather | solution.py:845
  312.0 35.5 %collective-permute-start.18 = (bf16[512,1024]{1,0:T(8,128)(2,1)}, bf16[512,1024]{1,0:T(8,128)(2,1)S(1)}, u32[]{:S(2)}, u32[]{:S(2)}) collective-permute-start(bf16[512,1024]{1,0:T(8,128)(2,1)} %convolution_convert_fusion.2), channel_id=1, source_target_pairs={{0,8},{8,0},{16,24},{24,16},{1,9},{9,1},{17,25},{25,17},{2,10},{10... | collective-permute-start | bytes 3145736 | tf_op jit(solution)/shard_map/ppermute | solution.py:37
  316.6 41.5 %collective-permute-start.20 = (bf16[512,1024]{1,0:T(8,128)(2,1)}, bf16[512,1024]{1,0:T(8,128)(2,1)}, u32[]{:S(2)}, u32[]{:S(2)}) collective-permute-start(bf16[512,1024]{1,0:T(8,128)(2,1)} %convolution_convert_fusion), channel_id=1, source_target_pairs={{0,24},{8,16},{16,8},{24,0},{1,25},{9,17},{17,9},{25,1},{2,26},{10... | collective-permute-start | bytes 3145736 | tf_op jit(solution)/shard_map/ppermute | solution.py:37
  321.4 45.1 %collective-permute-start.19 = (bf16[512,1024]{1,0:T(8,128)(2,1)}, bf16[512,1024]{1,0:T(8,128)(2,1)}, u32[]{:S(2)}, u32[]{:S(2)}) collective-permute-start(bf16[512,1024]{1,0:T(8,128)(2,1)} %convolution_convert_fusion.1), channel_id=1, source_target_pairs={{0,16},{8,24},{16,0},{24,8},{1,17},{9,25},{17,1},{25,9},{2,18},{10... | collective-permute-start | bytes 3145736 | tf_op jit(solution)/shard_map/ppermute | solution.py:37
  369.8 189.9 %all-gather.21.cloned.1.call-start = ((), (), s32[]{:S(2)}) async-start(), calls=%async_computation.7 | async-start | bytes 7299072 | tf_op jit(solution)/shard_map/all_gather | solution.py:845
  369.8 4.4 collective-permute-start.24
  377.2 18.6 %collective-permute-start.25 = (bf16[128,2048]{1,0:T(8,128)(2,1)S(1)}, bf16[128,2048]{1,0:T(8,128)(2,1)S(1)}, u32[]{:S(2)}, u32[]{:S(2)}) collective-permute-start(bf16[128,2048]{1,0:T(8,128)(2,1)S(1)} %slice.263), channel_id=1, source_target_pairs={{0,2},{1,3},{6,4},{7,5},{8,10},{9,11},{14,12},{15,13},{16,18},{17,... | collective-permute-start | bytes 1572872 | tf_op jit(solution)/shard_map/ppermute | solution.py:45
  395.9 7.1 %collective-permute-start.28 = (bf16[128,2048]{1,0:T(8,128)(2,1)S(1)}, bf16[128,2048]{1,0:T(8,128)(2,1)S(1)}, u32[]{:S(2)}, u32[]{:S(2)}) collective-permute-start(bf16[128,2048]{1,0:T(8,128)(2,1)S(1)} %fusion.10), channel_id=1, source_target_pairs={{6,4},{7,5},{4,2},{5,3},{14,12},{15,13},{12,10},{13,11},{22,20},{2... | collective-permute-start | bytes 1572872 | tf_op jit(solution)/shard_map/ppermute | solution.py:45
  396.6 27.7 %collective-permute-start.26 = (bf16[128,2048]{1,0:T(8,128)(2,1)S(1)}, bf16[128,2048]{1,0:T(8,128)(2,1)S(1)}, u32[]{:S(2)}, u32[]{:S(2)}) collective-permute-start(bf16[128,2048]{1,0:T(8,128)(2,1)S(1)} %fusion.10), channel_id=1, source_target_pairs={{0,2},{1,3},{2,4},{3,5},{8,10},{9,11},{10,12},{11,13},{16,18},{17,... | collective-permute-start | bytes 1572872 | tf_op jit(solution)/shard_map/ppermute | solution.py:45
  401.7 41.7 %copy-start.4 = (bf16[1024,2048]{1,0:T(8,128)(2,1)S(1)}, bf16[1024,2048]{1,0:T(8,128)(2,1)}, u32[]{:S(2)}) copy-start(bf16[1024,2048]{1,0:T(8,128)(2,1)} %all-gather.13.cloned.1.call-done.grads) | copy-start | bytes 12582916
  426.1 21.9 %copy-start.2 = (bf16[1024,1792]{1,0:T(8,128)(2,1)S(1)}, bf16[1024,1792]{1,0:T(8,128)(2,1)}, u32[]{:S(2)}) copy-start(bf16[1024,1792]{1,0:T(8,128)(2,1)} %attend_back.1.entered) | copy-start | bytes 11010052
  426.1 37.4 %collective-permute-start.27 = (bf16[128,2048]{1,0:T(8,128)(2,1)S(1)}, bf16[128,2048]{1,0:T(8,128)(2,1)S(1)}, u32[]{:S(2)}, u32[]{:S(2)}) collective-permute-start(bf16[128,2048]{1,0:T(8,128)(2,1)S(1)} %get-tuple-element.146), channel_id=1, source_target_pairs={{0,2},{1,3},{2,4},{3,5},{4,6},{5,7},{8,10},{9,11},{10,12},{11,13},... | collective-permute-start | bytes 1572872 | tf_op jit(solution)/shard_map/ppermute | solution.py:45
  441.8 29.4 %collective-permute-start.29 = (bf16[128,2048]{1,0:T(8,128)(2,1)S(1)}, bf16[128,2048]{1,0:T(8,128)(2,1)S(1)}, u32[]{:S(2)}, u32[]{:S(2)}) collective-permute-start(bf16[128,2048]{1,0:T(8,128)(2,1)S(1)} %get-tuple-element.147), channel_id=1, source_target_pairs={{6,4},{7,5},{4,2},{5,3},{2,0},{3,1},{14,12},{15,13},{12,10},{13,11... | collective-permute-start | bytes 1572872 | tf_op jit(solution)/shard_map/ppermute | solution.py:45
  444.6 29.0 %collective-permute-start.21 = (bf16[512,768]{1,0:T(8,128)(2,1)}, bf16[512,768]{1,0:T(8,128)(2,1)S(1)}, u32[]{:S(2)}, u32[]{:S(2)}) collective-permute-start(bf16[512,768]{1,0:T(8,128)(2,1)} %convolution_convert_fusion.8), channel_id=1, source_target_pairs={{0,8},{8,0},{16,24},{24,16},{1,9},{9,1},{17,25},{25,17},{2,10},{10... | collective-permute-start | bytes 2359304 | tf_op jit(solution)/shard_map/ppermute | solution.py:37
  444.6 29.0 %collective-permute-start.22 = (bf16[512,768]{1,0:T(8,128)(2,1)}, bf16[512,768]{1,0:T(8,128)(2,1)}, u32[]{:S(2)}, u32[]{:S(2)}) collective-permute-start(bf16[512,768]{1,0:T(8,128)(2,1)} %convolution_convert_fusion.7), channel_id=1, source_target_pairs={{0,16},{8,24},{16,0},{24,8},{1,17},{9,25},{17,1},{25,9},{2,18},{10... | collective-permute-start | bytes 2359304 | tf_op jit(solution)/shard_map/ppermute | solution.py:37
  446.1 31.6 %collective-permute-start.23 = (bf16[512,768]{1,0:T(8,128)(2,1)}, bf16[512,768]{1,0:T(8,128)(2,1)}, u32[]{:S(2)}, u32[]{:S(2)}) collective-permute-start(bf16[512,768]{1,0:T(8,128)(2,1)} %convolution_convert_fusion.6), channel_id=1, source_target_pairs={{0,24},{8,16},{16,8},{24,0},{1,25},{9,17},{17,9},{25,1},{2,26},{10... | collective-permute-start | bytes 2359304 | tf_op jit(solution)/shard_map/ppermute | solution.py:37
  448.6 37.8 %copy-start.11 = (f32[512,768]{1,0:T(8,128)S(1)}, f32[512,768]{1,0:T(8,128)}, u32[]{:S(2)}) copy-start(f32[512,768]{1,0:T(8,128)} %fusion.13) | copy-start | bytes 4718596
  482.9 5.3 collective-permute-start.31
  483.6 4.8 collective-permute-start.32
  485.4 3.9 collective-permute-start.30
  503.3 69.3 %copy-start.18 = (f32[1,2048]{1,0:T(1,128)}, f32[1,2048]{1,0:T(1,128)S(1)}, u32[]{:S(2)}) copy-start(f32[1,2048]{1,0:T(1,128)S(1)} %slice.173) | copy-start | bytes 24580
  (13 other events, 80.1 us)
Sparse Core Ops, SparseCore 0:
  13.9 52.2 all-gather.10
  132.7 53.3 reduce-scatter.1
  189.1 45.3 all-gather.12
  260.9 36.0 all-gather.14
  306.2 71.4 all-gather.16
  379.2 102.0 all-gather.18
  490.5 69.1 all-gather.20

commit v5 on v4

--- a/solution.py
+++ b/solution.py
@@ -337,21 +337,47 @@
 
 def emit_kernel(owners, counts, stacked, *refs):
     counted, refs = refs[:counts], refs[counts:]
-    weights, out = refs[: 2 * owners], refs[-1]
-    middle = weights[0].shape[0]
-    for k in range(owners):
-
-        @pl.when(pl.program_id(0) // 2 == k)
-        def _(k=k):
-            total = jnp.dot(
-                stacked[:, :middle], weights[2 * k][...], preferred_element_type=wide
-            ) + jnp.dot(stacked[:, middle:], weights[2 * k + 1][...], preferred_element_type=wide)
-            out[...] = total.astype(low)
+    weights, (out, slots, arrived) = refs[: 2 * owners], refs[-3:]
+    middle, size = slots.shape[2:]
+    step = pl.program_id(0)
+
+    def fetch(n):
+        columns = pl.ds(n % 2 * size, size)
+        return [
+            pltpu.make_async_copy(
+                weights[n // 2 * 2 + half].at[:, columns],
+                slots.at[n % 2, half],
+                arrived.at[n % 2, half],
+            )
+            for half in range(2)
+        ]
+
+    @pl.when(step == 0)
+    def _():
+        for copy in fetch(0):
+            copy.start()
+
+    for n in range(2 * owners):
+
+        @pl.when(step == n)
+        def _(n=n):
+            if n + 1 < 2 * owners:
+                for copy in fetch(n + 1):
+                    copy.start()
+            for copy in fetch(n):
+                copy.wait()
+
+    @pl.when(step < 2 * owners)
+    def _():
+        slot = lax.rem(step, 2)
+        total = jnp.dot(stacked[:, :middle], slots[slot, 0], preferred_element_type=wide)
+        total = total + jnp.dot(stacked[:, middle:], slots[slot, 1], preferred_element_type=wide)
+        out[...] = total.astype(low)
 
     if not counted:
         return
 
-    @pl.when(pl.program_id(0) == 2 * owners)
+    @pl.when(step == 2 * owners)
     def _():
         count = counted[0][...].astype(wide)
         for ref in counted[1:]:
@@ -370,14 +396,11 @@
     size = depth // 2
     steps = 2 * owners + (first + owners == all_owners)
 
-    def at(k):
-        return pl.BlockSpec((middle, size), lambda t: (0, jnp.clip(t - 2 * k, 0, 1)))
-
     row = size // SPARE
     operands = [stacked, *counted, *[item for pair in weights for item in pair]]
     in_specs = [pl.BlockSpec((length, behind), lambda t: (0, 0))]
     in_specs += [pl.BlockSpec((SPARE, LANES), lambda t: (row, 0))] * len(counted)
-    in_specs += [at(k) for k in range(owners) for _ in range(2)]
+    in_specs += [pl.BlockSpec(memory_space=pl.ANY)] * (2 * owners)
     aliases = {}
     if into is not None:
         aliases = {len(operands): 0}
@@ -390,6 +413,10 @@
         out_specs=pl.BlockSpec((length, size), lambda t: (0, 2 * first + t)),
         out_shape=jax.ShapeDtypeStruct((length, all_owners * depth + LANES), low),
         input_output_aliases=aliases,
+        scratch_shapes=[
+            pltpu.VMEM((2, 2, middle, size), low),
+            pltpu.SemaphoreType.DMA((2, 2)),
+        ],
         cost_estimate=pl.CostEstimate(
             flops=2 * length * behind * owners * depth,
             bytes_accessed=2 * behind * (length + owners * depth) + 2 * length * steps * size,
@@ -406,27 +433,44 @@
     return jnp.where(kept, raw * HEAD_DIM ** (-0.5), masked_fill)
 
 
+def by_blocks(length, head_width, step, body):
+    pairs = head_width // LANES
+    blocks = length // 2 // step
+    for half in range(2):
+
+        def one(n, carry, half=half):
+            row = pl.multiple_of(half * (length // 2) + lax.rem(n, blocks) * step, step)
+            body(row, pl.multiple_of(lax.div(n, blocks) * LANES, LANES), (half + 1) * length // 2)
+            return carry
+
+        lax.fori_loop(0, pairs * blocks, one, 0)
+
+
 def attend_kernel(step, qkv, stacked, out, logsum):
     del stacked
     length, head_width = out.shape
     lane = lax.broadcasted_iota(jnp.int32, (step, LANES), 1)
-    for first in range(0, length, step):
-        last = first + step
-        sums = jnp.zeros((step, LANES), wide)
+
+    def body(row, at, last):
+        rows = pl.ds(row, step)
+        queries = qkv[rows, pl.ds(at, LANES)]
+        keys = qkv[:last, pl.ds(head_width + at, LANES)]
+        values = qkv[:last, pl.ds(2 * head_width + at, LANES)]
+        sums = logsum[rows, :]
         outs = []
-        for h in range(head_width // HEAD_DIM):
-            a, b = h * HEAD_DIM, (h + 1) * HEAD_DIM
-            keys = qkv[:last, head_width + a : head_width + b]
-            values = qkv[:last, 2 * head_width + a : 2 * head_width + b]
-            scores = scores_of(qkv[first:last, a:b], keys, first)
+        for n, h in enumerate((slice(0, HEAD_DIM), slice(HEAD_DIM, LANES))):
+            scores = scores_of(queries[:, h], keys[:, h], row)
             top = jnp.max(scores, axis=-1, keepdims=True)
             expd = jnp.exp(scores - top)
             total = jnp.sum(expd, axis=-1, keepdims=True)
             probs = (expd * (1.0 / total)).astype(low)
-            outs.append(jnp.dot(probs, values, preferred_element_type=wide))
-            sums = jnp.where(lane == h, top + jnp.log(total), sums)
-        out[first:last, :] = jnp.concatenate(outs, axis=1).astype(low)
-        logsum[first:last, :] = sums
+            outs.append(jnp.dot(probs, values[:, h], preferred_element_type=wide))
+            sums = jnp.where(lane == at // HEAD_DIM + n, top + jnp.log(total), sums)
+        out[rows, pl.ds(at, LANES)] = jnp.concatenate(outs, axis=1).astype(low)
+        logsum[rows, :] = sums
+
+    logsum[...] = jnp.zeros(logsum.shape, wide)
+    by_blocks(length, head_width, step, body)
 
 
 def attend(qkv, stacked):
@@ -435,7 +479,7 @@
     heads = head_width // HEAD_DIM
     whole = pl.BlockSpec(memory_space=pltpu.VMEM)
     return pl.pallas_call(
-        functools.partial(attend_kernel, min(256, length)),
+        functools.partial(attend_kernel, 256),
         grid=(1,),
         in_specs=[whole, pl.BlockSpec(memory_space=pl.ANY)],
         out_specs=[pl.BlockSpec((length, head_width), lambda n: (0, 0)), whole],
@@ -458,49 +502,52 @@
     length, head_width = grad.shape
     scale = HEAD_DIM ** (-0.5)
     over_rows = (((0,), (0,)), ((), ()))
-    for first in reversed(range(0, length, step)):
-        last = first + step
+    lane = lax.broadcasted_iota(jnp.int32, (step, LANES), 1)
+
+    def body(row, at, last):
+        rows = pl.ds(row, step)
+        spots = [pl.ds(t * head_width + at, LANES) for t in range(3)]
+        queries, keys, values = qkv[rows, spots[0]], qkv[:last, spots[1]], qkv[:last, spots[2]]
+        upstreams = grad[rows, spots[0]]
         parts = [[], [], []]
-        for h in range(head_width // HEAD_DIM):
-            a, b = h * HEAD_DIM, (h + 1) * HEAD_DIM
-            query = qkv[first:last, a:b]
-            keys = qkv[:last, head_width + a : head_width + b]
-            values = qkv[:last, 2 * head_width + a : 2 * head_width + b]
-            upstream = grad[first:last, a:b]
-            probs = jnp.exp(scores_of(query, keys, first) - logsum[first:last, h : h + 1])
+        for n, h in enumerate((slice(0, HEAD_DIM), slice(HEAD_DIM, LANES))):
+            sums = jnp.where(lane == at // HEAD_DIM + n, logsum[rows, :], 0.0)
+            sums = jnp.sum(sums, axis=1, keepdims=True)
+            probs = jnp.exp(scores_of(queries[:, h], keys[:, h], row) - sums)
             prob_grad = lax.dot_general(
-                upstream, values, (((1,), (1,)), ((), ())), preferred_element_type=wide
+                upstreams[:, h],
+                values[:, h],
+                (((1,), (1,)), ((), ())),
+                preferred_element_type=wide,
             )
             inner = jnp.sum(probs * prob_grad, axis=-1, keepdims=True)
             score_grad = (probs * (prob_grad - inner)).astype(low)
-            parts[0].append(jnp.dot(score_grad, keys, preferred_element_type=wide) * scale)
+            parts[0].append(jnp.dot(score_grad, keys[:, h], preferred_element_type=wide))
             parts[1].append(
-                lax.dot_general(score_grad, query, over_rows, preferred_element_type=wide) * scale
+                lax.dot_general(score_grad, queries[:, h], over_rows, preferred_element_type=wide)
             )
             parts[2].append(
                 lax.dot_general(
-                    probs.astype(low), upstream, over_rows, preferred_element_type=wide
+                    probs.astype(low), upstreams[:, h], over_rows, preferred_element_type=wide
                 )
             )
-        parts = [jnp.concatenate(part_list, axis=1) for part_list in parts]
-        gone[first:last, :head_width] = parts[0]
-        for t in (1, 2):
-            columns = slice(t * head_width, (t + 1) * head_width)
-            if last == length:
-                gone[:, columns] = parts[t]
-            else:
-                gone[:last, columns] += parts[t]
-    repeats = head_width // LANES
-    for first in range(0, length, step):
-        here = slice(first, first + step)
-        ahead = jnp.concatenate([cosine[here, :]] * repeats, axis=1)
-        aside = -jnp.concatenate([sine[here, :]] * repeats, axis=1)
-        for t in range(3):
-            columns = slice(t * head_width, (t + 1) * head_width)
-            value = gone[here, columns].astype(low)
-            if t < 2:
-                value = turn(value.astype(wide), ahead, aside).astype(low)
-            out[here, columns] = value
+        parts = [jnp.concatenate(part, axis=1) for part in parts]
+        gone[rows, spots[0]] = parts[0] * scale
+        gone[:last, spots[1]] += parts[1] * scale
+        gone[:last, spots[2]] += parts[2]
+
+    gone[:, head_width:] = jnp.zeros((length, 2 * head_width), wide)
+    by_blocks(length, head_width, step, body)
+
+    def turn_back(n, carry):
+        rows = pl.ds(pl.multiple_of(lax.rem(n, length // step) * step, step), step)
+        at = pl.multiple_of(lax.div(n, length // step) * LANES, LANES)
+        value = gone[rows, pl.ds(at, LANES)].astype(low).astype(wide)
+        out[rows, pl.ds(at, LANES)] = turn(value, cosine[rows, :], -sine[rows, :]).astype(low)
+        return carry
+
+    lax.fori_loop(0, length // step * (2 * head_width // LANES), turn_back, 0)
+    out[:, 2 * head_width :] = gone[:, 2 * head_width :].astype(low)
 
 
 def attend_back(qkv, grad, logsum, cosine, sine, entered):
@@ -509,7 +556,7 @@
     heads = head_width // HEAD_DIM
     whole = pl.BlockSpec(memory_space=pltpu.VMEM)
     return pl.pallas_call(
-        functools.partial(attend_back_kernel, min(256, length)),
+        functools.partial(attend_back_kernel, 128),
         grid=(1,),
         in_specs=[whole] * 5 + [pl.BlockSpec(memory_space=pl.ANY)],
         out_specs=pl.BlockSpec((length, three), lambda n: (0, 0)),
@@ -577,24 +624,78 @@
     )(hidden, grads, *weights)
 
 
-def answer_kernel(count, chips, part, entered, *refs):
-    weights, (kept, sent, held) = refs[:count], refs[count:]
+def sort_blocks(held, part, chips, kept, sent):
     rows = kept.shape[0] // chips
-    over = (((1,), (1,)), ((), ()))
-    for n in range(count):
-
-        @pl.when(pl.program_id(0) == n)
-        def _(n=n):
-            held[...] = lax.dot_general(
-                entered[...], weights[n][...], over, preferred_element_type=wide
-            )
-
     for k in range(chips):
         here = slice(k * rows, (k + 1) * rows)
         for core, out in enumerate((kept, sent)):
-            block = part[0] ^ (2 * k + core)
+            block = part ^ (2 * k + core)
             source = pl.ds(pl.multiple_of(block * rows, rows), rows)
             out[here, :] = held[source, :].astype(out.dtype)
+
+
+def outer_kernel(left, right, *outs):
+    total = lax.dot_general(
+        left[...], right[...], (((0,), (0,)), ((), ())), preferred_element_type=wide
+    )
+    for n, out in enumerate(outs):
+
+        @pl.when(pl.program_id(0) == n)
+        def _(out=out):
+            out[...] = total.astype(out.dtype)
+
+
+def outer(left, right, count, left_size, right_size):
+    length = left.shape[0]
+    left_step = int(left.shape[1] >= count * left_size)
+    flops = 2 * length * count * left_size * right_size
+    kinds = [wide] + [low] * (count - 1)
+    results = pl.pallas_call(
+        outer_kernel,
+        grid=(count,),
+        in_specs=[
+            pl.BlockSpec((length, left_size), lambda k: (0, k * left_step)),
+            pl.BlockSpec((length, right_size), lambda k: (0, k * (1 - left_step))),
+        ],
+        out_specs=[pl.BlockSpec((left_size, right_size), lambda k: (0, 0))] * count,
+        out_shape=[jax.ShapeDtypeStruct((left_size, right_size), kind) for kind in kinds],
+        cost_estimate=pl.CostEstimate(
+            flops=flops, bytes_accessed=flops // length, transcendentals=0
+        ),
+        name="outer",
+    )(left, right)
+    return results[0], list(results[1:])
+
+
+def answer_kernel(count, chips, part, entered, *refs):
+    weights, (kept, sent, held, slots, arrived) = refs[:count], refs[count:]
+    tall = slots.shape[1]
+    step = pl.program_id(0)
+
+    def fetch(n):
+        return pltpu.make_async_copy(
+            weights[n].at[pl.ds(0, tall)], slots.at[n % 2], arrived.at[n % 2]
+        )
+
+    @pl.when(step == 0)
+    def _():
+        fetch(0).start()
+
+    for n in range(count):
+
+        @pl.when(step == n)
+        def _(n=n):
+            if n + 1 < count:
+                fetch(n + 1).start()
+            fetch(n).wait()
+
+    held[...] = lax.dot_general(
+        entered[...],
+        slots[lax.rem(step, 2)],
+        (((1,), (1,)), ((), ())),
+        preferred_element_type=wide,
+    )
+    sort_blocks(held, part[0], chips, kept, sent)
 
 
 def answer(entered, pieces, part, chips, tall):
@@ -608,13 +709,17 @@
             pl.BlockSpec(memory_space=pltpu.SMEM),
             pl.BlockSpec((length, inside), lambda t: (0, 0)),
         ]
-        + [pl.BlockSpec((tall, inside), lambda t: (0, 0))] * count,
+        + [pl.BlockSpec(memory_space=pl.ANY)] * count,
         out_specs=[pl.BlockSpec((half, tall), lambda t: (0, t))] * 2,
         out_shape=[
             jax.ShapeDtypeStruct((half, count * tall), wide),
             jax.ShapeDtypeStruct((half, count * tall), low),
         ],
-        scratch_shapes=[pltpu.VMEM((length, tall), wide)],
+        scratch_shapes=[
+            pltpu.VMEM((length, tall), wide),
+            pltpu.VMEM((2, tall, inside), low),
+            pltpu.SemaphoreType.DMA((2,)),
+        ],
         cost_estimate=pl.CostEstimate(
             flops=2 * length * inside * count * tall,
             bytes_accessed=2 * inside * (length + count * tall) + 3 * length * count * tall,
@@ -844,13 +949,10 @@
     def gather(array):
         return lax.all_gather(array, "seq", axis=0, tiled=False)
 
-    cut = units * 5 // 8
+    cut = units * 5 // 8 // LANES * LANES
 
     def of_stacked(first, last):
         return [owned(stacked[:, first:last], piece(grad_all, k)) for k in range(data_count)]
-
-    def of_normed(right):
-        return [owned(piece(normed_all, k), right) for k in range(data_count)]
 
     def prepare(pieces):
         return pieces[0], [item.astype(low) for item in pieces[1:]]
@@ -866,18 +968,20 @@
         return own.astype(low)
 
     own_a, sent_a = prepare(of_stacked(head_width + cut, head_width + units))
-    own_b, sent_b = prepare(of_stacked(0, head_width + cut))
+    own_b, sent_b = outer(stacked, grad_all, data_count, head_width + cut, depth)
     got, ((own_b, sent_b),) = send(sent_a, (own_b, sent_b))
     down_a = total(own_a, got)
     all_a = gather(down_a)
     head_grad, in_low = reject(after(grad_all, down_a), w_back, hidden, head_width)
-    in_low = attend_back(qkv, head_grad, logsum, cosine, sine, in_low)
-    got, (in_low,) = send(sent_b, in_low)
+    own_up, sent_up = outer(normed_all, in_low[:, three:], data_count, depth, units)
+    got, (head_grad, in_low, (own_up, sent_up)) = send(
+        sent_b, head_grad, in_low, (own_up, sent_up)
+    )
     down_b = total(own_b, got)
     all_b = gather(down_b)
-    in_low = after(in_low, down_b)
-    own_up, sent_up = prepare(of_normed(in_low[:, three:]))
-    own_qkv, sent_qkv = prepare(of_normed(after(in_low[:, :three], *sent_up)))
+    head_grad = after(head_grad, down_b)
+    in_low = attend_back(qkv, head_grad, logsum, cosine, sine, in_low)
+    own_qkv, sent_qkv = outer(normed_all, after(in_low, *sent_up), data_count, depth, three)
     kept, sent = answer(in_low, flat_in, part, seq_count // 2, tall)
     got, ((own_qkv, sent_qkv), kept, all_a) = send(sent_up, (own_qkv, sent_qkv), kept, all_a)
     up_grad = total(own_up, got)

time: 592 us -> 586 us (0.990); the launches traced: 581 us -> 583 us
  Pallas kernels: 136 us -> 180 us
  matrix products: 35.4 us -> 10.6 us
  waiting for transfers between devices: 290 us -> 270 us
    pallas_call x2 -> x5, Pallas kernels: 27 us -> 70.6 us  [the longest x1 29.7 us: attend_back(): pl.pallas_call(functools.partial(attend_back_kernel, 128), grid=(1,), in_...]
    dot_general x16 -> x4, matrix products: 35.4 us -> 10.6 us  [dot(): return lax.dot_general(a, b, (dims, ((), ())), preferred_element_type=wide)]
    ppermute x28, waiting for transfers between devices: 93.7 us -> 75.4 us  [swap(): lax.ppermute(array, axis, [(s, s ^ bit) for s in range(lax.axis_size(axis...]
  transfers between devices with their start and end apart: 40 -> 40, of which waited for: 21 -> 19; matrix products, arithmetic and copies ran while one was open for 12% -> 7% of each run, Pallas kernels for 19% -> 27%
where the time goes in v5:
time: 586 us; the launch traced here: 583 us
  waiting for transfers between devices  270 us (46%)
  Pallas kernels  180 us (31%)
  starting transfers between devices  61.1 us (10%)
  other arithmetic  31.3 us (5%)
  between operations  17 us (3%)
  local copies, waits for them, and re-layouts  13.8 us (2%)
  matrix products  10.6 us (2%)
    ppermute x28, waiting for transfers between devices, swap(): lax.ppermute(array, axis, [(s, s ^ bit) for s in range(lax.axis_size(axis...  75.4 us
    ppermute x5, waiting for transfers between devices, between(): lax.ppermute(array, 'seq', [(2 * a + core, 2 * b + core) for a, b in pair...  57.5 us
    all_gather x4, waiting for transfers between devices, gather(): return lax.all_gather(array, 'seq', axis=0, tiled=False)  47 us
    all_gather x2, waiting for transfers between devices, gather_seq(): return lax.all_gather(rows, 'seq', axis=0, tiled=True)  45.3 us
    reduce_scatter x1, waiting for transfers between devices, scatter_seq(): return lax.psum_scatter(partial, 'seq', scatter_dimension=0, tiled=True)  44.9 us
    ppermute x28, starting transfers between devices, swap(): lax.ppermute(array, axis, [(s, s ^ bit) for s in range(lax.axis_size(axis...  33.6 us
    pallas_call x1, Pallas kernels, attend_back(): pl.pallas_call(functools.partial(attend_back_kernel, 128), grid=(1,), in_...  29.7 us
    pallas_call x3, Pallas kernels, outer(): pl.pallas_call(outer_kernel, grid=(count,), in_specs=[pl.BlockSpec((lengt...  27.4 us
  transfers between devices with their start and end apart: 40, of which 19 were waited for; matrix products, arithmetic and copies ran while one was open for 7% of the time, Pallas kernels for 27%

profile of v5, /device:TPU:0, one launch (start us, length us, event | category | flops | bytes accessed | tf_op | source)
XLA Modules:
  0.0 583.5 jit_solution(6822097337071169543)
XLA Ops:
  7.2 3.6 pick.2
  10.8 3.0 enter.1
  13.9 3.0 collective-permute-start.3
  18.4 20.3 %collective-permute-done.3.refs_5_.refs_2_ = bf16[272,1792]{1,0:T(8,128)(2,1)S(1)} collective-permute-done((bf16[272,1792]{1,0:T(8,128)(2,1)}, bf16[272,1792]{1,0:T(8,128)(2,1)S(1)}, u32[]{:S(2)}, u32[]{:S(2)}) %collective-permute-start.3) | collective-permute-done | bytes 974880 | tf_op jit(solution)/shard_map/ppermute | solution.py:37
  44.3 3.0 pick.3
  47.9 16.1 %collective-permute-done.4.refs_6_ = bf16[256,1792]{1,0:T(8,128)(2,1)} collective-permute-done((bf16[256,1792]{1,0:T(8,128)(2,1)}, bf16[256,1792]{1,0:T(8,128)(2,1)}, u32[]{:S(2)}, u32[]{:S(2)}) %collective-permute-start.4) | collective-permute-done | bytes 917536 | tf_op jit(solution)/shard_map/ppermute | solution.py:37
  69.0 3.1 fusion.7
  72.1 11.6 %collective-permute-done.2.refs_4_ = bf16[256,1792]{1,0:T(8,128)(2,1)} collective-permute-done((bf16[256,1792]{1,0:T(8,128)(2,1)}, bf16[256,1792]{1,0:T(8,128)(2,1)}, u32[]{:S(2)}, u32[]{:S(2)}) %collective-permute-start.2) | collective-permute-done | bytes 917536 | tf_op jit(solution)/shard_map/ppermute | solution.py:37
  86.2 16.9 %project.1 = (bf16[1024,768]{1,0:T(8,128)(2,1)}, f32[1024,1024]{1,0:T(8,128)}, bf16[1024,1280]{1,0:T(8,128)(2,1)}) custom-call(bf16[1024,2176]{1,0:T(8,128)(2,1)} %all-gather.11.cloned.1.call-done.normed.left, f32[1024,128]{1,0:T(8,128)} %get-tuple-element.190.cosine, f32[1024,128]{1,0:T(8,128)} %get-tuple-element.189.sine, ...), custom_call_target="tpu_custom_call" | custom-call | flops 7516192768 | bytes 26214400 | tf_op jit(solution)/shard_map/project/pallas_call | solution.py:309
  103.0 13.5 %attend.1 = (bf16[1024,1280]{1,0:T(8,128)(2,1)}, f32[1024,128]{1,0:T(8,128)}) custom-call(bf16[1024,768]{1,0:T(8,128)(2,1)} %get-tuple-element.100.qkv, bf16[1024,1280]{1,0:T(8,128)(2,1)} %get-tuple-element.101.stacked), custom_call_target="tpu_custom_call", output_to_operand_aliasing={{0}: (1, {})} | custom-call | flops 2147483648 | bytes 6291456 | tf_op jit(solution)/shard_map/attend/pallas_call | solution.py:481
  118.8 10.2 %emit.2.refs_6_ = bf16[1024,2176]{1,0:T(8,128)(2,1)} custom-call(bf16[1024,1280]{1,0:T(8,128)(2,1)} %get-tuple-element.102.stacked.left, bf16[640,512]{1,0:T(8,128)(2,1)} %get-tuple-element.106.refs_0_, bf16[640,512]{1,0:T(8,128)(2,1)} %get-tuple-element.108.refs_1_, bf16[640,512]{1,0:T(8,128)(2,1)} %collective-permute-done.6.refs_2_, ...), custom_call_target="tpu_custom_call" | custom-call | flops 4026531840 | bytes 9699328 | tf_op jit(solution)/shard_map/emit/pallas_call | solution.py:409
  131.0 5.7 emit.3
  139.2 2.6 pad_maximum_fusion.1.refs_1_
  141.8 2.4 pad_maximum_fusion.2.refs_2_
  145.3 44.9 %reduce-scatter.2.cloned.1.call-done.branches = bf16[128,2176]{1,0:T(8,128)(2,1)} async-done(((bf16[1024,2176]{1,0:T(8,128)(2,1)}), bf16[128,2176]{1,0:T(8,128)(2,1)}) %reduce-scatter.2.cloned.1.call-update) | async-done | bytes 557072 | tf_op jit(solution)/shard_map/reduce_scatter | solution.py:77
  190.2 3.0 grade.1
  193.5 45.3 %all-gather.13.cloned.1.call-done.right.grads = bf16[1024,2048]{1,0:T(8,128)(2,1)} async-done(((bf16[128,2048]{1,0:T(8,128)(2,1)}), bf16[1024,2048]{1,0:T(8,128)(2,1)}) %all-gather.13.cloned.1.call-update) | async-done | bytes 4194320 | tf_op jit(solution)/shard_map/all_gather | solution.py:41
  238.7 2.6 convolution_convert_fusion.2
  242.8 2.6 convolution_convert_fusion.1
  246.8 2.6 convolution_convert_fusion
  249.9 9.0 %outer.3 = (f32[896,512]{1,0:T(8,128)}, bf16[896,512]{1,0:T(8,128)(2,1)}, bf16[896,512]{1,0:T(8,128)(2,1)}, bf16[896,512]{1,0:T(8,128)(2,1)}) custom-call(bf16[1024,1280]{1,0:T(8,128)(2,1)} %get-tuple-element.102.stacked.left, bf16[1024,2048]{1,0:T(8,128)(2,1)} %all-gather.13.cloned.1.call-done.right.grads), custom_call_target="tpu_custom_call" | custom-call | flops 3758096384 | bytes 3670016 | tf_op jit(solution)/shard_map/outer/pallas_call | solution.py:653
  258.9 6.0 %collective-permute-done.13 = bf16[384,512]{1,0:T(8,128)(2,1)S(1)} collective-permute-done((bf16[384,512]{1,0:T(8,128)(2,1)}, bf16[384,512]{1,0:T(8,128)(2,1)S(1)}, u32[]{:S(2)}, u32[]{:S(2)}) %collective-permute-start.13) | collective-permute-done | bytes 393248 | tf_op jit(solution)/shard_map/ppermute | solution.py:37
  265.0 2.9 add_convert_fusion.5
  271.5 13.7 %reject.1 = (bf16[1024,256]{1,0:T(8,128)(2,1)}, bf16[1024,1792]{1,0:T(8,128)(2,1)}) custom-call(f32[1024,1024]{1,0:T(8,128)} %get-tuple-element.122.hidden, bf16[1024,2048]{1,0:T(8,128)(2,1)} %all-gather.13.cloned.1.call-done.right.grads, bf16[1280,512]{1,0:T(8,128)(2,1)} %pad_maximum_fusion.refs_0_, bf16[1280,512]{1,0:T(8,128)(2,1)} %pad_maximum_fusion.1.refs_1_, ...), custom_call_target="tpu_custom_call" | custom-call | flops 5368709120 | bytes 19922944 | tf_op jit(solution)/shard_map/reject/pallas_call | solution.py:604
  285.2 3.1 slice.95.right
  288.2 10.1 %outer.4 = (f32[512,1024]{1,0:T(8,128)}, bf16[512,1024]{1,0:T(8,128)(2,1)}, bf16[512,1024]{1,0:T(8,128)(2,1)}, bf16[512,1024]{1,0:T(8,128)(2,1)}) custom-call(bf16[1024,2176]{1,0:T(8,128)(2,1)} %all-gather.11.cloned.1.call-done.normed.left, bf16[1024,1024]{1,0:T(8,128)(2,1)} %slice.95.right), custom_call_target="tpu_custom_call" | custom-call | flops 4294967296 | bytes 4194304 | tf_op jit(solution)/shard_map/outer/pallas_call | solution.py:653
  298.4 10.3 %collective-permute-done.16 = bf16[896,512]{1,0:T(8,128)(2,1)} collective-permute-done((bf16[896,512]{1,0:T(8,128)(2,1)}, bf16[896,512]{1,0:T(8,128)(2,1)}, u32[]{:S(2)}, u32[]{:S(2)}) %collective-permute-start.16) | collective-permute-done | bytes 917536 | tf_op jit(solution)/shard_map/ppermute | solution.py:37
  310.2 2.9 add_convert_fusion.1
  317.0 29.7 %attend_back.1.right.entered = bf16[1024,1792]{1,0:T(8,128)(2,1)} custom-call(bf16[1024,768]{1,0:T(8,128)(2,1)} %get-tuple-element.100.qkv, bf16[1024,256]{1,0:T(8,128)(2,1)} %get-tuple-element.145.grad, f32[1024,128]{1,0:T(8,128)} %get-tuple-element.146.logsum, f32[1024,128]{1,0:T(8,128)} %get-tuple-element.190.cosine, ...), custom_call_target="tpu_custom_call", output_to_operand_aliasing={{}: (5, {})} | custom-call | flops 5368709120 | bytes 6291456 | tf_op jit(solution)/shard_map/attend_back/pallas_call | solution.py:558
  346.7 8.3 %outer.5 = (f32[512,768]{1,0:T(8,128)}, bf16[512,768]{1,0:T(8,128)(2,1)}, bf16[512,768]{1,0:T(8,128)(2,1)}, bf16[512,768]{1,0:T(8,128)(2,1)}) custom-call(bf16[1024,2176]{1,0:T(8,128)(2,1)} %all-gather.11.cloned.1.call-done.normed.left, bf16[1024,1792]{1,0:T(8,128)(2,1)} %attend_back.1.right.entered), custom_call_target="tpu_custom_call" | custom-call | flops 3221225472 | bytes 3145728 | tf_op jit(solution)/shard_map/outer/pallas_call | solution.py:653
  355.0 14.9 %answer.1 = (f32[512,2048]{1,0:T(8,128)}, bf16[512,2048]{1,0:T(8,128)(2,1)}) custom-call(s32[1]{0:T(128)} %bitcast.part, bf16[1024,1792]{1,0:T(8,128)(2,1)} %attend_back.1.right.entered, bf16[256,1792]{1,0:T(8,128)(2,1)} %get-tuple-element.96.refs_0_, bf16[272,1792]{1,0:T(8,128)(2,1)} %get-tuple-element.97.refs_1_.refs_0_, ...), custom_call_target="tpu_custom_call" | custom-call | flops 7516192768 | bytes 17301504 | tf_op jit(solution)/shard_map/answer/pallas_call | solution.py:705
  370.0 3.3 add_convert_fusion
  373.4 4.4 collective-permute-done.24
  377.8 2.8 convert_add_fusion
  382.2 11.5 %collective-permute-done.25 = bf16[128,2048]{1,0:T(8,128)(2,1)S(1)} collective-permute-done((bf16[128,2048]{1,0:T(8,128)(2,1)S(1)}, bf16[128,2048]{1,0:T(8,128)(2,1)S(1)}, u32[]{:S(2)}, u32[]{:S(2)}) %collective-permute-start.25) | collective-permute-done | bytes 524320 | tf_op jit(solution)/shard_map/ppermute | solution.py:45
  394.6 5.0 collective-permute-start.26
  401.0 21.5 %collective-permute-done.26 = bf16[128,2048]{1,0:T(8,128)(2,1)S(1)} collective-permute-done((bf16[128,2048]{1,0:T(8,128)(2,1)S(1)}, bf16[128,2048]{1,0:T(8,128)(2,1)S(1)}, u32[]{:S(2)}, u32[]{:S(2)}) %collective-permute-start.26) | collective-permute-done | bytes 524320 | tf_op jit(solution)/shard_map/ppermute | solution.py:45
  424.4 18.0 %collective-permute-start.27 = (bf16[128,2048]{1,0:T(8,128)(2,1)S(1)}, bf16[128,2048]{1,0:T(8,128)(2,1)S(1)}, u32[]{:S(2)}, u32[]{:S(2)}) collective-permute-start(bf16[128,2048]{1,0:T(8,128)(2,1)S(1)} %get-tuple-element.180), channel_id=1, source_target_pairs={{0,2},{1,3},{2,4},{3,5},{4,6},{5,7},{8,10},{9,11},{10,12},{11,13},... | collective-permute-start | bytes 1572872 | tf_op jit(solution)/shard_map/ppermute | solution.py:45
  445.4 3.4 collective-permute-start.23
  449.3 15.1 %collective-permute-done.27 = bf16[128,2048]{1,0:T(8,128)(2,1)S(1)} collective-permute-done((bf16[128,2048]{1,0:T(8,128)(2,1)S(1)}, bf16[128,2048]{1,0:T(8,128)(2,1)S(1)}, u32[]{:S(2)}, u32[]{:S(2)}) %collective-permute-start.27) | collective-permute-done | bytes 524320 | tf_op jit(solution)/shard_map/ppermute | solution.py:45
  464.4 9.3 %collective-permute-done.29 = bf16[128,2048]{1,0:T(8,128)(2,1)S(1)} collective-permute-done((bf16[128,2048]{1,0:T(8,128)(2,1)S(1)}, bf16[128,2048]{1,0:T(8,128)(2,1)S(1)}, u32[]{:S(2)}, u32[]{:S(2)}) %collective-permute-start.29) | collective-permute-done | bytes 524320 | tf_op jit(solution)/shard_map/ppermute | solution.py:45
  473.7 2.4 fusion.1.summed
  476.1 2.7 collective-permute-done.22
  478.8 3.7 leave.1
  492.4 12.1 %widen_rows.1 = (f32[8192,512]{1,0:T(8,128)}, f32[2048,512]{1,0:T(8,128)}) custom-call(bf16[8,384,512]{2,1,0:T(8,128)(2,1)} %bitcast.35, bf16[8,896,512]{2,1,0:T(8,128)(2,1)} %bitcast.32), custom_call_target="tpu_custom_call" | custom-call | bytes 31457280 | tf_op jit(solution)/shard_map/widen_rows/pallas_call | solution.py:743
  504.6 10.4 %widen_columns.2 = f32[512,8192]{1,0:T(8,128)} custom-call(bf16[8,512,1024]{2,1,0:T(8,128)(2,1)} %bitcast.31), custom_call_target="tpu_custom_call" | custom-call | bytes 25165824 | tf_op jit(solution)/shard_map/widen_columns/pallas_call | solution.py:778
  515.0 47.0 %all-gather.21.cloned.1.call-done = bf16[4224,768]{1,0:T(8,128)(2,1)} async-done(((bf16[528,768]{1,0:T(8,128)(2,1)}), bf16[4224,768]{1,0:T(8,128)(2,1)}) %all-gather.21.cloned.1.call-update) | async-done | bytes 6488080 | tf_op jit(solution)/shard_map/all_gather | solution.py:950
  564.2 8.8 %widen_columns.3 = f32[512,6144]{1,0:T(8,128)} custom-call(bf16[8,528,768]{2,1,0:T(8,128)(2,1)} %bitcast.34), custom_call_target="tpu_custom_call" | custom-call | bytes 18874368 | tf_op jit(solution)/shard_map/widen_columns/pallas_call | solution.py:778
  (144 shorter events, 58.4 us)
Async XLA Ops:
  7.2 60.4 %all-gather.11.cloned.1.call-start = ((), (), s32[]{:S(2)}) async-start(), calls=%async_computation.1 | async-start | bytes 5013504 | tf_op jit(solution)/shard_map/all_gather | solution.py:41
  13.8 176.4 %reduce-scatter.2.cloned.1.call-start = ((), (), s32[]{:S(2)}) async-start(), calls=%async_computation.2 | async-start | bytes 5013504 | tf_op jit(solution)/shard_map/reduce_scatter | solution.py:77
  13.9 24.8 %collective-permute-start.3 = (bf16[272,1792]{1,0:T(8,128)(2,1)}, bf16[272,1792]{1,0:T(8,128)(2,1)S(1)}, u32[]{:S(2)}, u32[]{:S(2)}) collective-permute-start(bf16[272,1792]{1,0:T(8,128)(2,1)} %get-tuple-element.97.refs_1_.refs_0_), channel_id=1, source_target_pairs={{0,16},{8,24},{16,0},{24,8},{1,17},{9,25},{17,1},{25,9},{2,18},{10... | collective-permute-start | bytes 2924552 | tf_op jit(solution)/shard_map/ppermute | solution.py:37
  16.9 23.5 %collective-permute-start = (bf16[256,1792]{1,0:T(8,128)(2,1)}, bf16[256,1792]{1,0:T(8,128)(2,1)}, u32[]{:S(2)}, u32[]{:S(2)}) collective-permute-start(bf16[256,1792]{1,0:T(8,128)(2,1)} %get-tuple-element.96.refs_0_), channel_id=1, source_target_pairs={{0,8},{8,0},{16,24},{24,16},{1,9},{9,1},{17,25},{25,17},{2,10},{10... | collective-permute-start | bytes 2752520 | tf_op jit(solution)/shard_map/ppermute | solution.py:37
  38.7 25.3 %collective-permute-start.5 = (bf16[272,1792]{1,0:T(8,128)(2,1)S(1)}, bf16[272,1792]{1,0:T(8,128)(2,1)S(1)}, u32[]{:S(2)}, u32[]{:S(2)}) collective-permute-start(bf16[272,1792]{1,0:T(8,128)(2,1)S(1)} %collective-permute-done.3.refs_5_.refs_2_), channel_id=1, source_target_pairs={{0,8},{8,0},{16,24},{24,16},{1,9},{9,1},{17,25},{25,17},{2,10},{10... | collective-permute-start | bytes 2924552 | tf_op jit(solution)/shard_map/ppermute | solution.py:37
  40.4 23.6 %collective-permute-start.4 = (bf16[256,1792]{1,0:T(8,128)(2,1)}, bf16[256,1792]{1,0:T(8,128)(2,1)}, u32[]{:S(2)}, u32[]{:S(2)}) collective-permute-start(bf16[256,1792]{1,0:T(8,128)(2,1)} %collective-permute-done.refs_2_), channel_id=1, source_target_pairs={{0,16},{8,24},{16,0},{24,8},{1,17},{9,25},{17,1},{25,9},{2,18},{10... | collective-permute-start | bytes 2752520 | tf_op jit(solution)/shard_map/ppermute | solution.py:37
  41.9 41.7 %collective-permute-start.2 = (bf16[256,1792]{1,0:T(8,128)(2,1)}, bf16[256,1792]{1,0:T(8,128)(2,1)}, u32[]{:S(2)}, u32[]{:S(2)}) collective-permute-start(bf16[256,1792]{1,0:T(8,128)(2,1)} %get-tuple-element.96.refs_0_), channel_id=1, source_target_pairs={{0,16},{8,24},{16,0},{24,8},{1,17},{9,25},{17,1},{25,9},{2,18},{10... | collective-permute-start | bytes 2752520 | tf_op jit(solution)/shard_map/ppermute | solution.py:37
  42.4 42.8 %collective-permute-start.1 = (bf16[272,1792]{1,0:T(8,128)(2,1)}, bf16[272,1792]{1,0:T(8,128)(2,1)S(1)}, u32[]{:S(2)}, u32[]{:S(2)}) collective-permute-start(bf16[272,1792]{1,0:T(8,128)(2,1)} %get-tuple-element.97.refs_1_.refs_0_), channel_id=1, source_target_pairs={{0,8},{8,0},{16,24},{24,16},{1,9},{9,1},{17,25},{25,17},{2,10},{10... | collective-permute-start | bytes 2924552 | tf_op jit(solution)/shard_map/ppermute | solution.py:37
  64.0 21.2 %copy-start.12 = (bf16[272,1792]{1,0:T(8,128)(2,1)}, bf16[272,1792]{1,0:T(8,128)(2,1)S(1)}, u32[]{:S(2)}) copy-start(bf16[272,1792]{1,0:T(8,128)(2,1)S(1)} %collective-permute-done.5.refs_7_.refs_3_) | copy-start | bytes 2924548
  64.0 19.7 %copy-start.15 = (bf16[640,512]{1,0:T(8,128)(2,1)S(1)}, bf16[640,512]{1,0:T(8,128)(2,1)}, u32[]{:S(2)}) copy-start(bf16[640,512]{1,0:T(8,128)(2,1)} %get-tuple-element.108.refs_1_) | copy-start | bytes 1966084
  64.0 54.7 %collective-permute-start.11 = (bf16[640,512]{1,0:T(8,128)(2,1)}, bf16[640,512]{1,0:T(8,128)(2,1)}, u32[]{:S(2)}, u32[]{:S(2)}) collective-permute-start(bf16[640,512]{1,0:T(8,128)(2,1)} %get-tuple-element.106.refs_0_), channel_id=1, source_target_pairs={{0,16},{8,24},{16,0},{24,8},{1,17},{9,25},{17,1},{25,9},{2,18},{10... | collective-permute-start | bytes 1966088 | tf_op jit(solution)/shard_map/ppermute | solution.py:37
  65.6 51.0 %collective-permute-start.6 = (bf16[640,512]{1,0:T(8,128)(2,1)}, bf16[640,512]{1,0:T(8,128)(2,1)}, u32[]{:S(2)}, u32[]{:S(2)}) collective-permute-start(bf16[640,512]{1,0:T(8,128)(2,1)} %get-tuple-element.106.refs_0_), channel_id=1, source_target_pairs={{0,8},{8,0},{16,24},{24,16},{1,9},{9,1},{17,25},{25,17},{2,10},{10... | collective-permute-start | bytes 1966088 | tf_op jit(solution)/shard_map/ppermute | solution.py:37
  66.4 52.3 %collective-permute-start.10 = (bf16[640,512]{1,0:T(8,128)(2,1)}, bf16[640,512]{1,0:T(8,128)(2,1)}, u32[]{:S(2)}, u32[]{:S(2)}) collective-permute-start(bf16[640,512]{1,0:T(8,128)(2,1)} %get-tuple-element.108.refs_1_), channel_id=1, source_target_pairs={{0,8},{8,0},{16,24},{24,16},{1,9},{9,1},{17,25},{25,17},{2,10},{10... | collective-permute-start | bytes 1966088 | tf_op jit(solution)/shard_map/ppermute | solution.py:37
  83.7 32.9 %collective-permute-start.8 = (bf16[640,512]{1,0:T(8,128)(2,1)S(1)}, bf16[640,512]{1,0:T(8,128)(2,1)}, u32[]{:S(2)}, u32[]{:S(2)}) collective-permute-start(bf16[640,512]{1,0:T(8,128)(2,1)S(1)} %copy-done.15), channel_id=1, source_target_pairs={{0,16},{8,24},{16,0},{24,8},{1,17},{9,25},{17,1},{25,9},{2,18},{10... | collective-permute-start | bytes 1966088 | tf_op jit(solution)/shard_map/ppermute | solution.py:37
  116.5 12.7 %collective-permute-start.7 = (bf16[640,512]{1,0:T(8,128)(2,1)}, bf16[640,512]{1,0:T(8,128)(2,1)S(1)}, u32[]{:S(2)}, u32[]{:S(2)}) collective-permute-start(bf16[640,512]{1,0:T(8,128)(2,1)} %collective-permute-done.6.refs_2_), channel_id=1, source_target_pairs={{0,16},{8,24},{16,0},{24,8},{1,17},{9,25},{17,1},{25,9},{2,18},{10... | collective-permute-start | bytes 1966088 | tf_op jit(solution)/shard_map/ppermute | solution.py:37
  117.3 12.9 %collective-permute-start.9 = (bf16[640,512]{1,0:T(8,128)(2,1)}, bf16[640,512]{1,0:T(8,128)(2,1)S(1)}, u32[]{:S(2)}, u32[]{:S(2)}) collective-permute-start(bf16[640,512]{1,0:T(8,128)(2,1)} %collective-permute-done.8.refs_5_), channel_id=1, source_target_pairs={{0,8},{8,0},{16,24},{24,16},{1,9},{9,1},{17,25},{25,17},{2,10},{10... | collective-permute-start | bytes 1966088 | tf_op jit(solution)/shard_map/ppermute | solution.py:37
  136.8 101.9 %all-gather.13.cloned.1.call-start = ((), (), s32[]{:S(2)}) async-start(), calls=%async_computation.3 | async-start | bytes 4718592 | tf_op jit(solution)/shard_map/all_gather | solution.py:41
  144.2 94.5 %copy-start.7 = (bf16[1024,1280]{1,0:T(8,128)(2,1)S(1)}, bf16[1024,1280]{1,0:T(8,128)(2,1)}, u32[]{:S(2)}) copy-start(bf16[1024,1280]{1,0:T(8,128)(2,1)} %get-tuple-element.102.stacked.left) | copy-start | bytes 7864324
  193.2 176.7 %all-gather.15.cloned.1.call-start = ((), (), s32[]{:S(2)}) async-start(), calls=%async_computation.4 | async-start | bytes 3538944 | tf_op jit(solution)/shard_map/all_gather | solution.py:950
  241.3 17.6 %collective-permute-start.12 = (bf16[384,512]{1,0:T(8,128)(2,1)}, bf16[384,512]{1,0:T(8,128)(2,1)S(1)}, u32[]{:S(2)}, u32[]{:S(2)}) collective-permute-start(bf16[384,512]{1,0:T(8,128)(2,1)} %convolution_convert_fusion.2), channel_id=1, source_target_pairs={{0,8},{8,0},{16,24},{24,16},{1,9},{9,1},{17,25},{25,17},{2,10},{10... | collective-permute-start | bytes 1179656 | tf_op jit(solution)/shard_map/ppermute | solution.py:37
  245.3 19.6 %collective-permute-start.13 = (bf16[384,512]{1,0:T(8,128)(2,1)}, bf16[384,512]{1,0:T(8,128)(2,1)S(1)}, u32[]{:S(2)}, u32[]{:S(2)}) collective-permute-start(bf16[384,512]{1,0:T(8,128)(2,1)} %convolution_convert_fusion.1), channel_id=1, source_target_pairs={{0,16},{8,24},{16,0},{24,8},{1,17},{9,25},{17,1},{25,9},{2,18},{10... | collective-permute-start | bytes 1179656 | tf_op jit(solution)/shard_map/ppermute | solution.py:37
  249.4 15.6 %collective-permute-start.14 = (bf16[384,512]{1,0:T(8,128)(2,1)}, bf16[384,512]{1,0:T(8,128)(2,1)S(1)}, u32[]{:S(2)}, u32[]{:S(2)}) collective-permute-start(bf16[384,512]{1,0:T(8,128)(2,1)} %convolution_convert_fusion), channel_id=1, source_target_pairs={{0,24},{8,16},{16,8},{24,0},{1,25},{9,17},{17,9},{25,1},{2,26},{10... | collective-permute-start | bytes 1179656 | tf_op jit(solution)/shard_map/ppermute | solution.py:37
  267.9 210.9 %all-gather.17.cloned.1.call-start = ((), (), s32[]{:S(2)}) async-start(), calls=%async_computation.5 | async-start | bytes 8257536 | tf_op jit(solution)/shard_map/all_gather | solution.py:950
  267.9 30.4 %collective-permute-start.15 = (bf16[896,512]{1,0:T(8,128)(2,1)}, bf16[896,512]{1,0:T(8,128)(2,1)S(1)}, u32[]{:S(2)}, u32[]{:S(2)}) collective-permute-start(bf16[896,512]{1,0:T(8,128)(2,1)} %get-tuple-element.119), channel_id=1, source_target_pairs={{0,8},{8,0},{16,24},{24,16},{1,9},{9,1},{17,25},{25,17},{2,10},{10... | collective-permute-start | bytes 2752520 | tf_op jit(solution)/shard_map/ppermute | solution.py:37
  268.6 40.1 %collective-permute-start.16 = (bf16[896,512]{1,0:T(8,128)(2,1)}, bf16[896,512]{1,0:T(8,128)(2,1)}, u32[]{:S(2)}, u32[]{:S(2)}) collective-permute-start(bf16[896,512]{1,0:T(8,128)(2,1)} %get-tuple-element.120), channel_id=1, source_target_pairs={{0,16},{8,24},{16,0},{24,8},{1,17},{9,25},{17,1},{25,9},{2,18},{10... | collective-permute-start | bytes 2752520 | tf_op jit(solution)/shard_map/ppermute | solution.py:37
  270.0 40.2 %collective-permute-start.17 = (bf16[896,512]{1,0:T(8,128)(2,1)}, bf16[896,512]{1,0:T(8,128)(2,1)}, u32[]{:S(2)}, u32[]{:S(2)}) collective-permute-start(bf16[896,512]{1,0:T(8,128)(2,1)} %get-tuple-element.121), channel_id=1, source_target_pairs={{0,24},{8,16},{16,8},{24,0},{1,25},{9,17},{17,9},{25,1},{2,26},{10... | collective-permute-start | bytes 2752520 | tf_op jit(solution)/shard_map/ppermute | solution.py:37
  288.2 22.0 %copy-start.9 = (f32[896,512]{1,0:T(8,128)S(1)}, f32[896,512]{1,0:T(8,128)}, u32[]{:S(2)}) copy-start(f32[896,512]{1,0:T(8,128)} %get-tuple-element.141) | copy-start | bytes 5505028
  313.2 178.6 %all-gather.19.cloned.1.call-start = ((), (), s32[]{:S(2)}) async-start(), calls=%async_computation.6 | async-start | bytes 9437184 | tf_op jit(solution)/shard_map/all_gather | solution.py:950
  313.5 56.4 %collective-permute-start.18 = (bf16[512,1024]{1,0:T(8,128)(2,1)}, bf16[512,1024]{1,0:T(8,128)(2,1)S(1)}, u32[]{:S(2)}, u32[]{:S(2)}) collective-permute-start(bf16[512,1024]{1,0:T(8,128)(2,1)} %get-tuple-element.137), channel_id=1, source_target_pairs={{0,8},{8,0},{16,24},{24,16},{1,9},{9,1},{17,25},{25,17},{2,10},{10... | collective-permute-start | bytes 3145736 | tf_op jit(solution)/shard_map/ppermute | solution.py:37
  314.4 55.5 %collective-permute-start.19 = (bf16[512,1024]{1,0:T(8,128)(2,1)}, bf16[512,1024]{1,0:T(8,128)(2,1)}, u32[]{:S(2)}, u32[]{:S(2)}) collective-permute-start(bf16[512,1024]{1,0:T(8,128)(2,1)} %get-tuple-element.138), channel_id=1, source_target_pairs={{0,16},{8,24},{16,0},{24,8},{1,17},{9,25},{17,1},{25,9},{2,18},{10... | collective-permute-start | bytes 3145736 | tf_op jit(solution)/shard_map/ppermute | solution.py:37
  315.8 54.1 %collective-permute-start.20 = (bf16[512,1024]{1,0:T(8,128)(2,1)}, bf16[512,1024]{1,0:T(8,128)(2,1)}, u32[]{:S(2)}, u32[]{:S(2)}) collective-permute-start(bf16[512,1024]{1,0:T(8,128)(2,1)} %get-tuple-element.139), channel_id=1, source_target_pairs={{0,24},{8,16},{16,8},{24,0},{1,25},{9,17},{17,9},{25,1},{2,26},{10... | collective-permute-start | bytes 3145736 | tf_op jit(solution)/shard_map/ppermute | solution.py:37
  373.3 188.7 %all-gather.21.cloned.1.call-start = ((), (), s32[]{:S(2)}) async-start(), calls=%async_computation.7 | async-start | bytes 7299072 | tf_op jit(solution)/shard_map/all_gather | solution.py:950
  373.3 4.4 collective-permute-start.24
  380.7 13.1 %collective-permute-start.25 = (bf16[128,2048]{1,0:T(8,128)(2,1)S(1)}, bf16[128,2048]{1,0:T(8,128)(2,1)S(1)}, u32[]{:S(2)}, u32[]{:S(2)}) collective-permute-start(bf16[128,2048]{1,0:T(8,128)(2,1)S(1)} %slice.184), channel_id=1, source_target_pairs={{0,2},{1,3},{6,4},{7,5},{8,10},{9,11},{14,12},{15,13},{16,18},{17,... | collective-permute-start | bytes 1572872 | tf_op jit(solution)/shard_map/ppermute | solution.py:45
  393.9 7.1 %collective-permute-start.28 = (bf16[128,2048]{1,0:T(8,128)(2,1)S(1)}, bf16[128,2048]{1,0:T(8,128)(2,1)S(1)}, u32[]{:S(2)}, u32[]{:S(2)}) collective-permute-start(bf16[128,2048]{1,0:T(8,128)(2,1)S(1)} %fusion), channel_id=1, source_target_pairs={{6,4},{7,5},{4,2},{5,3},{14,12},{15,13},{12,10},{13,11},{22,20},{2... | collective-permute-start | bytes 1572872 | tf_op jit(solution)/shard_map/ppermute | solution.py:45
  394.6 28.0 %collective-permute-start.26 = (bf16[128,2048]{1,0:T(8,128)(2,1)S(1)}, bf16[128,2048]{1,0:T(8,128)(2,1)S(1)}, u32[]{:S(2)}, u32[]{:S(2)}) collective-permute-start(bf16[128,2048]{1,0:T(8,128)(2,1)S(1)} %fusion), channel_id=1, source_target_pairs={{0,2},{1,3},{2,4},{3,5},{8,10},{9,11},{10,12},{11,13},{16,18},{17,... | collective-permute-start | bytes 1572872 | tf_op jit(solution)/shard_map/ppermute | solution.py:45
  399.6 44.4 %copy-start.2 = (bf16[1024,2048]{1,0:T(8,128)(2,1)S(1)}, bf16[1024,2048]{1,0:T(8,128)(2,1)}, u32[]{:S(2)}) copy-start(bf16[1024,2048]{1,0:T(8,128)(2,1)} %all-gather.13.cloned.1.call-done.right.grads) | copy-start | bytes 12582916
  424.4 24.3 %copy-start.1 = (bf16[1024,1792]{1,0:T(8,128)(2,1)S(1)}, bf16[1024,1792]{1,0:T(8,128)(2,1)}, u32[]{:S(2)}) copy-start(bf16[1024,1792]{1,0:T(8,128)(2,1)} %attend_back.1.right.entered) | copy-start | bytes 11010052
  424.4 40.0 %collective-permute-start.27 = (bf16[128,2048]{1,0:T(8,128)(2,1)S(1)}, bf16[128,2048]{1,0:T(8,128)(2,1)S(1)}, u32[]{:S(2)}, u32[]{:S(2)}) collective-permute-start(bf16[128,2048]{1,0:T(8,128)(2,1)S(1)} %get-tuple-element.180), channel_id=1, source_target_pairs={{0,2},{1,3},{2,4},{3,5},{4,6},{5,7},{8,10},{9,11},{10,12},{11,13},... | collective-permute-start | bytes 1572872 | tf_op jit(solution)/shard_map/ppermute | solution.py:45
  442.4 31.3 %collective-permute-start.29 = (bf16[128,2048]{1,0:T(8,128)(2,1)S(1)}, bf16[128,2048]{1,0:T(8,128)(2,1)S(1)}, u32[]{:S(2)}, u32[]{:S(2)}) collective-permute-start(bf16[128,2048]{1,0:T(8,128)(2,1)S(1)} %get-tuple-element.181), channel_id=1, source_target_pairs={{6,4},{7,5},{4,2},{5,3},{2,0},{3,1},{14,12},{15,13},{12,10},{13,11... | collective-permute-start | bytes 1572872 | tf_op jit(solution)/shard_map/ppermute | solution.py:45
  445.2 30.8 %collective-permute-start.21 = (bf16[512,768]{1,0:T(8,128)(2,1)}, bf16[512,768]{1,0:T(8,128)(2,1)S(1)}, u32[]{:S(2)}, u32[]{:S(2)}) collective-permute-start(bf16[512,768]{1,0:T(8,128)(2,1)} %get-tuple-element.155), channel_id=1, source_target_pairs={{0,8},{8,0},{16,24},{24,16},{1,9},{9,1},{17,25},{25,17},{2,10},{10... | collective-permute-start | bytes 2359304 | tf_op jit(solution)/shard_map/ppermute | solution.py:37
  445.2 33.5 %collective-permute-start.22 = (bf16[512,768]{1,0:T(8,128)(2,1)}, bf16[512,768]{1,0:T(8,128)(2,1)}, u32[]{:S(2)}, u32[]{:S(2)}) collective-permute-start(bf16[512,768]{1,0:T(8,128)(2,1)} %get-tuple-element.156), channel_id=1, source_target_pairs={{0,16},{8,24},{16,0},{24,8},{1,17},{9,25},{17,1},{25,9},{2,18},{10... | collective-permute-start | bytes 2359304 | tf_op jit(solution)/shard_map/ppermute | solution.py:37
  445.4 33.4 %collective-permute-start.23 = (bf16[512,768]{1,0:T(8,128)(2,1)}, bf16[512,768]{1,0:T(8,128)(2,1)}, u32[]{:S(2)}, u32[]{:S(2)}) collective-permute-start(bf16[512,768]{1,0:T(8,128)(2,1)} %get-tuple-element.157), channel_id=1, source_target_pairs={{0,24},{8,16},{16,8},{24,0},{1,25},{9,17},{17,9},{25,1},{2,26},{10... | collective-permute-start | bytes 2359304 | tf_op jit(solution)/shard_map/ppermute | solution.py:37
  449.3 38.3 %copy-start.10 = (f32[512,768]{1,0:T(8,128)S(1)}, f32[512,768]{1,0:T(8,128)}, u32[]{:S(2)}) copy-start(f32[512,768]{1,0:T(8,128)} %get-tuple-element.154) | copy-start | bytes 4718596
  484.0 5.3 collective-permute-start.31
  485.5 4.8 collective-permute-start.32
  486.7 3.9 collective-permute-start.30
  504.6 70.3 %copy-start.17 = (f32[1,2048]{1,0:T(1,128)}, f32[1,2048]{1,0:T(1,128)S(1)}, u32[]{:S(2)}) copy-start(f32[1,2048]{1,0:T(1,128)S(1)} %slice.134) | copy-start | bytes 24580
  (10 other events, 51.8 us)
Sparse Core Ops, SparseCore 0:
  13.9 52.2 all-gather.10
  136.9 53.2 reduce-scatter.1
  193.4 45.3 all-gather.12
  268.0 36.0 all-gather.14
  313.3 71.4 all-gather.16
  386.9 102.6 all-gather.18
  491.9 70.0 all-gather.20

commit v6 on v5

--- a/solution.py
+++ b/solution.py
@@ -773,7 +773,7 @@
 
 def widen_columns(gathered, rows, groups):
     count, _, columns = gathered.shape
-    tall = min(64, rows)
+    tall = min(128, rows)
     moved = 6 * count * rows * columns
     return pl.pallas_call(
         functools.partial(widen_columns_kernel, groups),
@@ -949,7 +949,7 @@
     def gather(array):
         return lax.all_gather(array, "seq", axis=0, tiled=False)
 
-    cut = units * 5 // 8 // LANES * LANES
+    cut = units // 2 // LANES * LANES
 
     def of_stacked(first, last):
         return [owned(stacked[:, first:last], piece(grad_all, k)) for k in range(data_count)]

time: 586 us -> 583 us (level)
  transfers between devices with their start and end apart: 40 -> 40, of which waited for: 19 -> 19; matrix products, arithmetic and copies ran while one was open for 7% -> 7% of each run, Pallas kernels for 27% -> 26%
where the time goes in v6:
time: 583 us; the launch traced here: 581 us
  waiting for transfers between devices  273 us (47%)
  Pallas kernels  177 us (30%)
  starting transfers between devices  61.1 us (10%)
  other arithmetic  30.9 us (5%)
  between operations  17 us (3%)
  local copies, waits for them, and re-layouts  13.8 us (2%)
  matrix products  9.28 us (2%)
    ppermute x28, waiting for transfers between devices, swap(): lax.ppermute(array, axis, [(s, s ^ bit) for s in range(lax.axis_size(axis...  77.8 us
    ppermute x5, waiting for transfers between devices, between(): lax.ppermute(array, 'seq', [(2 * a + core, 2 * b + core) for a, b in pair...  57 us
    all_gather x4, waiting for transfers between devices, gather(): return lax.all_gather(array, 'seq', axis=0, tiled=False)  47.4 us
    all_gather x2, waiting for transfers between devices, gather_seq(): return lax.all_gather(rows, 'seq', axis=0, tiled=True)  45.3 us
    reduce_scatter x1, waiting for transfers between devices, scatter_seq(): return lax.psum_scatter(partial, 'seq', scatter_dimension=0, tiled=True)  44.9 us
    ppermute x28, starting transfers between devices, swap(): lax.ppermute(array, axis, [(s, s ^ bit) for s in range(lax.axis_size(axis...  33.6 us
    pallas_call x1, Pallas kernels, attend_back(): pl.pallas_call(functools.partial(attend_back_kernel, 128), grid=(1,), in_...  29.4 us
    ppermute x5, starting transfers between devices, between(): lax.ppermute(array, 'seq', [(2 * a + core, 2 * b + core) for a, b in pair...  26.8 us
  transfers between devices with their start and end apart: 40, of which 19 were waited for; matrix products, arithmetic and copies ran while one was open for 7% of the time, Pallas kernels for 26%

profile of v6, /device:TPU:0, one launch (start us, length us, event | category | flops | bytes accessed | tf_op | source)
XLA Modules:
  0.0 581.4 jit_solution(7710388457260358932)
XLA Ops:
  7.2 3.6 pick.2
  10.8 3.0 enter.1
  13.9 3.0 collective-permute-start.3
  18.4 20.3 %collective-permute-done.3.refs_5_.refs_2_ = bf16[272,1792]{1,0:T(8,128)(2,1)S(1)} collective-permute-done((bf16[272,1792]{1,0:T(8,128)(2,1)}, bf16[272,1792]{1,0:T(8,128)(2,1)S(1)}, u32[]{:S(2)}, u32[]{:S(2)}) %collective-permute-start.3) | collective-permute-done | bytes 974880 | tf_op jit(solution)/shard_map/ppermute | solution.py:37
  44.3 3.1 pick.3
  48.0 16.1 %collective-permute-done.4.refs_6_ = bf16[256,1792]{1,0:T(8,128)(2,1)} collective-permute-done((bf16[256,1792]{1,0:T(8,128)(2,1)}, bf16[256,1792]{1,0:T(8,128)(2,1)}, u32[]{:S(2)}, u32[]{:S(2)}) %collective-permute-start.4) | collective-permute-done | bytes 917536 | tf_op jit(solution)/shard_map/ppermute | solution.py:37
  69.0 3.1 fusion.15
  72.1 11.6 %collective-permute-done.2.refs_4_ = bf16[256,1792]{1,0:T(8,128)(2,1)} collective-permute-done((bf16[256,1792]{1,0:T(8,128)(2,1)}, bf16[256,1792]{1,0:T(8,128)(2,1)}, u32[]{:S(2)}, u32[]{:S(2)}) %collective-permute-start.2) | collective-permute-done | bytes 917536 | tf_op jit(solution)/shard_map/ppermute | solution.py:37
  86.2 16.9 %project.1 = (bf16[1024,768]{1,0:T(8,128)(2,1)}, f32[1024,1024]{1,0:T(8,128)}, bf16[1024,1280]{1,0:T(8,128)(2,1)}) custom-call(bf16[1024,2176]{1,0:T(8,128)(2,1)} %all-gather.11.cloned.1.call-done.normed.left, f32[1024,128]{1,0:T(8,128)} %get-tuple-element.190.cosine, f32[1024,128]{1,0:T(8,128)} %get-tuple-element.189.sine, ...), custom_call_target="tpu_custom_call" | custom-call | flops 7516192768 | bytes 26214400 | tf_op jit(solution)/shard_map/project/pallas_call | solution.py:309
  103.1 13.5 %attend.1 = (bf16[1024,1280]{1,0:T(8,128)(2,1)}, f32[1024,128]{1,0:T(8,128)}) custom-call(bf16[1024,768]{1,0:T(8,128)(2,1)} %get-tuple-element.100.qkv, bf16[1024,1280]{1,0:T(8,128)(2,1)} %get-tuple-element.101.stacked), custom_call_target="tpu_custom_call", output_to_operand_aliasing={{0}: (1, {})} | custom-call | flops 2147483648 | bytes 6291456 | tf_op jit(solution)/shard_map/attend/pallas_call | solution.py:481
  118.8 10.2 %emit.2.refs_6_ = bf16[1024,2176]{1,0:T(8,128)(2,1)} custom-call(bf16[1024,1280]{1,0:T(8,128)(2,1)} %get-tuple-element.102.stacked.left, bf16[640,512]{1,0:T(8,128)(2,1)} %get-tuple-element.106.refs_0_, bf16[640,512]{1,0:T(8,128)(2,1)} %get-tuple-element.108.refs_1_, bf16[640,512]{1,0:T(8,128)(2,1)} %collective-permute-done.6.refs_2_, ...), custom_call_target="tpu_custom_call" | custom-call | flops 4026531840 | bytes 9699328 | tf_op jit(solution)/shard_map/emit/pallas_call | solution.py:409
  131.0 5.7 emit.3
  139.2 2.5 pad_maximum_fusion.1.refs_1_
  141.7 2.4 pad_maximum_fusion.2.refs_2_
  145.3 44.9 %reduce-scatter.2.cloned.1.call-done.branches = bf16[128,2176]{1,0:T(8,128)(2,1)} async-done(((bf16[1024,2176]{1,0:T(8,128)(2,1)}), bf16[128,2176]{1,0:T(8,128)(2,1)}) %reduce-scatter.2.cloned.1.call-update) | async-done | bytes 557072 | tf_op jit(solution)/shard_map/reduce_scatter | solution.py:77
  190.3 3.0 grade.1
  193.5 45.3 %all-gather.13.cloned.1.call-done.right.grads = bf16[1024,2048]{1,0:T(8,128)(2,1)} async-done(((bf16[128,2048]{1,0:T(8,128)(2,1)}), bf16[1024,2048]{1,0:T(8,128)(2,1)}) %all-gather.13.cloned.1.call-update) | async-done | bytes 4194320 | tf_op jit(solution)/shard_map/all_gather | solution.py:41
  238.8 2.9 convolution_convert_fusion.2
  248.2 8.2 %outer.3 = (f32[768,512]{1,0:T(8,128)}, bf16[768,512]{1,0:T(8,128)(2,1)}, bf16[768,512]{1,0:T(8,128)(2,1)}, bf16[768,512]{1,0:T(8,128)(2,1)}) custom-call(bf16[1024,1280]{1,0:T(8,128)(2,1)} %get-tuple-element.102.stacked.left, bf16[1024,2048]{1,0:T(8,128)(2,1)} %all-gather.13.cloned.1.call-done.right.grads), custom_call_target="tpu_custom_call" | custom-call | flops 3221225472 | bytes 3145728 | tf_op jit(solution)/shard_map/outer/pallas_call | solution.py:653
  256.6 13.4 %collective-permute-done.13 = bf16[512,512]{1,0:T(8,128)(2,1)} collective-permute-done((bf16[512,512]{1,0:T(8,128)(2,1)}, bf16[512,512]{1,0:T(8,128)(2,1)}, u32[]{:S(2)}, u32[]{:S(2)}) %collective-permute-start.13) | collective-permute-done | bytes 524320 | tf_op jit(solution)/shard_map/ppermute | solution.py:37
  270.0 3.3 add_convert_fusion.5
  277.0 13.7 %reject.1 = (bf16[1024,256]{1,0:T(8,128)(2,1)}, bf16[1024,1792]{1,0:T(8,128)(2,1)}) custom-call(f32[1024,1024]{1,0:T(8,128)} %get-tuple-element.122.hidden, bf16[1024,2048]{1,0:T(8,128)(2,1)} %all-gather.13.cloned.1.call-done.right.grads, bf16[1280,512]{1,0:T(8,128)(2,1)} %pad_maximum_fusion.refs_0_, bf16[1280,512]{1,0:T(8,128)(2,1)} %pad_maximum_fusion.1.refs_1_, ...), custom_call_target="tpu_custom_call" | custom-call | flops 5368709120 | bytes 19922944 | tf_op jit(solution)/shard_map/reject/pallas_call | solution.py:604
  290.6 3.1 slice.95.right
  293.7 10.1 %outer.4 = (f32[512,1024]{1,0:T(8,128)}, bf16[512,1024]{1,0:T(8,128)(2,1)}, bf16[512,1024]{1,0:T(8,128)(2,1)}, bf16[512,1024]{1,0:T(8,128)(2,1)}) custom-call(bf16[1024,2176]{1,0:T(8,128)(2,1)} %all-gather.11.cloned.1.call-done.normed.left, bf16[1024,1024]{1,0:T(8,128)(2,1)} %slice.95.right), custom_call_target="tpu_custom_call" | custom-call | flops 4294967296 | bytes 4194304 | tf_op jit(solution)/shard_map/outer/pallas_call | solution.py:653
  303.8 6.3 %collective-permute-done.17 = bf16[768,512]{1,0:T(8,128)(2,1)} collective-permute-done((bf16[768,512]{1,0:T(8,128)(2,1)}, bf16[768,512]{1,0:T(8,128)(2,1)}, u32[]{:S(2)}, u32[]{:S(2)}) %collective-permute-start.17) | collective-permute-done | bytes 786464 | tf_op jit(solution)/shard_map/ppermute | solution.py:37
  310.1 2.5 add_convert_fusion.2
  316.4 29.4 %attend_back.1.right.entered = bf16[1024,1792]{1,0:T(8,128)(2,1)} custom-call(bf16[1024,768]{1,0:T(8,128)(2,1)} %get-tuple-element.100.qkv, bf16[1024,256]{1,0:T(8,128)(2,1)} %get-tuple-element.145.grad, f32[1024,128]{1,0:T(8,128)} %get-tuple-element.146.logsum, f32[1024,128]{1,0:T(8,128)} %get-tuple-element.190.cosine, ...), custom_call_target="tpu_custom_call", output_to_operand_aliasing={{}: (5, {})} | custom-call | flops 5368709120 | bytes 6291456 | tf_op jit(solution)/shard_map/attend_back/pallas_call | solution.py:558
  345.8 8.4 %outer.5 = (f32[512,768]{1,0:T(8,128)}, bf16[512,768]{1,0:T(8,128)(2,1)}, bf16[512,768]{1,0:T(8,128)(2,1)}, bf16[512,768]{1,0:T(8,128)(2,1)}) custom-call(bf16[1024,2176]{1,0:T(8,128)(2,1)} %all-gather.11.cloned.1.call-done.normed.left, bf16[1024,1792]{1,0:T(8,128)(2,1)} %attend_back.1.right.entered), custom_call_target="tpu_custom_call" | custom-call | flops 3221225472 | bytes 3145728 | tf_op jit(solution)/shard_map/outer/pallas_call | solution.py:653
  354.2 14.8 %answer.1 = (f32[512,2048]{1,0:T(8,128)}, bf16[512,2048]{1,0:T(8,128)(2,1)}) custom-call(s32[1]{0:T(128)} %bitcast.part, bf16[1024,1792]{1,0:T(8,128)(2,1)} %attend_back.1.right.entered, bf16[256,1792]{1,0:T(8,128)(2,1)} %get-tuple-element.96.refs_0_, bf16[272,1792]{1,0:T(8,128)(2,1)} %get-tuple-element.97.refs_1_.refs_0_, ...), custom_call_target="tpu_custom_call" | custom-call | flops 7516192768 | bytes 17301504 | tf_op jit(solution)/shard_map/answer/pallas_call | solution.py:705
  369.1 3.3 add_convert_fusion
  372.5 4.4 collective-permute-done.24
  376.8 2.8 convert_add_fusion
  379.7 2.0 collective-permute-start.25
  381.7 11.4 %collective-permute-done.25 = bf16[128,2048]{1,0:T(8,128)(2,1)S(1)} collective-permute-done((bf16[128,2048]{1,0:T(8,128)(2,1)S(1)}, bf16[128,2048]{1,0:T(8,128)(2,1)S(1)}, u32[]{:S(2)}, u32[]{:S(2)}) %collective-permute-start.25) | collective-permute-done | bytes 524320 | tf_op jit(solution)/shard_map/ppermute | solution.py:45
  393.9 5.1 collective-permute-start.26
  400.4 21.5 %collective-permute-done.26 = bf16[128,2048]{1,0:T(8,128)(2,1)S(1)} collective-permute-done((bf16[128,2048]{1,0:T(8,128)(2,1)S(1)}, bf16[128,2048]{1,0:T(8,128)(2,1)S(1)}, u32[]{:S(2)}, u32[]{:S(2)}) %collective-permute-start.26) | collective-permute-done | bytes 524320 | tf_op jit(solution)/shard_map/ppermute | solution.py:45
  421.9 2.0 add_convert_fusion.4
  423.9 17.5 %collective-permute-start.27 = (bf16[128,2048]{1,0:T(8,128)(2,1)S(1)}, bf16[128,2048]{1,0:T(8,128)(2,1)S(1)}, u32[]{:S(2)}, u32[]{:S(2)}) collective-permute-start(bf16[128,2048]{1,0:T(8,128)(2,1)S(1)} %get-tuple-element.180), channel_id=1, source_target_pairs={{0,2},{1,3},{2,4},{3,5},{4,6},{5,7},{8,10},{9,11},{10,12},{11,13},... | collective-permute-start | bytes 1572872 | tf_op jit(solution)/shard_map/ppermute | solution.py:45
  444.5 3.2 collective-permute-start.23
  448.2 15.2 %collective-permute-done.27 = bf16[128,2048]{1,0:T(8,128)(2,1)S(1)} collective-permute-done((bf16[128,2048]{1,0:T(8,128)(2,1)S(1)}, bf16[128,2048]{1,0:T(8,128)(2,1)S(1)}, u32[]{:S(2)}, u32[]{:S(2)}) %collective-permute-start.27) | collective-permute-done | bytes 524320 | tf_op jit(solution)/shard_map/ppermute | solution.py:45
  463.5 8.9 %collective-permute-done.29 = bf16[128,2048]{1,0:T(8,128)(2,1)S(1)} collective-permute-done((bf16[128,2048]{1,0:T(8,128)(2,1)S(1)}, bf16[128,2048]{1,0:T(8,128)(2,1)S(1)}, u32[]{:S(2)}, u32[]{:S(2)}) %collective-permute-start.29) | collective-permute-done | bytes 524320 | tf_op jit(solution)/shard_map/ppermute | solution.py:45
  472.4 2.4 fusion.1.summed
  474.8 2.9 collective-permute-done.22
  477.7 3.7 leave.1
  491.6 12.1 %widen_rows.1 = (f32[8192,512]{1,0:T(8,128)}, f32[2048,512]{1,0:T(8,128)}) custom-call(bf16[8,512,512]{2,1,0:T(8,128)(2,1)} %bitcast.35, bf16[8,768,512]{2,1,0:T(8,128)(2,1)} %bitcast.34), custom_call_target="tpu_custom_call" | custom-call | bytes 31457280 | tf_op jit(solution)/shard_map/widen_rows/pallas_call | solution.py:743
  503.8 9.6 %widen_columns.2 = f32[512,8192]{1,0:T(8,128)} custom-call(bf16[8,512,1024]{2,1,0:T(8,128)(2,1)} %bitcast.31), custom_call_target="tpu_custom_call" | custom-call | bytes 25165824 | tf_op jit(solution)/shard_map/widen_columns/pallas_call | solution.py:778
  513.4 47.4 %all-gather.21.cloned.1.call-done = bf16[4224,768]{1,0:T(8,128)(2,1)} async-done(((bf16[528,768]{1,0:T(8,128)(2,1)}), bf16[4224,768]{1,0:T(8,128)(2,1)}) %all-gather.21.cloned.1.call-update) | async-done | bytes 6488080 | tf_op jit(solution)/shard_map/all_gather | solution.py:950
  563.0 7.9 %widen_columns.3 = f32[512,6144]{1,0:T(8,128)} custom-call(bf16[8,528,768]{2,1,0:T(8,128)(2,1)} %bitcast.33), custom_call_target="tpu_custom_call" | custom-call | bytes 18874368 | tf_op jit(solution)/shard_map/widen_columns/pallas_call | solution.py:778
  (146 shorter events, 57.1 us)
Async XLA Ops:
  7.2 60.5 %all-gather.11.cloned.1.call-start = ((), (), s32[]{:S(2)}) async-start(), calls=%async_computation.1 | async-start | bytes 5013504 | tf_op jit(solution)/shard_map/all_gather | solution.py:41
  13.8 176.4 %reduce-scatter.2.cloned.1.call-start = ((), (), s32[]{:S(2)}) async-start(), calls=%async_computation.2 | async-start | bytes 5013504 | tf_op jit(solution)/shard_map/reduce_scatter | solution.py:77
  13.9 24.8 %collective-permute-start.3 = (bf16[272,1792]{1,0:T(8,128)(2,1)}, bf16[272,1792]{1,0:T(8,128)(2,1)S(1)}, u32[]{:S(2)}, u32[]{:S(2)}) collective-permute-start(bf16[272,1792]{1,0:T(8,128)(2,1)} %get-tuple-element.97.refs_1_.refs_0_), channel_id=1, source_target_pairs={{0,16},{8,24},{16,0},{24,8},{1,17},{9,25},{17,1},{25,9},{2,18},{10... | collective-permute-start | bytes 2924552 | tf_op jit(solution)/shard_map/ppermute | solution.py:37
  16.9 23.5 %collective-permute-start = (bf16[256,1792]{1,0:T(8,128)(2,1)}, bf16[256,1792]{1,0:T(8,128)(2,1)}, u32[]{:S(2)}, u32[]{:S(2)}) collective-permute-start(bf16[256,1792]{1,0:T(8,128)(2,1)} %get-tuple-element.96.refs_0_), channel_id=1, source_target_pairs={{0,8},{8,0},{16,24},{24,16},{1,9},{9,1},{17,25},{25,17},{2,10},{10... | collective-permute-start | bytes 2752520 | tf_op jit(solution)/shard_map/ppermute | solution.py:37
  38.7 25.3 %collective-permute-start.5 = (bf16[272,1792]{1,0:T(8,128)(2,1)S(1)}, bf16[272,1792]{1,0:T(8,128)(2,1)S(1)}, u32[]{:S(2)}, u32[]{:S(2)}) collective-permute-start(bf16[272,1792]{1,0:T(8,128)(2,1)S(1)} %collective-permute-done.3.refs_5_.refs_2_), channel_id=1, source_target_pairs={{0,8},{8,0},{16,24},{24,16},{1,9},{9,1},{17,25},{25,17},{2,10},{10... | collective-permute-start | bytes 2924552 | tf_op jit(solution)/shard_map/ppermute | solution.py:37
  40.4 23.6 %collective-permute-start.4 = (bf16[256,1792]{1,0:T(8,128)(2,1)}, bf16[256,1792]{1,0:T(8,128)(2,1)}, u32[]{:S(2)}, u32[]{:S(2)}) collective-permute-start(bf16[256,1792]{1,0:T(8,128)(2,1)} %collective-permute-done.refs_2_), channel_id=1, source_target_pairs={{0,16},{8,24},{16,0},{24,8},{1,17},{9,25},{17,1},{25,9},{2,18},{10... | collective-permute-start | bytes 2752520 | tf_op jit(solution)/shard_map/ppermute | solution.py:37
  41.9 41.7 %collective-permute-start.2 = (bf16[256,1792]{1,0:T(8,128)(2,1)}, bf16[256,1792]{1,0:T(8,128)(2,1)}, u32[]{:S(2)}, u32[]{:S(2)}) collective-permute-start(bf16[256,1792]{1,0:T(8,128)(2,1)} %get-tuple-element.96.refs_0_), channel_id=1, source_target_pairs={{0,16},{8,24},{16,0},{24,8},{1,17},{9,25},{17,1},{25,9},{2,18},{10... | collective-permute-start | bytes 2752520 | tf_op jit(solution)/shard_map/ppermute | solution.py:37
  42.4 42.8 %collective-permute-start.1 = (bf16[272,1792]{1,0:T(8,128)(2,1)}, bf16[272,1792]{1,0:T(8,128)(2,1)S(1)}, u32[]{:S(2)}, u32[]{:S(2)}) collective-permute-start(bf16[272,1792]{1,0:T(8,128)(2,1)} %get-tuple-element.97.refs_1_.refs_0_), channel_id=1, source_target_pairs={{0,8},{8,0},{16,24},{24,16},{1,9},{9,1},{17,25},{25,17},{2,10},{10... | collective-permute-start | bytes 2924552 | tf_op jit(solution)/shard_map/ppermute | solution.py:37
  64.0 21.2 %copy-start.13 = (bf16[272,1792]{1,0:T(8,128)(2,1)}, bf16[272,1792]{1,0:T(8,128)(2,1)S(1)}, u32[]{:S(2)}) copy-start(bf16[272,1792]{1,0:T(8,128)(2,1)S(1)} %collective-permute-done.5.refs_7_.refs_3_) | copy-start | bytes 2924548
  64.0 19.7 %copy-start.16 = (bf16[640,512]{1,0:T(8,128)(2,1)S(1)}, bf16[640,512]{1,0:T(8,128)(2,1)}, u32[]{:S(2)}) copy-start(bf16[640,512]{1,0:T(8,128)(2,1)} %get-tuple-element.108.refs_1_) | copy-start | bytes 1966084
  64.0 54.7 %collective-permute-start.11 = (bf16[640,512]{1,0:T(8,128)(2,1)}, bf16[640,512]{1,0:T(8,128)(2,1)}, u32[]{:S(2)}, u32[]{:S(2)}) collective-permute-start(bf16[640,512]{1,0:T(8,128)(2,1)} %get-tuple-element.106.refs_0_), channel_id=1, source_target_pairs={{0,16},{8,24},{16,0},{24,8},{1,17},{9,25},{17,1},{25,9},{2,18},{10... | collective-permute-start | bytes 1966088 | tf_op jit(solution)/shard_map/ppermute | solution.py:37
  65.6 51.0 %collective-permute-start.6 = (bf16[640,512]{1,0:T(8,128)(2,1)}, bf16[640,512]{1,0:T(8,128)(2,1)}, u32[]{:S(2)}, u32[]{:S(2)}) collective-permute-start(bf16[640,512]{1,0:T(8,128)(2,1)} %get-tuple-element.106.refs_0_), channel_id=1, source_target_pairs={{0,8},{8,0},{16,24},{24,16},{1,9},{9,1},{17,25},{25,17},{2,10},{10... | collective-permute-start | bytes 1966088 | tf_op jit(solution)/shard_map/ppermute | solution.py:37
  66.5 52.3 %collective-permute-start.10 = (bf16[640,512]{1,0:T(8,128)(2,1)}, bf16[640,512]{1,0:T(8,128)(2,1)}, u32[]{:S(2)}, u32[]{:S(2)}) collective-permute-start(bf16[640,512]{1,0:T(8,128)(2,1)} %get-tuple-element.108.refs_1_), channel_id=1, source_target_pairs={{0,8},{8,0},{16,24},{24,16},{1,9},{9,1},{17,25},{25,17},{2,10},{10... | collective-permute-start | bytes 1966088 | tf_op jit(solution)/shard_map/ppermute | solution.py:37
  83.7 32.9 %collective-permute-start.8 = (bf16[640,512]{1,0:T(8,128)(2,1)S(1)}, bf16[640,512]{1,0:T(8,128)(2,1)}, u32[]{:S(2)}, u32[]{:S(2)}) collective-permute-start(bf16[640,512]{1,0:T(8,128)(2,1)S(1)} %copy-done.16), channel_id=1, source_target_pairs={{0,16},{8,24},{16,0},{24,8},{1,17},{9,25},{17,1},{25,9},{2,18},{10... | collective-permute-start | bytes 1966088 | tf_op jit(solution)/shard_map/ppermute | solution.py:37
  116.6 12.7 %collective-permute-start.7 = (bf16[640,512]{1,0:T(8,128)(2,1)}, bf16[640,512]{1,0:T(8,128)(2,1)S(1)}, u32[]{:S(2)}, u32[]{:S(2)}) collective-permute-start(bf16[640,512]{1,0:T(8,128)(2,1)} %collective-permute-done.6.refs_2_), channel_id=1, source_target_pairs={{0,16},{8,24},{16,0},{24,8},{1,17},{9,25},{17,1},{25,9},{2,18},{10... | collective-permute-start | bytes 1966088 | tf_op jit(solution)/shard_map/ppermute | solution.py:37
  117.3 12.9 %collective-permute-start.9 = (bf16[640,512]{1,0:T(8,128)(2,1)}, bf16[640,512]{1,0:T(8,128)(2,1)S(1)}, u32[]{:S(2)}, u32[]{:S(2)}) collective-permute-start(bf16[640,512]{1,0:T(8,128)(2,1)} %collective-permute-done.8.refs_5_), channel_id=1, source_target_pairs={{0,8},{8,0},{16,24},{24,16},{1,9},{9,1},{17,25},{25,17},{2,10},{10... | collective-permute-start | bytes 1966088 | tf_op jit(solution)/shard_map/ppermute | solution.py:37
  136.8 102.0 %all-gather.13.cloned.1.call-start = ((), (), s32[]{:S(2)}) async-start(), calls=%async_computation.3 | async-start | bytes 4718592 | tf_op jit(solution)/shard_map/all_gather | solution.py:41
  144.2 94.6 %copy-start.8 = (bf16[1024,1280]{1,0:T(8,128)(2,1)S(1)}, bf16[1024,1280]{1,0:T(8,128)(2,1)}, u32[]{:S(2)}) copy-start(bf16[1024,1280]{1,0:T(8,128)(2,1)} %get-tuple-element.102.stacked.left) | copy-start | bytes 7864324
  193.3 175.8 %all-gather.15.cloned.1.call-start = ((), (), s32[]{:S(2)}) async-start(), calls=%async_computation.4 | async-start | bytes 4718592 | tf_op jit(solution)/shard_map/all_gather | solution.py:950
  241.7 15.0 %collective-permute-start.12 = (bf16[512,512]{1,0:T(8,128)(2,1)}, bf16[512,512]{1,0:T(8,128)(2,1)S(1)}, u32[]{:S(2)}, u32[]{:S(2)}) collective-permute-start(bf16[512,512]{1,0:T(8,128)(2,1)} %convolution_convert_fusion.2), channel_id=1, source_target_pairs={{0,8},{8,0},{16,24},{24,16},{1,9},{9,1},{17,25},{25,17},{2,10},{10... | collective-permute-start | bytes 1572872 | tf_op jit(solution)/shard_map/ppermute | solution.py:37
  244.7 25.3 %collective-permute-start.13 = (bf16[512,512]{1,0:T(8,128)(2,1)}, bf16[512,512]{1,0:T(8,128)(2,1)}, u32[]{:S(2)}, u32[]{:S(2)}) collective-permute-start(bf16[512,512]{1,0:T(8,128)(2,1)} %convolution_convert_fusion.1), channel_id=1, source_target_pairs={{0,16},{8,24},{16,0},{24,8},{1,17},{9,25},{17,1},{25,9},{2,18},{10... | collective-permute-start | bytes 1572872 | tf_op jit(solution)/shard_map/ppermute | solution.py:37
  247.7 22.3 %collective-permute-start.14 = (bf16[512,512]{1,0:T(8,128)(2,1)}, bf16[512,512]{1,0:T(8,128)(2,1)S(1)}, u32[]{:S(2)}, u32[]{:S(2)}) collective-permute-start(bf16[512,512]{1,0:T(8,128)(2,1)} %convolution_convert_fusion), channel_id=1, source_target_pairs={{0,24},{8,16},{16,8},{24,0},{1,25},{9,17},{17,9},{25,1},{2,26},{10... | collective-permute-start | bytes 1572872 | tf_op jit(solution)/shard_map/ppermute | solution.py:37
  273.4 204.4 %all-gather.17.cloned.1.call-start = ((), (), s32[]{:S(2)}) async-start(), calls=%async_computation.5 | async-start | bytes 7077888 | tf_op jit(solution)/shard_map/all_gather | solution.py:950
  273.4 30.4 %collective-permute-start.15 = (bf16[768,512]{1,0:T(8,128)(2,1)}, bf16[768,512]{1,0:T(8,128)(2,1)S(1)}, u32[]{:S(2)}, u32[]{:S(2)}) collective-permute-start(bf16[768,512]{1,0:T(8,128)(2,1)} %get-tuple-element.119), channel_id=1, source_target_pairs={{0,8},{8,0},{16,24},{24,16},{1,9},{9,1},{17,25},{25,17},{2,10},{10... | collective-permute-start | bytes 2359304 | tf_op jit(solution)/shard_map/ppermute | solution.py:37
  274.0 29.8 %collective-permute-start.16 = (bf16[768,512]{1,0:T(8,128)(2,1)}, bf16[768,512]{1,0:T(8,128)(2,1)S(1)}, u32[]{:S(2)}, u32[]{:S(2)}) collective-permute-start(bf16[768,512]{1,0:T(8,128)(2,1)} %get-tuple-element.120), channel_id=1, source_target_pairs={{0,16},{8,24},{16,0},{24,8},{1,17},{9,25},{17,1},{25,9},{2,18},{10... | collective-permute-start | bytes 2359304 | tf_op jit(solution)/shard_map/ppermute | solution.py:37
  275.5 34.6 %collective-permute-start.17 = (bf16[768,512]{1,0:T(8,128)(2,1)}, bf16[768,512]{1,0:T(8,128)(2,1)}, u32[]{:S(2)}, u32[]{:S(2)}) collective-permute-start(bf16[768,512]{1,0:T(8,128)(2,1)} %get-tuple-element.121), channel_id=1, source_target_pairs={{0,24},{8,16},{16,8},{24,0},{1,25},{9,17},{17,9},{25,1},{2,26},{10... | collective-permute-start | bytes 2359304 | tf_op jit(solution)/shard_map/ppermute | solution.py:37
  293.7 16.4 %copy-start.11 = (f32[768,512]{1,0:T(8,128)S(1)}, f32[768,512]{1,0:T(8,128)}, u32[]{:S(2)}) copy-start(f32[768,512]{1,0:T(8,128)} %get-tuple-element.141) | copy-start | bytes 4718596
  312.6 178.3 %all-gather.19.cloned.1.call-start = ((), (), s32[]{:S(2)}) async-start(), calls=%async_computation.6 | async-start | bytes 9437184 | tf_op jit(solution)/shard_map/all_gather | solution.py:950
  312.9 56.1 %collective-permute-start.18 = (bf16[512,1024]{1,0:T(8,128)(2,1)}, bf16[512,1024]{1,0:T(8,128)(2,1)S(1)}, u32[]{:S(2)}, u32[]{:S(2)}) collective-permute-start(bf16[512,1024]{1,0:T(8,128)(2,1)} %get-tuple-element.137), channel_id=1, source_target_pairs={{0,8},{8,0},{16,24},{24,16},{1,9},{9,1},{17,25},{25,17},{2,10},{10... | collective-permute-start | bytes 3145736 | tf_op jit(solution)/shard_map/ppermute | solution.py:37
  313.7 55.3 %collective-permute-start.19 = (bf16[512,1024]{1,0:T(8,128)(2,1)}, bf16[512,1024]{1,0:T(8,128)(2,1)}, u32[]{:S(2)}, u32[]{:S(2)}) collective-permute-start(bf16[512,1024]{1,0:T(8,128)(2,1)} %get-tuple-element.138), channel_id=1, source_target_pairs={{0,16},{8,24},{16,0},{24,8},{1,17},{9,25},{17,1},{25,9},{2,18},{10... | collective-permute-start | bytes 3145736 | tf_op jit(solution)/shard_map/ppermute | solution.py:37
  315.2 53.8 %collective-permute-start.20 = (bf16[512,1024]{1,0:T(8,128)(2,1)}, bf16[512,1024]{1,0:T(8,128)(2,1)}, u32[]{:S(2)}, u32[]{:S(2)}) collective-permute-start(bf16[512,1024]{1,0:T(8,128)(2,1)} %get-tuple-element.139), channel_id=1, source_target_pairs={{0,24},{8,16},{16,8},{24,0},{1,25},{9,17},{17,9},{25,1},{2,26},{10... | collective-permute-start | bytes 3145736 | tf_op jit(solution)/shard_map/ppermute | solution.py:37
  372.3 188.4 %all-gather.21.cloned.1.call-start = ((), (), s32[]{:S(2)}) async-start(), calls=%async_computation.7 | async-start | bytes 7299072 | tf_op jit(solution)/shard_map/all_gather | solution.py:950
  372.4 4.4 collective-permute-start.24
  379.7 13.4 %collective-permute-start.25 = (bf16[128,2048]{1,0:T(8,128)(2,1)S(1)}, bf16[128,2048]{1,0:T(8,128)(2,1)S(1)}, u32[]{:S(2)}, u32[]{:S(2)}) collective-permute-start(bf16[128,2048]{1,0:T(8,128)(2,1)S(1)} %slice.184), channel_id=1, source_target_pairs={{0,2},{1,3},{6,4},{7,5},{8,10},{9,11},{14,12},{15,13},{16,18},{17,... | collective-permute-start | bytes 1572872 | tf_op jit(solution)/shard_map/ppermute | solution.py:45
  393.2 7.2 %collective-permute-start.28 = (bf16[128,2048]{1,0:T(8,128)(2,1)S(1)}, bf16[128,2048]{1,0:T(8,128)(2,1)S(1)}, u32[]{:S(2)}, u32[]{:S(2)}) collective-permute-start(bf16[128,2048]{1,0:T(8,128)(2,1)S(1)} %fusion), channel_id=1, source_target_pairs={{6,4},{7,5},{4,2},{5,3},{14,12},{15,13},{12,10},{13,11},{22,20},{2... | collective-permute-start | bytes 1572872 | tf_op jit(solution)/shard_map/ppermute | solution.py:45
  393.9 27.9 %collective-permute-start.26 = (bf16[128,2048]{1,0:T(8,128)(2,1)S(1)}, bf16[128,2048]{1,0:T(8,128)(2,1)S(1)}, u32[]{:S(2)}, u32[]{:S(2)}) collective-permute-start(bf16[128,2048]{1,0:T(8,128)(2,1)S(1)} %fusion), channel_id=1, source_target_pairs={{0,2},{1,3},{2,4},{3,5},{8,10},{9,11},{10,12},{11,13},{16,18},{17,... | collective-permute-start | bytes 1572872 | tf_op jit(solution)/shard_map/ppermute | solution.py:45
  399.0 43.9 %copy-start.3 = (bf16[1024,2048]{1,0:T(8,128)(2,1)S(1)}, bf16[1024,2048]{1,0:T(8,128)(2,1)}, u32[]{:S(2)}) copy-start(bf16[1024,2048]{1,0:T(8,128)(2,1)} %all-gather.13.cloned.1.call-done.right.grads) | copy-start | bytes 12582916
  423.8 23.8 %copy-start.1 = (bf16[1024,1792]{1,0:T(8,128)(2,1)S(1)}, bf16[1024,1792]{1,0:T(8,128)(2,1)}, u32[]{:S(2)}) copy-start(bf16[1024,1792]{1,0:T(8,128)(2,1)} %attend_back.1.right.entered) | copy-start | bytes 11010052
  423.9 39.6 %collective-permute-start.27 = (bf16[128,2048]{1,0:T(8,128)(2,1)S(1)}, bf16[128,2048]{1,0:T(8,128)(2,1)S(1)}, u32[]{:S(2)}, u32[]{:S(2)}) collective-permute-start(bf16[128,2048]{1,0:T(8,128)(2,1)S(1)} %get-tuple-element.180), channel_id=1, source_target_pairs={{0,2},{1,3},{2,4},{3,5},{4,6},{5,7},{8,10},{9,11},{10,12},{11,13},... | collective-permute-start | bytes 1572872 | tf_op jit(solution)/shard_map/ppermute | solution.py:45
  441.4 31.0 %collective-permute-start.29 = (bf16[128,2048]{1,0:T(8,128)(2,1)S(1)}, bf16[128,2048]{1,0:T(8,128)(2,1)S(1)}, u32[]{:S(2)}, u32[]{:S(2)}) collective-permute-start(bf16[128,2048]{1,0:T(8,128)(2,1)S(1)} %get-tuple-element.181), channel_id=1, source_target_pairs={{6,4},{7,5},{4,2},{5,3},{2,0},{3,1},{14,12},{15,13},{12,10},{13,11... | collective-permute-start | bytes 1572872 | tf_op jit(solution)/shard_map/ppermute | solution.py:45
  444.2 30.6 %collective-permute-start.21 = (bf16[512,768]{1,0:T(8,128)(2,1)}, bf16[512,768]{1,0:T(8,128)(2,1)S(1)}, u32[]{:S(2)}, u32[]{:S(2)}) collective-permute-start(bf16[512,768]{1,0:T(8,128)(2,1)} %get-tuple-element.155), channel_id=1, source_target_pairs={{0,8},{8,0},{16,24},{24,16},{1,9},{9,1},{17,25},{25,17},{2,10},{10... | collective-permute-start | bytes 2359304 | tf_op jit(solution)/shard_map/ppermute | solution.py:37
  444.2 33.5 %collective-permute-start.22 = (bf16[512,768]{1,0:T(8,128)(2,1)}, bf16[512,768]{1,0:T(8,128)(2,1)}, u32[]{:S(2)}, u32[]{:S(2)}) collective-permute-start(bf16[512,768]{1,0:T(8,128)(2,1)} %get-tuple-element.156), channel_id=1, source_target_pairs={{0,16},{8,24},{16,0},{24,8},{1,17},{9,25},{17,1},{25,9},{2,18},{10... | collective-permute-start | bytes 2359304 | tf_op jit(solution)/shard_map/ppermute | solution.py:37
  444.5 33.3 %collective-permute-start.23 = (bf16[512,768]{1,0:T(8,128)(2,1)}, bf16[512,768]{1,0:T(8,128)(2,1)}, u32[]{:S(2)}, u32[]{:S(2)}) collective-permute-start(bf16[512,768]{1,0:T(8,128)(2,1)} %get-tuple-element.157), channel_id=1, source_target_pairs={{0,24},{8,16},{16,8},{24,0},{1,25},{9,17},{17,9},{25,1},{2,26},{10... | collective-permute-start | bytes 2359304 | tf_op jit(solution)/shard_map/ppermute | solution.py:37
  448.2 38.3 %copy-start.10 = (f32[512,768]{1,0:T(8,128)S(1)}, f32[512,768]{1,0:T(8,128)}, u32[]{:S(2)}) copy-start(f32[512,768]{1,0:T(8,128)} %get-tuple-element.154) | copy-start | bytes 4718596
  482.9 5.3 collective-permute-start.31
  484.5 4.8 collective-permute-start.32
  485.9 3.9 collective-permute-start.30
  503.8 69.0 %copy-start.18 = (f32[1,2048]{1,0:T(1,128)}, f32[1,2048]{1,0:T(1,128)S(1)}, u32[]{:S(2)}) copy-start(f32[1,2048]{1,0:T(1,128)S(1)} %slice.134) | copy-start | bytes 24580
  (11 other events, 56.4 us)
Sparse Core Ops, SparseCore 0:
  13.9 52.2 all-gather.10
  136.9 53.3 reduce-scatter.1
  193.4 45.3 all-gather.12
  273.5 44.9 all-gather.14
  319.9 63.4 all-gather.16
  385.5 102.6 all-gather.18
  491.0 69.6 all-gather.20

commit v7 on v6

--- a/solution.py
+++ b/solution.py
@@ -981,10 +981,10 @@
     all_b = gather(down_b)
     head_grad = after(head_grad, down_b)
     in_low = attend_back(qkv, head_grad, logsum, cosine, sine, in_low)
-    own_qkv, sent_qkv = outer(normed_all, after(in_low, *sent_up), data_count, depth, three)
     kept, sent = answer(in_low, flat_in, part, seq_count // 2, tall)
-    got, ((own_qkv, sent_qkv), kept, all_a) = send(sent_up, (own_qkv, sent_qkv), kept, all_a)
+    got, (kept, all_a) = send(sent_up, kept, all_a)
     up_grad = total(own_up, got)
+    own_qkv, sent_qkv = outer(normed_all, after(in_low, up_grad), data_count, depth, three)
     all_up = gather(up_grad)
     summed = scatter_blocks(kept, sent)
     got, (summed, all_b) = send(sent_qkv, summed, all_b)

time: 583 us -> 582 us (level)
  waiting for transfers between devices: 273 us -> 266 us
  transfers between devices with their start and end apart: 40 -> 40, of which waited for: 19 -> 20; matrix products, arithmetic and copies ran while one was open for 7% -> 8% of each run, Pallas kernels for 26% -> 27%
where the time goes in v7:
time: 582 us; the launch traced here: 580 us
  waiting for transfers between devices  266 us (46%)
  Pallas kernels  177 us (30%)
  starting transfers between devices  61.2 us (11%)
  other arithmetic  35.1 us (6%)
  between operations  17 us (3%)
  local copies, waits for them, and re-layouts  13.8 us (2%)
  matrix products  9.3 us (2%)
    ppermute x28, waiting for transfers between devices, swap(): lax.ppermute(array, axis, [(s, s ^ bit) for s in range(lax.axis_size(axis...  74.7 us
    ppermute x5, waiting for transfers between devices, between(): lax.ppermute(array, 'seq', [(2 * a + core, 2 * b + core) for a, b in pair...  52.7 us
    all_gather x4, waiting for transfers between devices, gather(): return lax.all_gather(array, 'seq', axis=0, tiled=False)  48.7 us
    all_gather x2, waiting for transfers between devices, gather_seq(): return lax.all_gather(rows, 'seq', axis=0, tiled=True)  45.3 us
    reduce_scatter x1, waiting for transfers between devices, scatter_seq(): return lax.psum_scatter(partial, 'seq', scatter_dimension=0, tiled=True)  44.9 us
    ppermute x28, starting transfers between devices, swap(): lax.ppermute(array, axis, [(s, s ^ bit) for s in range(lax.axis_size(axis...  33.6 us
    pallas_call x1, Pallas kernels, attend_back(): pl.pallas_call(functools.partial(attend_back_kernel, 128), grid=(1,), in_...  29.4 us
    ppermute x5, starting transfers between devices, between(): lax.ppermute(array, 'seq', [(2 * a + core, 2 * b + core) for a, b in pair...  26.9 us
  transfers between devices with their start and end apart: 40, of which 20 were waited for; matrix products, arithmetic and copies ran while one was open for 8% of the time, Pallas kernels for 27%

profile of v7, /device:TPU:0, one launch (start us, length us, event | category | flops | bytes accessed | tf_op | source)
XLA Modules:
  0.0 579.7 jit_solution(16135357367801633238)
XLA Ops:
  7.2 3.6 pick.2
  10.8 3.0 enter.1
  13.9 3.0 collective-permute-start.3
  18.4 20.3 %collective-permute-done.3.refs_5_.refs_2_ = bf16[272,1792]{1,0:T(8,128)(2,1)S(1)} collective-permute-done((bf16[272,1792]{1,0:T(8,128)(2,1)}, bf16[272,1792]{1,0:T(8,128)(2,1)S(1)}, u32[]{:S(2)}, u32[]{:S(2)}) %collective-permute-start.3) | collective-permute-done | bytes 974880 | tf_op jit(solution)/shard_map/ppermute | solution.py:37
  38.7 1.7 collective-permute-start.5
  44.2 3.1 pick.3
  48.0 16.0 %collective-permute-done.4.refs_6_ = bf16[256,1792]{1,0:T(8,128)(2,1)} collective-permute-done((bf16[256,1792]{1,0:T(8,128)(2,1)}, bf16[256,1792]{1,0:T(8,128)(2,1)}, u32[]{:S(2)}, u32[]{:S(2)}) %collective-permute-start.4) | collective-permute-done | bytes 917536 | tf_op jit(solution)/shard_map/ppermute | solution.py:37
  69.0 3.1 fusion.15
  72.1 11.6 %collective-permute-done.2.refs_4_ = bf16[256,1792]{1,0:T(8,128)(2,1)} collective-permute-done((bf16[256,1792]{1,0:T(8,128)(2,1)}, bf16[256,1792]{1,0:T(8,128)(2,1)}, u32[]{:S(2)}, u32[]{:S(2)}) %collective-permute-start.2) | collective-permute-done | bytes 917536 | tf_op jit(solution)/shard_map/ppermute | solution.py:37
  86.2 16.9 %project.1 = (bf16[1024,768]{1,0:T(8,128)(2,1)}, f32[1024,1024]{1,0:T(8,128)}, bf16[1024,1280]{1,0:T(8,128)(2,1)}) custom-call(bf16[1024,2176]{1,0:T(8,128)(2,1)} %all-gather.11.cloned.1.call-done.normed.left, f32[1024,128]{1,0:T(8,128)} %get-tuple-element.182.cosine, f32[1024,128]{1,0:T(8,128)} %get-tuple-element.181.sine, ...), custom_call_target="tpu_custom_call" | custom-call | flops 7516192768 | bytes 26214400 | tf_op jit(solution)/shard_map/project/pallas_call | solution.py:309
  103.1 13.5 %attend.1 = (bf16[1024,1280]{1,0:T(8,128)(2,1)}, f32[1024,128]{1,0:T(8,128)}) custom-call(bf16[1024,768]{1,0:T(8,128)(2,1)} %get-tuple-element.96.qkv, bf16[1024,1280]{1,0:T(8,128)(2,1)} %get-tuple-element.97.stacked), custom_call_target="tpu_custom_call", output_to_operand_aliasing={{0}: (1, {})} | custom-call | flops 2147483648 | bytes 6291456 | tf_op jit(solution)/shard_map/attend/pallas_call | solution.py:481
  118.8 10.2 %emit.2.refs_6_ = bf16[1024,2176]{1,0:T(8,128)(2,1)} custom-call(bf16[1024,1280]{1,0:T(8,128)(2,1)} %get-tuple-element.98.stacked.left, bf16[640,512]{1,0:T(8,128)(2,1)} %get-tuple-element.102.refs_0_, bf16[640,512]{1,0:T(8,128)(2,1)} %get-tuple-element.104.refs_1_, bf16[640,512]{1,0:T(8,128)(2,1)} %collective-permute-done.6.refs_2_, ...), custom_call_target="tpu_custom_call" | custom-call | flops 4026531840 | bytes 9699328 | tf_op jit(solution)/shard_map/emit/pallas_call | solution.py:409
  131.0 5.7 emit.3
  139.2 2.5 pad_maximum_fusion.1.refs_1_
  141.7 2.4 pad_maximum_fusion.2.refs_2_
  145.3 44.9 %reduce-scatter.2.cloned.1.call-done.branches = bf16[128,2176]{1,0:T(8,128)(2,1)} async-done(((bf16[1024,2176]{1,0:T(8,128)(2,1)}), bf16[128,2176]{1,0:T(8,128)(2,1)}) %reduce-scatter.2.cloned.1.call-update) | async-done | bytes 557072 | tf_op jit(solution)/shard_map/reduce_scatter | solution.py:77
  190.3 3.0 grade.1
  193.5 45.3 %all-gather.13.cloned.1.call-done.right.grads = bf16[1024,2048]{1,0:T(8,128)(2,1)} async-done(((bf16[128,2048]{1,0:T(8,128)(2,1)}), bf16[1024,2048]{1,0:T(8,128)(2,1)}) %all-gather.13.cloned.1.call-update) | async-done | bytes 4194320 | tf_op jit(solution)/shard_map/all_gather | solution.py:41
  238.7 2.9 convolution_convert_fusion.2
  248.2 8.3 %outer.3 = (f32[768,512]{1,0:T(8,128)}, bf16[768,512]{1,0:T(8,128)(2,1)}, bf16[768,512]{1,0:T(8,128)(2,1)}, bf16[768,512]{1,0:T(8,128)(2,1)}) custom-call(bf16[1024,1280]{1,0:T(8,128)(2,1)} %get-tuple-element.98.stacked.left, bf16[1024,2048]{1,0:T(8,128)(2,1)} %all-gather.13.cloned.1.call-done.right.grads), custom_call_target="tpu_custom_call" | custom-call | flops 3221225472 | bytes 3145728 | tf_op jit(solution)/shard_map/outer/pallas_call | solution.py:653
  256.6 13.4 %collective-permute-done.13 = bf16[512,512]{1,0:T(8,128)(2,1)} collective-permute-done((bf16[512,512]{1,0:T(8,128)(2,1)}, bf16[512,512]{1,0:T(8,128)(2,1)}, u32[]{:S(2)}, u32[]{:S(2)}) %collective-permute-start.13) | collective-permute-done | bytes 524320 | tf_op jit(solution)/shard_map/ppermute | solution.py:37
  270.0 3.3 add_convert_fusion.5
  276.9 13.7 %reject.1 = (bf16[1024,256]{1,0:T(8,128)(2,1)}, bf16[1024,1792]{1,0:T(8,128)(2,1)}) custom-call(f32[1024,1024]{1,0:T(8,128)} %get-tuple-element.118.hidden, bf16[1024,2048]{1,0:T(8,128)(2,1)} %all-gather.13.cloned.1.call-done.right.grads, bf16[1280,512]{1,0:T(8,128)(2,1)} %pad_maximum_fusion.refs_0_, bf16[1280,512]{1,0:T(8,128)(2,1)} %pad_maximum_fusion.1.refs_1_, ...), custom_call_target="tpu_custom_call" | custom-call | flops 5368709120 | bytes 19922944 | tf_op jit(solution)/shard_map/reject/pallas_call | solution.py:604
  290.6 3.1 slice.95.right
  293.7 10.0 %outer.4 = (f32[512,1024]{1,0:T(8,128)}, bf16[512,1024]{1,0:T(8,128)(2,1)}, bf16[512,1024]{1,0:T(8,128)(2,1)}, bf16[512,1024]{1,0:T(8,128)(2,1)}) custom-call(bf16[1024,2176]{1,0:T(8,128)(2,1)} %all-gather.11.cloned.1.call-done.normed.left, bf16[1024,1024]{1,0:T(8,128)(2,1)} %slice.95.right), custom_call_target="tpu_custom_call" | custom-call | flops 4294967296 | bytes 4194304 | tf_op jit(solution)/shard_map/outer/pallas_call | solution.py:653
  303.7 4.7 collective-permute-done.16
  310.1 2.4 add_convert_fusion.2
  316.2 29.4 %attend_back.1.entered.right = bf16[1024,1792]{1,0:T(8,128)(2,1)} custom-call(bf16[1024,768]{1,0:T(8,128)(2,1)} %get-tuple-element.96.qkv, bf16[1024,256]{1,0:T(8,128)(2,1)} %get-tuple-element.138.grad, f32[1024,128]{1,0:T(8,128)} %get-tuple-element.139.logsum, f32[1024,128]{1,0:T(8,128)} %get-tuple-element.182.cosine, ...), custom_call_target="tpu_custom_call", output_to_operand_aliasing={{}: (5, {})} | custom-call | flops 5368709120 | bytes 6291456 | tf_op jit(solution)/shard_map/attend_back/pallas_call | solution.py:558
  345.5 14.8 %answer.1 = (f32[512,2048]{1,0:T(8,128)}, bf16[512,2048]{1,0:T(8,128)(2,1)}) custom-call(s32[1]{0:T(128)} %bitcast.part, bf16[1024,1792]{1,0:T(8,128)(2,1)} %attend_back.1.entered.right, bf16[256,1792]{1,0:T(8,128)(2,1)} %get-tuple-element.92.refs_0_, bf16[272,1792]{1,0:T(8,128)(2,1)} %get-tuple-element.93.refs_1_.refs_0_, ...), custom_call_target="tpu_custom_call" | custom-call | flops 7516192768 | bytes 17301504 | tf_op jit(solution)/shard_map/answer/pallas_call | solution.py:705
  360.4 3.3 add_convert_fusion
  364.1 4.4 collective-permute-done.24
  368.4 2.8 convert_add_fusion
  371.3 2.0 collective-permute-start.25
  373.4 16.1 %collective-permute-done.25 = bf16[128,2048]{1,0:T(8,128)(2,1)S(1)} collective-permute-done((bf16[128,2048]{1,0:T(8,128)(2,1)S(1)}, bf16[128,2048]{1,0:T(8,128)(2,1)S(1)}, u32[]{:S(2)}, u32[]{:S(2)}) %collective-permute-start.25) | collective-permute-done | bytes 524320 | tf_op jit(solution)/shard_map/ppermute | solution.py:45
  390.3 5.0 collective-permute-start.26
  396.7 4.0 convert_reduce_fusion
  400.7 13.8 %collective-permute-done.26 = bf16[128,2048]{1,0:T(8,128)(2,1)S(1)} collective-permute-done((bf16[128,2048]{1,0:T(8,128)(2,1)S(1)}, bf16[128,2048]{1,0:T(8,128)(2,1)S(1)}, u32[]{:S(2)}, u32[]{:S(2)}) %collective-permute-start.26) | collective-permute-done | bytes 524320 | tf_op jit(solution)/shard_map/ppermute | solution.py:45
  415.8 17.9 %collective-permute-start.27 = (bf16[128,2048]{1,0:T(8,128)(2,1)}, bf16[128,2048]{1,0:T(8,128)(2,1)S(1)}, u32[]{:S(2)}, u32[]{:S(2)}) collective-permute-start(bf16[128,2048]{1,0:T(8,128)(2,1)} %get-tuple-element.172), channel_id=1, source_target_pairs={{0,2},{1,3},{2,4},{3,5},{4,6},{5,7},{8,10},{9,11},{10,12},{11,13},... | collective-permute-start | bytes 1572872 | tf_op jit(solution)/shard_map/ppermute | solution.py:45
  435.0 8.3 %outer.5 = (f32[512,768]{1,0:T(8,128)}, bf16[512,768]{1,0:T(8,128)(2,1)}, bf16[512,768]{1,0:T(8,128)(2,1)}, bf16[512,768]{1,0:T(8,128)(2,1)}) custom-call(bf16[1024,2176]{1,0:T(8,128)(2,1)} %all-gather.11.cloned.1.call-done.normed.left, bf16[1024,1792]{1,0:T(8,128)(2,1)} %attend_back.1.entered.right), custom_call_target="tpu_custom_call" | custom-call | flops 3221225472 | bytes 3145728 | tf_op jit(solution)/shard_map/outer/pallas_call | solution.py:653
  446.8 2.6 convert_reduce_fusion.1
  449.4 5.7 collective-permute-done.27
  455.1 17.1 %collective-permute-done.29 = bf16[128,2048]{1,0:T(8,128)(2,1)} collective-permute-done((bf16[128,2048]{1,0:T(8,128)(2,1)}, bf16[128,2048]{1,0:T(8,128)(2,1)}, u32[]{:S(2)}, u32[]{:S(2)}) %collective-permute-start.29) | collective-permute-done | bytes 524320 | tf_op jit(solution)/shard_map/ppermute | solution.py:45
  472.2 2.5 fusion.1.summed
  474.8 3.7 leave.1
  489.1 12.1 %widen_rows.1 = (f32[8192,512]{1,0:T(8,128)}, f32[2048,512]{1,0:T(8,128)}) custom-call(bf16[8,512,512]{2,1,0:T(8,128)(2,1)} %bitcast.35, bf16[8,768,512]{2,1,0:T(8,128)(2,1)} %bitcast.34), custom_call_target="tpu_custom_call" | custom-call | bytes 31457280 | tf_op jit(solution)/shard_map/widen_rows/pallas_call | solution.py:743
  501.3 9.8 %widen_columns.2 = f32[512,8192]{1,0:T(8,128)} custom-call(bf16[8,512,1024]{2,1,0:T(8,128)(2,1)} %bitcast.31), custom_call_target="tpu_custom_call" | custom-call | bytes 25165824 | tf_op jit(solution)/shard_map/widen_columns/pallas_call | solution.py:778
  511.1 48.0 %all-gather.21.cloned.1.call-done = bf16[4224,768]{1,0:T(8,128)(2,1)} async-done(((bf16[528,768]{1,0:T(8,128)(2,1)}), bf16[4224,768]{1,0:T(8,128)(2,1)}) %all-gather.21.cloned.1.call-update) | async-done | bytes 6488080 | tf_op jit(solution)/shard_map/all_gather | solution.py:950
  561.4 7.9 %widen_columns.3 = f32[512,6144]{1,0:T(8,128)} custom-call(bf16[8,528,768]{2,1,0:T(8,128)(2,1)} %bitcast.33), custom_call_target="tpu_custom_call" | custom-call | bytes 18874368 | tf_op jit(solution)/shard_map/widen_columns/pallas_call | solution.py:778
  (144 shorter events, 59.9 us)
Async XLA Ops:
  7.2 60.4 %all-gather.11.cloned.1.call-start = ((), (), s32[]{:S(2)}) async-start(), calls=%async_computation.1 | async-start | bytes 5013504 | tf_op jit(solution)/shard_map/all_gather | solution.py:41
  13.8 176.4 %reduce-scatter.2.cloned.1.call-start = ((), (), s32[]{:S(2)}) async-start(), calls=%async_computation.2 | async-start | bytes 5013504 | tf_op jit(solution)/shard_map/reduce_scatter | solution.py:77
  13.9 24.8 %collective-permute-start.3 = (bf16[272,1792]{1,0:T(8,128)(2,1)}, bf16[272,1792]{1,0:T(8,128)(2,1)S(1)}, u32[]{:S(2)}, u32[]{:S(2)}) collective-permute-start(bf16[272,1792]{1,0:T(8,128)(2,1)} %get-tuple-element.93.refs_1_.refs_0_), channel_id=1, source_target_pairs={{0,16},{8,24},{16,0},{24,8},{1,17},{9,25},{17,1},{25,9},{2,18},{10... | collective-permute-start | bytes 2924552 | tf_op jit(solution)/shard_map/ppermute | solution.py:37
  16.9 23.5 %collective-permute-start = (bf16[256,1792]{1,0:T(8,128)(2,1)}, bf16[256,1792]{1,0:T(8,128)(2,1)}, u32[]{:S(2)}, u32[]{:S(2)}) collective-permute-start(bf16[256,1792]{1,0:T(8,128)(2,1)} %get-tuple-element.92.refs_0_), channel_id=1, source_target_pairs={{0,8},{8,0},{16,24},{24,16},{1,9},{9,1},{17,25},{25,17},{2,10},{10... | collective-permute-start | bytes 2752520 | tf_op jit(solution)/shard_map/ppermute | solution.py:37
  38.7 25.3 %collective-permute-start.5 = (bf16[272,1792]{1,0:T(8,128)(2,1)S(1)}, bf16[272,1792]{1,0:T(8,128)(2,1)S(1)}, u32[]{:S(2)}, u32[]{:S(2)}) collective-permute-start(bf16[272,1792]{1,0:T(8,128)(2,1)S(1)} %collective-permute-done.3.refs_5_.refs_2_), channel_id=1, source_target_pairs={{0,8},{8,0},{16,24},{24,16},{1,9},{9,1},{17,25},{25,17},{2,10},{10... | collective-permute-start | bytes 2924552 | tf_op jit(solution)/shard_map/ppermute | solution.py:37
  40.4 23.6 %collective-permute-start.4 = (bf16[256,1792]{1,0:T(8,128)(2,1)}, bf16[256,1792]{1,0:T(8,128)(2,1)}, u32[]{:S(2)}, u32[]{:S(2)}) collective-permute-start(bf16[256,1792]{1,0:T(8,128)(2,1)} %collective-permute-done.refs_2_), channel_id=1, source_target_pairs={{0,16},{8,24},{16,0},{24,8},{1,17},{9,25},{17,1},{25,9},{2,18},{10... | collective-permute-start | bytes 2752520 | tf_op jit(solution)/shard_map/ppermute | solution.py:37
  41.9 41.7 %collective-permute-start.2 = (bf16[256,1792]{1,0:T(8,128)(2,1)}, bf16[256,1792]{1,0:T(8,128)(2,1)}, u32[]{:S(2)}, u32[]{:S(2)}) collective-permute-start(bf16[256,1792]{1,0:T(8,128)(2,1)} %get-tuple-element.92.refs_0_), channel_id=1, source_target_pairs={{0,16},{8,24},{16,0},{24,8},{1,17},{9,25},{17,1},{25,9},{2,18},{10... | collective-permute-start | bytes 2752520 | tf_op jit(solution)/shard_map/ppermute | solution.py:37
  42.4 42.8 %collective-permute-start.1 = (bf16[272,1792]{1,0:T(8,128)(2,1)}, bf16[272,1792]{1,0:T(8,128)(2,1)S(1)}, u32[]{:S(2)}, u32[]{:S(2)}) collective-permute-start(bf16[272,1792]{1,0:T(8,128)(2,1)} %get-tuple-element.93.refs_1_.refs_0_), channel_id=1, source_target_pairs={{0,8},{8,0},{16,24},{24,16},{1,9},{9,1},{17,25},{25,17},{2,10},{10... | collective-permute-start | bytes 2924552 | tf_op jit(solution)/shard_map/ppermute | solution.py:37
  64.0 21.2 %copy-start.12 = (bf16[272,1792]{1,0:T(8,128)(2,1)}, bf16[272,1792]{1,0:T(8,128)(2,1)S(1)}, u32[]{:S(2)}) copy-start(bf16[272,1792]{1,0:T(8,128)(2,1)S(1)} %collective-permute-done.5.refs_7_.refs_3_) | copy-start | bytes 2924548
  64.0 19.7 %copy-start.15 = (bf16[640,512]{1,0:T(8,128)(2,1)S(1)}, bf16[640,512]{1,0:T(8,128)(2,1)}, u32[]{:S(2)}) copy-start(bf16[640,512]{1,0:T(8,128)(2,1)} %get-tuple-element.104.refs_1_) | copy-start | bytes 1966084
  64.0 54.8 %collective-permute-start.11 = (bf16[640,512]{1,0:T(8,128)(2,1)}, bf16[640,512]{1,0:T(8,128)(2,1)}, u32[]{:S(2)}, u32[]{:S(2)}) collective-permute-start(bf16[640,512]{1,0:T(8,128)(2,1)} %get-tuple-element.102.refs_0_), channel_id=1, source_target_pairs={{0,16},{8,24},{16,0},{24,8},{1,17},{9,25},{17,1},{25,9},{2,18},{10... | collective-permute-start | bytes 1966088 | tf_op jit(solution)/shard_map/ppermute | solution.py:37
  65.6 51.0 %collective-permute-start.6 = (bf16[640,512]{1,0:T(8,128)(2,1)}, bf16[640,512]{1,0:T(8,128)(2,1)}, u32[]{:S(2)}, u32[]{:S(2)}) collective-permute-start(bf16[640,512]{1,0:T(8,128)(2,1)} %get-tuple-element.102.refs_0_), channel_id=1, source_target_pairs={{0,8},{8,0},{16,24},{24,16},{1,9},{9,1},{17,25},{25,17},{2,10},{10... | collective-permute-start | bytes 1966088 | tf_op jit(solution)/shard_map/ppermute | solution.py:37
  66.4 52.3 %collective-permute-start.10 = (bf16[640,512]{1,0:T(8,128)(2,1)}, bf16[640,512]{1,0:T(8,128)(2,1)}, u32[]{:S(2)}, u32[]{:S(2)}) collective-permute-start(bf16[640,512]{1,0:T(8,128)(2,1)} %get-tuple-element.104.refs_1_), channel_id=1, source_target_pairs={{0,8},{8,0},{16,24},{24,16},{1,9},{9,1},{17,25},{25,17},{2,10},{10... | collective-permute-start | bytes 1966088 | tf_op jit(solution)/shard_map/ppermute | solution.py:37
  83.7 32.9 %collective-permute-start.8 = (bf16[640,512]{1,0:T(8,128)(2,1)S(1)}, bf16[640,512]{1,0:T(8,128)(2,1)}, u32[]{:S(2)}, u32[]{:S(2)}) collective-permute-start(bf16[640,512]{1,0:T(8,128)(2,1)S(1)} %copy-done.15), channel_id=1, source_target_pairs={{0,16},{8,24},{16,0},{24,8},{1,17},{9,25},{17,1},{25,9},{2,18},{10... | collective-permute-start | bytes 1966088 | tf_op jit(solution)/shard_map/ppermute | solution.py:37
  116.6 12.7 %collective-permute-start.7 = (bf16[640,512]{1,0:T(8,128)(2,1)}, bf16[640,512]{1,0:T(8,128)(2,1)S(1)}, u32[]{:S(2)}, u32[]{:S(2)}) collective-permute-start(bf16[640,512]{1,0:T(8,128)(2,1)} %collective-permute-done.6.refs_2_), channel_id=1, source_target_pairs={{0,16},{8,24},{16,0},{24,8},{1,17},{9,25},{17,1},{25,9},{2,18},{10... | collective-permute-start | bytes 1966088 | tf_op jit(solution)/shard_map/ppermute | solution.py:37
  117.3 12.9 %collective-permute-start.9 = (bf16[640,512]{1,0:T(8,128)(2,1)}, bf16[640,512]{1,0:T(8,128)(2,1)S(1)}, u32[]{:S(2)}, u32[]{:S(2)}) collective-permute-start(bf16[640,512]{1,0:T(8,128)(2,1)} %collective-permute-done.8.refs_5_), channel_id=1, source_target_pairs={{0,8},{8,0},{16,24},{24,16},{1,9},{9,1},{17,25},{25,17},{2,10},{10... | collective-permute-start | bytes 1966088 | tf_op jit(solution)/shard_map/ppermute | solution.py:37
  136.8 101.9 %all-gather.13.cloned.1.call-start = ((), (), s32[]{:S(2)}) async-start(), calls=%async_computation.3 | async-start | bytes 4718592 | tf_op jit(solution)/shard_map/all_gather | solution.py:41
  144.1 94.6 %copy-start.7 = (bf16[1024,1280]{1,0:T(8,128)(2,1)S(1)}, bf16[1024,1280]{1,0:T(8,128)(2,1)}, u32[]{:S(2)}) copy-start(bf16[1024,1280]{1,0:T(8,128)(2,1)} %get-tuple-element.98.stacked.left) | copy-start | bytes 7864324
  193.2 167.2 %all-gather.15.cloned.1.call-start = ((), (), s32[]{:S(2)}) async-start(), calls=%async_computation.4 | async-start | bytes 4718592 | tf_op jit(solution)/shard_map/all_gather | solution.py:950
  241.6 15.0 %collective-permute-start.12 = (bf16[512,512]{1,0:T(8,128)(2,1)}, bf16[512,512]{1,0:T(8,128)(2,1)S(1)}, u32[]{:S(2)}, u32[]{:S(2)}) collective-permute-start(bf16[512,512]{1,0:T(8,128)(2,1)} %convolution_convert_fusion.2), channel_id=1, source_target_pairs={{0,8},{8,0},{16,24},{24,16},{1,9},{9,1},{17,25},{25,17},{2,10},{10... | collective-permute-start | bytes 1572872 | tf_op jit(solution)/shard_map/ppermute | solution.py:37
  244.6 25.3 %collective-permute-start.13 = (bf16[512,512]{1,0:T(8,128)(2,1)}, bf16[512,512]{1,0:T(8,128)(2,1)}, u32[]{:S(2)}, u32[]{:S(2)}) collective-permute-start(bf16[512,512]{1,0:T(8,128)(2,1)} %convolution_convert_fusion.1), channel_id=1, source_target_pairs={{0,16},{8,24},{16,0},{24,8},{1,17},{9,25},{17,1},{25,9},{2,18},{10... | collective-permute-start | bytes 1572872 | tf_op jit(solution)/shard_map/ppermute | solution.py:37
  247.6 22.3 %collective-permute-start.14 = (bf16[512,512]{1,0:T(8,128)(2,1)}, bf16[512,512]{1,0:T(8,128)(2,1)S(1)}, u32[]{:S(2)}, u32[]{:S(2)}) collective-permute-start(bf16[512,512]{1,0:T(8,128)(2,1)} %convolution_convert_fusion), channel_id=1, source_target_pairs={{0,24},{8,16},{16,8},{24,0},{1,25},{9,17},{17,9},{25,1},{2,26},{10... | collective-permute-start | bytes 1572872 | tf_op jit(solution)/shard_map/ppermute | solution.py:37
  273.3 201.4 %all-gather.17.cloned.1.call-start = ((), (), s32[]{:S(2)}) async-start(), calls=%async_computation.5 | async-start | bytes 7077888 | tf_op jit(solution)/shard_map/all_gather | solution.py:950
  273.4 30.4 %collective-permute-start.15 = (bf16[768,512]{1,0:T(8,128)(2,1)}, bf16[768,512]{1,0:T(8,128)(2,1)S(1)}, u32[]{:S(2)}, u32[]{:S(2)}) collective-permute-start(bf16[768,512]{1,0:T(8,128)(2,1)} %get-tuple-element.115), channel_id=1, source_target_pairs={{0,8},{8,0},{16,24},{24,16},{1,9},{9,1},{17,25},{25,17},{2,10},{10... | collective-permute-start | bytes 2359304 | tf_op jit(solution)/shard_map/ppermute | solution.py:37
  274.0 34.5 %collective-permute-start.16 = (bf16[768,512]{1,0:T(8,128)(2,1)}, bf16[768,512]{1,0:T(8,128)(2,1)S(1)}, u32[]{:S(2)}, u32[]{:S(2)}) collective-permute-start(bf16[768,512]{1,0:T(8,128)(2,1)} %get-tuple-element.116), channel_id=1, source_target_pairs={{0,16},{8,24},{16,0},{24,8},{1,17},{9,25},{17,1},{25,9},{2,18},{10... | collective-permute-start | bytes 2359304 | tf_op jit(solution)/shard_map/ppermute | solution.py:37
  275.5 34.6 %collective-permute-start.17 = (bf16[768,512]{1,0:T(8,128)(2,1)}, bf16[768,512]{1,0:T(8,128)(2,1)}, u32[]{:S(2)}, u32[]{:S(2)}) collective-permute-start(bf16[768,512]{1,0:T(8,128)(2,1)} %get-tuple-element.117), channel_id=1, source_target_pairs={{0,24},{8,16},{16,8},{24,0},{1,25},{9,17},{17,9},{25,1},{2,26},{10... | collective-permute-start | bytes 2359304 | tf_op jit(solution)/shard_map/ppermute | solution.py:37
  293.7 16.4 %copy-start.10 = (f32[768,512]{1,0:T(8,128)S(1)}, f32[768,512]{1,0:T(8,128)}, u32[]{:S(2)}) copy-start(f32[768,512]{1,0:T(8,128)} %get-tuple-element.134) | copy-start | bytes 4718596
  312.6 175.9 %all-gather.19.cloned.1.call-start = ((), (), s32[]{:S(2)}) async-start(), calls=%async_computation.6 | async-start | bytes 9437184 | tf_op jit(solution)/shard_map/all_gather | solution.py:950
  312.6 47.8 %collective-permute-start.18 = (bf16[512,1024]{1,0:T(8,128)(2,1)}, bf16[512,1024]{1,0:T(8,128)(2,1)S(1)}, u32[]{:S(2)}, u32[]{:S(2)}) collective-permute-start(bf16[512,1024]{1,0:T(8,128)(2,1)} %get-tuple-element.142), channel_id=1, source_target_pairs={{0,8},{8,0},{16,24},{24,16},{1,9},{9,1},{17,25},{25,17},{2,10},{10... | collective-permute-start | bytes 3145736 | tf_op jit(solution)/shard_map/ppermute | solution.py:37
  313.4 47.0 %collective-permute-start.19 = (bf16[512,1024]{1,0:T(8,128)(2,1)}, bf16[512,1024]{1,0:T(8,128)(2,1)}, u32[]{:S(2)}, u32[]{:S(2)}) collective-permute-start(bf16[512,1024]{1,0:T(8,128)(2,1)} %get-tuple-element.143), channel_id=1, source_target_pairs={{0,16},{8,24},{16,0},{24,8},{1,17},{9,25},{17,1},{25,9},{2,18},{10... | collective-permute-start | bytes 3145736 | tf_op jit(solution)/shard_map/ppermute | solution.py:37
  314.9 45.5 %collective-permute-start.20 = (bf16[512,1024]{1,0:T(8,128)(2,1)}, bf16[512,1024]{1,0:T(8,128)(2,1)}, u32[]{:S(2)}, u32[]{:S(2)}) collective-permute-start(bf16[512,1024]{1,0:T(8,128)(2,1)} %get-tuple-element.144), channel_id=1, source_target_pairs={{0,24},{8,16},{16,8},{24,0},{1,25},{9,17},{17,9},{25,1},{2,26},{10... | collective-permute-start | bytes 3145736 | tf_op jit(solution)/shard_map/ppermute | solution.py:37
  363.7 195.4 %all-gather.21.cloned.1.call-start = ((), (), s32[]{:S(2)}) async-start(), calls=%async_computation.7 | async-start | bytes 7299072 | tf_op jit(solution)/shard_map/all_gather | solution.py:950
  364.0 4.4 collective-permute-start.24
  371.3 18.2 %copy-start = (f32[512,2048]{1,0:T(8,128)}, f32[512,2048]{1,0:T(8,128)S(1)}, u32[]{:S(2)}) copy-start(f32[512,2048]{1,0:T(8,128)S(1)} %convert_add_fusion) | copy-start | bytes 12582916
  371.3 18.1 %collective-permute-start.25 = (bf16[128,2048]{1,0:T(8,128)(2,1)S(1)}, bf16[128,2048]{1,0:T(8,128)(2,1)S(1)}, u32[]{:S(2)}, u32[]{:S(2)}) collective-permute-start(bf16[128,2048]{1,0:T(8,128)(2,1)S(1)} %slice.184), channel_id=1, source_target_pairs={{0,2},{1,3},{6,4},{7,5},{8,10},{9,11},{14,12},{15,13},{16,18},{17,... | collective-permute-start | bytes 1572872 | tf_op jit(solution)/shard_map/ppermute | solution.py:45
  389.6 11.1 %collective-permute-start.28 = (bf16[128,2048]{1,0:T(8,128)(2,1)S(1)}, bf16[128,2048]{1,0:T(8,128)(2,1)S(1)}, u32[]{:S(2)}, u32[]{:S(2)}) collective-permute-start(bf16[128,2048]{1,0:T(8,128)(2,1)S(1)} %fusion), channel_id=1, source_target_pairs={{6,4},{7,5},{4,2},{5,3},{14,12},{15,13},{12,10},{13,11},{22,20},{2... | collective-permute-start | bytes 1572872 | tf_op jit(solution)/shard_map/ppermute | solution.py:45
  390.3 24.2 %collective-permute-start.26 = (bf16[128,2048]{1,0:T(8,128)(2,1)S(1)}, bf16[128,2048]{1,0:T(8,128)(2,1)S(1)}, u32[]{:S(2)}, u32[]{:S(2)}) collective-permute-start(bf16[128,2048]{1,0:T(8,128)(2,1)S(1)} %fusion), channel_id=1, source_target_pairs={{0,2},{1,3},{2,4},{3,5},{8,10},{9,11},{10,12},{11,13},{16,18},{17,... | collective-permute-start | bytes 1572872 | tf_op jit(solution)/shard_map/ppermute | solution.py:45
  395.3 19.1 %copy-start.1 = (f32[512,2048]{1,0:T(8,128)S(1)}, f32[512,2048]{1,0:T(8,128)}, u32[]{:S(2)}) copy-start(f32[512,2048]{1,0:T(8,128)} %copy-done) | copy-start | bytes 12582916
  415.8 39.3 %collective-permute-start.27 = (bf16[128,2048]{1,0:T(8,128)(2,1)}, bf16[128,2048]{1,0:T(8,128)(2,1)S(1)}, u32[]{:S(2)}, u32[]{:S(2)}) collective-permute-start(bf16[128,2048]{1,0:T(8,128)(2,1)} %get-tuple-element.172), channel_id=1, source_target_pairs={{0,2},{1,3},{2,4},{3,5},{4,6},{5,7},{8,10},{9,11},{10,12},{11,13},... | collective-permute-start | bytes 1572872 | tf_op jit(solution)/shard_map/ppermute | solution.py:45
  433.7 38.5 %collective-permute-start.29 = (bf16[128,2048]{1,0:T(8,128)(2,1)}, bf16[128,2048]{1,0:T(8,128)(2,1)}, u32[]{:S(2)}, u32[]{:S(2)}) collective-permute-start(bf16[128,2048]{1,0:T(8,128)(2,1)} %get-tuple-element.173), channel_id=1, source_target_pairs={{6,4},{7,5},{4,2},{5,3},{2,0},{3,1},{14,12},{15,13},{12,10},{13,11... | collective-permute-start | bytes 1572872 | tf_op jit(solution)/shard_map/ppermute | solution.py:45
  443.3 31.4 %collective-permute-start.21 = (bf16[512,768]{1,0:T(8,128)(2,1)}, bf16[512,768]{1,0:T(8,128)(2,1)S(1)}, u32[]{:S(2)}, u32[]{:S(2)}) collective-permute-start(bf16[512,768]{1,0:T(8,128)(2,1)} %get-tuple-element.151), channel_id=1, source_target_pairs={{0,8},{8,0},{16,24},{24,16},{1,9},{9,1},{17,25},{25,17},{2,10},{10... | collective-permute-start | bytes 2359304 | tf_op jit(solution)/shard_map/ppermute | solution.py:37
  444.6 30.1 %collective-permute-start.22 = (bf16[512,768]{1,0:T(8,128)(2,1)}, bf16[512,768]{1,0:T(8,128)(2,1)}, u32[]{:S(2)}, u32[]{:S(2)}) collective-permute-start(bf16[512,768]{1,0:T(8,128)(2,1)} %get-tuple-element.152), channel_id=1, source_target_pairs={{0,16},{8,24},{16,0},{24,8},{1,17},{9,25},{17,1},{25,9},{2,18},{10... | collective-permute-start | bytes 2359304 | tf_op jit(solution)/shard_map/ppermute | solution.py:37
  446.1 28.7 %collective-permute-start.23 = (bf16[512,768]{1,0:T(8,128)(2,1)}, bf16[512,768]{1,0:T(8,128)(2,1)}, u32[]{:S(2)}, u32[]{:S(2)}) collective-permute-start(bf16[512,768]{1,0:T(8,128)(2,1)} %get-tuple-element.153), channel_id=1, source_target_pairs={{0,24},{8,16},{16,8},{24,0},{1,25},{9,17},{17,9},{25,1},{2,26},{10... | collective-permute-start | bytes 2359304 | tf_op jit(solution)/shard_map/ppermute | solution.py:37
  449.4 34.2 %copy-start.9 = (f32[512,768]{1,0:T(8,128)S(1)}, f32[512,768]{1,0:T(8,128)}, u32[]{:S(2)}) copy-start(f32[512,768]{1,0:T(8,128)} %get-tuple-element.150) | copy-start | bytes 4718596
  480.0 5.3 collective-permute-start.31
  481.3 4.8 collective-permute-start.32
  482.8 3.9 collective-permute-start.30
  501.3 69.8 %copy-start.17 = (f32[1,2048]{1,0:T(1,128)}, f32[1,2048]{1,0:T(1,128)S(1)}, u32[]{:S(2)}) copy-start(f32[1,2048]{1,0:T(1,128)S(1)} %slice.134) | copy-start | bytes 24580
  (10 other events, 43.0 us)
Sparse Core Ops, SparseCore 0:
  13.9 52.2 all-gather.10
  136.9 53.3 reduce-scatter.1
  193.4 45.3 all-gather.12
  273.5 44.9 all-gather.14
  319.9 62.8 all-gather.16
  384.9 103.5 all-gather.18
  490.7 68.4 all-gather.20

commit v8 on v7

--- a/solution.py
+++ b/solution.py
@@ -1013,7 +1013,7 @@
     beside = jnp.concatenate([qkv_grad, first.astype(low), (high - first).astype(low)])
 
     down_weight_grad, out_weight_grad = widen_rows(all_a, all_b, head_width, width)
-    all_qkv = gather(after(beside, all_up))
+    all_qkv = gather(beside)
     up_weight_grad = widen_columns(all_up, depth, 1)
     all_qkv = after(all_qkv, down_weight_grad, up_weight_grad)
     qkv_weight_grad = widen_columns(all_qkv, depth, 3)

time: 582 us -> 582 us (level)
  transfers between devices with their start and end apart: 40 -> 40, of which waited for: 20 -> 19; matrix products, arithmetic and copies ran while one was open for 8% -> 8% of each run, Pallas kernels for 27% -> 27%
where the time goes in v8:
time: 582 us; the launch traced here: 580 us
  waiting for transfers between devices  266 us (46%)
  Pallas kernels  177 us (30%)
  starting transfers between devices  61.2 us (11%)
  other arithmetic  35.2 us (6%)
  between operations  17 us (3%)
  local copies, waits for them, and re-layouts  13.8 us (2%)
  matrix products  9.3 us (2%)
    ppermute x28, waiting for transfers between devices, swap(): lax.ppermute(array, axis, [(s, s ^ bit) for s in range(lax.axis_size(axis...  74.5 us
    ppermute x5, waiting for transfers between devices, between(): lax.ppermute(array, 'seq', [(2 * a + core, 2 * b + core) for a, b in pair...  53.3 us
    all_gather x4, waiting for transfers between devices, gather(): return lax.all_gather(array, 'seq', axis=0, tiled=False)  48.1 us
    all_gather x2, waiting for transfers between devices, gather_seq(): return lax.all_gather(rows, 'seq', axis=0, tiled=True)  45.3 us
    reduce_scatter x1, waiting for transfers between devices, scatter_seq(): return lax.psum_scatter(partial, 'seq', scatter_dimension=0, tiled=True)  44.9 us
    ppermute x28, starting transfers between devices, swap(): lax.ppermute(array, axis, [(s, s ^ bit) for s in range(lax.axis_size(axis...  33.6 us
    pallas_call x1, Pallas kernels, attend_back(): pl.pallas_call(functools.partial(attend_back_kernel, 128), grid=(1,), in_...  29.4 us
    ppermute x5, starting transfers between devices, between(): lax.ppermute(array, 'seq', [(2 * a + core, 2 * b + core) for a, b in pair...  26.9 us
  transfers between devices with their start and end apart: 40, of which 19 were waited for; matrix products, arithmetic and copies ran while one was open for 8% of the time, Pallas kernels for 27%

profile of v8, /device:TPU:0, one launch (start us, length us, event | category | flops | bytes accessed | tf_op | source)
XLA Modules:
  0.0 579.7 jit_solution(9983621246004632985)
XLA Ops:
  7.2 3.6 pick.2
  10.8 3.0 enter.1
  13.9 3.0 collective-permute-start.3
  18.4 20.3 %collective-permute-done.3.refs_5_.refs_2_ = bf16[272,1792]{1,0:T(8,128)(2,1)S(1)} collective-permute-done((bf16[272,1792]{1,0:T(8,128)(2,1)}, bf16[272,1792]{1,0:T(8,128)(2,1)S(1)}, u32[]{:S(2)}, u32[]{:S(2)}) %collective-permute-start.3) | collective-permute-done | bytes 974880 | tf_op jit(solution)/shard_map/ppermute | solution.py:37
  38.7 1.7 collective-permute-start.5
  44.2 3.1 pick.3
  48.0 16.0 %collective-permute-done.4.refs_6_ = bf16[256,1792]{1,0:T(8,128)(2,1)} collective-permute-done((bf16[256,1792]{1,0:T(8,128)(2,1)}, bf16[256,1792]{1,0:T(8,128)(2,1)}, u32[]{:S(2)}, u32[]{:S(2)}) %collective-permute-start.4) | collective-permute-done | bytes 917536 | tf_op jit(solution)/shard_map/ppermute | solution.py:37
  69.0 3.1 fusion.15
  72.1 11.6 %collective-permute-done.2.refs_4_ = bf16[256,1792]{1,0:T(8,128)(2,1)} collective-permute-done((bf16[256,1792]{1,0:T(8,128)(2,1)}, bf16[256,1792]{1,0:T(8,128)(2,1)}, u32[]{:S(2)}, u32[]{:S(2)}) %collective-permute-start.2) | collective-permute-done | bytes 917536 | tf_op jit(solution)/shard_map/ppermute | solution.py:37
  86.2 16.9 %project.1 = (bf16[1024,768]{1,0:T(8,128)(2,1)}, f32[1024,1024]{1,0:T(8,128)}, bf16[1024,1280]{1,0:T(8,128)(2,1)}) custom-call(bf16[1024,2176]{1,0:T(8,128)(2,1)} %all-gather.11.cloned.1.call-done.normed.left, f32[1024,128]{1,0:T(8,128)} %get-tuple-element.180.cosine, f32[1024,128]{1,0:T(8,128)} %get-tuple-element.179.sine, ...), custom_call_target="tpu_custom_call" | custom-call | flops 7516192768 | bytes 26214400 | tf_op jit(solution)/shard_map/project/pallas_call | solution.py:309
  103.1 13.5 %attend.1 = (bf16[1024,1280]{1,0:T(8,128)(2,1)}, f32[1024,128]{1,0:T(8,128)}) custom-call(bf16[1024,768]{1,0:T(8,128)(2,1)} %get-tuple-element.95.qkv, bf16[1024,1280]{1,0:T(8,128)(2,1)} %get-tuple-element.96.stacked), custom_call_target="tpu_custom_call", output_to_operand_aliasing={{0}: (1, {})} | custom-call | flops 2147483648 | bytes 6291456 | tf_op jit(solution)/shard_map/attend/pallas_call | solution.py:481
  118.8 10.2 %emit.2.refs_6_ = bf16[1024,2176]{1,0:T(8,128)(2,1)} custom-call(bf16[1024,1280]{1,0:T(8,128)(2,1)} %get-tuple-element.97.stacked.left, bf16[640,512]{1,0:T(8,128)(2,1)} %get-tuple-element.101.refs_0_, bf16[640,512]{1,0:T(8,128)(2,1)} %get-tuple-element.103.refs_1_, bf16[640,512]{1,0:T(8,128)(2,1)} %collective-permute-done.6.refs_2_, ...), custom_call_target="tpu_custom_call" | custom-call | flops 4026531840 | bytes 9699328 | tf_op jit(solution)/shard_map/emit/pallas_call | solution.py:409
  131.0 5.7 emit.3
  139.2 2.5 pad_maximum_fusion.1.refs_1_
  141.7 2.4 pad_maximum_fusion.2.refs_2_
  145.3 44.9 %reduce-scatter.2.cloned.1.call-done.branches = bf16[128,2176]{1,0:T(8,128)(2,1)} async-done(((bf16[1024,2176]{1,0:T(8,128)(2,1)}), bf16[128,2176]{1,0:T(8,128)(2,1)}) %reduce-scatter.2.cloned.1.call-update) | async-done | bytes 557072 | tf_op jit(solution)/shard_map/reduce_scatter | solution.py:77
  190.3 3.0 grade.1
  193.5 45.3 %all-gather.13.cloned.1.call-done.right.grads = bf16[1024,2048]{1,0:T(8,128)(2,1)} async-done(((bf16[128,2048]{1,0:T(8,128)(2,1)}), bf16[1024,2048]{1,0:T(8,128)(2,1)}) %all-gather.13.cloned.1.call-update) | async-done | bytes 4194320 | tf_op jit(solution)/shard_map/all_gather | solution.py:41
  238.7 2.9 convolution_convert_fusion.2
  248.2 8.3 %outer.3 = (f32[768,512]{1,0:T(8,128)}, bf16[768,512]{1,0:T(8,128)(2,1)}, bf16[768,512]{1,0:T(8,128)(2,1)}, bf16[768,512]{1,0:T(8,128)(2,1)}) custom-call(bf16[1024,1280]{1,0:T(8,128)(2,1)} %get-tuple-element.97.stacked.left, bf16[1024,2048]{1,0:T(8,128)(2,1)} %all-gather.13.cloned.1.call-done.right.grads), custom_call_target="tpu_custom_call" | custom-call | flops 3221225472 | bytes 3145728 | tf_op jit(solution)/shard_map/outer/pallas_call | solution.py:653
  256.6 13.4 %collective-permute-done.13 = bf16[512,512]{1,0:T(8,128)(2,1)} collective-permute-done((bf16[512,512]{1,0:T(8,128)(2,1)}, bf16[512,512]{1,0:T(8,128)(2,1)}, u32[]{:S(2)}, u32[]{:S(2)}) %collective-permute-start.13) | collective-permute-done | bytes 524320 | tf_op jit(solution)/shard_map/ppermute | solution.py:37
  270.0 3.3 add_convert_fusion.5
  276.9 13.7 %reject.1 = (bf16[1024,256]{1,0:T(8,128)(2,1)}, bf16[1024,1792]{1,0:T(8,128)(2,1)}) custom-call(f32[1024,1024]{1,0:T(8,128)} %get-tuple-element.117.hidden, bf16[1024,2048]{1,0:T(8,128)(2,1)} %all-gather.13.cloned.1.call-done.right.grads, bf16[1280,512]{1,0:T(8,128)(2,1)} %pad_maximum_fusion.refs_0_, bf16[1280,512]{1,0:T(8,128)(2,1)} %pad_maximum_fusion.1.refs_1_, ...), custom_call_target="tpu_custom_call" | custom-call | flops 5368709120 | bytes 19922944 | tf_op jit(solution)/shard_map/reject/pallas_call | solution.py:604
  290.6 3.1 slice.95.right
  293.7 10.0 %outer.4 = (f32[512,1024]{1,0:T(8,128)}, bf16[512,1024]{1,0:T(8,128)(2,1)}, bf16[512,1024]{1,0:T(8,128)(2,1)}, bf16[512,1024]{1,0:T(8,128)(2,1)}) custom-call(bf16[1024,2176]{1,0:T(8,128)(2,1)} %all-gather.11.cloned.1.call-done.normed.left, bf16[1024,1024]{1,0:T(8,128)(2,1)} %slice.95.right), custom_call_target="tpu_custom_call" | custom-call | flops 4294967296 | bytes 4194304 | tf_op jit(solution)/shard_map/outer/pallas_call | solution.py:653
  303.7 4.7 collective-permute-done.16
  310.1 2.4 add_convert_fusion.2
  316.2 29.4 %attend_back.1.entered.right = bf16[1024,1792]{1,0:T(8,128)(2,1)} custom-call(bf16[1024,768]{1,0:T(8,128)(2,1)} %get-tuple-element.95.qkv, bf16[1024,256]{1,0:T(8,128)(2,1)} %get-tuple-element.137.grad, f32[1024,128]{1,0:T(8,128)} %get-tuple-element.138.logsum, f32[1024,128]{1,0:T(8,128)} %get-tuple-element.180.cosine, ...), custom_call_target="tpu_custom_call", output_to_operand_aliasing={{}: (5, {})} | custom-call | flops 5368709120 | bytes 6291456 | tf_op jit(solution)/shard_map/attend_back/pallas_call | solution.py:558
  345.5 14.8 %answer.1 = (f32[512,2048]{1,0:T(8,128)}, bf16[512,2048]{1,0:T(8,128)(2,1)}) custom-call(s32[1]{0:T(128)} %bitcast.part, bf16[1024,1792]{1,0:T(8,128)(2,1)} %attend_back.1.entered.right, bf16[256,1792]{1,0:T(8,128)(2,1)} %get-tuple-element.91.refs_0_, bf16[272,1792]{1,0:T(8,128)(2,1)} %get-tuple-element.92.refs_1_.refs_0_, ...), custom_call_target="tpu_custom_call" | custom-call | flops 7516192768 | bytes 17301504 | tf_op jit(solution)/shard_map/answer/pallas_call | solution.py:705
  360.4 3.3 add_convert_fusion
  364.1 4.4 collective-permute-done.24
  368.4 2.8 convert_add_fusion
  371.3 2.0 collective-permute-start.25
  373.4 16.1 %collective-permute-done.25 = bf16[128,2048]{1,0:T(8,128)(2,1)S(1)} collective-permute-done((bf16[128,2048]{1,0:T(8,128)(2,1)S(1)}, bf16[128,2048]{1,0:T(8,128)(2,1)S(1)}, u32[]{:S(2)}, u32[]{:S(2)}) %collective-permute-start.25) | collective-permute-done | bytes 524320 | tf_op jit(solution)/shard_map/ppermute | solution.py:45
  390.3 5.0 collective-permute-start.26
  396.7 4.1 convert_reduce_fusion
  400.8 14.2 %collective-permute-done.26 = bf16[128,2048]{1,0:T(8,128)(2,1)S(1)} collective-permute-done((bf16[128,2048]{1,0:T(8,128)(2,1)S(1)}, bf16[128,2048]{1,0:T(8,128)(2,1)S(1)}, u32[]{:S(2)}, u32[]{:S(2)}) %collective-permute-start.26) | collective-permute-done | bytes 524320 | tf_op jit(solution)/shard_map/ppermute | solution.py:45
  416.4 17.9 %collective-permute-start.27 = (bf16[128,2048]{1,0:T(8,128)(2,1)}, bf16[128,2048]{1,0:T(8,128)(2,1)S(1)}, u32[]{:S(2)}, u32[]{:S(2)}) collective-permute-start(bf16[128,2048]{1,0:T(8,128)(2,1)} %get-tuple-element.170), channel_id=1, source_target_pairs={{0,2},{1,3},{2,4},{3,5},{4,6},{5,7},{8,10},{9,11},{10,12},{11,13},... | collective-permute-start | bytes 1572872 | tf_op jit(solution)/shard_map/ppermute | solution.py:45
  435.6 8.3 %outer.5 = (f32[512,768]{1,0:T(8,128)}, bf16[512,768]{1,0:T(8,128)(2,1)}, bf16[512,768]{1,0:T(8,128)(2,1)}, bf16[512,768]{1,0:T(8,128)(2,1)}) custom-call(bf16[1024,2176]{1,0:T(8,128)(2,1)} %all-gather.11.cloned.1.call-done.normed.left, bf16[1024,1792]{1,0:T(8,128)(2,1)} %attend_back.1.entered.right), custom_call_target="tpu_custom_call" | custom-call | flops 3221225472 | bytes 3145728 | tf_op jit(solution)/shard_map/outer/pallas_call | solution.py:653
  447.4 2.6 convert_reduce_fusion.1
  450.0 5.7 collective-permute-done.27
  455.7 17.3 %collective-permute-done.29 = bf16[128,2048]{1,0:T(8,128)(2,1)} collective-permute-done((bf16[128,2048]{1,0:T(8,128)(2,1)}, bf16[128,2048]{1,0:T(8,128)(2,1)}, u32[]{:S(2)}, u32[]{:S(2)}) %collective-permute-start.29) | collective-permute-done | bytes 524320 | tf_op jit(solution)/shard_map/ppermute | solution.py:45
  472.9 2.5 fusion.1.summed
  475.5 3.8 leave.1
  489.1 12.1 %widen_rows.1 = (f32[8192,512]{1,0:T(8,128)}, f32[2048,512]{1,0:T(8,128)}) custom-call(bf16[8,512,512]{2,1,0:T(8,128)(2,1)} %bitcast.35, bf16[8,768,512]{2,1,0:T(8,128)(2,1)} %bitcast.34), custom_call_target="tpu_custom_call" | custom-call | bytes 31457280 | tf_op jit(solution)/shard_map/widen_rows/pallas_call | solution.py:743
  501.3 9.8 %widen_columns.2 = f32[512,8192]{1,0:T(8,128)} custom-call(bf16[8,512,1024]{2,1,0:T(8,128)(2,1)} %bitcast.31), custom_call_target="tpu_custom_call" | custom-call | bytes 25165824 | tf_op jit(solution)/shard_map/widen_columns/pallas_call | solution.py:778
  511.1 48.0 %all-gather.19.cloned.1.call-done = bf16[4224,768]{1,0:T(8,128)(2,1)} async-done(((bf16[528,768]{1,0:T(8,128)(2,1)}), bf16[4224,768]{1,0:T(8,128)(2,1)}) %all-gather.19.cloned.1.call-update) | async-done | bytes 6488080 | tf_op jit(solution)/shard_map/all_gather | solution.py:950
  561.4 7.9 %widen_columns.3 = f32[512,6144]{1,0:T(8,128)} custom-call(bf16[8,528,768]{2,1,0:T(8,128)(2,1)} %bitcast.33), custom_call_target="tpu_custom_call" | custom-call | bytes 18874368 | tf_op jit(solution)/shard_map/widen_columns/pallas_call | solution.py:778
  (144 shorter events, 59.1 us)
Async XLA Ops:
  7.2 60.4 %all-gather.11.cloned.1.call-start = ((), (), s32[]{:S(2)}) async-start(), calls=%async_computation.1 | async-start | bytes 5013504 | tf_op jit(solution)/shard_map/all_gather | solution.py:41
  13.8 176.4 %reduce-scatter.2.cloned.1.call-start = ((), (), s32[]{:S(2)}) async-start(), calls=%async_computation.2 | async-start | bytes 5013504 | tf_op jit(solution)/shard_map/reduce_scatter | solution.py:77
  13.9 24.8 %collective-permute-start.3 = (bf16[272,1792]{1,0:T(8,128)(2,1)}, bf16[272,1792]{1,0:T(8,128)(2,1)S(1)}, u32[]{:S(2)}, u32[]{:S(2)}) collective-permute-start(bf16[272,1792]{1,0:T(8,128)(2,1)} %get-tuple-element.92.refs_1_.refs_0_), channel_id=1, source_target_pairs={{0,16},{8,24},{16,0},{24,8},{1,17},{9,25},{17,1},{25,9},{2,18},{10... | collective-permute-start | bytes 2924552 | tf_op jit(solution)/shard_map/ppermute | solution.py:37
  16.9 23.5 %collective-permute-start = (bf16[256,1792]{1,0:T(8,128)(2,1)}, bf16[256,1792]{1,0:T(8,128)(2,1)}, u32[]{:S(2)}, u32[]{:S(2)}) collective-permute-start(bf16[256,1792]{1,0:T(8,128)(2,1)} %get-tuple-element.91.refs_0_), channel_id=1, source_target_pairs={{0,8},{8,0},{16,24},{24,16},{1,9},{9,1},{17,25},{25,17},{2,10},{10... | collective-permute-start | bytes 2752520 | tf_op jit(solution)/shard_map/ppermute | solution.py:37
  38.7 25.3 %collective-permute-start.5 = (bf16[272,1792]{1,0:T(8,128)(2,1)S(1)}, bf16[272,1792]{1,0:T(8,128)(2,1)S(1)}, u32[]{:S(2)}, u32[]{:S(2)}) collective-permute-start(bf16[272,1792]{1,0:T(8,128)(2,1)S(1)} %collective-permute-done.3.refs_5_.refs_2_), channel_id=1, source_target_pairs={{0,8},{8,0},{16,24},{24,16},{1,9},{9,1},{17,25},{25,17},{2,10},{10... | collective-permute-start | bytes 2924552 | tf_op jit(solution)/shard_map/ppermute | solution.py:37
  40.4 23.6 %collective-permute-start.4 = (bf16[256,1792]{1,0:T(8,128)(2,1)}, bf16[256,1792]{1,0:T(8,128)(2,1)}, u32[]{:S(2)}, u32[]{:S(2)}) collective-permute-start(bf16[256,1792]{1,0:T(8,128)(2,1)} %collective-permute-done.refs_2_), channel_id=1, source_target_pairs={{0,16},{8,24},{16,0},{24,8},{1,17},{9,25},{17,1},{25,9},{2,18},{10... | collective-permute-start | bytes 2752520 | tf_op jit(solution)/shard_map/ppermute | solution.py:37
  41.9 41.7 %collective-permute-start.2 = (bf16[256,1792]{1,0:T(8,128)(2,1)}, bf16[256,1792]{1,0:T(8,128)(2,1)}, u32[]{:S(2)}, u32[]{:S(2)}) collective-permute-start(bf16[256,1792]{1,0:T(8,128)(2,1)} %get-tuple-element.91.refs_0_), channel_id=1, source_target_pairs={{0,16},{8,24},{16,0},{24,8},{1,17},{9,25},{17,1},{25,9},{2,18},{10... | collective-permute-start | bytes 2752520 | tf_op jit(solution)/shard_map/ppermute | solution.py:37
  42.4 42.8 %collective-permute-start.1 = (bf16[272,1792]{1,0:T(8,128)(2,1)}, bf16[272,1792]{1,0:T(8,128)(2,1)S(1)}, u32[]{:S(2)}, u32[]{:S(2)}) collective-permute-start(bf16[272,1792]{1,0:T(8,128)(2,1)} %get-tuple-element.92.refs_1_.refs_0_), channel_id=1, source_target_pairs={{0,8},{8,0},{16,24},{24,16},{1,9},{9,1},{17,25},{25,17},{2,10},{10... | collective-permute-start | bytes 2924552 | tf_op jit(solution)/shard_map/ppermute | solution.py:37
  64.0 21.2 %copy-start.12 = (bf16[272,1792]{1,0:T(8,128)(2,1)}, bf16[272,1792]{1,0:T(8,128)(2,1)S(1)}, u32[]{:S(2)}) copy-start(bf16[272,1792]{1,0:T(8,128)(2,1)S(1)} %collective-permute-done.5.refs_7_.refs_3_) | copy-start | bytes 2924548
  64.0 19.7 %copy-start.15 = (bf16[640,512]{1,0:T(8,128)(2,1)S(1)}, bf16[640,512]{1,0:T(8,128)(2,1)}, u32[]{:S(2)}) copy-start(bf16[640,512]{1,0:T(8,128)(2,1)} %get-tuple-element.103.refs_1_) | copy-start | bytes 1966084
  64.0 54.8 %collective-permute-start.11 = (bf16[640,512]{1,0:T(8,128)(2,1)}, bf16[640,512]{1,0:T(8,128)(2,1)}, u32[]{:S(2)}, u32[]{:S(2)}) collective-permute-start(bf16[640,512]{1,0:T(8,128)(2,1)} %get-tuple-element.101.refs_0_), channel_id=1, source_target_pairs={{0,16},{8,24},{16,0},{24,8},{1,17},{9,25},{17,1},{25,9},{2,18},{10... | collective-permute-start | bytes 1966088 | tf_op jit(solution)/shard_map/ppermute | solution.py:37
  65.6 51.0 %collective-permute-start.6 = (bf16[640,512]{1,0:T(8,128)(2,1)}, bf16[640,512]{1,0:T(8,128)(2,1)}, u32[]{:S(2)}, u32[]{:S(2)}) collective-permute-start(bf16[640,512]{1,0:T(8,128)(2,1)} %get-tuple-element.101.refs_0_), channel_id=1, source_target_pairs={{0,8},{8,0},{16,24},{24,16},{1,9},{9,1},{17,25},{25,17},{2,10},{10... | collective-permute-start | bytes 1966088 | tf_op jit(solution)/shard_map/ppermute | solution.py:37
  66.4 52.3 %collective-permute-start.10 = (bf16[640,512]{1,0:T(8,128)(2,1)}, bf16[640,512]{1,0:T(8,128)(2,1)}, u32[]{:S(2)}, u32[]{:S(2)}) collective-permute-start(bf16[640,512]{1,0:T(8,128)(2,1)} %get-tuple-element.103.refs_1_), channel_id=1, source_target_pairs={{0,8},{8,0},{16,24},{24,16},{1,9},{9,1},{17,25},{25,17},{2,10},{10... | collective-permute-start | bytes 1966088 | tf_op jit(solution)/shard_map/ppermute | solution.py:37
  83.7 32.9 %collective-permute-start.8 = (bf16[640,512]{1,0:T(8,128)(2,1)S(1)}, bf16[640,512]{1,0:T(8,128)(2,1)}, u32[]{:S(2)}, u32[]{:S(2)}) collective-permute-start(bf16[640,512]{1,0:T(8,128)(2,1)S(1)} %copy-done.15), channel_id=1, source_target_pairs={{0,16},{8,24},{16,0},{24,8},{1,17},{9,25},{17,1},{25,9},{2,18},{10... | collective-permute-start | bytes 1966088 | tf_op jit(solution)/shard_map/ppermute | solution.py:37
  116.6 12.7 %collective-permute-start.7 = (bf16[640,512]{1,0:T(8,128)(2,1)}, bf16[640,512]{1,0:T(8,128)(2,1)S(1)}, u32[]{:S(2)}, u32[]{:S(2)}) collective-permute-start(bf16[640,512]{1,0:T(8,128)(2,1)} %collective-permute-done.6.refs_2_), channel_id=1, source_target_pairs={{0,16},{8,24},{16,0},{24,8},{1,17},{9,25},{17,1},{25,9},{2,18},{10... | collective-permute-start | bytes 1966088 | tf_op jit(solution)/shard_map/ppermute | solution.py:37
  117.3 12.9 %collective-permute-start.9 = (bf16[640,512]{1,0:T(8,128)(2,1)}, bf16[640,512]{1,0:T(8,128)(2,1)S(1)}, u32[]{:S(2)}, u32[]{:S(2)}) collective-permute-start(bf16[640,512]{1,0:T(8,128)(2,1)} %collective-permute-done.8.refs_5_), channel_id=1, source_target_pairs={{0,8},{8,0},{16,24},{24,16},{1,9},{9,1},{17,25},{25,17},{2,10},{10... | collective-permute-start | bytes 1966088 | tf_op jit(solution)/shard_map/ppermute | solution.py:37
  136.8 101.9 %all-gather.13.cloned.1.call-start = ((), (), s32[]{:S(2)}) async-start(), calls=%async_computation.3 | async-start | bytes 4718592 | tf_op jit(solution)/shard_map/all_gather | solution.py:41
  144.1 94.6 %copy-start.7 = (bf16[1024,1280]{1,0:T(8,128)(2,1)S(1)}, bf16[1024,1280]{1,0:T(8,128)(2,1)}, u32[]{:S(2)}) copy-start(bf16[1024,1280]{1,0:T(8,128)(2,1)} %get-tuple-element.97.stacked.left) | copy-start | bytes 7864324
  193.2 167.2 %all-gather.15.cloned.1.call-start = ((), (), s32[]{:S(2)}) async-start(), calls=%async_computation.4 | async-start | bytes 4718592 | tf_op jit(solution)/shard_map/all_gather | solution.py:950
  241.6 15.0 %collective-permute-start.12 = (bf16[512,512]{1,0:T(8,128)(2,1)}, bf16[512,512]{1,0:T(8,128)(2,1)S(1)}, u32[]{:S(2)}, u32[]{:S(2)}) collective-permute-start(bf16[512,512]{1,0:T(8,128)(2,1)} %convolution_convert_fusion.2), channel_id=1, source_target_pairs={{0,8},{8,0},{16,24},{24,16},{1,9},{9,1},{17,25},{25,17},{2,10},{10... | collective-permute-start | bytes 1572872 | tf_op jit(solution)/shard_map/ppermute | solution.py:37
  244.6 25.3 %collective-permute-start.13 = (bf16[512,512]{1,0:T(8,128)(2,1)}, bf16[512,512]{1,0:T(8,128)(2,1)}, u32[]{:S(2)}, u32[]{:S(2)}) collective-permute-start(bf16[512,512]{1,0:T(8,128)(2,1)} %convolution_convert_fusion.1), channel_id=1, source_target_pairs={{0,16},{8,24},{16,0},{24,8},{1,17},{9,25},{17,1},{25,9},{2,18},{10... | collective-permute-start | bytes 1572872 | tf_op jit(solution)/shard_map/ppermute | solution.py:37
  247.6 22.3 %collective-permute-start.14 = (bf16[512,512]{1,0:T(8,128)(2,1)}, bf16[512,512]{1,0:T(8,128)(2,1)S(1)}, u32[]{:S(2)}, u32[]{:S(2)}) collective-permute-start(bf16[512,512]{1,0:T(8,128)(2,1)} %convolution_convert_fusion), channel_id=1, source_target_pairs={{0,24},{8,16},{16,8},{24,0},{1,25},{9,17},{17,9},{25,1},{2,26},{10... | collective-permute-start | bytes 1572872 | tf_op jit(solution)/shard_map/ppermute | solution.py:37
  273.3 202.1 %all-gather.17.cloned.1.call-start = ((), (), s32[]{:S(2)}) async-start(), calls=%async_computation.5 | async-start | bytes 7077888 | tf_op jit(solution)/shard_map/all_gather | solution.py:950
  273.4 30.4 %collective-permute-start.15 = (bf16[768,512]{1,0:T(8,128)(2,1)}, bf16[768,512]{1,0:T(8,128)(2,1)S(1)}, u32[]{:S(2)}, u32[]{:S(2)}) collective-permute-start(bf16[768,512]{1,0:T(8,128)(2,1)} %get-tuple-element.114), channel_id=1, source_target_pairs={{0,8},{8,0},{16,24},{24,16},{1,9},{9,1},{17,25},{25,17},{2,10},{10... | collective-permute-start | bytes 2359304 | tf_op jit(solution)/shard_map/ppermute | solution.py:37
  274.0 34.5 %collective-permute-start.16 = (bf16[768,512]{1,0:T(8,128)(2,1)}, bf16[768,512]{1,0:T(8,128)(2,1)S(1)}, u32[]{:S(2)}, u32[]{:S(2)}) collective-permute-start(bf16[768,512]{1,0:T(8,128)(2,1)} %get-tuple-element.115), channel_id=1, source_target_pairs={{0,16},{8,24},{16,0},{24,8},{1,17},{9,25},{17,1},{25,9},{2,18},{10... | collective-permute-start | bytes 2359304 | tf_op jit(solution)/shard_map/ppermute | solution.py:37
  275.5 34.6 %collective-permute-start.17 = (bf16[768,512]{1,0:T(8,128)(2,1)}, bf16[768,512]{1,0:T(8,128)(2,1)}, u32[]{:S(2)}, u32[]{:S(2)}) collective-permute-start(bf16[768,512]{1,0:T(8,128)(2,1)} %get-tuple-element.116), channel_id=1, source_target_pairs={{0,24},{8,16},{16,8},{24,0},{1,25},{9,17},{17,9},{25,1},{2,26},{10... | collective-permute-start | bytes 2359304 | tf_op jit(solution)/shard_map/ppermute | solution.py:37
  293.7 16.4 %copy-start.10 = (f32[768,512]{1,0:T(8,128)S(1)}, f32[768,512]{1,0:T(8,128)}, u32[]{:S(2)}) copy-start(f32[768,512]{1,0:T(8,128)} %get-tuple-element.133) | copy-start | bytes 4718596
  312.6 188.7 %all-gather.21.cloned.1.call-start = ((), (), s32[]{:S(2)}) async-start(), calls=%async_computation.7 | async-start | bytes 9437184 | tf_op jit(solution)/shard_map/all_gather | solution.py:950
  312.6 47.8 %collective-permute-start.18 = (bf16[512,1024]{1,0:T(8,128)(2,1)}, bf16[512,1024]{1,0:T(8,128)(2,1)S(1)}, u32[]{:S(2)}, u32[]{:S(2)}) collective-permute-start(bf16[512,1024]{1,0:T(8,128)(2,1)} %get-tuple-element.141), channel_id=1, source_target_pairs={{0,8},{8,0},{16,24},{24,16},{1,9},{9,1},{17,25},{25,17},{2,10},{10... | collective-permute-start | bytes 3145736 | tf_op jit(solution)/shard_map/ppermute | solution.py:37
  313.4 47.0 %collective-permute-start.19 = (bf16[512,1024]{1,0:T(8,128)(2,1)}, bf16[512,1024]{1,0:T(8,128)(2,1)}, u32[]{:S(2)}, u32[]{:S(2)}) collective-permute-start(bf16[512,1024]{1,0:T(8,128)(2,1)} %get-tuple-element.142), channel_id=1, source_target_pairs={{0,16},{8,24},{16,0},{24,8},{1,17},{9,25},{17,1},{25,9},{2,18},{10... | collective-permute-start | bytes 3145736 | tf_op jit(solution)/shard_map/ppermute | solution.py:37
  314.9 45.5 %collective-permute-start.20 = (bf16[512,1024]{1,0:T(8,128)(2,1)}, bf16[512,1024]{1,0:T(8,128)(2,1)}, u32[]{:S(2)}, u32[]{:S(2)}) collective-permute-start(bf16[512,1024]{1,0:T(8,128)(2,1)} %get-tuple-element.143), channel_id=1, source_target_pairs={{0,24},{8,16},{16,8},{24,0},{1,25},{9,17},{17,9},{25,1},{2,26},{10... | collective-permute-start | bytes 3145736 | tf_op jit(solution)/shard_map/ppermute | solution.py:37
  363.7 195.4 %all-gather.19.cloned.1.call-start = ((), (), s32[]{:S(2)}) async-start(), calls=%async_computation.6 | async-start | bytes 7299072 | tf_op jit(solution)/shard_map/all_gather | solution.py:950
  364.0 4.4 collective-permute-start.24
  371.3 18.2 %copy-start = (f32[512,2048]{1,0:T(8,128)}, f32[512,2048]{1,0:T(8,128)S(1)}, u32[]{:S(2)}) copy-start(f32[512,2048]{1,0:T(8,128)S(1)} %convert_add_fusion) | copy-start | bytes 12582916
  371.3 18.1 %collective-permute-start.25 = (bf16[128,2048]{1,0:T(8,128)(2,1)S(1)}, bf16[128,2048]{1,0:T(8,128)(2,1)S(1)}, u32[]{:S(2)}, u32[]{:S(2)}) collective-permute-start(bf16[128,2048]{1,0:T(8,128)(2,1)S(1)} %slice.184), channel_id=1, source_target_pairs={{0,2},{1,3},{6,4},{7,5},{8,10},{9,11},{14,12},{15,13},{16,18},{17,... | collective-permute-start | bytes 1572872 | tf_op jit(solution)/shard_map/ppermute | solution.py:45
  389.6 11.3 %collective-permute-start.28 = (bf16[128,2048]{1,0:T(8,128)(2,1)S(1)}, bf16[128,2048]{1,0:T(8,128)(2,1)S(1)}, u32[]{:S(2)}, u32[]{:S(2)}) collective-permute-start(bf16[128,2048]{1,0:T(8,128)(2,1)S(1)} %fusion), channel_id=1, source_target_pairs={{6,4},{7,5},{4,2},{5,3},{14,12},{15,13},{12,10},{13,11},{22,20},{2... | collective-permute-start | bytes 1572872 | tf_op jit(solution)/shard_map/ppermute | solution.py:45
  390.3 24.8 %collective-permute-start.26 = (bf16[128,2048]{1,0:T(8,128)(2,1)S(1)}, bf16[128,2048]{1,0:T(8,128)(2,1)S(1)}, u32[]{:S(2)}, u32[]{:S(2)}) collective-permute-start(bf16[128,2048]{1,0:T(8,128)(2,1)S(1)} %fusion), channel_id=1, source_target_pairs={{0,2},{1,3},{2,4},{3,5},{8,10},{9,11},{10,12},{11,13},{16,18},{17,... | collective-permute-start | bytes 1572872 | tf_op jit(solution)/shard_map/ppermute | solution.py:45
  395.3 19.7 %copy-start.1 = (f32[512,2048]{1,0:T(8,128)S(1)}, f32[512,2048]{1,0:T(8,128)}, u32[]{:S(2)}) copy-start(f32[512,2048]{1,0:T(8,128)} %copy-done) | copy-start | bytes 12582916
  416.4 39.3 %collective-permute-start.27 = (bf16[128,2048]{1,0:T(8,128)(2,1)}, bf16[128,2048]{1,0:T(8,128)(2,1)S(1)}, u32[]{:S(2)}, u32[]{:S(2)}) collective-permute-start(bf16[128,2048]{1,0:T(8,128)(2,1)} %get-tuple-element.170), channel_id=1, source_target_pairs={{0,2},{1,3},{2,4},{3,5},{4,6},{5,7},{8,10},{9,11},{10,12},{11,13},... | collective-permute-start | bytes 1572872 | tf_op jit(solution)/shard_map/ppermute | solution.py:45
  434.3 38.7 %collective-permute-start.29 = (bf16[128,2048]{1,0:T(8,128)(2,1)}, bf16[128,2048]{1,0:T(8,128)(2,1)}, u32[]{:S(2)}, u32[]{:S(2)}) collective-permute-start(bf16[128,2048]{1,0:T(8,128)(2,1)} %get-tuple-element.171), channel_id=1, source_target_pairs={{6,4},{7,5},{4,2},{5,3},{2,0},{3,1},{14,12},{15,13},{12,10},{13,11... | collective-permute-start | bytes 1572872 | tf_op jit(solution)/shard_map/ppermute | solution.py:45
  443.9 31.5 %collective-permute-start.21 = (bf16[512,768]{1,0:T(8,128)(2,1)}, bf16[512,768]{1,0:T(8,128)(2,1)S(1)}, u32[]{:S(2)}, u32[]{:S(2)}) collective-permute-start(bf16[512,768]{1,0:T(8,128)(2,1)} %get-tuple-element.150), channel_id=1, source_target_pairs={{0,8},{8,0},{16,24},{24,16},{1,9},{9,1},{17,25},{25,17},{2,10},{10... | collective-permute-start | bytes 2359304 | tf_op jit(solution)/shard_map/ppermute | solution.py:37
  445.2 30.2 %collective-permute-start.22 = (bf16[512,768]{1,0:T(8,128)(2,1)}, bf16[512,768]{1,0:T(8,128)(2,1)}, u32[]{:S(2)}, u32[]{:S(2)}) collective-permute-start(bf16[512,768]{1,0:T(8,128)(2,1)} %get-tuple-element.151), channel_id=1, source_target_pairs={{0,16},{8,24},{16,0},{24,8},{1,17},{9,25},{17,1},{25,9},{2,18},{10... | collective-permute-start | bytes 2359304 | tf_op jit(solution)/shard_map/ppermute | solution.py:37
  446.7 28.8 %collective-permute-start.23 = (bf16[512,768]{1,0:T(8,128)(2,1)}, bf16[512,768]{1,0:T(8,128)(2,1)}, u32[]{:S(2)}, u32[]{:S(2)}) collective-permute-start(bf16[512,768]{1,0:T(8,128)(2,1)} %get-tuple-element.152), channel_id=1, source_target_pairs={{0,24},{8,16},{16,8},{24,0},{1,25},{9,17},{17,9},{25,1},{2,26},{10... | collective-permute-start | bytes 2359304 | tf_op jit(solution)/shard_map/ppermute | solution.py:37
  450.0 34.4 %copy-start.9 = (f32[512,768]{1,0:T(8,128)S(1)}, f32[512,768]{1,0:T(8,128)}, u32[]{:S(2)}) copy-start(f32[512,768]{1,0:T(8,128)} %get-tuple-element.149) | copy-start | bytes 4718596
  480.8 5.3 collective-permute-start.31
  481.9 4.8 collective-permute-start.32
  483.4 3.9 collective-permute-start.30
  501.3 69.9 %copy-start.17 = (f32[1,2048]{1,0:T(1,128)}, f32[1,2048]{1,0:T(1,128)S(1)}, u32[]{:S(2)}) copy-start(f32[1,2048]{1,0:T(1,128)S(1)} %slice.134) | copy-start | bytes 24580
  (10 other events, 43.0 us)
Sparse Core Ops, SparseCore 0:
  13.9 52.2 all-gather.10
  136.9 53.3 reduce-scatter.1
  193.4 45.3 all-gather.12
  273.5 44.9 all-gather.14
  319.9 62.7 all-gather.16
  384.2 104.1 all-gather.20
  490.7 68.4 all-gather.18
